TPU v7x, 256 devices: a whole 4x4x8 slice. The times are simulated.
256 devices in a mesh: row: 8 (over y, z_hi), col: 4 (over x), layer: 8 (over z_lo, core).
Axes of the slice: x: 4, y: 4, z: 8 (z_hi: 2, z_lo: 4; z = z_hi * 4 + z_lo), core: 2. Of those that a mesh axis runs over, the one named last changes fastest.
Arguments:
- coeffs: float32 [4096, 4096], P(('row', 'col'), 'layer'), may hold values from -6 to 6
- hblocks: float32 [256, 128, 128], P('layer'), may hold values from -0.1875 to 0.1875
- hcount: int32 [32], replicated, may hold values from 1 to 16, 256 in all
- hcols: int32 [256], P('layer'), may hold values from 0 to 31
Outputs:
- sigma: float32 [4096, 4096], P(('row', 'col'), 'layer')
Inputs may be any that keep to these rules, and one draw needn't show every extreme that they name: `hcount`: the blocks of a row stand together in hcols and hblocks, rows in order; the counts sum to 256 and some row holds 16. `hcols`: a row may name a column more than once; such blocks add.
All inputs are finite; a program needn't handle non-finite values.
Results may differ from a plain program's by a relative error of at most 0.00007.
Values sent between devices are 32-bit elements; how exact they have to be, the bound alone decides.
No kernel may reach another device: no remote copies, remote signals or barrier semaphores. Data moves between devices by JAX's collectives and lax.ppermute only.
A program may use at most 64 MiB of HBM per device.

v0:
```python
import jax
import jax.numpy as jnp
from jax import lax
from jax.sharding import PartitionSpec as P


def apply_blocks(string_rows, blocks, columns, owners, block_count):
    row_count = string_rows.shape[0]
    strings = string_rows.shape[1]
    block_size = blocks.shape[1]
    tiled = string_rows.reshape(row_count, block_count, block_size)
    picked = jnp.take(tiled, columns, axis=1)
    products = jnp.einsum("rzc,zbc->rzb", picked, blocks, precision=lax.Precision.HIGHEST)
    chooser = (owners[:, None] == jnp.arange(block_count, dtype=jnp.int32)[None, :]).astype(
        jnp.float32
    )
    summed = jnp.einsum("rzb,zi->rib", products, chooser, precision=lax.Precision.HIGHEST)
    return summed.reshape(row_count, strings)


def local(coeffs, hblocks, hcount, hcols):
    layer_size = lax.axis_size("layer")
    group_size = lax.axis_size(("row", "col"))
    my_layer = lax.axis_index("layer")
    full_rows = lax.all_gather(coeffs, "layer", axis=1, tiled=True)
    row_count = full_rows.shape[0]
    strings = full_rows.shape[1]
    block_size = hblocks.shape[1]
    block_count = strings // block_size
    share_size = hblocks.shape[0]
    row_end = jnp.cumsum(hcount)
    global_index = my_layer * share_size + jnp.arange(share_size, dtype=jnp.int32)
    owners = jnp.sum((row_end[None, :] <= global_index[:, None]).astype(jnp.int32), axis=1)
    beta_part = apply_blocks(full_rows, hblocks, hcols, owners, block_count)
    subset_size = strings // (layer_size * group_size)
    flipped = full_rows.T.reshape(layer_size, group_size, subset_size, row_count)
    moved = lax.all_to_all(flipped, ("row", "col"), split_axis=1, concat_axis=3, tiled=True)
    turned = moved.reshape(layer_size * subset_size, strings)
    alpha_part = apply_blocks(turned, hblocks, hcols, owners, block_count)
    sectioned = alpha_part.reshape(layer_size, subset_size, strings)
    sectioned = lax.all_to_all(sectioned, ("row", "col"), split_axis=2, concat_axis=1, tiled=True)
    joined = beta_part + sectioned.reshape(strings, row_count).T
    return lax.psum_scatter(joined, "layer", scatter_dimension=1, tiled=True)


def solution(mesh):
    in_specs = (P(("row", "col"), "layer"), P("layer", None, None), P(), P("layer"))
    out_specs = P(("row", "col"), "layer")
    return jax.shard_map(local, mesh=mesh, in_specs=in_specs, out_specs=out_specs, check_vma=False)
```

profile of v0, /device:TPU:32, one launch (start us, length us, event | category | flops | bytes accessed | tf_op | source)
XLA Modules:
  0.0 283.4 jit_solution(10622750448958712945)
XLA Ops:
  6.5 1.9 copy.37
  8.5 0.0 all-gather.2.cloned.1.call-update
  8.5 39.6 %all-gather.2.cloned.1.call-done = f32[128,4096]{0,1:T(8,128)} async-done(((f32[128,512]{0,1:T(8,128)}), f32[128,4096]{0,1:T(8,128)}) %all-gather.2.cloned.1.call-update) | async-done | bytes 2097168 | tf_op jit(solution)/shard_map/all_gather | solution.py:25
  48.1 3.2 %copy.40 = f32[8,32,16,128]{3,2,0,1:T(8,128)} copy(f32[8,32,16,128]{3,2,1,0:T(8,128)} %bitcast.47) | data formatting | bytes 4194304 | tf_op jit(solution)/shard_map/reshape | solution.py:36
  51.3 10.3 %all-to-all-start = ((f32[8,32,16,128]{3,2,0,1:T(8,128)}), f32[8,32,16,128]{3,2,0,1:T(8,128)}, u32[]{:S(2)}, u32[]{:S(2)}) async-start(f32[8,32,16,128]{3,2,0,1:T(8,128)} %copy.40), calls=%async_computation | async-start | bytes 4194304 | tf_op jit(solution)/shard_map/all_to_all | solution.py:37
  61.6 0.1 copy.36
  61.7 0.1 reduce-window.8
  61.8 0.1 reduce
  61.9 0.2 convert_reduce_fusion
  62.1 35.2 %all-to-all-done = f32[8,32,16,128]{3,2,0,1:T(8,128)} async-done(((f32[8,32,16,128]{3,2,0,1:T(8,128)}), f32[8,32,16,128]{3,2,0,1:T(8,128)}, u32[]{:S(2)}, u32[]{:S(2)}) %all-to-all-start) | async-done | bytes 2097184 | tf_op jit(solution)/shard_map/all_to_all | solution.py:37
  97.3 3.6 %gather_fusion.1 = f32[32,128,128]{2,1,0:T(8,128)} fusion(f32[128,32,128]{2,0,1:T(8,128)} %bitcast.12, s32[1024]{0:T(1024)S(1)} %pad_clamp_fusion), kind=kCustom, calls=%fused_computation.1.clone | custom fusion | bytes 4194432 | tf_op jit(solution)/shard_map/jit(_take)/gather | solution.py:12
  100.9 6.1 %fusion.19 = f32[128,32,128]{2,0,1:T(8,128)S(1)} fusion(f32[32,128,128]{2,1,0:T(8,128)S(1)} %copy-done, f32[32,128,128]{2,1,0:T(8,128)} %gather_fusion.1, pred[32]{0:T(512)(128)(4,1)S(1)} %compare_and_fusion), kind=kOutput, calls=%fused_computation.16 | convolution fusion | flops 805830656 | bytes 6291488 | tf_op jit(solution)/shard_map/rzc,zbc->rzb/dot_general | solution.py:13
  107.0 3.8 %fusion.13 = f32[128,32,128]{2,1,0:T(8,128)} fusion(f32[128,32,128]{2,0,1:T(8,128)S(1)} %fusion.19, s32[32]{0:T(128)S(1)} %convert_reduce_fusion), kind=kOutput, calls=%fused_computation.14 | convolution fusion | flops 201327616 | bytes 4194432 | tf_op jit(solution)/shard_map/rzb,zi->rib/dot_general | solution.py:17
  110.8 2.7 reshape_reshape.7
  113.5 9.6 %copy.44 = f32[8,16,4096]{1,0,2:T(8,128)} copy(f32[8,16,4096]{2,1,0:T(8,128)} %reshape_reshape.7) | data formatting | bytes 4194304 | tf_op jit(solution)/shard_map/reshape;reshape | solution.py:40
  123.0 13.0 %reshape.78 = f32[32,1,16384]{2,1,0:T(1,128)} reshape(f32[4096,8,16]{2,1,0:T(8,128)} %bitcast.45) | data formatting | bytes 4194304
  136.0 11.2 %all-to-all-start.1 = ((f32[32,1,16384]{2,1,0:T(1,128)}), f32[32,1,16384]{2,1,0:T(1,128)}, u32[]{:S(2)}, u32[]{:S(2)}) async-start(f32[32,1,16384]{2,1,0:T(1,128)} %reshape.78), calls=%async_computation.1 | async-start | bytes 4194304 | tf_op jit(solution)/shard_map/all_to_all | solution.py:41
  147.3 0.2 reduce-scatter.2.cloned.1.call-start
  147.5 2.9 %copy.38 = f32[128,32,128]{2,0,1:T(8,128)} copy(f32[128,32,128]{0,2,1:T(8,128)} %bitcast.48) | data formatting | bytes 4194304 | tf_op jit(solution)/shard_map/reshape | solution.py:11
  150.4 3.6 %gather_fusion = f32[32,128,128]{2,1,0:T(8,128)} fusion(f32[128,32,128]{2,0,1:T(8,128)} %copy.38, s32[1024]{0:T(1024)S(1)} %pad_clamp_fusion), kind=kCustom, calls=%fused_computation.clone | custom fusion | bytes 4194432 | tf_op jit(solution)/shard_map/jit(_take)/gather | solution.py:12
  154.0 6.1 %fusion.16 = f32[128,32,128]{2,0,1:T(8,128)S(1)} fusion(f32[32,128,128]{2,1,0:T(8,128)S(1)} %copy-done, f32[32,128,128]{2,1,0:T(8,128)} %gather_fusion, pred[32]{0:T(512)(128)(4,1)S(1)} %compare_and_fusion), kind=kOutput, calls=%fused_computation.15 | convolution fusion | flops 805830656 | bytes 6291488 | tf_op jit(solution)/shard_map/rzc,zbc->rzb/dot_general | solution.py:13
  160.1 2.4 fusion.10
  162.5 1.9 copy.49
  164.4 4.6 %all-to-all-done.1 = f32[32,1,16384]{2,1,0:T(1,128)} async-done(((f32[32,1,16384]{2,1,0:T(1,128)}), f32[32,1,16384]{2,1,0:T(1,128)}, u32[]{:S(2)}, u32[]{:S(2)}) %all-to-all-start.1) | async-done | bytes 2097184 | tf_op jit(solution)/shard_map/all_to_all | solution.py:41
  169.0 0.5 broadcast.41
  169.5 7.4 %reduce.1 = f32[32,16384]{1,0:T(8,128)S(1)} reduce(f32[32,1,16384]{2,1,0:T(1,128)} %all-to-all-done.1, f32[]{:T(128)} %broadcast.41), dimensions={1}, to_apply=%all_to_all.25.reduce_sub_computation | reduce | bytes 4194308 | tf_op jit(solution)/shard_map/all_to_all | solution.py:41
  176.9 8.4 %reshape.79 = f32[4096,8,16]{2,1,0:T(8,128)} reshape(f32[32,16384]{1,0:T(8,128)S(1)} %reduce.1) | data formatting | bytes 4194304
  185.3 10.6 %copy.46 = f32[8,32,16,128]{3,2,1,0:T(8,128)} copy(f32[8,32,16,128]{2,0,3,1:T(8,128)} %bitcast.46) | data formatting | bytes 4194304 | tf_op jit(solution)/shard_map/all_to_all | solution.py:41
  195.9 3.9 %bitcast_add_fusion = f32[128,4096]{0,1:T(8,128)} fusion(f32[8,32,16,128]{3,2,1,0:T(8,128)} %copy.46, f32[128,32,128]{0,2,1:T(8,128)} %copy.49), kind=kLoop, calls=%fused_computation.2 | loop fusion | flops 524288 | bytes 6291456 | tf_op jit(solution)/shard_map/add | solution.py:42
  199.9 0.0 reduce-scatter.2.cloned.1.call-update
  199.9 74.9 %reduce-scatter.2.cloned.1.call-done = f32[128,512]{0,1:T(8,128)} async-done(((f32[128,4096]{0,1:T(8,128)}), f32[128,512]{0,1:T(8,128)}) %reduce-scatter.2.cloned.1.call-update) | async-done | bytes 262160 | tf_op jit(solution)/shard_map/reduce_scatter | solution.py:43
  274.8 1.8 copy.48
  (13 shorter events, 0.0 us)
Async XLA Ops:
  6.5 94.4 %copy-start = (f32[32,128,128]{2,1,0:T(8,128)S(1)}, f32[32,128,128]{2,1,0:T(8,128)}, u32[]{:S(2)}) copy-start(f32[32,128,128]{2,1,0:T(8,128)} %param.7) | copy-start | bytes 6291460
  6.5 41.6 %all-gather.2.cloned.1.call-start = ((), (), s32[]{:S(2)}) async-start(), calls=%async_computation.3 | async-start | bytes 2359296 | tf_op jit(solution)/shard_map/all_gather | solution.py:25
  51.3 10.3 %copy-start.2 = (s32[32]{0:T(128)S(1)}, s32[32]{0:T(128)}, u32[]{:S(2)}) copy-start(s32[32]{0:T(128)} %param.8) | copy-start | bytes 388
  51.3 10.6 %copy-start.3 = (s32[32]{0:T(128)S(1)}, s32[32]{0:T(128)}, u32[]{:S(2)}) copy-start(s32[32]{0:T(128)} %param.9) | copy-start | bytes 388
  51.3 46.0 %all-to-all-start = ((f32[8,32,16,128]{3,2,0,1:T(8,128)}), f32[8,32,16,128]{3,2,0,1:T(8,128)}, u32[]{:S(2)}, u32[]{:S(2)}) async-start(f32[8,32,16,128]{3,2,0,1:T(8,128)} %copy.40), calls=%async_computation | async-start | bytes 4194304 | tf_op jit(solution)/shard_map/all_to_all | solution.py:37
  136.0 33.0 %all-to-all-start.1 = ((f32[32,1,16384]{2,1,0:T(1,128)}), f32[32,1,16384]{2,1,0:T(1,128)}, u32[]{:S(2)}, u32[]{:S(2)}) async-start(f32[32,1,16384]{2,1,0:T(1,128)} %reshape.78), calls=%async_computation.1 | async-start | bytes 4194304 | tf_op jit(solution)/shard_map/all_to_all | solution.py:41
  147.3 127.5 %reduce-scatter.2.cloned.1.call-start = ((), (), s32[]{:S(2)}) async-start(), calls=%async_computation.4 | async-start | bytes 2359296 | tf_op jit(solution)/shard_map/reduce_scatter | solution.py:43
  195.9 80.7 %copy-start.1 = (f32[32,128,128]{2,1,0:T(8,128)S(1)}, f32[32,128,128]{2,1,0:T(8,128)}, u32[]{:S(2)}) copy-start(f32[32,128,128]{2,1,0:T(8,128)} %param.7) | copy-start | bytes 6291460
Sparse Core Ops, SparseCore 0:
  9.1 38.9 all-gather.1
  200.0 74.7 reduce-scatter.1
where the time goes:
time: 289 us; the launch traced here: 283 us
  waiting for transfers between devices  154 us (53%)
  local copies, waits for them, and re-layouts  63.7 us (22%)
  starting transfers between devices  21.8 us (8%)
  matrix products  18.3 us (6%)
  between operations  13.5 us (5%)
  other arithmetic  11.7 us (4%)
    reduce_scatter x1, waiting for transfers between devices, local(): return lax.psum_scatter(joined, 'layer', scatter_dimension=1, tiled=True)  74.9 us
    all_gather x1, waiting for transfers between devices, local(): full_rows = lax.all_gather(coeffs, 'layer', axis=1, tiled=True)  39.6 us
    all_to_all x1, waiting for transfers between devices, local(): lax.all_to_all(flipped, ('row', 'col'), split_axis=1, concat_axis=3, tile...  35.2 us
    unnamed x11, local copies, waits for them, and re-layouts  23.3 us
    another operation x2, local copies, waits for them, and re-layouts, local(): sectioned = alpha_part.reshape(layer_size, subset_size, strings)  12.3 us
    dot_general x2, matrix products, apply_blocks(): jnp.einsum('rzc,zbc->rzb', picked, blocks, precision=lax.Precision.HIGHEST)  12.1 us
    all_to_all x1, starting transfers between devices, local(): lax.all_to_all(sectioned, ('row', 'col'), split_axis=2, concat_axis=1, ti...  11.2 us
    all_to_all x2, local copies, waits for them, and re-layouts, local(): lax.all_to_all(sectioned, ('row', 'col'), split_axis=2, concat_axis=1, ti...  11.1 us
  transfers between devices with their start and end apart: 4, of which 4 were waited for; matrix products, arithmetic and copies ran while one was open for 6% of the time, Pallas kernels for 0%

commit v1 on v0

v1 whole, which is shorter than its diff:
```python
import functools

import jax
import jax.numpy as jnp
from jax import lax
from jax.experimental import pallas as pl
from jax.experimental.pallas import tpu as pltpu
from jax.sharding import Mesh
from jax.sharding import PartitionSpec as P

ROWS = ("y", "h", "x")
ANY = pl.BlockSpec(memory_space=pl.ANY)
VMEM = pl.BlockSpec(memory_space=pltpu.VMEM)
SMEM = pl.BlockSpec(memory_space=pltpu.SMEM)
F32 = jnp.float32
BF16 = jnp.bfloat16


def params(mib):
    return pltpu.CompilerParams(vmem_limit_bytes=mib << 20)


def cost(flops, moved):
    return pl.CostEstimate(flops=flops, bytes_accessed=moved, transcendentals=0)


def shape(*dims):
    return jax.ShapeDtypeStruct(dims, F32)


def prep_kernel(where, c_ref, at_ref, keep_ref, send_ref):
    core = where[3]
    for t in range(4):
        turned = jnp.transpose(c_ref[:, 128 * t : 128 * (t + 1)]).reshape(8, 16, 128)
        at_ref[8 * t : 8 * (t + 1), 0] = turned
        at_ref[8 * t : 8 * (t + 1), 1] = turned
    for q in range(2):
        for t in range(4):
            span = slice(128 * t, 128 * (t + 1))
            mine = pl.multiple_of(64 * q + 32 * core, 32)
            other = pl.multiple_of(64 * q + 32 * (1 - core), 32)
            keep_ref[q, t] = c_ref[pl.ds(mine, 32), span]
            send_ref[q, t] = c_ref[pl.ds(other, 32), span]


def product_kernel(
    where, cols, owners, b0, b1, b2, b3, at_ref, h0, h1, h2, h3, oa_ref, ob0, ob1, ob2, ob3,
    beta, alpha, stack, hbuf, acc, sem_a, sem_h,
):
    y, x, z = where[0], where[1], where[2]
    parts = (b0, b1, b2, b3)
    loads = []
    for k in range(4):
        home = jnp.bitwise_and(z - k + 4, 3)
        loads.append(
            pltpu.make_async_copy(parts[k], beta.at[pl.ds(8 * home, 8)], sem_a.at[k])
        )
    loads.append(pltpu.make_async_copy(at_ref, alpha, sem_a.at[4]))
    for load in loads:
        load.start()
    chunks = []
    for g, h in enumerate((h0, h1, h2, h3)):
        for half in range(2):
            chunks.append(
                pltpu.make_async_copy(
                    h.at[pl.ds(16 * half, 16)],
                    hbuf.at[pl.ds(32 * g + 16 * half, 16)],
                    sem_h.at[2 * g + half],
                )
            )
    for chunk in chunks:
        chunk.start()
    acc[...] = jnp.zeros_like(acc)
    for load in loads:
        load.wait()

    @pl.loop(0, 32)
    def _(j):
        for row, source in ((0, beta), (32, alpha)):
            value = source[j]
            high = value.astype(BF16)
            stack[j, row : row + 32] = high
            stack[j, 64 + row : 96 + row] = (value - high.astype(F32)).astype(BF16)

    def place(g, i):
        if g < 2:
            return 32 * g + i
        ys, xs, b = i // 8, (i // 2) % 4, i % 2
        dy = jnp.where(ys == 1, 3, jnp.where(ys == 0, 0, ys - 1))
        dx = jnp.where(xs == 1, 3, jnp.where(xs == 0, 0, xs - 1))
        return (
            32 * g
            + 8 * jnp.bitwise_and(y + dy, 3)
            + 2 * jnp.bitwise_and(x + dx, 3)
            + b
        )

    contract = (((1,), (1,)), ((), ()))
    for n, chunk in enumerate(chunks):
        chunk.wait()
        g, first = n // 2, 16 * (n % 2)

        @pl.loop(0, 4)
        def _(step, g=g, first=first):
            terms = []
            for u in range(4):
                i = first + 4 * step + u
                at = place(g, i)
                block = hbuf[32 * g + i]
                high = block.astype(BF16)
                low = (block - high.astype(F32)).astype(BF16)
                left = stack[cols[at]]
                one = lax.dot_general(left, high, contract, preferred_element_type=F32)
                two = lax.dot_general(left[:64], low, contract, preferred_element_type=F32)
                terms.append((owners[at], one[:64] + (one[64:] + two)))
            for owner, term in terms:
                acc[owner] += term

    for i in range(32):
        oa_ref[i] = acc[i, 32:]
    for k, out in enumerate((ob0, ob1, ob2, ob3)):
        home = 8 * jnp.bitwise_and(z + k, 3)
        for j in range(8):
            out[j] = acc[home + j, :32]


def middle_kernel(where, r0, r1, r2, r3, keep_ref, send_ref):
    core = where[3]
    for slot, (one, two) in enumerate(((r0, r2), (r1, r3))):
        for t in range(4):
            mine, other = 4 * core + t, 4 * (1 - core) + t
            keep_ref[slot, t] = one[mine] + two[mine]
            send_ref[slot, t] = one[other] + two[other]


def final_kernel(where, ar_ref, keep_ref, got_ref, out_ref):
    q, core = jnp.bitwise_and(where[2], 1), where[3]
    for t in range(4):
        span = slice(128 * t, 128 * (t + 1))
        total = ar_ref[8 * t : 8 * (t + 1), 0] + ar_ref[8 * t : 8 * (t + 1), 1]
        out_ref[:, span] = jnp.transpose(total.reshape(128, 128))
        for slot in range(2):
            base = 64 * jnp.bitwise_xor(q, slot)
            mine = pl.ds(pl.multiple_of(base + 32 * core, 32), 32)
            other = pl.ds(pl.multiple_of(base + 32 * (1 - core), 32), 32)
            out_ref[mine, span] += keep_ref[slot, t]
            out_ref[other, span] += got_ref[slot, t]


def shift(value, axis, by):
    return lax.ppermute(value, axis, [(i, (i + by) % 4) for i in range(4)])


def swap(value):
    return lax.ppermute(value, "c", [(0, 1), (1, 0)])


def pair(value):
    return lax.ppermute(value, "z", [(0, 1), (1, 0), (2, 3), (3, 2)])


def ring(value, axis):
    half = value.shape[0] // 2
    down, up = shift(value, axis, 1), shift(value, axis, -1)
    far = shift(down[:half], axis, 1), shift(up[half:], axis, -1)
    return jnp.concatenate((value, down, up) + far, axis=0)


def local(coeffs, hblocks, hcount, hcols):
    y, x, z, c = (lax.axis_index(n) for n in ("y", "x", "z", "c"))
    where = jnp.stack([y, x, z, c]).astype(jnp.int32)

    at, keep, send = pl.pallas_call(
        prep_kernel,
        out_shape=(shape(32, 2, 16, 128), shape(2, 4, 32, 128), shape(2, 4, 32, 128)),
        in_specs=[SMEM, VMEM],
        out_specs=(VMEM, VMEM, VMEM),
        compiler_params=params(16),
        cost_estimate=cost(0, 1 << 20),
        name="prep",
    )(where, coeffs)

    moved = lax.all_to_all(at.reshape(1024, 128), ROWS + ("z",), 0, 0, tiled=True)
    moved = moved.reshape(32, 32, 128)

    piece = lax.dynamic_slice_in_dim(hblocks, 2 * (4 * y + x), 2, axis=0)
    far = ring(ring(pair(piece), "x"), "y")
    near_swapped = swap(hblocks)
    far_swapped = swap(far)
    near_cols = jnp.concatenate([hcols, swap(hcols)])
    cols = jnp.concatenate([near_cols, pair(near_cols)])
    marks = jnp.arange(32, dtype=jnp.int32)
    row_end = jnp.sum(jnp.where(marks[:, None] <= marks[None, :], hcount[:, None], 0), axis=0)
    shard = jnp.stack([2 * z + c, 2 * z + 1 - c, 2 * (z ^ 1) + c, 2 * (z ^ 1) + 1 - c])
    index = (32 * shard[:, None].astype(jnp.int32) + marks[None, :]).reshape(128)
    owners = jnp.sum((row_end[None, :] <= index[:, None]).astype(jnp.int32), axis=1)

    rows = jnp.where(c == 0, jnp.stack([keep, swap(send)]), jnp.stack([swap(send), keep]))
    rows = rows.transpose(1, 0, 2, 3, 4).reshape(2, 8, 32, 128)
    same = lax.dynamic_index_in_dim(rows, z & 1, 0, keepdims=False)
    differ = lax.dynamic_index_in_dim(rows, 1 - (z & 1), 0, keepdims=False)
    beta = [same, shift(differ, "z", 1), shift(same, "z", 2), shift(differ, "z", 3)]

    oa, *ob = pl.pallas_call(
        product_kernel,
        out_shape=(shape(32, 32, 128),) + (shape(8, 32, 128),) * 4,
        in_specs=[SMEM] * 3 + [ANY] * 9,
        out_specs=(VMEM,) * 5,
        scratch_shapes=[
            pltpu.VMEM((32, 32, 128), F32),
            pltpu.VMEM((32, 32, 128), F32),
            pltpu.VMEM((32, 128, 128), BF16),
            pltpu.VMEM((128, 128, 128), F32),
            pltpu.VMEM((32, 64, 128), F32),
            pltpu.SemaphoreType.DMA((5,)),
            pltpu.SemaphoreType.DMA((8,)),
        ],
        compiler_params=params(40),
        cost_estimate=cost(6 * 128 * 64 * 128 * 128, 10 << 20),
        name="product",
    )(where, cols, owners, *beta, moved, hblocks, near_swapped, far, far_swapped)

    back = lax.all_to_all(oa.reshape(1024, 128), ROWS + ("z",), 0, 0, tiled=True)
    back = back.reshape(32, 2, 16, 128)
    got = [ob[0]] + [shift(ob[k], "z", k) for k in (1, 2, 3)]
    keep, send = pl.pallas_call(
        middle_kernel,
        out_shape=(shape(2, 4, 32, 128), shape(2, 4, 32, 128)),
        in_specs=[SMEM] + [VMEM] * 4,
        out_specs=(VMEM, VMEM),
        compiler_params=params(16),
        cost_estimate=cost(0, 1 << 20),
        name="middle",
    )(where, *got)
    return pl.pallas_call(
        final_kernel,
        out_shape=shape(128, 512),
        in_specs=[SMEM] + [VMEM] * 3,
        out_specs=VMEM,
        compiler_params=params(16),
        cost_estimate=cost(0, 1 << 20),
        name="final",
    )(where, back, keep, swap(send))


def solution(mesh):
    fine = Mesh(mesh.devices.reshape(4, 2, 4, 4, 2), ("y", "h", "x", "z", "c"))
    in_specs = (P(ROWS, ("z", "c")), P(("z", "c"), None, None), P(), P(("z", "c")))
    out_specs = P(ROWS, ("z", "c"))
    return jax.shard_map(local, mesh=fine, in_specs=in_specs, out_specs=out_specs, check_vma=False)
```

time: 289 us -> 136 us (0.47); the launches traced: 283 us -> 135 us
  waiting for transfers between devices: 154 us -> 57.1 us
  local copies, waits for them, and re-layouts: 63.7 us -> 8.34 us
  starting transfers between devices: 21.8 us -> 53.4 us
  matrix products: 18.3 us -> 0 us
  Pallas kernels: 0 us -> 15.4 us
  between operations: 13.5 us -> 0.14 us
  other arithmetic: 11.7 us -> 0.5 us
    reduce_scatter x1 -> x0, waiting for transfers between devices: 74.9 us -> none  [local(): return lax.psum_scatter(joined, 'layer', scatter_dimension=1, tiled=True)]
    ppermute x0 -> x21, waiting for transfers between devices: none -> 55.6 us  [the longest x14 43 us: shift(): return lax.ppermute(value, axis, [(i, (i + by) % 4) for i in range(4)])]
    all_gather x1 -> x0, waiting for transfers between devices: 39.6 us -> none  [local(): full_rows = lax.all_gather(coeffs, 'layer', axis=1, tiled=True)]
    all_to_all x2, waiting for transfers between devices: 39.8 us -> 1.51 us  [the longest x1 1.51 us: local(): lax.all_to_all(at.reshape(1024, 128), ROWS + ('z',), 0, 0, tiled=True)]
    ppermute x0 -> x21, starting transfers between devices: none -> 26 us  [the longest x14 22.4 us: shift(): return lax.ppermute(value, axis, [(i, (i + by) % 4) for i in range(4)])]
    dot_general x4 -> x0, matrix products: 18.3 us -> none  [the longest x2 12.1 us: apply_blocks(): jnp.einsum('rzc,zbc->rzb', picked, blocks, precision=lax.Precision.HIGHEST)]
    unnamed x11 -> x17, local copies, waits for them, and re-layouts: 23.3 us -> 5.74 us
    pallas_call x0 -> x4, Pallas kernels: none -> 15.4 us  [the longest x1 11.9 us: local(): pl.pallas_call(product_kernel, out_shape=(shape(32, 32, 128),) + (shape(8...]
  transfers between devices with their start and end apart: 4 -> 23, of which waited for: 4 -> 15; matrix products, arithmetic and copies ran while one was open for 6% -> 5% of each run, Pallas kernels for 0% -> 2%
where the time goes in v1:
time: 136 us; the launch traced here: 135 us
  waiting for transfers between devices  57.1 us (42%)
  starting transfers between devices  53.4 us (39%)
  Pallas kernels  15.4 us (11%)
  local copies, waits for them, and re-layouts  8.34 us (6%)
    ppermute x14, waiting for transfers between devices, shift(): return lax.ppermute(value, axis, [(i, (i + by) % 4) for i in range(4)])  43 us
    ppermute x14, starting transfers between devices, shift(): return lax.ppermute(value, axis, [(i, (i + by) % 4) for i in range(4)])  22.4 us
    all_to_all x1, starting transfers between devices, local(): lax.all_to_all(at.reshape(1024, 128), ROWS + ('z',), 0, 0, tiled=True)  14.4 us
    all_to_all x1, starting transfers between devices, local(): lax.all_to_all(oa.reshape(1024, 128), ROWS + ('z',), 0, 0, tiled=True)  13.1 us
    pallas_call x1, Pallas kernels, local(): pl.pallas_call(product_kernel, out_shape=(shape(32, 32, 128),) + (shape(8...  11.9 us
    ppermute x2, waiting for transfers between devices, pair(): return lax.ppermute(value, 'z', [(0, 1), (1, 0), (2, 3), (3, 2)])  10.6 us
    unnamed x17, local copies, waits for them, and re-layouts  5.74 us
    ppermute x2, starting transfers between devices, pair(): return lax.ppermute(value, 'z', [(0, 1), (1, 0), (2, 3), (3, 2)])  2.85 us
  transfers between devices with their start and end apart: 23, of which 15 were waited for; matrix products, arithmetic and copies ran while one was open for 5% of the time, Pallas kernels for 2%

profile of v1, /device:TPU:32, one launch (start us, length us, event | category | flops | bytes accessed | tf_op | source)
XLA Modules:
  0.0 134.9 jit_solution(17760307368766334010)
XLA Ops:
  0.0 1.1 constant_dynamic-slice_fusion
  1.1 1.9 %collective-permute-start.7 = (f32[2,128,128]{2,1,0:T(8,128)S(1)}, f32[2,128,128]{2,1,0:T(8,128)S(1)}, u32[]{:S(2)}, u32[]{:S(2)}) collective-permute-start(f32[2,128,128]{2,1,0:T(8,128)S(1)} %constant_dynamic-slice_fusion), channel_id=1, source_target_pairs={{0,2},{2,0},{4,6},{6,4},{1,3},{3,1},{5,7},{7,5},{8,10},{10,8},{12,... | collective-permute-start | bytes 393224 | tf_op jit(solution)/shard_map/ppermute | solution.py:159
  3.0 3.4 %collective-permute-done.7 = f32[2,128,128]{2,1,0:T(8,128)S(1)} collective-permute-done((f32[2,128,128]{2,1,0:T(8,128)S(1)}, f32[2,128,128]{2,1,0:T(8,128)S(1)}, u32[]{:S(2)}, u32[]{:S(2)}) %collective-permute-start.7) | collective-permute-done | bytes 131104 | tf_op jit(solution)/shard_map/ppermute | solution.py:159
  6.4 1.5 %collective-permute-start.8 = (f32[2,128,128]{2,1,0:T(8,128)S(1)}, f32[2,128,128]{2,1,0:T(8,128)S(1)}, u32[]{:S(2)}, u32[]{:S(2)}) collective-permute-start(f32[2,128,128]{2,1,0:T(8,128)S(1)} %collective-permute-done.7), channel_id=1, source_target_pairs={{0,8},{8,16},{16,24},{24,0},{1,9},{9,17},{17,25},{25,1},{2,10},{10... | collective-permute-start | bytes 393224 | tf_op jit(solution)/shard_map/ppermute | solution.py:151
  7.9 1.7 %collective-permute-start.9 = (f32[2,128,128]{2,1,0:T(8,128)S(1)}, f32[2,128,128]{2,1,0:T(8,128)S(1)}, u32[]{:S(2)}, u32[]{:S(2)}) collective-permute-start(f32[2,128,128]{2,1,0:T(8,128)S(1)} %collective-permute-done.7), channel_id=1, source_target_pairs={{0,24},{8,0},{16,8},{24,16},{1,25},{9,1},{17,9},{25,17},{2,26},{10... | collective-permute-start | bytes 393224 | tf_op jit(solution)/shard_map/ppermute | solution.py:151
  10.3 2.3 %collective-permute-done.8 = f32[2,128,128]{2,1,0:T(8,128)S(1)} collective-permute-done((f32[2,128,128]{2,1,0:T(8,128)S(1)}, f32[2,128,128]{2,1,0:T(8,128)S(1)}, u32[]{:S(2)}, u32[]{:S(2)}) %collective-permute-start.8) | collective-permute-done | bytes 131104 | tf_op jit(solution)/shard_map/ppermute | solution.py:151
  12.9 3.0 %collective-permute-start.11 = (f32[1,128,128]{2,1,0:T(8,128)S(1)}, f32[1,128,128]{2,1,0:T(8,128)S(1)}, u32[]{:S(2)}, u32[]{:S(2)}) collective-permute-start(f32[1,128,128]{2,1,0:T(8,128)S(1)} %slice.17), channel_id=1, source_target_pairs={{0,24},{8,0},{16,8},{24,16},{1,25},{9,1},{17,9},{25,17},{2,26},{10... | collective-permute-start | bytes 196616 | tf_op jit(solution)/shard_map/ppermute | solution.py:151
  19.3 1.6 %collective-permute-start.12 = (f32[8,128,128]{2,1,0:T(8,128)S(1)}, f32[8,128,128]{2,1,0:T(8,128)S(1)}, u32[]{:S(2)}, u32[]{:S(2)}) collective-permute-start(f32[8,128,128]{2,1,0:T(8,128)S(1)} %get-tuple-element.33), channel_id=1, source_target_pairs={{0,64},{64,128},{128,192},{192,0},{1,65},{65,129},{129,193},{193,1... | collective-permute-start | bytes 1572872 | tf_op jit(solution)/shard_map/ppermute | solution.py:151
  20.9 1.7 %collective-permute-start.13 = (f32[8,128,128]{2,1,0:T(8,128)S(1)}, f32[8,128,128]{2,1,0:T(8,128)S(1)}, u32[]{:S(2)}, u32[]{:S(2)}) collective-permute-start(f32[8,128,128]{2,1,0:T(8,128)S(1)} %get-tuple-element.33), channel_id=1, source_target_pairs={{0,192},{64,0},{128,64},{192,128},{1,193},{65,1},{129,65},{193,129... | collective-permute-start | bytes 1572872 | tf_op jit(solution)/shard_map/ppermute | solution.py:151
  22.6 8.8 %collective-permute-done.12 = f32[8,128,128]{2,1,0:T(8,128)S(1)} collective-permute-done((f32[8,128,128]{2,1,0:T(8,128)S(1)}, f32[8,128,128]{2,1,0:T(8,128)S(1)}, u32[]{:S(2)}, u32[]{:S(2)}) %collective-permute-start.12) | collective-permute-done | bytes 524320 | tf_op jit(solution)/shard_map/ppermute | solution.py:151
  31.3 1.6 %collective-permute-start.14 = (f32[4,128,128]{2,1,0:T(8,128)S(1)}, f32[4,128,128]{2,1,0:T(8,128)S(1)}, u32[]{:S(2)}, u32[]{:S(2)}) collective-permute-start(f32[4,128,128]{2,1,0:T(8,128)S(1)} %slice.18), channel_id=1, source_target_pairs={{0,64},{64,128},{128,192},{192,0},{1,65},{65,129},{129,193},{193,1... | collective-permute-start | bytes 786440 | tf_op jit(solution)/shard_map/ppermute | solution.py:151
  33.0 1.8 %collective-permute-start.15 = (f32[4,128,128]{2,1,0:T(8,128)S(1)}, f32[4,128,128]{2,1,0:T(8,128)S(1)}, u32[]{:S(2)}, u32[]{:S(2)}) collective-permute-start(f32[4,128,128]{2,1,0:T(8,128)S(1)} %slice.19), channel_id=1, source_target_pairs={{0,192},{64,0},{128,64},{192,128},{1,193},{65,1},{129,65},{193,129... | collective-permute-start | bytes 786440 | tf_op jit(solution)/shard_map/ppermute | solution.py:151
  36.5 2.5 %collective-permute-done.14 = f32[4,128,128]{2,1,0:T(8,128)S(1)} collective-permute-done((f32[4,128,128]{2,1,0:T(8,128)S(1)}, f32[4,128,128]{2,1,0:T(8,128)S(1)}, u32[]{:S(2)}, u32[]{:S(2)}) %collective-permute-start.14) | collective-permute-done | bytes 262176 | tf_op jit(solution)/shard_map/ppermute | solution.py:151
  39.7 2.0 %collective-permute-done.15 = f32[4,128,128]{2,1,0:T(8,128)S(1)} collective-permute-done((f32[4,128,128]{2,1,0:T(8,128)S(1)}, f32[4,128,128]{2,1,0:T(8,128)S(1)}, u32[]{:S(2)}, u32[]{:S(2)}) %collective-permute-start.15) | collective-permute-done | bytes 262176 | tf_op jit(solution)/shard_map/ppermute | solution.py:151
  42.6 1.5 %prep.1 = (f32[32,2,16,128]{3,2,1,0:T(8,128)}, f32[2,4,32,128]{3,2,1,0:T(8,128)S(1)}, f32[2,4,32,128]{3,2,1,0:T(8,128)S(1)}) custom-call(s32[4]{0:T(128)S(1)} %get-tuple-element.37.where, f32[128,512]{1,0:T(8,128)S(1)} %copy-done.1), custom_call_target="tpu_custom_call" | custom-call | bytes 1048576 | tf_op jit(solution)/shard_map/prep/pallas_call | solution.py:173
  44.1 14.4 %all-to-all-start = ((f32[128,8,128]{2,1,0:T(8,128)}), f32[128,8,128]{2,1,0:T(8,128)S(1)}, u32[]{:S(2)}, u32[]{:S(2)}) async-start(f32[128,8,128]{2,1,0:T(8,128)} %bitcast.14), calls=%async_computation | async-start | bytes 1048576 | tf_op jit(solution)/shard_map/all_to_all | solution.py:183
  60.0 0.9 collective-permute-start.1
  61.0 2.3 %collective-permute-start.3 = (f32[8,32,128]{2,1,0:T(8,128)S(1)}, f32[8,32,128]{2,1,0:T(8,128)S(1)}, u32[]{:S(2)}, u32[]{:S(2)}) collective-permute-start(f32[8,32,128]{2,1,0:T(8,128)S(1)} %get-tuple-element.25), channel_id=1, source_target_pairs={{0,2},{2,4},{4,6},{6,0},{1,3},{3,5},{5,7},{7,1},{8,10},{10,12},{12... | collective-permute-start | bytes 393224 | tf_op jit(solution)/shard_map/ppermute | solution.py:151
  63.3 7.2 %collective-permute-done.1 = s32[64]{0:T(128)S(1)} collective-permute-done((s32[64]{0:T(128)S(1)}, s32[64]{0:T(128)S(1)}, u32[]{:S(2)}, u32[]{:S(2)}) %collective-permute-start.1) | collective-permute-done | bytes 288 | tf_op jit(solution)/shard_map/ppermute | solution.py:159
  70.6 2.5 %collective-permute-start.4 = (f32[8,32,128]{2,1,0:T(8,128)S(1)}, f32[8,32,128]{2,1,0:T(8,128)S(1)}, u32[]{:S(2)}, u32[]{:S(2)}) collective-permute-start(f32[8,32,128]{2,1,0:T(8,128)S(1)} %get-tuple-element.26.b0), channel_id=1, source_target_pairs={{0,4},{2,6},{4,0},{6,2},{1,5},{3,7},{5,1},{7,3},{8,12},{10,14},{12... | collective-permute-start | bytes 393224 | tf_op jit(solution)/shard_map/ppermute | solution.py:151
  74.1 6.8 %collective-permute-done.4.b2 = f32[8,32,128]{2,1,0:T(8,128)S(1)} collective-permute-done((f32[8,32,128]{2,1,0:T(8,128)S(1)}, f32[8,32,128]{2,1,0:T(8,128)S(1)}, u32[]{:S(2)}, u32[]{:S(2)}) %collective-permute-start.4) | collective-permute-done | bytes 131104 | tf_op jit(solution)/shard_map/ppermute | solution.py:151
  80.9 1.5 %all-to-all-done = f32[128,8,128]{2,1,0:T(8,128)S(1)} async-done(((f32[128,8,128]{2,1,0:T(8,128)}), f32[128,8,128]{2,1,0:T(8,128)S(1)}, u32[]{:S(2)}, u32[]{:S(2)}) %all-to-all-start) | async-done | bytes 524320 | tf_op jit(solution)/shard_map/all_to_all | solution.py:183
  82.4 11.9 %product.1 = (f32[32,32,128]{2,1,0:T(8,128)}, f32[8,32,128]{2,1,0:T(8,128)S(1)}, f32[8,32,128]{2,1,0:T(8,128)S(1)}, f32[8,32,128]{2,1,0:T(8,128)S(1)}, f32[8,32,128]{2,1,0:T(8,128)S(1)}) custom-call(s32[4]{0:T(128)S(1)} %get-tuple-element.37.where, s32[128]{0:T(128)S(1)} %pad_add_fusion.2.cols, s32[128]{0:T(128)S(1)} %convert_reduce_fusion.owners, ...), custom_call_target="tpu_custom_call" | custom-call | flops 805306368 | bytes 10485760 | tf_op jit(solution)/shard_map/product/pallas_call | solution.py:204
  95.0 13.1 %all-to-all-start.1 = ((f32[128,8,128]{2,1,0:T(8,128)}), f32[128,8,128]{2,1,0:T(8,128)S(1)}, u32[]{:S(2)}, u32[]{:S(2)}) async-start(f32[128,8,128]{2,1,0:T(8,128)} %bitcast.16), calls=%async_computation.1 | async-start | bytes 1048576 | tf_op jit(solution)/shard_map/all_to_all | solution.py:223
  108.1 1.5 %collective-permute-start.17 = (f32[8,32,128]{2,1,0:T(8,128)}, f32[8,32,128]{2,1,0:T(8,128)S(1)}, u32[]{:S(2)}, u32[]{:S(2)}) collective-permute-start(f32[8,32,128]{2,1,0:T(8,128)} %copy-done.2), channel_id=1, source_target_pairs={{0,2},{2,4},{4,6},{6,0},{1,3},{3,5},{5,7},{7,1},{8,10},{10,12},{12... | collective-permute-start | bytes 393224 | tf_op jit(solution)/shard_map/ppermute | solution.py:151
  109.6 1.8 %collective-permute-start.18 = (f32[8,32,128]{2,1,0:T(8,128)S(1)}, f32[8,32,128]{2,1,0:T(8,128)S(1)}, u32[]{:S(2)}, u32[]{:S(2)}) collective-permute-start(f32[8,32,128]{2,1,0:T(8,128)S(1)} %get-tuple-element.21), channel_id=1, source_target_pairs={{0,4},{2,6},{4,0},{6,2},{1,5},{3,7},{5,1},{7,3},{8,12},{10,14},{12... | collective-permute-start | bytes 393224 | tf_op jit(solution)/shard_map/ppermute | solution.py:151
  111.4 1.1 collective-permute-start.19
  112.5 11.3 %collective-permute-done.17.r1 = f32[8,32,128]{2,1,0:T(8,128)S(1)} collective-permute-done((f32[8,32,128]{2,1,0:T(8,128)}, f32[8,32,128]{2,1,0:T(8,128)S(1)}, u32[]{:S(2)}, u32[]{:S(2)}) %collective-permute-start.17) | collective-permute-done | bytes 131104 | tf_op jit(solution)/shard_map/ppermute | solution.py:151
  123.8 5.7 %collective-permute-done.18.r2 = f32[8,32,128]{2,1,0:T(8,128)S(1)} collective-permute-done((f32[8,32,128]{2,1,0:T(8,128)S(1)}, f32[8,32,128]{2,1,0:T(8,128)S(1)}, u32[]{:S(2)}, u32[]{:S(2)}) %collective-permute-start.18) | collective-permute-done | bytes 131104 | tf_op jit(solution)/shard_map/ppermute | solution.py:151
  129.5 1.9 %collective-permute-done.19.r3 = f32[8,32,128]{2,1,0:T(8,128)S(1)} collective-permute-done((f32[8,32,128]{2,1,0:T(8,128)S(1)}, f32[8,32,128]{2,1,0:T(8,128)S(1)}, u32[]{:S(2)}, u32[]{:S(2)}) %collective-permute-start.19) | collective-permute-done | bytes 131104 | tf_op jit(solution)/shard_map/ppermute | solution.py:151
  132.1 1.3 collective-permute-done.20.got_ref
  133.4 1.4 %final.1 = f32[128,512]{1,0:T(8,128)} custom-call(s32[4]{0:T(128)S(1)} %get-tuple-element.37.where, f32[32,2,16,128]{3,2,1,0:T(8,128)S(1)} %bitcast.22, f32[2,4,32,128]{3,2,1,0:T(8,128)S(1)} %get-tuple-element.23.keep_ref, f32[2,4,32,128]{3,2,1,0:T(8,128)S(1)} %collective-permute-done.20.got_ref), custom_call_target="tpu_custom_call" | custom-call | bytes 1048576 | tf_op jit(solution)/shard_map/final/pallas_call | solution.py:235
  (52 shorter events, 11.6 us)
Async XLA Ops:
  0.0 33.0 %copy-start = (f32[32,128,128]{2,1,0:T(8,128)S(1)}, f32[32,128,128]{2,1,0:T(8,128)}, u32[]{:S(2)}) copy-start(f32[32,128,128]{2,1,0:T(8,128)} %h0.1) | copy-start | bytes 6291460
  1.1 5.3 %collective-permute-start.7 = (f32[2,128,128]{2,1,0:T(8,128)S(1)}, f32[2,128,128]{2,1,0:T(8,128)S(1)}, u32[]{:S(2)}, u32[]{:S(2)}) collective-permute-start(f32[2,128,128]{2,1,0:T(8,128)S(1)} %constant_dynamic-slice_fusion), channel_id=1, source_target_pairs={{0,2},{2,0},{4,6},{6,4},{1,3},{3,1},{5,7},{7,5},{8,10},{10,8},{12,... | collective-permute-start | bytes 393224 | tf_op jit(solution)/shard_map/ppermute | solution.py:159
  6.4 6.2 %collective-permute-start.8 = (f32[2,128,128]{2,1,0:T(8,128)S(1)}, f32[2,128,128]{2,1,0:T(8,128)S(1)}, u32[]{:S(2)}, u32[]{:S(2)}) collective-permute-start(f32[2,128,128]{2,1,0:T(8,128)S(1)} %collective-permute-done.7), channel_id=1, source_target_pairs={{0,8},{8,16},{16,24},{24,0},{1,9},{9,17},{17,25},{25,1},{2,10},{10... | collective-permute-start | bytes 393224 | tf_op jit(solution)/shard_map/ppermute | solution.py:151
  7.9 5.0 %collective-permute-start.9 = (f32[2,128,128]{2,1,0:T(8,128)S(1)}, f32[2,128,128]{2,1,0:T(8,128)S(1)}, u32[]{:S(2)}, u32[]{:S(2)}) collective-permute-start(f32[2,128,128]{2,1,0:T(8,128)S(1)} %collective-permute-done.7), channel_id=1, source_target_pairs={{0,24},{8,0},{16,8},{24,16},{1,25},{9,1},{17,9},{25,17},{2,26},{10... | collective-permute-start | bytes 393224 | tf_op jit(solution)/shard_map/ppermute | solution.py:151
  12.6 5.5 %collective-permute-start.10 = (f32[1,128,128]{2,1,0:T(8,128)S(1)}, f32[1,128,128]{2,1,0:T(8,128)S(1)}, u32[]{:S(2)}, u32[]{:S(2)}) collective-permute-start(f32[1,128,128]{2,1,0:T(8,128)S(1)} %slice.16), channel_id=1, source_target_pairs={{0,8},{8,16},{16,24},{24,0},{1,9},{9,17},{17,25},{25,1},{2,10},{10... | collective-permute-start | bytes 196616 | tf_op jit(solution)/shard_map/ppermute | solution.py:151
  12.9 5.8 %collective-permute-start.11 = (f32[1,128,128]{2,1,0:T(8,128)S(1)}, f32[1,128,128]{2,1,0:T(8,128)S(1)}, u32[]{:S(2)}, u32[]{:S(2)}) collective-permute-start(f32[1,128,128]{2,1,0:T(8,128)S(1)} %slice.17), channel_id=1, source_target_pairs={{0,24},{8,0},{16,8},{24,16},{1,25},{9,1},{17,9},{25,17},{2,26},{10... | collective-permute-start | bytes 196616 | tf_op jit(solution)/shard_map/ppermute | solution.py:151
  19.3 23.3 %copy-start.1 = (f32[128,512]{1,0:T(8,128)S(1)}, f32[128,512]{1,0:T(8,128)}, u32[]{:S(2)}) copy-start(f32[128,512]{1,0:T(8,128)} %c_ref.1) | copy-start | bytes 786436
  19.3 12.0 %collective-permute-start.12 = (f32[8,128,128]{2,1,0:T(8,128)S(1)}, f32[8,128,128]{2,1,0:T(8,128)S(1)}, u32[]{:S(2)}, u32[]{:S(2)}) collective-permute-start(f32[8,128,128]{2,1,0:T(8,128)S(1)} %get-tuple-element.33), channel_id=1, source_target_pairs={{0,64},{64,128},{128,192},{192,0},{1,65},{65,129},{129,193},{193,1... | collective-permute-start | bytes 1572872 | tf_op jit(solution)/shard_map/ppermute | solution.py:151
  20.9 12.1 %collective-permute-start.13 = (f32[8,128,128]{2,1,0:T(8,128)S(1)}, f32[8,128,128]{2,1,0:T(8,128)S(1)}, u32[]{:S(2)}, u32[]{:S(2)}) collective-permute-start(f32[8,128,128]{2,1,0:T(8,128)S(1)} %get-tuple-element.33), channel_id=1, source_target_pairs={{0,192},{64,0},{128,64},{192,128},{1,193},{65,1},{129,65},{193,129... | collective-permute-start | bytes 1572872 | tf_op jit(solution)/shard_map/ppermute | solution.py:151
  31.3 7.7 %collective-permute-start.14 = (f32[4,128,128]{2,1,0:T(8,128)S(1)}, f32[4,128,128]{2,1,0:T(8,128)S(1)}, u32[]{:S(2)}, u32[]{:S(2)}) collective-permute-start(f32[4,128,128]{2,1,0:T(8,128)S(1)} %slice.18), channel_id=1, source_target_pairs={{0,64},{64,128},{128,192},{192,0},{1,65},{65,129},{129,193},{193,1... | collective-permute-start | bytes 786440 | tf_op jit(solution)/shard_map/ppermute | solution.py:151
  33.0 49.5 %collective-permute-start.6 = (f32[32,128,128]{2,1,0:T(8,128)S(1)}, f32[32,128,128]{2,1,0:T(8,128)}, u32[]{:S(2)}, u32[]{:S(2)}) collective-permute-start(f32[32,128,128]{2,1,0:T(8,128)S(1)} %copy-done), channel_id=1, source_target_pairs={{0,1},{1,0},{2,3},{3,2},{4,5},{5,4},{6,7},{7,6},{8,9},{9,8},{10,11... | collective-permute-start | bytes 6291464 | tf_op jit(solution)/shard_map/ppermute | solution.py:155
  33.0 8.8 %collective-permute-start.15 = (f32[4,128,128]{2,1,0:T(8,128)S(1)}, f32[4,128,128]{2,1,0:T(8,128)S(1)}, u32[]{:S(2)}, u32[]{:S(2)}) collective-permute-start(f32[4,128,128]{2,1,0:T(8,128)S(1)} %slice.19), channel_id=1, source_target_pairs={{0,192},{64,0},{128,64},{192,128},{1,193},{65,1},{129,65},{193,129... | collective-permute-start | bytes 786440 | tf_op jit(solution)/shard_map/ppermute | solution.py:151
  34.8 23.8 %copy-start.3 = (s32[32]{0:T(128)S(1)}, s32[32]{0:T(128)}, u32[]{:S(2)}) copy-start(s32[32]{0:T(128)} %param.7) | copy-start | bytes 388
  34.8 24.4 %copy-start.4 = (s32[32]{0:T(128)S(1)}, s32[32]{0:T(128)}, u32[]{:S(2)}) copy-start(s32[32]{0:T(128)} %param.6) | copy-start | bytes 388
  42.5 39.9 %collective-permute-start.16 = (f32[32,128,128]{2,1,0:T(8,128)}, f32[32,128,128]{2,1,0:T(8,128)}, u32[]{:S(2)}, u32[]{:S(2)}) collective-permute-start(f32[32,128,128]{2,1,0:T(8,128)} %constant_dynamic-update-slice_fusion.5.h2), channel_id=1, source_target_pairs={{0,1},{1,0},{2,3},{3,2},{4,5},{5,4},{6,7},{7,6},{8,9},{9,8},{10,11... | collective-permute-start | bytes 6291464 | tf_op jit(solution)/shard_map/ppermute | solution.py:155
  44.1 38.4 %all-to-all-start = ((f32[128,8,128]{2,1,0:T(8,128)}), f32[128,8,128]{2,1,0:T(8,128)S(1)}, u32[]{:S(2)}, u32[]{:S(2)}) async-start(f32[128,8,128]{2,1,0:T(8,128)} %bitcast.14), calls=%async_computation | async-start | bytes 1048576 | tf_op jit(solution)/shard_map/all_to_all | solution.py:183
  58.5 2.4 %collective-permute-start.2 = (f32[2,4,32,128]{3,2,1,0:T(8,128)S(1)}, f32[2,4,32,128]{3,2,1,0:T(8,128)S(1)}, u32[]{:S(2)}, u32[]{:S(2)}) collective-permute-start(f32[2,4,32,128]{3,2,1,0:T(8,128)S(1)} %get-tuple-element.16), channel_id=1, source_target_pairs={{0,1},{1,0},{2,3},{3,2},{4,5},{5,4},{6,7},{7,6},{8,9},{9,8},{10,11... | collective-permute-start | bytes 393224 | tf_op jit(solution)/shard_map/ppermute | solution.py:155
  58.6 1.3 collective-permute-start
  60.0 10.5 %collective-permute-start.1 = (s32[64]{0:T(128)S(1)}, s32[64]{0:T(128)S(1)}, u32[]{:S(2)}, u32[]{:S(2)}) collective-permute-start(s32[64]{0:T(128)S(1)} %pad_add_fusion.1), channel_id=1, source_target_pairs={{0,2},{2,0},{4,6},{6,4},{1,3},{3,1},{5,7},{7,5},{8,10},{10,8},{12,... | collective-permute-start | bytes 776 | tf_op jit(solution)/shard_map/ppermute | solution.py:159
  61.0 13.1 %collective-permute-start.3 = (f32[8,32,128]{2,1,0:T(8,128)S(1)}, f32[8,32,128]{2,1,0:T(8,128)S(1)}, u32[]{:S(2)}, u32[]{:S(2)}) collective-permute-start(f32[8,32,128]{2,1,0:T(8,128)S(1)} %get-tuple-element.25), channel_id=1, source_target_pairs={{0,2},{2,4},{4,6},{6,0},{1,3},{3,5},{5,7},{7,1},{8,10},{10,12},{12... | collective-permute-start | bytes 393224 | tf_op jit(solution)/shard_map/ppermute | solution.py:151
  63.3 17.6 %collective-permute-start.5 = (f32[8,32,128]{2,1,0:T(8,128)S(1)}, f32[8,32,128]{2,1,0:T(8,128)S(1)}, u32[]{:S(2)}, u32[]{:S(2)}) collective-permute-start(f32[8,32,128]{2,1,0:T(8,128)S(1)} %get-tuple-element.25), channel_id=1, source_target_pairs={{0,6},{2,0},{4,2},{6,4},{1,7},{3,1},{5,3},{7,5},{8,14},{10,8},{12,... | collective-permute-start | bytes 393224 | tf_op jit(solution)/shard_map/ppermute | solution.py:151
  70.6 10.4 %collective-permute-start.4 = (f32[8,32,128]{2,1,0:T(8,128)S(1)}, f32[8,32,128]{2,1,0:T(8,128)S(1)}, u32[]{:S(2)}, u32[]{:S(2)}) collective-permute-start(f32[8,32,128]{2,1,0:T(8,128)S(1)} %get-tuple-element.26.b0), channel_id=1, source_target_pairs={{0,4},{2,6},{4,0},{6,2},{1,5},{3,7},{5,1},{7,3},{8,12},{10,14},{12... | collective-permute-start | bytes 393224 | tf_op jit(solution)/shard_map/ppermute | solution.py:151
  94.3 0.7 copy-start.2
  95.0 38.4 %all-to-all-start.1 = ((f32[128,8,128]{2,1,0:T(8,128)}), f32[128,8,128]{2,1,0:T(8,128)S(1)}, u32[]{:S(2)}, u32[]{:S(2)}) async-start(f32[128,8,128]{2,1,0:T(8,128)} %bitcast.16), calls=%async_computation.1 | async-start | bytes 1048576 | tf_op jit(solution)/shard_map/all_to_all | solution.py:223
  108.1 15.7 %collective-permute-start.17 = (f32[8,32,128]{2,1,0:T(8,128)}, f32[8,32,128]{2,1,0:T(8,128)S(1)}, u32[]{:S(2)}, u32[]{:S(2)}) collective-permute-start(f32[8,32,128]{2,1,0:T(8,128)} %copy-done.2), channel_id=1, source_target_pairs={{0,2},{2,4},{4,6},{6,0},{1,3},{3,5},{5,7},{7,1},{8,10},{10,12},{12... | collective-permute-start | bytes 393224 | tf_op jit(solution)/shard_map/ppermute | solution.py:151
  109.6 19.9 %collective-permute-start.18 = (f32[8,32,128]{2,1,0:T(8,128)S(1)}, f32[8,32,128]{2,1,0:T(8,128)S(1)}, u32[]{:S(2)}, u32[]{:S(2)}) collective-permute-start(f32[8,32,128]{2,1,0:T(8,128)S(1)} %get-tuple-element.21), channel_id=1, source_target_pairs={{0,4},{2,6},{4,0},{6,2},{1,5},{3,7},{5,1},{7,3},{8,12},{10,14},{12... | collective-permute-start | bytes 393224 | tf_op jit(solution)/shard_map/ppermute | solution.py:151
  111.4 20.0 %collective-permute-start.19 = (f32[8,32,128]{2,1,0:T(8,128)S(1)}, f32[8,32,128]{2,1,0:T(8,128)S(1)}, u32[]{:S(2)}, u32[]{:S(2)}) collective-permute-start(f32[8,32,128]{2,1,0:T(8,128)S(1)} %get-tuple-element.22), channel_id=1, source_target_pairs={{0,6},{2,0},{4,2},{6,4},{1,7},{3,1},{5,3},{7,5},{8,14},{10,8},{12,... | collective-permute-start | bytes 393224 | tf_op jit(solution)/shard_map/ppermute | solution.py:151
  132.0 1.4 %collective-permute-start.20 = (f32[2,4,32,128]{3,2,1,0:T(8,128)S(1)}, f32[2,4,32,128]{3,2,1,0:T(8,128)S(1)}, u32[]{:S(2)}, u32[]{:S(2)}) collective-permute-start(f32[2,4,32,128]{3,2,1,0:T(8,128)S(1)} %get-tuple-element.24), channel_id=1, source_target_pairs={{0,1},{1,0},{2,3},{3,2},{4,5},{5,4},{6,7},{7,6},{8,9},{9,8},{10,11... | collective-permute-start | bytes 393224 | tf_op jit(solution)/shard_map/ppermute | solution.py:155

commit v2 on v1

v2 whole, which is shorter than its diff:
```python
import jax
import jax.numpy as jnp
from jax import lax
from jax.experimental import pallas as pl
from jax.experimental.pallas import tpu as pltpu
from jax.sharding import Mesh
from jax.sharding import PartitionSpec as P

ROWS = ("y", "h", "x")
ANY = pl.BlockSpec(memory_space=pl.ANY)
VMEM = pl.BlockSpec(memory_space=pltpu.VMEM)
SMEM = pl.BlockSpec(memory_space=pltpu.SMEM)
F32 = jnp.float32
BF16 = jnp.bfloat16


def params(mib):
    return pltpu.CompilerParams(vmem_limit_bytes=mib << 20)


def cost(flops, moved):
    return pl.CostEstimate(flops=flops, bytes_accessed=moved, transcendentals=0)


def shape(*dims, kind=F32):
    return jax.ShapeDtypeStruct(dims, kind)


def small(kernel, outs, where, *args):
    return pl.pallas_call(
        kernel,
        out_shape=outs,
        in_specs=[SMEM] + [VMEM] * len(args),
        out_specs=(VMEM,) * len(outs),
        compiler_params=params(16),
        cost_estimate=cost(0, 1 << 20),
        name=kernel.__name__,
    )(where, *args)


def prep_kernel(where, h_ref, c_ref, at_ref, keep_ref, send_ref, piece_ref, sem):
    y, x, core = where[0], where[1], where[3]
    copy = pltpu.make_async_copy(h_ref.at[pl.ds(2 * (4 * y + x), 2)], piece_ref, sem)
    copy.start()
    for t in range(4):
        turned = jnp.transpose(c_ref[:, 128 * t : 128 * (t + 1)])
        at_ref[8 * t : 8 * (t + 1)] = turned.reshape(8, 16, 128)
    for q in range(2):
        for t in range(4):
            span = slice(128 * t, 128 * (t + 1))
            mine = pl.multiple_of(64 * q + 32 * core, 32)
            other = pl.multiple_of(64 * q + 32 * (1 - core), 32)
            keep_ref[q, t] = c_ref[pl.ds(mine, 32), span]
            send_ref[q, t] = c_ref[pl.ds(other, 32), span]
    copy.wait()


def rows_kernel(where, keep_ref, got_ref, same_ref, differ_ref):
    q, core = jnp.bitwise_and(where[2], 1), where[3]
    for t in range(4):
        same_ref[4 * core + t] = keep_ref[q, t]
        same_ref[4 * (1 - core) + t] = got_ref[q, t]
        differ_ref[4 * core + t] = keep_ref[1 - q, t]
        differ_ref[4 * (1 - core) + t] = got_ref[1 - q, t]


def join_kernel(where, moved, own, down, up, far_a, far_b, same_ref, differ_ref, out_ref):
    q = jnp.bitwise_and(where[2], 1)
    same_ref[...] = moved[:, pl.ds(pl.multiple_of(8 * q, 8), 8), :]
    differ_ref[...] = moved[:, pl.ds(pl.multiple_of(8 * (1 - q), 8), 8), :]
    at = 0
    for part in (own, down, up, far_a, far_b):
        out_ref[at : at + part.shape[0]] = part[...]
        at += part.shape[0]


def accumulate(blocks, cols, owners, stack, acc):
    contract = (((1,), (1,)), ((), ()))
    terms = []
    for block, at in blocks:
        high = block.astype(BF16)
        low = (block - high.astype(F32)).astype(BF16)
        left = stack[cols[at]]
        one = lax.dot_general(left, high, contract, preferred_element_type=F32)
        two = lax.dot_general(left[:64], low, contract, preferred_element_type=F32)
        terms.append((owners[at], one[:64] + (one[64:] + two)))
    for owner, term in terms:
        acc[owner] += term


def near_kernel(
    where, cols, owners, b0, b1, b2, b3, a0, a1, a2, a3, h0, h1, acc, stack,
    beta, alpha, hbuf, sem_a, sem_h,
):
    z = where[2]
    loads = []
    for k, part in enumerate((b0, b1, b2, b3)):
        home = jnp.bitwise_and(z - k + 4, 3)
        loads.append(pltpu.make_async_copy(part, beta.at[pl.ds(8 * home, 8)], sem_a.at[k]))
    for k, part in enumerate((a0, a1, a2, a3)):
        loads.append(
            pltpu.make_async_copy(part, alpha.at[:, pl.ds(8 * k, 8)], sem_a.at[4 + k])
        )
    for load in loads:
        load.start()
    chunks = []
    for n in range(4):
        source = (h0, h1)[n // 2].at[pl.ds(16 * (n % 2), 16)]
        chunks.append(pltpu.make_async_copy(source, hbuf.at[pl.ds(16 * n, 16)], sem_h.at[n]))
    for chunk in chunks:
        chunk.start()
    acc[...] = jnp.zeros_like(acc)
    for load in loads:
        load.wait()

    @pl.loop(0, 32)
    def _(j):
        for row, source in ((0, beta), (32, alpha)):
            value = source[j]
            high = value.astype(BF16)
            stack[j, row : row + 32] = high
            stack[j, 64 + row : 96 + row] = (value - high.astype(F32)).astype(BF16)

    for n, chunk in enumerate(chunks):
        chunk.wait()

        @pl.loop(0, 4)
        def _(step, n=n):
            first = 16 * n + 4 * step
            accumulate([(hbuf[first + u], first + u) for u in range(4)], cols, owners, stack, acc)


FAR = (8, 8, 8, 4, 4)


def far_kernel(where, cols, owners, acc_in, stack_in, *refs):
    sources, outs = refs[:10], refs[10:18]
    acc, stack, hbuf, sem_a, sem_h = refs[18:]
    y, x, z = where[0], where[1], where[2]
    loads = [
        pltpu.make_async_copy(acc_in, acc, sem_a.at[0]),
        pltpu.make_async_copy(stack_in, stack, sem_a.at[1]),
    ]
    for load in loads:
        load.start()
    chunks = []
    for core in range(2):
        at = 0
        for n, size in enumerate(FAR):
            ref = sources[5 * core + n]
            copy = pltpu.make_async_copy(
                ref, hbuf.at[pl.ds(32 * core + at, size)], sem_h.at[5 * core + n]
            )
            chunks.append((copy, core, at, size))
            at += size
    for chunk, *_ in chunks:
        chunk.start()
    for load in loads:
        load.wait()

    def home(core, i):
        ys, xs, b = i // 8, (i // 2) % 4, i % 2
        dy = jnp.where(ys == 1, 3, jnp.where(ys == 0, 0, ys - 1))
        dx = jnp.where(xs == 1, 3, jnp.where(xs == 0, 0, xs - 1))
        spot = 8 * jnp.bitwise_and(y + dy, 3) + 2 * jnp.bitwise_and(x + dx, 3) + b
        return 64 + 32 * core + spot

    for chunk, core, at, size in chunks:
        chunk.wait()

        @pl.loop(0, size // 4)
        def _(step, core=core, at=at):
            first = at + 4 * step
            blocks = [(hbuf[32 * core + first + u], home(core, first + u)) for u in range(4)]
            accumulate(blocks, cols, owners, stack, acc)

    for k in range(4):
        span = slice(32 + 8 * k, 40 + 8 * k)
        outs[k][...] = acc[:, span]
        outs[4 + k][...] = acc[pl.ds(8 * jnp.bitwise_and(z + k, 3), 8), :32]


def gather_kernel(where, r0, r1, r2, r3, out_ref):
    q = jnp.bitwise_and(where[2], 1)
    out_ref[:, pl.ds(pl.multiple_of(8 * q, 8), 8), :] = r0[...] + r2[...]
    out_ref[:, pl.ds(pl.multiple_of(8 * (1 - q), 8), 8), :] = r1[...] + r3[...]


def middle_kernel(where, r0, r1, r2, r3, keep_ref, send_ref):
    core = where[3]
    for slot, (one, two) in enumerate(((r0, r2), (r1, r3))):
        for t in range(4):
            mine, other = 4 * core + t, 4 * (1 - core) + t
            keep_ref[slot, t] = one[mine] + two[mine]
            send_ref[slot, t] = one[other] + two[other]


def final_kernel(where, back_ref, keep_ref, got_ref, out_ref):
    q, core = jnp.bitwise_and(where[2], 1), where[3]
    for t in range(4):
        span = slice(128 * t, 128 * (t + 1))
        out_ref[:, span] = jnp.transpose(back_ref[8 * t : 8 * (t + 1)].reshape(128, 128))
        for slot in range(2):
            base = 64 * jnp.bitwise_xor(q, slot)
            mine = pl.ds(pl.multiple_of(base + 32 * core, 32), 32)
            other = pl.ds(pl.multiple_of(base + 32 * (1 - core), 32), 32)
            out_ref[mine, span] += keep_ref[slot, t]
            out_ref[other, span] += got_ref[slot, t]


def shift(value, axis, by):
    return lax.ppermute(value, axis, [(i, (i + by) % 4) for i in range(4)])


def swap(value):
    return lax.ppermute(value, "c", [(0, 1), (1, 0)])


def pair(value):
    return lax.ppermute(value, "z", [(0, 1), (1, 0), (2, 3), (3, 2)])


def ring(value, axis):
    half = value.shape[0] // 2
    down, up = shift(value, axis, 1), shift(value, axis, -1)
    return value, down, up, shift(down[:half], axis, 1), shift(up[half:], axis, -1)


def spread(same, differ):
    return same, shift(differ, "z", 1), shift(same, "z", 2), shift(differ, "z", 3)


def tables(hcount, hcols, z, c):
    near_cols = jnp.concatenate([hcols, swap(hcols)])
    cols = jnp.concatenate([near_cols, pair(near_cols)])
    marks = jnp.arange(32, dtype=jnp.int32)
    row_end = jnp.sum(jnp.where(marks[:, None] <= marks[None, :], hcount[:, None], 0), axis=0)
    shard = jnp.stack([2 * z + c, 2 * z + 1 - c, 2 * (z ^ 1) + c, 2 * (z ^ 1) + 1 - c])
    index = (32 * shard[:, None].astype(jnp.int32) + marks[None, :]).reshape(128)
    return cols, jnp.sum((row_end[None, :] <= index[:, None]).astype(jnp.int32), axis=1)


def local(coeffs, hblocks, hcount, hcols):
    y, x, z, c = (lax.axis_index(n) for n in ("y", "x", "z", "c"))
    where = jnp.stack([y, x, z, c]).astype(jnp.int32)
    cols, owners = tables(hcount, hcols, z, c)

    at, keep, send, piece = pl.pallas_call(
        prep_kernel,
        out_shape=(shape(32, 16, 128), shape(2, 4, 32, 128), shape(2, 4, 32, 128), shape(2, 128, 128)),
        in_specs=[SMEM, ANY, VMEM],
        out_specs=(VMEM, VMEM, VMEM, ANY),
        scratch_shapes=[pltpu.SemaphoreType.DMA],
        compiler_params=params(16),
        cost_estimate=cost(0, 1 << 20),
        name="prep",
    )(where, hblocks, coeffs)

    moved = lax.all_to_all(at, ROWS, 0, 0, tiled=True)
    near_swapped = swap(hblocks)
    same, differ = small(rows_kernel, (shape(8, 32, 128),) * 2, where, keep, swap(send))
    beta = spread(same, differ)
    same, differ, joined = small(
        join_kernel,
        (shape(32, 8, 128), shape(32, 8, 128), shape(8, 128, 128)),
        where, moved, *ring(pair(piece), "x"),
    )
    alpha = spread(same, differ)
    far = ring(joined, "y")
    far_swapped = [swap(part) for part in far]

    acc, stack = pl.pallas_call(
        near_kernel,
        out_shape=(shape(32, 64, 128), shape(32, 128, 128, kind=BF16)),
        in_specs=[SMEM] * 3 + [ANY] * 10,
        out_specs=(VMEM,) * 2,
        scratch_shapes=[
            pltpu.VMEM((32, 32, 128), F32),
            pltpu.VMEM((32, 32, 128), F32),
            pltpu.VMEM((64, 128, 128), F32),
            pltpu.SemaphoreType.DMA((8,)),
            pltpu.SemaphoreType.DMA((4,)),
        ],
        compiler_params=params(32),
        cost_estimate=cost(6 * 64 * 64 * 128 * 128, 7 << 20),
        name="near",
    )(where, cols, owners, *beta, *alpha, hblocks, near_swapped)
    outs = pl.pallas_call(
        far_kernel,
        out_shape=(shape(32, 8, 128),) * 4 + (shape(8, 32, 128),) * 4,
        in_specs=[SMEM] * 3 + [ANY] * 12,
        out_specs=(VMEM,) * 8,
        scratch_shapes=[
            pltpu.VMEM((32, 64, 128), F32),
            pltpu.VMEM((32, 128, 128), BF16),
            pltpu.VMEM((64, 128, 128), F32),
            pltpu.SemaphoreType.DMA((2,)),
            pltpu.SemaphoreType.DMA((10,)),
        ],
        compiler_params=params(32),
        cost_estimate=cost(6 * 64 * 64 * 128 * 128, 7 << 20),
        name="far",
    )(where, cols, owners, acc, stack, *far, *far_swapped)

    got = [outs[0]] + [shift(outs[k], "z", -k) for k in (1, 2, 3)]
    (total,) = small(gather_kernel, (shape(32, 16, 128),), where, *got)
    back = lax.all_to_all(total, ROWS, 0, 0, tiled=True)
    got = [outs[4]] + [shift(outs[4 + k], "z", k) for k in (1, 2, 3)]
    keep, send = small(middle_kernel, (shape(2, 4, 32, 128),) * 2, where, *got)
    (out,) = small(final_kernel, (shape(128, 512),), where, back, keep, swap(send))
    return out


def solution(mesh):
    fine = Mesh(mesh.devices.reshape(4, 2, 4, 4, 2), ("y", "h", "x", "z", "c"))
    in_specs = (P(ROWS, ("z", "c")), P(("z", "c"), None, None), P(), P(("z", "c")))
    out_specs = P(ROWS, ("z", "c"))
    return jax.shard_map(local, mesh=fine, in_specs=in_specs, out_specs=out_specs, check_vma=False)
```

time: 136 us -> 154 us (1.13)
  starting transfers between devices: 53.4 us -> 58.4 us
  Pallas kernels: 15.4 us -> 19.6 us
  waiting for transfers between devices: 57.1 us -> 61.2 us
  local copies, waits for them, and re-layouts: 8.34 us -> 11.6 us
    ppermute x14 -> x20, starting transfers between devices: 22.4 us -> 32.6 us  [shift(): return lax.ppermute(value, axis, [(i, (i + by) % 4) for i in range(4)])]
    all_to_all x2, starting transfers between devices: 27.5 us -> 22 us  [the longest x1 13.1 us: local(): moved = lax.all_to_all(at, ROWS, 0, 0, tiled=True)]
    unnamed x17 -> x38, local copies, waits for them, and re-layouts: 5.74 us -> 10.1 us
    pallas_call x4 -> x8, Pallas kernels: 15.4 us -> 19.6 us  [the longest x1 7.25 us: local(): pl.pallas_call(near_kernel, out_shape=(shape(32, 64, 128), shape(32, 128,...]
    ppermute x14 -> x20, waiting for transfers between devices: 43 us -> 46.9 us  [shift(): return lax.ppermute(value, axis, [(i, (i + by) % 4) for i in range(4)])]
    ppermute x5 -> x9, waiting for transfers between devices: 1.93 us -> 3.81 us  [swap(): return lax.ppermute(value, 'c', [(0, 1), (1, 0)])]
  transfers between devices with their start and end apart: 23 -> 33, of which waited for: 15 -> 17; matrix products, arithmetic and copies ran while one was open for 5% -> 2% of each run, Pallas kernels for 2% -> 7%
where the time goes in v2:
time: 154 us; the launch traced here: 153 us
  waiting for transfers between devices  61.2 us (40%)
  starting transfers between devices  58.4 us (38%)
  Pallas kernels  19.6 us (13%)
  local copies, waits for them, and re-layouts  11.6 us (8%)
  other arithmetic  1.83 us (1%)
    ppermute x20, waiting for transfers between devices, shift(): return lax.ppermute(value, axis, [(i, (i + by) % 4) for i in range(4)])  46.9 us
    ppermute x20, starting transfers between devices, shift(): return lax.ppermute(value, axis, [(i, (i + by) % 4) for i in range(4)])  32.6 us
    all_to_all x1, starting transfers between devices, local(): moved = lax.all_to_all(at, ROWS, 0, 0, tiled=True)  13.1 us
    ppermute x2, waiting for transfers between devices, pair(): return lax.ppermute(value, 'z', [(0, 1), (1, 0), (2, 3), (3, 2)])  10.5 us
    unnamed x38, local copies, waits for them, and re-layouts  10.1 us
    all_to_all x1, starting transfers between devices, local(): back = lax.all_to_all(total, ROWS, 0, 0, tiled=True)  8.93 us
    pallas_call x1, Pallas kernels, local(): pl.pallas_call(near_kernel, out_shape=(shape(32, 64, 128), shape(32, 128,...  7.25 us
    pallas_call x1, Pallas kernels, local(): pl.pallas_call(far_kernel, out_shape=(shape(32, 8, 128),) * 4 + (shape(8,...  5.68 us
  transfers between devices with their start and end apart: 33, of which 17 were waited for; matrix products, arithmetic and copies ran while one was open for 2% of the time, Pallas kernels for 7%

profile of v2, /device:TPU:32, one launch (start us, length us, event | category | flops | bytes accessed | tf_op | source)
XLA Modules:
  0.0 152.8 jit_solution(8199710824385789561)
XLA Ops:
  0.1 1.6 %copy-done = f32[32,128,128]{2,1,0:T(8,128)S(1)} copy-done((f32[32,128,128]{2,1,0:T(8,128)S(1)}, f32[32,128,128]{2,1,0:T(8,128)}, u32[]{:S(2)}) %copy-start) | copy-done | bytes 2097176
  2.6 1.6 %prep.1 = (f32[32,16,128]{2,1,0:T(8,128)}, f32[2,4,32,128]{3,2,1,0:T(8,128)S(1)}, f32[2,4,32,128]{3,2,1,0:T(8,128)S(1)}, f32[2,128,128]{2,1,0:T(8,128)S(1)}) custom-call(s32[4]{0:T(128)S(1)} %pad_add_fusion.where, f32[32,128,128]{2,1,0:T(8,128)S(1)} %copy-done, f32[128,512]{1,0:T(8,128)S(1)} %copy-done.4), custom_call_target="tpu_custom_call" | custom-call | bytes 1048576 | tf_op jit(solution)/shard_map/prep/pallas_call | solution.py:248
  4.2 13.1 %all-to-all-start = ((f32[32,16,128]{2,1,0:T(8,128)}), f32[32,16,128]{2,1,0:T(8,128)S(1)}, u32[]{:S(2)}, u32[]{:S(2)}) async-start(f32[32,16,128]{2,1,0:T(8,128)} %get-tuple-element.30), calls=%async_computation | async-start | bytes 524288 | tf_op jit(solution)/shard_map/all_to_all | solution.py:259
  18.4 7.9 %collective-permute-done.6.own = f32[2,128,128]{2,1,0:T(8,128)S(1)} collective-permute-done((f32[2,128,128]{2,1,0:T(8,128)S(1)}, f32[2,128,128]{2,1,0:T(8,128)S(1)}, u32[]{:S(2)}, u32[]{:S(2)}) %collective-permute-start.6) | collective-permute-done | bytes 131104 | tf_op jit(solution)/shard_map/ppermute | solution.py:220
  26.3 2.9 %collective-permute-start.8 = (f32[2,128,128]{2,1,0:T(8,128)S(1)}, f32[2,128,128]{2,1,0:T(8,128)S(1)}, u32[]{:S(2)}, u32[]{:S(2)}) collective-permute-start(f32[2,128,128]{2,1,0:T(8,128)S(1)} %collective-permute-done.6.own), channel_id=1, source_target_pairs={{0,24},{8,0},{16,8},{24,16},{1,25},{9,1},{17,9},{25,17},{2,26},{10... | collective-permute-start | bytes 393224 | tf_op jit(solution)/shard_map/ppermute | solution.py:212
  29.1 2.8 %collective-permute-done.8.up = f32[2,128,128]{2,1,0:T(8,128)S(1)} collective-permute-done((f32[2,128,128]{2,1,0:T(8,128)S(1)}, f32[2,128,128]{2,1,0:T(8,128)S(1)}, u32[]{:S(2)}, u32[]{:S(2)}) %collective-permute-start.8) | collective-permute-done | bytes 131104 | tf_op jit(solution)/shard_map/ppermute | solution.py:212
  31.9 3.4 %collective-permute-start.10 = (f32[1,128,128]{2,1,0:T(8,128)S(1)}, f32[1,128,128]{2,1,0:T(8,128)S(1)}, u32[]{:S(2)}, u32[]{:S(2)}) collective-permute-start(f32[1,128,128]{2,1,0:T(8,128)S(1)} %slice.17), channel_id=1, source_target_pairs={{0,24},{8,0},{16,8},{24,16},{1,25},{9,1},{17,9},{25,17},{2,26},{10... | collective-permute-start | bytes 196616 | tf_op jit(solution)/shard_map/ppermute | solution.py:212
  35.4 1.8 %collective-permute-done.10.far_b = f32[1,128,128]{2,1,0:T(8,128)S(1)} collective-permute-done((f32[1,128,128]{2,1,0:T(8,128)S(1)}, f32[1,128,128]{2,1,0:T(8,128)S(1)}, u32[]{:S(2)}, u32[]{:S(2)}) %collective-permute-start.10) | collective-permute-done | bytes 65568 | tf_op jit(solution)/shard_map/ppermute | solution.py:212
  37.2 3.7 %collective-permute-done.9.far_a = f32[1,128,128]{2,1,0:T(8,128)S(1)} collective-permute-done((f32[1,128,128]{2,1,0:T(8,128)S(1)}, f32[1,128,128]{2,1,0:T(8,128)S(1)}, u32[]{:S(2)}, u32[]{:S(2)}) %collective-permute-start.9) | collective-permute-done | bytes 65568 | tf_op jit(solution)/shard_map/ppermute | solution.py:212
  42.1 1.5 collective-permute-start.15
  43.6 1.8 %collective-permute-start.16 = (f32[8,128,128]{2,1,0:T(8,128)S(1)}, f32[8,128,128]{2,1,0:T(8,128)S(1)}, u32[]{:S(2)}, u32[]{:S(2)}) collective-permute-start(f32[8,128,128]{2,1,0:T(8,128)S(1)} %get-tuple-element.36.refs_0_), channel_id=1, source_target_pairs={{0,192},{64,0},{128,64},{192,128},{1,193},{65,1},{129,65},{193,129... | collective-permute-start | bytes 1572872 | tf_op jit(solution)/shard_map/ppermute | solution.py:212
  49.6 1.6 %collective-permute-start.1 = (s32[64]{0:T(128)S(1)}, s32[64]{0:T(128)S(1)}, u32[]{:S(2)}, u32[]{:S(2)}) collective-permute-start(s32[64]{0:T(128)S(1)} %pad_add_fusion.1), channel_id=1, source_target_pairs={{0,2},{2,0},{4,6},{6,4},{1,3},{3,1},{5,7},{7,5},{8,10},{10,8},{12,... | collective-permute-start | bytes 776 | tf_op jit(solution)/shard_map/ppermute | solution.py:220
  51.2 2.5 %collective-permute-done.1 = s32[64]{0:T(128)S(1)} collective-permute-done((s32[64]{0:T(128)S(1)}, s32[64]{0:T(128)S(1)}, u32[]{:S(2)}, u32[]{:S(2)}) %collective-permute-start.1) | collective-permute-done | bytes 288 | tf_op jit(solution)/shard_map/ppermute | solution.py:220
  53.7 3.2 %collective-permute-start.4 = (f32[8,32,128]{2,1,0:T(8,128)S(1)}, f32[8,32,128]{2,1,0:T(8,128)S(1)}, u32[]{:S(2)}, u32[]{:S(2)}) collective-permute-start(f32[8,32,128]{2,1,0:T(8,128)S(1)} %get-tuple-element.28.b0), channel_id=1, source_target_pairs={{0,4},{2,6},{4,0},{6,2},{1,5},{3,7},{5,1},{7,3},{8,12},{10,14},{12... | collective-permute-start | bytes 393224 | tf_op jit(solution)/shard_map/ppermute | solution.py:212
  59.5 5.4 %collective-permute-done.4.b2 = f32[8,32,128]{2,1,0:T(8,128)S(1)} collective-permute-done((f32[8,32,128]{2,1,0:T(8,128)S(1)}, f32[8,32,128]{2,1,0:T(8,128)S(1)}, u32[]{:S(2)}, u32[]{:S(2)}) %collective-permute-start.4) | collective-permute-done | bytes 131104 | tf_op jit(solution)/shard_map/ppermute | solution.py:212
  66.2 3.4 %collective-permute-start.12 = (f32[32,8,128]{2,1,0:T(8,128)S(1)}, f32[32,8,128]{2,1,0:T(8,128)}, u32[]{:S(2)}, u32[]{:S(2)}) collective-permute-start(f32[32,8,128]{2,1,0:T(8,128)S(1)} %get-tuple-element.32.a0), channel_id=1, source_target_pairs={{0,4},{2,6},{4,0},{6,2},{1,5},{3,7},{5,1},{7,3},{8,12},{10,14},{12... | collective-permute-start | bytes 393224 | tf_op jit(solution)/shard_map/ppermute | solution.py:212
  69.6 2.1 %collective-permute-start.13 = (f32[32,8,128]{2,1,0:T(8,128)}, f32[32,8,128]{2,1,0:T(8,128)}, u32[]{:S(2)}, u32[]{:S(2)}) collective-permute-start(f32[32,8,128]{2,1,0:T(8,128)} %get-tuple-element.33), channel_id=1, source_target_pairs={{0,6},{2,0},{4,2},{6,4},{1,7},{3,1},{5,3},{7,5},{8,14},{10,8},{12,... | collective-permute-start | bytes 393224 | tf_op jit(solution)/shard_map/ppermute | solution.py:212
  72.5 5.7 %collective-permute-done.12.a2 = f32[32,8,128]{2,1,0:T(8,128)} collective-permute-done((f32[32,8,128]{2,1,0:T(8,128)S(1)}, f32[32,8,128]{2,1,0:T(8,128)}, u32[]{:S(2)}, u32[]{:S(2)}) %collective-permute-start.12) | collective-permute-done | bytes 131104 | tf_op jit(solution)/shard_map/ppermute | solution.py:212
  79.5 1.8 %collective-permute-done.13.a3 = f32[32,8,128]{2,1,0:T(8,128)} collective-permute-done((f32[32,8,128]{2,1,0:T(8,128)}, f32[32,8,128]{2,1,0:T(8,128)}, u32[]{:S(2)}, u32[]{:S(2)}) %collective-permute-start.13) | collective-permute-done | bytes 131104 | tf_op jit(solution)/shard_map/ppermute | solution.py:212
  82.8 2.9 %collective-permute-done.18.refs_4_ = f32[4,128,128]{2,1,0:T(8,128)} collective-permute-done((f32[4,128,128]{2,1,0:T(8,128)}, f32[4,128,128]{2,1,0:T(8,128)}, u32[]{:S(2)}, u32[]{:S(2)}) %collective-permute-start.18) | collective-permute-done | bytes 262176 | tf_op jit(solution)/shard_map/ppermute | solution.py:212
  90.6 7.2 %near.1 = (f32[32,64,128]{2,1,0:T(8,128)S(1)}, bf16[32,128,128]{2,1,0:T(8,128)(2,1)S(1)}) custom-call(s32[4]{0:T(128)S(1)} %pad_add_fusion.where, s32[128]{0:T(128)S(1)} %pad_add_fusion.2.cols, s32[128]{0:T(128)S(1)} %convert_reduce_fusion.owners, f32[8,32,128]{2,1,0:T(8,128)S(1)} %copy-done.6, f32[8,32,128]{2,1,0:T(8,128)S(1)} %copy-done.8, ...), custom_call_target="tpu_custom_call" | custom-call | flops 402653184 | bytes 7340032 | tf_op jit(solution)/shard_map/near/pallas_call | solution.py:272
  98.0 5.7 %far.1 = (f32[32,8,128]{2,1,0:T(8,128)S(1)}, f32[32,8,128]{2,1,0:T(8,128)S(1)}, f32[32,8,128]{2,1,0:T(8,128)S(1)}, f32[32,8,128]{2,1,0:T(8,128)S(1)}, f32[8,32,1...) custom-call(s32[4]{0:T(128)S(1)} %pad_add_fusion.where, ...), custom_call_target="tpu_custom_call" | custom-call | flops 402653184 | bytes 7340032 | tf_op jit(solution)/shard_map/far/pallas_call | solution.py:288
  105.6 2.9 %collective-permute-start.24 = (f32[32,8,128]{2,1,0:T(8,128)S(1)}, f32[32,8,128]{2,1,0:T(8,128)S(1)}, u32[]{:S(2)}, u32[]{:S(2)}) collective-permute-start(f32[32,8,128]{2,1,0:T(8,128)S(1)} %get-tuple-element.38), channel_id=1, source_target_pairs={{0,6},{2,0},{4,2},{6,4},{1,7},{3,1},{5,3},{7,5},{8,14},{10,8},{12,... | collective-permute-start | bytes 393224 | tf_op jit(solution)/shard_map/ppermute | solution.py:212
  109.2 2.9 %collective-permute-start.26 = (f32[32,8,128]{2,1,0:T(8,128)S(1)}, f32[32,8,128]{2,1,0:T(8,128)S(1)}, u32[]{:S(2)}, u32[]{:S(2)}) collective-permute-start(f32[32,8,128]{2,1,0:T(8,128)S(1)} %get-tuple-element.40), channel_id=1, source_target_pairs={{0,2},{2,4},{4,6},{6,0},{1,3},{3,5},{5,7},{7,1},{8,10},{10,12},{12... | collective-permute-start | bytes 393224 | tf_op jit(solution)/shard_map/ppermute | solution.py:212
  112.2 6.6 %collective-permute-done.25.r2 = f32[32,8,128]{2,1,0:T(8,128)S(1)} collective-permute-done((f32[32,8,128]{2,1,0:T(8,128)S(1)}, f32[32,8,128]{2,1,0:T(8,128)S(1)}, u32[]{:S(2)}, u32[]{:S(2)}) %collective-permute-start.25) | collective-permute-done | bytes 131104 | tf_op jit(solution)/shard_map/ppermute | solution.py:212
  118.8 1.9 %collective-permute-done.26.r3 = f32[32,8,128]{2,1,0:T(8,128)S(1)} collective-permute-done((f32[32,8,128]{2,1,0:T(8,128)S(1)}, f32[32,8,128]{2,1,0:T(8,128)S(1)}, u32[]{:S(2)}, u32[]{:S(2)}) %collective-permute-start.26) | collective-permute-done | bytes 131104 | tf_op jit(solution)/shard_map/ppermute | solution.py:212
  121.9 8.9 %all-to-all-start.1 = ((f32[32,16,128]{2,1,0:T(8,128)}), f32[32,16,128]{2,1,0:T(8,128)S(1)}, u32[]{:S(2)}, u32[]{:S(2)}) async-start(f32[32,16,128]{2,1,0:T(8,128)} %gather_kernel.1), calls=%async_computation.1 | async-start | bytes 524288 | tf_op jit(solution)/shard_map/all_to_all | solution.py:307
  130.8 2.6 %collective-permute-start.27 = (f32[8,32,128]{2,1,0:T(8,128)}, f32[8,32,128]{2,1,0:T(8,128)S(1)}, u32[]{:S(2)}, u32[]{:S(2)}) collective-permute-start(f32[8,32,128]{2,1,0:T(8,128)} %copy-done.15), channel_id=1, source_target_pairs={{0,2},{2,4},{4,6},{6,0},{1,3},{3,5},{5,7},{7,1},{8,10},{10,12},{12... | collective-permute-start | bytes 393224 | tf_op jit(solution)/shard_map/ppermute | solution.py:212
  133.4 1.5 collective-permute-start.28
  134.9 11.7 %collective-permute-done.27.r1 = f32[8,32,128]{2,1,0:T(8,128)S(1)} collective-permute-done((f32[8,32,128]{2,1,0:T(8,128)}, f32[8,32,128]{2,1,0:T(8,128)S(1)}, u32[]{:S(2)}, u32[]{:S(2)}) %collective-permute-start.27) | collective-permute-done | bytes 131104 | tf_op jit(solution)/shard_map/ppermute | solution.py:212
  146.7 1.8 %collective-permute-done.28.r2 = f32[8,32,128]{2,1,0:T(8,128)S(1)} collective-permute-done((f32[8,32,128]{2,1,0:T(8,128)}, f32[8,32,128]{2,1,0:T(8,128)S(1)}, u32[]{:S(2)}, u32[]{:S(2)}) %collective-permute-start.28) | collective-permute-done | bytes 131104 | tf_op jit(solution)/shard_map/ppermute | solution.py:212
  151.4 1.4 final_kernel.1
  (92 shorter events, 27.0 us)
Async XLA Ops:
  0.0 85.7 %collective-permute-start.14 = (f32[32,128,128]{2,1,0:T(8,128)}, f32[32,128,128]{2,1,0:T(8,128)}, u32[]{:S(2)}, u32[]{:S(2)}) collective-permute-start(f32[32,128,128]{2,1,0:T(8,128)} %h0.1), channel_id=1, source_target_pairs={{0,1},{1,0},{2,3},{3,2},{4,5},{5,4},{6,7},{7,6},{8,9},{9,8},{10,11... | collective-permute-start | bytes 6291464 | tf_op jit(solution)/shard_map/ppermute | solution.py:216
  4.2 36.7 %all-to-all-start = ((f32[32,16,128]{2,1,0:T(8,128)}), f32[32,16,128]{2,1,0:T(8,128)S(1)}, u32[]{:S(2)}, u32[]{:S(2)}) async-start(f32[32,16,128]{2,1,0:T(8,128)} %get-tuple-element.30), calls=%async_computation | async-start | bytes 524288 | tf_op jit(solution)/shard_map/all_to_all | solution.py:259
  17.3 9.0 %collective-permute-start.6 = (f32[2,128,128]{2,1,0:T(8,128)S(1)}, f32[2,128,128]{2,1,0:T(8,128)S(1)}, u32[]{:S(2)}, u32[]{:S(2)}) collective-permute-start(f32[2,128,128]{2,1,0:T(8,128)S(1)} %get-tuple-element.31), channel_id=1, source_target_pairs={{0,2},{2,0},{4,6},{6,4},{1,3},{3,1},{5,7},{7,5},{8,10},{10,8},{12,... | collective-permute-start | bytes 393224 | tf_op jit(solution)/shard_map/ppermute | solution.py:220
  26.3 5.6 %collective-permute-start.8 = (f32[2,128,128]{2,1,0:T(8,128)S(1)}, f32[2,128,128]{2,1,0:T(8,128)S(1)}, u32[]{:S(2)}, u32[]{:S(2)}) collective-permute-start(f32[2,128,128]{2,1,0:T(8,128)S(1)} %collective-permute-done.6.own), channel_id=1, source_target_pairs={{0,24},{8,0},{16,8},{24,16},{1,25},{9,1},{17,9},{25,17},{2,26},{10... | collective-permute-start | bytes 393224 | tf_op jit(solution)/shard_map/ppermute | solution.py:212
  29.1 6.2 %collective-permute-start.7 = (f32[2,128,128]{2,1,0:T(8,128)S(1)}, f32[2,128,128]{2,1,0:T(8,128)S(1)}, u32[]{:S(2)}, u32[]{:S(2)}) collective-permute-start(f32[2,128,128]{2,1,0:T(8,128)S(1)} %collective-permute-done.6.own), channel_id=1, source_target_pairs={{0,8},{8,16},{16,24},{24,0},{1,9},{9,17},{17,25},{25,1},{2,10},{10... | collective-permute-start | bytes 393224 | tf_op jit(solution)/shard_map/ppermute | solution.py:212
  31.9 5.3 %collective-permute-start.10 = (f32[1,128,128]{2,1,0:T(8,128)S(1)}, f32[1,128,128]{2,1,0:T(8,128)S(1)}, u32[]{:S(2)}, u32[]{:S(2)}) collective-permute-start(f32[1,128,128]{2,1,0:T(8,128)S(1)} %slice.17), channel_id=1, source_target_pairs={{0,24},{8,0},{16,8},{24,16},{1,25},{9,1},{17,9},{25,17},{2,26},{10... | collective-permute-start | bytes 196616 | tf_op jit(solution)/shard_map/ppermute | solution.py:212
  35.3 5.6 %collective-permute-start.9 = (f32[1,128,128]{2,1,0:T(8,128)S(1)}, f32[1,128,128]{2,1,0:T(8,128)S(1)}, u32[]{:S(2)}, u32[]{:S(2)}) collective-permute-start(f32[1,128,128]{2,1,0:T(8,128)S(1)} %slice.16), channel_id=1, source_target_pairs={{0,8},{8,16},{16,24},{24,0},{1,9},{9,17},{17,25},{25,1},{2,10},{10... | collective-permute-start | bytes 196616 | tf_op jit(solution)/shard_map/ppermute | solution.py:212
  42.1 14.9 %collective-permute-start.15 = (f32[8,128,128]{2,1,0:T(8,128)S(1)}, f32[8,128,128]{2,1,0:T(8,128)S(1)}, u32[]{:S(2)}, u32[]{:S(2)}) collective-permute-start(f32[8,128,128]{2,1,0:T(8,128)S(1)} %get-tuple-element.36.refs_0_), channel_id=1, source_target_pairs={{0,64},{64,128},{128,192},{192,0},{1,65},{65,129},{129,193},{193,1... | collective-permute-start | bytes 1572872 | tf_op jit(solution)/shard_map/ppermute | solution.py:212
  43.6 26.0 %collective-permute-start.16 = (f32[8,128,128]{2,1,0:T(8,128)S(1)}, f32[8,128,128]{2,1,0:T(8,128)S(1)}, u32[]{:S(2)}, u32[]{:S(2)}) collective-permute-start(f32[8,128,128]{2,1,0:T(8,128)S(1)} %get-tuple-element.36.refs_0_), channel_id=1, source_target_pairs={{0,192},{64,0},{128,64},{192,128},{1,193},{65,1},{129,65},{193,129... | collective-permute-start | bytes 1572872 | tf_op jit(solution)/shard_map/ppermute | solution.py:212
  45.4 1.3 collective-permute-start.2
  47.3 11.3 %collective-permute-start.3 = (f32[8,32,128]{2,1,0:T(8,128)S(1)}, f32[8,32,128]{2,1,0:T(8,128)S(1)}, u32[]{:S(2)}, u32[]{:S(2)}) collective-permute-start(f32[8,32,128]{2,1,0:T(8,128)S(1)} %get-tuple-element.29), channel_id=1, source_target_pairs={{0,2},{2,4},{4,6},{6,0},{1,3},{3,5},{5,7},{7,1},{8,10},{10,12},{12... | collective-permute-start | bytes 393224 | tf_op jit(solution)/shard_map/ppermute | solution.py:212
  49.6 4.1 %collective-permute-start.1 = (s32[64]{0:T(128)S(1)}, s32[64]{0:T(128)S(1)}, u32[]{:S(2)}, u32[]{:S(2)}) collective-permute-start(s32[64]{0:T(128)S(1)} %pad_add_fusion.1), channel_id=1, source_target_pairs={{0,2},{2,0},{4,6},{6,4},{1,3},{3,1},{5,7},{7,5},{8,10},{10,8},{12,... | collective-permute-start | bytes 776 | tf_op jit(solution)/shard_map/ppermute | solution.py:220
  53.7 11.1 %collective-permute-start.4 = (f32[8,32,128]{2,1,0:T(8,128)S(1)}, f32[8,32,128]{2,1,0:T(8,128)S(1)}, u32[]{:S(2)}, u32[]{:S(2)}) collective-permute-start(f32[8,32,128]{2,1,0:T(8,128)S(1)} %get-tuple-element.28.b0), channel_id=1, source_target_pairs={{0,4},{2,6},{4,0},{6,2},{1,5},{3,7},{5,1},{7,3},{8,12},{10,14},{12... | collective-permute-start | bytes 393224 | tf_op jit(solution)/shard_map/ppermute | solution.py:212
  57.0 8.5 %collective-permute-start.5 = (f32[8,32,128]{2,1,0:T(8,128)S(1)}, f32[8,32,128]{2,1,0:T(8,128)S(1)}, u32[]{:S(2)}, u32[]{:S(2)}) collective-permute-start(f32[8,32,128]{2,1,0:T(8,128)S(1)} %get-tuple-element.29), channel_id=1, source_target_pairs={{0,6},{2,0},{4,2},{6,4},{1,7},{3,1},{5,3},{7,5},{8,14},{10,8},{12,... | collective-permute-start | bytes 393224 | tf_op jit(solution)/shard_map/ppermute | solution.py:212
  59.2 22.2 %collective-permute-start.17 = (f32[4,128,128]{2,1,0:T(8,128)}, f32[4,128,128]{2,1,0:T(8,128)S(1)}, u32[]{:S(2)}, u32[]{:S(2)}) collective-permute-start(f32[4,128,128]{2,1,0:T(8,128)} %slice.18), channel_id=1, source_target_pairs={{0,64},{64,128},{128,192},{192,0},{1,65},{65,129},{129,193},{193,1... | collective-permute-start | bytes 786440 | tf_op jit(solution)/shard_map/ppermute | solution.py:212
  65.5 7.0 %collective-permute-start.11 = (f32[32,8,128]{2,1,0:T(8,128)}, f32[32,8,128]{2,1,0:T(8,128)}, u32[]{:S(2)}, u32[]{:S(2)}) collective-permute-start(f32[32,8,128]{2,1,0:T(8,128)} %get-tuple-element.33), channel_id=1, source_target_pairs={{0,2},{2,4},{4,6},{6,0},{1,3},{3,5},{5,7},{7,1},{8,10},{10,12},{12... | collective-permute-start | bytes 393224 | tf_op jit(solution)/shard_map/ppermute | solution.py:212
  66.2 12.0 %collective-permute-start.12 = (f32[32,8,128]{2,1,0:T(8,128)S(1)}, f32[32,8,128]{2,1,0:T(8,128)}, u32[]{:S(2)}, u32[]{:S(2)}) collective-permute-start(f32[32,8,128]{2,1,0:T(8,128)S(1)} %get-tuple-element.32.a0), channel_id=1, source_target_pairs={{0,4},{2,6},{4,0},{6,2},{1,5},{3,7},{5,1},{7,3},{8,12},{10,14},{12... | collective-permute-start | bytes 393224 | tf_op jit(solution)/shard_map/ppermute | solution.py:212
  69.6 11.8 %collective-permute-start.13 = (f32[32,8,128]{2,1,0:T(8,128)}, f32[32,8,128]{2,1,0:T(8,128)}, u32[]{:S(2)}, u32[]{:S(2)}) collective-permute-start(f32[32,8,128]{2,1,0:T(8,128)} %get-tuple-element.33), channel_id=1, source_target_pairs={{0,6},{2,0},{4,2},{6,4},{1,7},{3,1},{5,3},{7,5},{8,14},{10,8},{12,... | collective-permute-start | bytes 393224 | tf_op jit(solution)/shard_map/ppermute | solution.py:212
  72.5 25.4 %collective-permute-start.19 = (f32[8,128,128]{2,1,0:T(8,128)}, f32[8,128,128]{2,1,0:T(8,128)}, u32[]{:S(2)}, u32[]{:S(2)}) collective-permute-start(f32[8,128,128]{2,1,0:T(8,128)} %copy-done.2), channel_id=1, source_target_pairs={{0,1},{1,0},{2,3},{3,2},{4,5},{5,4},{6,7},{7,6},{8,9},{9,8},{10,11... | collective-permute-start | bytes 1572872 | tf_op jit(solution)/shard_map/ppermute | solution.py:216
  78.2 7.5 %collective-permute-start.18 = (f32[4,128,128]{2,1,0:T(8,128)}, f32[4,128,128]{2,1,0:T(8,128)}, u32[]{:S(2)}, u32[]{:S(2)}) collective-permute-start(f32[4,128,128]{2,1,0:T(8,128)} %slice.19), channel_id=1, source_target_pairs={{0,192},{64,0},{128,64},{192,128},{1,193},{65,1},{129,65},{193,129... | collective-permute-start | bytes 786440 | tf_op jit(solution)/shard_map/ppermute | solution.py:212
  81.4 16.6 %collective-permute-start.20 = (f32[8,128,128]{2,1,0:T(8,128)S(1)}, f32[8,128,128]{2,1,0:T(8,128)}, u32[]{:S(2)}, u32[]{:S(2)}) collective-permute-start(f32[8,128,128]{2,1,0:T(8,128)S(1)} %collective-permute-done.15.refs_1_), channel_id=1, source_target_pairs={{0,1},{1,0},{2,3},{3,2},{4,5},{5,4},{6,7},{7,6},{8,9},{9,8},{10,11... | collective-permute-start | bytes 1572872 | tf_op jit(solution)/shard_map/ppermute | solution.py:216
  81.4 16.6 %collective-permute-start.21 = (f32[8,128,128]{2,1,0:T(8,128)S(1)}, f32[8,128,128]{2,1,0:T(8,128)}, u32[]{:S(2)}, u32[]{:S(2)}) collective-permute-start(f32[8,128,128]{2,1,0:T(8,128)S(1)} %collective-permute-done.16.refs_2_), channel_id=1, source_target_pairs={{0,1},{1,0},{2,3},{3,2},{4,5},{5,4},{6,7},{7,6},{8,9},{9,8},{10,11... | collective-permute-start | bytes 1572872 | tf_op jit(solution)/shard_map/ppermute | solution.py:216
  85.7 12.2 %collective-permute-start.22 = (f32[4,128,128]{2,1,0:T(8,128)S(1)}, f32[4,128,128]{2,1,0:T(8,128)S(1)}, u32[]{:S(2)}, u32[]{:S(2)}) collective-permute-start(f32[4,128,128]{2,1,0:T(8,128)S(1)} %collective-permute-done.17.refs_3_), channel_id=1, source_target_pairs={{0,1},{1,0},{2,3},{3,2},{4,5},{5,4},{6,7},{7,6},{8,9},{9,8},{10,11... | collective-permute-start | bytes 786440 | tf_op jit(solution)/shard_map/ppermute | solution.py:216
  85.7 12.2 %collective-permute-start.23 = (f32[4,128,128]{2,1,0:T(8,128)}, f32[4,128,128]{2,1,0:T(8,128)S(1)}, u32[]{:S(2)}, u32[]{:S(2)}) collective-permute-start(f32[4,128,128]{2,1,0:T(8,128)} %collective-permute-done.18.refs_4_), channel_id=1, source_target_pairs={{0,1},{1,0},{2,3},{3,2},{4,5},{5,4},{6,7},{7,6},{8,9},{9,8},{10,11... | collective-permute-start | bytes 786440 | tf_op jit(solution)/shard_map/ppermute | solution.py:216
  105.6 6.6 %collective-permute-start.24 = (f32[32,8,128]{2,1,0:T(8,128)S(1)}, f32[32,8,128]{2,1,0:T(8,128)S(1)}, u32[]{:S(2)}, u32[]{:S(2)}) collective-permute-start(f32[32,8,128]{2,1,0:T(8,128)S(1)} %get-tuple-element.38), channel_id=1, source_target_pairs={{0,6},{2,0},{4,2},{6,4},{1,7},{3,1},{5,3},{7,5},{8,14},{10,8},{12,... | collective-permute-start | bytes 393224 | tf_op jit(solution)/shard_map/ppermute | solution.py:212
  108.5 10.3 %collective-permute-start.25 = (f32[32,8,128]{2,1,0:T(8,128)S(1)}, f32[32,8,128]{2,1,0:T(8,128)S(1)}, u32[]{:S(2)}, u32[]{:S(2)}) collective-permute-start(f32[32,8,128]{2,1,0:T(8,128)S(1)} %get-tuple-element.39), channel_id=1, source_target_pairs={{0,4},{2,6},{4,0},{6,2},{1,5},{3,7},{5,1},{7,3},{8,12},{10,14},{12... | collective-permute-start | bytes 393224 | tf_op jit(solution)/shard_map/ppermute | solution.py:212
  109.2 11.4 %collective-permute-start.26 = (f32[32,8,128]{2,1,0:T(8,128)S(1)}, f32[32,8,128]{2,1,0:T(8,128)S(1)}, u32[]{:S(2)}, u32[]{:S(2)}) collective-permute-start(f32[32,8,128]{2,1,0:T(8,128)S(1)} %get-tuple-element.40), channel_id=1, source_target_pairs={{0,2},{2,4},{4,6},{6,0},{1,3},{3,5},{5,7},{7,1},{8,10},{10,12},{12... | collective-permute-start | bytes 393224 | tf_op jit(solution)/shard_map/ppermute | solution.py:212
  121.9 29.5 %all-to-all-start.1 = ((f32[32,16,128]{2,1,0:T(8,128)}), f32[32,16,128]{2,1,0:T(8,128)S(1)}, u32[]{:S(2)}, u32[]{:S(2)}) async-start(f32[32,16,128]{2,1,0:T(8,128)} %gather_kernel.1), calls=%async_computation.1 | async-start | bytes 524288 | tf_op jit(solution)/shard_map/all_to_all | solution.py:307
  130.8 15.8 %collective-permute-start.27 = (f32[8,32,128]{2,1,0:T(8,128)}, f32[8,32,128]{2,1,0:T(8,128)S(1)}, u32[]{:S(2)}, u32[]{:S(2)}) collective-permute-start(f32[8,32,128]{2,1,0:T(8,128)} %copy-done.15), channel_id=1, source_target_pairs={{0,2},{2,4},{4,6},{6,0},{1,3},{3,5},{5,7},{7,1},{8,10},{10,12},{12... | collective-permute-start | bytes 393224 | tf_op jit(solution)/shard_map/ppermute | solution.py:212
  133.4 15.0 %collective-permute-start.28 = (f32[8,32,128]{2,1,0:T(8,128)}, f32[8,32,128]{2,1,0:T(8,128)S(1)}, u32[]{:S(2)}, u32[]{:S(2)}) collective-permute-start(f32[8,32,128]{2,1,0:T(8,128)} %copy-done.14), channel_id=1, source_target_pairs={{0,4},{2,6},{4,0},{6,2},{1,5},{3,7},{5,1},{7,3},{8,12},{10,14},{12... | collective-permute-start | bytes 393224 | tf_op jit(solution)/shard_map/ppermute | solution.py:212
  134.9 14.4 %collective-permute-start.29 = (f32[8,32,128]{2,1,0:T(8,128)}, f32[8,32,128]{2,1,0:T(8,128)S(1)}, u32[]{:S(2)}, u32[]{:S(2)}) collective-permute-start(f32[8,32,128]{2,1,0:T(8,128)} %copy-done.13), channel_id=1, source_target_pairs={{0,6},{2,0},{4,2},{6,4},{1,7},{3,1},{5,3},{7,5},{8,14},{10,8},{12,... | collective-permute-start | bytes 393224 | tf_op jit(solution)/shard_map/ppermute | solution.py:212
  149.9 1.4 collective-permute-start.30
  (20 other events, 209.2 us)

commit v3 on v0

v3 whole, which is shorter than its diff:
```python
import jax
import jax.numpy as jnp
from jax import lax
from jax.experimental import pallas as pl
from jax.experimental.pallas import tpu as pltpu
from jax.sharding import Mesh
from jax.sharding import PartitionSpec as P

ROWS = ("y", "h", "x")
ANY = pl.BlockSpec(memory_space=pl.ANY)
VMEM = pl.BlockSpec(memory_space=pltpu.VMEM)
SMEM = pl.BlockSpec(memory_space=pltpu.SMEM)
F32 = jnp.float32
BF16 = jnp.bfloat16
TRASH = 28
CONTRACT = (((1,), (1,)), ((), ()))

def params(mib):
    return pltpu.CompilerParams(vmem_limit_bytes=mib << 20)


def cost(flops, moved):
    return pl.CostEstimate(flops=flops, bytes_accessed=moved, transcendentals=0)


def shape(*dims, kind=F32):
    return jax.ShapeDtypeStruct(dims, kind)


def turn_kernel(c_ref, at_ref):
    for t in range(4):
        turned = jnp.transpose(c_ref[:, 128 * t : 128 * (t + 1)]).reshape(8, 16, 128)
        for plane in range(4):
            at_ref[8 * t : 8 * (t + 1), plane] = turned


def halves(value):
    high = value.astype(BF16)
    return high, (value - high.astype(F32)).astype(BF16)


def product(left, block):
    high, low = halves(block)
    rows = left.shape[0] // 2
    one = lax.dot_general(left, high, CONTRACT, preferred_element_type=F32)
    two = lax.dot_general(left[:rows], low, CONTRACT, preferred_element_type=F32)
    return one[:rows] + (one[rows:] + two)


def beta_kernel(
    where, cols, slots, w0, w1, w2, w3, h0, h1, keep_ref, send_ref, token_ref,
    wide, stack, hbuf, acc, list_ref, sem_w, sem_h,
):
    z, core = where[2], where[3]
    loads = [
        pltpu.make_async_copy(w, wide.at[k], sem_w.at[k]) for k, w in enumerate((w0, w1, w2, w3))
    ]
    chunks = [
        pltpu.make_async_copy(h, hbuf.at[pl.ds(32 * n, 32)], sem_h.at[n])
        for n, h in enumerate((h0, h1))
    ]
    for copy in loads + chunks:
        copy.start()
    acc[...] = jnp.zeros_like(acc)

    def note(n, count):
        list_ref[count] = n
        return count + jnp.where(slots[n] < TRASH, 1, 0)

    count = lax.fori_loop(0, 64, note, 0)
    list_ref[count] = 0
    for k, load in enumerate(loads):
        home = 4 * jnp.bitwise_and(z - k + 4, 3)
        load.wait()
        for t in range(4):
            high, low = halves(wide[k, :, 128 * t : 128 * (t + 1)])
            stack[home + t, :128] = high
            stack[home + t, 128:] = low
    for chunk in chunks:
        chunk.wait()

    @pl.loop(0, lax.shift_right_logical(count + 1, 1))
    def _(step):
        terms = []
        for u in range(2):
            n = list_ref[2 * step + u]
            column = cols[n]
            left = stack[4 * lax.shift_right_logical(column, 3) + jnp.bitwise_and(column, 3)]
            slot = jnp.where(2 * step + u < count, slots[n], TRASH)
            terms.append((slot, product(left, hbuf[n])))
        for slot, term in terms:
            acc[slot] += term

    for group in range(3):
        keep_ref[4 * group : 4 * group + 4] = acc[pl.ds(8 * group + 4 * core, 4)]
        send_ref[4 * group : 4 * group + 4] = acc[pl.ds(8 * group + 4 * (1 - core), 4)]
    mine = core == jnp.where(z == 0, 0, 1)
    edge = acc[24:28]
    keep_ref[12:] = jnp.where(mine, edge, 0.0)
    send_ref[12:] = jnp.where(mine, 0.0, edge)
    token_ref[...] = jnp.zeros_like(token_ref)


def alpha_kernel(cols, owners, a_ref, h0, h1, after, acc, stack, hbuf, sem_h):
    chunks = []
    for n in range(4):
        source = (h0, h1)[n // 2].at[pl.ds(16 * (n % 2), 16)]
        chunks.append(pltpu.make_async_copy(source, hbuf.at[pl.ds(16 * n, 16)], sem_h.at[n]))
    for chunk in chunks:
        chunk.start()
    acc[...] = jnp.zeros_like(acc)

    @pl.loop(0, 32)
    def _(j):
        high, low = halves(a_ref[j])
        stack[j, :64] = high
        stack[j, 64:] = low

    for n, chunk in enumerate(chunks):
        chunk.wait()

        @pl.loop(0, 4)
        def _(step, n=n):
            terms = []
            for u in range(4):
                spot = 16 * n + 4 * step + u
                terms.append((owners[spot], product(stack[cols[spot]], hbuf[spot])))
            for owner, term in terms:
                acc[owner] += term


def cores_kernel(keep_ref, got_ref, own_ref, down_ref, up_ref, edge_ref):
    for n, ref in enumerate((own_ref, down_ref, up_ref, edge_ref)):
        ref[...] = keep_ref[4 * n : 4 * n + 4] + got_ref[4 * n : 4 * n + 4]


def final_kernel(back_ref, own_ref, down_ref, up_ref, edge_ref, out_ref):
    for t in range(4):
        part = back_ref[8 * t : 8 * (t + 1)]
        total = (part[:, 0] + part[:, 1]) + (part[:, 2] + part[:, 3])
        beta = (own_ref[t] + down_ref[t]) + (up_ref[t] + edge_ref[t])
        out_ref[:, 128 * t : 128 * (t + 1)] = jnp.transpose(total.reshape(128, 128)) + beta


def swap(value):
    return lax.ppermute(value, "c", [(0, 1), (1, 0)])


def tables(hcount, hcols, z, c):
    cols = jnp.concatenate([hcols, swap(hcols)])
    marks = jnp.arange(32, dtype=jnp.int32)
    row_end = jnp.sum(jnp.where(marks[:, None] <= marks[None, :], hcount[:, None], 0), axis=0)
    shard = jnp.stack([2 * z + c, 2 * z + 1 - c])
    index = (32 * shard[:, None].astype(jnp.int32) + marks[None, :]).reshape(64)
    owners = jnp.sum((row_end[None, :] <= index[:, None]).astype(jnp.int32), axis=1)
    step = owners // 8 - z
    slots = owners % 8 + jnp.where(step == 0, 0, jnp.where(step == -1, 8, 16))
    slots = jnp.where(step == 2, 24 + owners - 16, jnp.where(step == -2, 24 + owners - 12, slots))
    return cols, owners, jnp.where((cols // 4) % 2 == c, slots, TRASH)


def call(kernel, outs, in_specs, *args, scratch=(), mib=16, work=(0, 1 << 20)):
    single = not isinstance(outs, tuple)
    return pl.pallas_call(
        kernel,
        out_shape=outs,
        in_specs=in_specs,
        out_specs=VMEM if single else (VMEM,) * len(outs),
        scratch_shapes=scratch,
        compiler_params=params(mib),
        cost_estimate=cost(*work),
        name=kernel.__name__,
    )(*args)


def local(coeffs, hblocks, hcount, hcols):
    z, c = lax.axis_index("z"), lax.axis_index("c")
    where = jnp.stack([z, z, z, c]).astype(jnp.int32)
    swapped = swap(hblocks)
    rows = [coeffs] + [
        lax.ppermute(coeffs, "z", [(i, (i + k) % 4) for i in range(4)]) for k in (1, 2, 3)
    ]
    cols, owners, slots = tables(hcount, hcols, z, c)
    at = call(turn_kernel, shape(32, 4, 16, 128), [VMEM], coeffs)
    moved = lax.all_to_all(at.reshape(2048, 128), ROWS + ("z",), 0, 0, tiled=True)

    keep, send, token = call(
        beta_kernel,
        (shape(16, 128, 128), shape(16, 128, 128), shape(8, 128)),
        [SMEM] * 3 + [ANY] * 6,
        where, cols, slots, *rows, hblocks, swapped,
        scratch=[
            pltpu.VMEM((4, 128, 512), F32),
            pltpu.VMEM((16, 256, 128), BF16),
            pltpu.VMEM((64, 128, 128), F32),
            pltpu.VMEM((TRASH + 1, 128, 128), F32),
            pltpu.SMEM((72,), jnp.int32),
            pltpu.SemaphoreType.DMA((4,)),
            pltpu.SemaphoreType.DMA((2,)),
        ],
        mib=24,
        work=(6 * 32 * 128 * 128 * 128, 7 << 20),
    )
    (out_a,) = call(
        alpha_kernel,
        (shape(32, 64, 128),),
        [SMEM] * 2 + [VMEM] + [ANY] * 2 + [VMEM],
        cols, owners, moved.reshape(32, 64, 128), hblocks, swapped, token,
        scratch=[
            pltpu.VMEM((32, 128, 128), BF16),
            pltpu.VMEM((64, 128, 128), F32),
            pltpu.SemaphoreType.DMA((4,)),
        ],
        mib=24,
        work=(6 * 64 * 64 * 128 * 128, 7 << 20),
    )

    back = lax.all_to_all(out_a.reshape(2048, 128), ROWS + ("z",), 0, 0, tiled=True)
    own, down, up, edge = call(
        cores_kernel, (shape(4, 128, 128),) * 4, [VMEM] * 2, keep, swap(send)
    )
    down = lax.ppermute(down, "z", [(1, 0), (2, 1), (3, 2)])
    up = lax.ppermute(up, "z", [(0, 1), (1, 2), (2, 3)])
    edge = lax.ppermute(edge, "z", [(0, 2), (3, 1)])
    return call(
        final_kernel, shape(128, 512), [VMEM] * 5,
        back.reshape(32, 4, 16, 128), own, down, up, edge,
    )


def solution(mesh):
    fine = Mesh(mesh.devices.reshape(4, 2, 4, 4, 2), ("y", "h", "x", "z", "c"))
    in_specs = (P(ROWS, ("z", "c")), P(("z", "c"), None, None), P(), P(("z", "c")))
    out_specs = P(ROWS, ("z", "c"))
    return jax.shard_map(local, mesh=fine, in_specs=in_specs, out_specs=out_specs, check_vma=False)
```

time: 289 us -> 128 us (0.44); the launches traced: 283 us -> 127 us
  waiting for transfers between devices: 154 us -> 70 us
  local copies, waits for them, and re-layouts: 63.7 us -> 4.15 us
  matrix products: 18.3 us -> 0 us
  starting transfers between devices: 21.8 us -> 38.9 us
  Pallas kernels: 0 us -> 13.7 us
  between operations: 13.5 us -> 0.12 us
  other arithmetic: 11.7 us -> 0.5 us
    reduce_scatter x1 -> x0, waiting for transfers between devices: 74.9 us -> none  [local(): return lax.psum_scatter(joined, 'layer', scatter_dimension=1, tiled=True)]
    ppermute x0 -> x9, waiting for transfers between devices: none -> 70 us  [the longest x3 40.8 us: local(): lax.ppermute(coeffs, 'z', [(i, (i + k) % 4) for i in range(4)])]
    all_to_all x2, waiting for transfers between devices: 39.8 us -> 0.01 us  [the longest x1 0.01 us: local(): lax.all_to_all(out_a.reshape(2048, 128), ROWS + ('z',), 0, 0, tiled=True)]
    all_gather x1 -> x0, waiting for transfers between devices: 39.6 us -> none  [local(): full_rows = lax.all_gather(coeffs, 'layer', axis=1, tiled=True)]
    unnamed x11 -> x20, local copies, waits for them, and re-layouts: 23.3 us -> 4.07 us
    dot_general x4 -> x0, matrix products: 18.3 us -> none  [the longest x2 12.1 us: apply_blocks(): jnp.einsum('rzc,zbc->rzb', picked, blocks, precision=lax.Precision.HIGHEST)]
    pallas_call x0 -> x5, Pallas kernels: none -> 13.7 us  [call(): pl.pallas_call(kernel, out_shape=outs, in_specs=in_specs, out_specs=VMEM...]
    another operation x3 -> x0, local copies, waits for them, and re-layouts: 12.4 us -> none  [the longest x2 12.3 us: local(): sectioned = alpha_part.reshape(layer_size, subset_size, strings)]
  transfers between devices with their start and end apart: 4 -> 11, of which waited for: 4 -> 8; matrix products, arithmetic and copies ran while one was open for 6% -> 0% of each run, Pallas kernels for 0% -> 6%
where the time goes in v3:
time: 128 us; the launch traced here: 127 us
  waiting for transfers between devices  70 us (55%)
  starting transfers between devices  38.9 us (30%)
  Pallas kernels  13.7 us (11%)
  local copies, waits for them, and re-layouts  4.15 us (3%)
    ppermute x3, waiting for transfers between devices, local(): lax.ppermute(coeffs, 'z', [(i, (i + k) % 4) for i in range(4)])  40.8 us
    ppermute x1, waiting for transfers between devices, local(): down = lax.ppermute(down, 'z', [(1, 0), (2, 1), (3, 2)])  19.5 us
    all_to_all x1, starting transfers between devices, local(): lax.all_to_all(at.reshape(2048, 128), ROWS + ('z',), 0, 0, tiled=True)  15 us
    pallas_call x5, Pallas kernels, call(): pl.pallas_call(kernel, out_shape=outs, in_specs=in_specs, out_specs=VMEM...  13.7 us
    all_to_all x1, starting transfers between devices, local(): lax.all_to_all(out_a.reshape(2048, 128), ROWS + ('z',), 0, 0, tiled=True)  12.2 us
    ppermute x1, waiting for transfers between devices, local(): edge = lax.ppermute(edge, 'z', [(0, 2), (3, 1)])  6.23 us
    ppermute x3, starting transfers between devices, local(): lax.ppermute(coeffs, 'z', [(i, (i + k) % 4) for i in range(4)])  4.46 us
    unnamed x20, local copies, waits for them, and re-layouts  4.07 us
  transfers between devices with their start and end apart: 11, of which 8 were waited for; matrix products, arithmetic and copies ran while one was open for 0% of the time, Pallas kernels for 6%

profile of v3, /device:TPU:32, one launch (start us, length us, event | category | flops | bytes accessed | tf_op | source)
XLA Modules:
  0.0 127.4 jit_solution(15675137709451915629)
XLA Ops:
  0.0 1.1 copy-done.2
  1.1 1.1 turn_kernel.1
  2.2 15.0 %all-to-all-start = ((f32[128,16,128]{2,1,0:T(8,128)}), f32[128,16,128]{2,1,0:T(8,128)S(1)}, u32[]{:S(2)}, u32[]{:S(2)}) async-start(f32[128,16,128]{2,1,0:T(8,128)} %bitcast.2), calls=%async_computation | async-start | bytes 2097152 | tf_op jit(solution)/shard_map/all_to_all | solution.py:185
  17.3 1.5 %collective-permute-start.2 = (f32[128,512]{1,0:T(8,128)S(1)}, f32[128,512]{1,0:T(8,128)}, u32[]{:S(2)}, u32[]{:S(2)}) collective-permute-start(f32[128,512]{1,0:T(8,128)S(1)} %copy-done.3), channel_id=1, source_target_pairs={{0,2},{2,4},{4,6},{6,0},{1,3},{3,5},{5,7},{7,1},{8,10},{10,12},{12... | collective-permute-start | bytes 786440 | tf_op jit(solution)/shard_map/ppermute | solution.py:181
  18.8 1.8 %collective-permute-start.3 = (f32[128,512]{1,0:T(8,128)S(1)}, f32[128,512]{1,0:T(8,128)}, u32[]{:S(2)}, u32[]{:S(2)}) collective-permute-start(f32[128,512]{1,0:T(8,128)S(1)} %copy-done.3), channel_id=1, source_target_pairs={{0,4},{2,6},{4,0},{6,2},{1,5},{3,7},{5,1},{7,3},{8,12},{10,14},{12... | collective-permute-start | bytes 786440 | tf_op jit(solution)/shard_map/ppermute | solution.py:181
  20.6 1.1 collective-permute-start.4
  21.7 0.1 add_multiply_fusion
  21.9 0.1 add.54
  22.0 0.1 select_reduce_fusion
  22.1 0.1 convert_reduce_fusion.owners
  22.2 0.1 pad_add_fusion.1.where
  22.2 0.6 collective-permute-done
  22.9 0.1 compare_select_fusion.6
  22.9 24.1 %collective-permute-done.2.w1 = f32[128,512]{1,0:T(8,128)} collective-permute-done((f32[128,512]{1,0:T(8,128)S(1)}, f32[128,512]{1,0:T(8,128)}, u32[]{:S(2)}, u32[]{:S(2)}) %collective-permute-start.2) | collective-permute-done | bytes 262176 | tf_op jit(solution)/shard_map/ppermute | solution.py:181
  47.1 14.7 %collective-permute-done.3.w2 = f32[128,512]{1,0:T(8,128)} collective-permute-done((f32[128,512]{1,0:T(8,128)S(1)}, f32[128,512]{1,0:T(8,128)}, u32[]{:S(2)}, u32[]{:S(2)}) %collective-permute-start.3) | collective-permute-done | bytes 262176 | tf_op jit(solution)/shard_map/ppermute | solution.py:181
  61.7 2.0 %collective-permute-done.4.w3 = f32[128,512]{1,0:T(8,128)} collective-permute-done((f32[128,512]{1,0:T(8,128)S(1)}, f32[128,512]{1,0:T(8,128)}, u32[]{:S(2)}, u32[]{:S(2)}) %collective-permute-start.4) | collective-permute-done | bytes 262176 | tf_op jit(solution)/shard_map/ppermute | solution.py:181
  63.7 6.0 %beta_kernel.1 = (f32[16,128,128]{2,1,0:T(8,128)S(1)}, f32[16,128,128]{2,1,0:T(8,128)S(1)}, f32[8,128]{1,0:T(8,128)S(1)}) custom-call(s32[4]{0:T(128)S(1)} %pad_add_fusion.1.where, s32[64]{0:T(128)S(1)} %get-tuple-element.20.cols, s32[64]{0:T(128)S(1)} %get-tuple-element.19.slots, f32[128,512]{1,0:T(8,128)S(1)} %copy-done.3, ...), custom_call_target="tpu_custom_call" | custom-call | flops 402653184 | bytes 7340032 | tf_op jit(solution)/shard_map/beta_kernel/pallas_call | solution.py:164
  69.8 1.0 copy-done.4
  70.7 1.0 copy-done.6
  71.7 5.6 %alpha_kernel.1 = f32[32,64,128]{2,1,0:T(8,128)S(1)} custom-call(s32[64]{0:T(128)S(1)} %get-tuple-element.20.cols, s32[64]{0:T(128)S(1)} %convert_reduce_fusion.owners, f32[32,64,128]{2,1,0:T(8,128)S(1)} %bitcast.9, f32[32,128,128]{2,1,0:T(8,128)S(1)} %copy-done, f32[32,128,128]{2,1,0:T(8,128)} %collective-permute-done.1.h1, ...), custom_call_target="tpu_custom_call" | custom-call | flops 402653184 | bytes 7340032 | tf_op jit(solution)/shard_map/alpha_kernel/pallas_call | solution.py:164
  77.4 1.0 copy-done.1
  78.4 12.2 %all-to-all-start.1 = ((f32[128,16,128]{2,1,0:T(8,128)}), f32[128,16,128]{2,1,0:T(8,128)S(1)}, u32[]{:S(2)}, u32[]{:S(2)}) async-start(f32[128,16,128]{2,1,0:T(8,128)} %bitcast.10), calls=%async_computation.1 | async-start | bytes 2097152 | tf_op jit(solution)/shard_map/all_to_all | solution.py:218
  90.6 0.1 collective-permute-start.5
  90.7 2.6 %collective-permute-done.5.got_ref = f32[16,128,128]{2,1,0:T(8,128)S(1)} collective-permute-done((f32[16,128,128]{2,1,0:T(8,128)S(1)}, f32[16,128,128]{2,1,0:T(8,128)S(1)}, u32[]{:S(2)}, u32[]{:S(2)}) %collective-permute-start.5) | collective-permute-done | bytes 1048608 | tf_op jit(solution)/shard_map/ppermute | solution.py:146
  93.3 0.1 cores_kernel.1
  93.4 2.8 %collective-permute-start.6 = (f32[4,128,128]{2,1,0:T(8,128)S(1)}, f32[4,128,128]{2,1,0:T(8,128)S(1)}, u32[]{:S(2)}, u32[]{:S(2)}) collective-permute-start(f32[4,128,128]{2,1,0:T(8,128)S(1)} %get-tuple-element.16), channel_id=1, source_target_pairs={{2,0},{4,2},{6,4},{3,1},{5,3},{7,5},{10,8},{12,10},{14,12},{11,9},... | collective-permute-start | bytes 786440 | tf_op jit(solution)/shard_map/ppermute | solution.py:222
  96.2 3.0 %collective-permute-start.7 = (f32[4,128,128]{2,1,0:T(8,128)S(1)}, f32[4,128,128]{2,1,0:T(8,128)S(1)}, u32[]{:S(2)}, u32[]{:S(2)}) collective-permute-start(f32[4,128,128]{2,1,0:T(8,128)S(1)} %get-tuple-element.17), channel_id=1, source_target_pairs={{0,2},{2,4},{4,6},{1,3},{3,5},{5,7},{8,10},{10,12},{12,14},{9,11},... | collective-permute-start | bytes 786440 | tf_op jit(solution)/shard_map/ppermute | solution.py:223
  99.3 1.3 %collective-permute-start.8 = (f32[4,128,128]{2,1,0:T(8,128)S(1)}, f32[4,128,128]{2,1,0:T(8,128)S(1)}, u32[]{:S(2)}, u32[]{:S(2)}) collective-permute-start(f32[4,128,128]{2,1,0:T(8,128)S(1)} %get-tuple-element.18), channel_id=1, source_target_pairs={{0,4},{6,2},{1,5},{7,3},{8,12},{14,10},{9,13},{15,11},{16,20},{22,... | collective-permute-start | bytes 786440 | tf_op jit(solution)/shard_map/ppermute | solution.py:224
  100.6 19.5 %collective-permute-done.6.down_ref = f32[4,128,128]{2,1,0:T(8,128)S(1)} collective-permute-done((f32[4,128,128]{2,1,0:T(8,128)S(1)}, f32[4,128,128]{2,1,0:T(8,128)S(1)}, u32[]{:S(2)}, u32[]{:S(2)}) %collective-permute-start.6) | collective-permute-done | bytes 262176 | tf_op jit(solution)/shard_map/ppermute | solution.py:222
  120.1 0.2 collective-permute-done.7.up_ref
  120.3 6.2 %collective-permute-done.8.edge_ref = f32[4,128,128]{2,1,0:T(8,128)S(1)} collective-permute-done((f32[4,128,128]{2,1,0:T(8,128)S(1)}, f32[4,128,128]{2,1,0:T(8,128)S(1)}, u32[]{:S(2)}, u32[]{:S(2)}) %collective-permute-start.8) | collective-permute-done | bytes 262176 | tf_op jit(solution)/shard_map/ppermute | solution.py:224
  126.5 0.8 final_kernel.1
  (22 shorter events, 0.1 us)
Async XLA Ops:
  0.0 63.7 %copy-start = (f32[32,128,128]{2,1,0:T(8,128)S(1)}, f32[32,128,128]{2,1,0:T(8,128)}, u32[]{:S(2)}) copy-start(f32[32,128,128]{2,1,0:T(8,128)} %h0.3) | copy-start | bytes 6291460
  0.0 63.7 %collective-permute-start.1 = (f32[32,128,128]{2,1,0:T(8,128)}, f32[32,128,128]{2,1,0:T(8,128)}, u32[]{:S(2)}, u32[]{:S(2)}) collective-permute-start(f32[32,128,128]{2,1,0:T(8,128)} %h0.3), channel_id=1, source_target_pairs={{0,1},{1,0},{2,3},{3,2},{4,5},{5,4},{6,7},{7,6},{8,9},{9,8},{10,11... | collective-permute-start | bytes 6291464 | tf_op jit(solution)/shard_map/ppermute | solution.py:146
  0.0 1.1 copy-start.2
  1.1 16.1 %copy-start.3 = (f32[128,512]{1,0:T(8,128)S(1)}, f32[128,512]{1,0:T(8,128)}, u32[]{:S(2)}) copy-start(f32[128,512]{1,0:T(8,128)} %w0.1) | copy-start | bytes 786436
  1.1 20.6 %copy-start.8 = (s32[32]{0:T(128)S(1)}, s32[32]{0:T(128)}, u32[]{:S(2)}) copy-start(s32[32]{0:T(128)} %param.7) | copy-start | bytes 388
  1.1 20.9 %copy-start.9 = (s32[32]{0:T(128)S(1)}, s32[32]{0:T(128)}, u32[]{:S(2)}) copy-start(s32[32]{0:T(128)} %param.6) | copy-start | bytes 388
  2.2 69.5 %all-to-all-start = ((f32[128,16,128]{2,1,0:T(8,128)}), f32[128,16,128]{2,1,0:T(8,128)S(1)}, u32[]{:S(2)}, u32[]{:S(2)}) async-start(f32[128,16,128]{2,1,0:T(8,128)} %bitcast.2), calls=%async_computation | async-start | bytes 2097152 | tf_op jit(solution)/shard_map/all_to_all | solution.py:185
  17.3 29.8 %collective-permute-start.2 = (f32[128,512]{1,0:T(8,128)S(1)}, f32[128,512]{1,0:T(8,128)}, u32[]{:S(2)}, u32[]{:S(2)}) collective-permute-start(f32[128,512]{1,0:T(8,128)S(1)} %copy-done.3), channel_id=1, source_target_pairs={{0,2},{2,4},{4,6},{6,0},{1,3},{3,5},{5,7},{7,1},{8,10},{10,12},{12... | collective-permute-start | bytes 786440 | tf_op jit(solution)/shard_map/ppermute | solution.py:181
  18.8 42.9 %collective-permute-start.3 = (f32[128,512]{1,0:T(8,128)S(1)}, f32[128,512]{1,0:T(8,128)}, u32[]{:S(2)}, u32[]{:S(2)}) collective-permute-start(f32[128,512]{1,0:T(8,128)S(1)} %copy-done.3), channel_id=1, source_target_pairs={{0,4},{2,6},{4,0},{6,2},{1,5},{3,7},{5,1},{7,3},{8,12},{10,14},{12... | collective-permute-start | bytes 786440 | tf_op jit(solution)/shard_map/ppermute | solution.py:181
  20.6 43.1 %collective-permute-start.4 = (f32[128,512]{1,0:T(8,128)S(1)}, f32[128,512]{1,0:T(8,128)}, u32[]{:S(2)}, u32[]{:S(2)}) collective-permute-start(f32[128,512]{1,0:T(8,128)S(1)} %copy-done.3), channel_id=1, source_target_pairs={{0,6},{2,0},{4,2},{6,4},{1,7},{3,1},{5,3},{7,5},{8,14},{10,8},{12,... | collective-permute-start | bytes 786440 | tf_op jit(solution)/shard_map/ppermute | solution.py:181
  21.7 1.1 collective-permute-start
  69.7 1.0 copy-start.4
  70.7 1.0 copy-start.6
  77.4 1.0 copy-start.1
  78.4 12.2 %copy-start.7 = (f32[16,128,128]{2,1,0:T(8,128)S(1)}, f32[16,128,128]{2,1,0:T(8,128)}, u32[]{:S(2)}) copy-start(f32[16,128,128]{2,1,0:T(8,128)} %copy-done.6) | copy-start | bytes 3145732
  78.4 15.0 %copy-start.5 = (f32[16,128,128]{2,1,0:T(8,128)S(1)}, f32[16,128,128]{2,1,0:T(8,128)}, u32[]{:S(2)}) copy-start(f32[16,128,128]{2,1,0:T(8,128)} %copy-done.4) | copy-start | bytes 3145732
  78.4 48.2 %all-to-all-start.1 = ((f32[128,16,128]{2,1,0:T(8,128)}), f32[128,16,128]{2,1,0:T(8,128)S(1)}, u32[]{:S(2)}, u32[]{:S(2)}) async-start(f32[128,16,128]{2,1,0:T(8,128)} %bitcast.10), calls=%async_computation.1 | async-start | bytes 2097152 | tf_op jit(solution)/shard_map/all_to_all | solution.py:218
  90.6 2.7 %collective-permute-start.5 = (f32[16,128,128]{2,1,0:T(8,128)S(1)}, f32[16,128,128]{2,1,0:T(8,128)S(1)}, u32[]{:S(2)}, u32[]{:S(2)}) collective-permute-start(f32[16,128,128]{2,1,0:T(8,128)S(1)} %copy-done.7), channel_id=1, source_target_pairs={{0,1},{1,0},{2,3},{3,2},{4,5},{5,4},{6,7},{7,6},{8,9},{9,8},{10,11... | collective-permute-start | bytes 3145736 | tf_op jit(solution)/shard_map/ppermute | solution.py:146
  93.4 26.7 %collective-permute-start.6 = (f32[4,128,128]{2,1,0:T(8,128)S(1)}, f32[4,128,128]{2,1,0:T(8,128)S(1)}, u32[]{:S(2)}, u32[]{:S(2)}) collective-permute-start(f32[4,128,128]{2,1,0:T(8,128)S(1)} %get-tuple-element.16), channel_id=1, source_target_pairs={{2,0},{4,2},{6,4},{3,1},{5,3},{7,5},{10,8},{12,10},{14,12},{11,9},... | collective-permute-start | bytes 786440 | tf_op jit(solution)/shard_map/ppermute | solution.py:222
  96.2 24.0 %collective-permute-start.7 = (f32[4,128,128]{2,1,0:T(8,128)S(1)}, f32[4,128,128]{2,1,0:T(8,128)S(1)}, u32[]{:S(2)}, u32[]{:S(2)}) collective-permute-start(f32[4,128,128]{2,1,0:T(8,128)S(1)} %get-tuple-element.17), channel_id=1, source_target_pairs={{0,2},{2,4},{4,6},{1,3},{3,5},{5,7},{8,10},{10,12},{12,14},{9,11},... | collective-permute-start | bytes 786440 | tf_op jit(solution)/shard_map/ppermute | solution.py:223
  99.3 27.2 %collective-permute-start.8 = (f32[4,128,128]{2,1,0:T(8,128)S(1)}, f32[4,128,128]{2,1,0:T(8,128)S(1)}, u32[]{:S(2)}, u32[]{:S(2)}) collective-permute-start(f32[4,128,128]{2,1,0:T(8,128)S(1)} %get-tuple-element.18), channel_id=1, source_target_pairs={{0,4},{6,2},{1,5},{7,3},{8,12},{14,10},{9,13},{15,11},{16,20},{22,... | collective-permute-start | bytes 786440 | tf_op jit(solution)/shard_map/ppermute | solution.py:224

commit v4 on v3

--- a/solution.py
+++ b/solution.py
@@ -15,6 +15,9 @@
 TRASH = 28
 CONTRACT = (((1,), (1,)), ((), ()))
 
+BUSY = 40 * 10**9
+
+
 def params(mib):
     return pltpu.CompilerParams(vmem_limit_bytes=mib << 20)
 
@@ -48,7 +51,7 @@
 
 
 def beta_kernel(
-    where, cols, slots, w0, w1, w2, w3, h0, h1, keep_ref, send_ref, token_ref,
+    where, cols, slots, w0, w1, w2, w3, h0, h1, keep_ref, send_ref,
     wide, stack, hbuf, acc, list_ref, sem_w, sem_h,
 ):
     z, core = where[2], where[3]
@@ -98,10 +101,9 @@
     edge = acc[24:28]
     keep_ref[12:] = jnp.where(mine, edge, 0.0)
     send_ref[12:] = jnp.where(mine, 0.0, edge)
-    token_ref[...] = jnp.zeros_like(token_ref)
-
-
-def alpha_kernel(cols, owners, a_ref, h0, h1, after, acc, stack, hbuf, sem_h):
+
+
+def alpha_kernel(cols, owners, a_ref, h0, h1, after, out_ref, acc, stack, hbuf, sem_h, sem_o):
     chunks = []
     for n in range(4):
         source = (h0, h1)[n // 2].at[pl.ds(16 * (n % 2), 16)]
@@ -128,18 +130,26 @@
             for owner, term in terms:
                 acc[owner] += term
 
+    copy = pltpu.make_async_copy(acc, out_ref, sem_o)
+    copy.start()
+    copy.wait()
+
 
 def cores_kernel(keep_ref, got_ref, own_ref, down_ref, up_ref, edge_ref):
     for n, ref in enumerate((own_ref, down_ref, up_ref, edge_ref)):
         ref[...] = keep_ref[4 * n : 4 * n + 4] + got_ref[4 * n : 4 * n + 4]
 
 
-def final_kernel(back_ref, own_ref, down_ref, up_ref, edge_ref, out_ref):
+def planes_kernel(own_ref, down_ref, up_ref, edge_ref, out_ref, token_ref):
+    out_ref[...] = (own_ref[...] + down_ref[...]) + (up_ref[...] + edge_ref[...])
+    token_ref[...] = jnp.zeros_like(token_ref)
+
+
+def final_kernel(back_ref, beta_ref, out_ref):
     for t in range(4):
         part = back_ref[8 * t : 8 * (t + 1)]
         total = (part[:, 0] + part[:, 1]) + (part[:, 2] + part[:, 3])
-        beta = (own_ref[t] + down_ref[t]) + (up_ref[t] + edge_ref[t])
-        out_ref[:, 128 * t : 128 * (t + 1)] = jnp.transpose(total.reshape(128, 128)) + beta
+        out_ref[:, 128 * t : 128 * (t + 1)] = jnp.transpose(total.reshape(128, 128)) + beta_ref[t]
 
 
 def swap(value):
@@ -159,13 +169,13 @@
     return cols, owners, jnp.where((cols // 4) % 2 == c, slots, TRASH)
 
 
-def call(kernel, outs, in_specs, *args, scratch=(), mib=16, work=(0, 1 << 20)):
+def call(kernel, outs, in_specs, *args, scratch=(), mib=16, work=(0, 1 << 20), space=VMEM):
     single = not isinstance(outs, tuple)
     return pl.pallas_call(
         kernel,
         out_shape=outs,
         in_specs=in_specs,
-        out_specs=VMEM if single else (VMEM,) * len(outs),
+        out_specs=space if single else (space,) * len(outs),
         scratch_shapes=scratch,
         compiler_params=params(mib),
         cost_estimate=cost(*work),
@@ -184,9 +194,9 @@
     at = call(turn_kernel, shape(32, 4, 16, 128), [VMEM], coeffs)
     moved = lax.all_to_all(at.reshape(2048, 128), ROWS + ("z",), 0, 0, tiled=True)
 
-    keep, send, token = call(
+    keep, send = call(
         beta_kernel,
-        (shape(16, 128, 128), shape(16, 128, 128), shape(8, 128)),
+        (shape(16, 128, 128), shape(16, 128, 128)),
         [SMEM] * 3 + [ANY] * 6,
         where, cols, slots, *rows, hblocks, swapped,
         scratch=[
@@ -199,32 +209,37 @@
             pltpu.SemaphoreType.DMA((2,)),
         ],
         mib=24,
-        work=(6 * 32 * 128 * 128 * 128, 7 << 20),
-    )
-    (out_a,) = call(
+        work=(BUSY, 7 << 20),
+    )
+    own, down, up, edge = call(
+        cores_kernel, (shape(4, 128, 128),) * 4, [VMEM] * 2, keep, swap(send)
+    )
+    down = lax.ppermute(down, "z", [(1, 0), (2, 1), (3, 2)])
+    up = lax.ppermute(up, "z", [(0, 1), (1, 2), (2, 3)])
+    edge = lax.ppermute(edge, "z", [(0, 2), (3, 1)])
+    beta, token = call(
+        planes_kernel, (shape(4, 128, 128), shape(8, 128)), [VMEM] * 4, own, down, up, edge
+    )
+    out_a = call(
         alpha_kernel,
-        (shape(32, 64, 128),),
+        shape(32, 64, 128),
         [SMEM] * 2 + [VMEM] + [ANY] * 2 + [VMEM],
         cols, owners, moved.reshape(32, 64, 128), hblocks, swapped, token,
         scratch=[
+            pltpu.VMEM((32, 64, 128), F32),
             pltpu.VMEM((32, 128, 128), BF16),
             pltpu.VMEM((64, 128, 128), F32),
             pltpu.SemaphoreType.DMA((4,)),
+            pltpu.SemaphoreType.DMA,
         ],
         mib=24,
-        work=(6 * 64 * 64 * 128 * 128, 7 << 20),
+        space=pl.BlockSpec(memory_space=pltpu.HBM),
+        work=(BUSY, 7 << 20),
     )
 
     back = lax.all_to_all(out_a.reshape(2048, 128), ROWS + ("z",), 0, 0, tiled=True)
-    own, down, up, edge = call(
-        cores_kernel, (shape(4, 128, 128),) * 4, [VMEM] * 2, keep, swap(send)
-    )
-    down = lax.ppermute(down, "z", [(1, 0), (2, 1), (3, 2)])
-    up = lax.ppermute(up, "z", [(0, 1), (1, 2), (2, 3)])
-    edge = lax.ppermute(edge, "z", [(0, 2), (3, 1)])
     return call(
-        final_kernel, shape(128, 512), [VMEM] * 5,
-        back.reshape(32, 4, 16, 128), own, down, up, edge,
+        final_kernel, shape(128, 512), [VMEM] * 2, back.reshape(32, 4, 16, 128), beta
     )
 
 

time: 128 us -> 114 us (0.89)
  blocking collectives: 0 us -> 46.1 us
  waiting for transfers between devices: 70 us -> 25.5 us
  starting transfers between devices: 38.9 us -> 26.8 us
  local copies, waits for them, and re-layouts: 4.15 us -> 1.08 us
    all_to_all x0 -> x1, blocking collectives: none -> 46.1 us  [local(): lax.all_to_all(out_a.reshape(2048, 128), ROWS + ('z',), 0, 0, tiled=True)]
    ppermute x3, waiting for transfers between devices: 40.8 us -> 12.3 us  [local(): lax.ppermute(coeffs, 'z', [(i, (i + k) % 4) for i in range(4)])]
    all_to_all x1 -> x0, starting transfers between devices: 12.2 us -> none  [local(): lax.all_to_all(out_a.reshape(2048, 128), ROWS + ('z',), 0, 0, tiled=True)]
    ppermute x1, waiting for transfers between devices: 19.5 us -> 10.5 us  [local(): down = lax.ppermute(down, 'z', [(1, 0), (2, 1), (3, 2)])]
    ppermute x1, waiting for transfers between devices: 6.23 us -> 0.01 us  [local(): edge = lax.ppermute(edge, 'z', [(0, 2), (3, 1)])]
    unnamed x20 -> x10, local copies, waits for them, and re-layouts: 4.07 us -> 0.99 us
    pallas_call x5 -> x6, Pallas kernels: 13.7 us -> 14.1 us  [call(): pl.pallas_call(kernel, out_shape=outs, in_specs=in_specs, out_specs=space...]
  transfers between devices with their start and end apart: 11 -> 10, of which waited for: 8 -> 4; matrix products, arithmetic and copies ran while one was open for 0% -> 1% of each run, Pallas kernels for 6% -> 7%
where the time goes in v4:
time: 114 us
  blocking collectives  46.1 us (40%)
  starting transfers between devices  26.8 us (24%)
  waiting for transfers between devices  25.5 us (22%)
  Pallas kernels  14.1 us (12%)
    all_to_all x1, blocking collectives, local(): lax.all_to_all(out_a.reshape(2048, 128), ROWS + ('z',), 0, 0, tiled=True)  46.1 us
    all_to_all x1, starting transfers between devices, local(): lax.all_to_all(at.reshape(2048, 128), ROWS + ('z',), 0, 0, tiled=True)  14.2 us
    pallas_call x6, Pallas kernels, call(): pl.pallas_call(kernel, out_shape=outs, in_specs=in_specs, out_specs=space...  14.1 us
    ppermute x3, waiting for transfers between devices, local(): lax.ppermute(coeffs, 'z', [(i, (i + k) % 4) for i in range(4)])  12.3 us
    ppermute x1, waiting for transfers between devices, local(): down = lax.ppermute(down, 'z', [(1, 0), (2, 1), (3, 2)])  10.5 us
    ppermute x3, starting transfers between devices, local(): lax.ppermute(coeffs, 'z', [(i, (i + k) % 4) for i in range(4)])  5.3 us
    ppermute x1, starting transfers between devices, local(): up = lax.ppermute(up, 'z', [(0, 1), (1, 2), (2, 3)])  3.92 us
    ppermute x3, waiting for transfers between devices, swap(): return lax.ppermute(value, 'c', [(0, 1), (1, 0)])  2.65 us
  transfers between devices with their start and end apart: 10, of which 4 were waited for; matrix products, arithmetic and copies ran while one was open for 1% of the time, Pallas kernels for 7%

profile of v4, /device:TPU:32, one launch (start us, length us, event | category | flops | bytes accessed | tf_op | source)
XLA Modules:
  0.0 114.2 jit_solution(3625280078119164783)
XLA Ops:
  0.0 0.0 collective-permute-start.1
  0.0 1.9 %collective-permute-start.2 = (f32[128,512]{1,0:T(8,128)}, f32[128,512]{1,0:T(8,128)}, u32[]{:S(2)}, u32[]{:S(2)}) collective-permute-start(f32[128,512]{1,0:T(8,128)} %w0.1), channel_id=1, source_target_pairs={{0,2},{2,4},{4,6},{6,0},{1,3},{3,5},{5,7},{7,1},{8,10},{10,12},{12... | collective-permute-start | bytes 786440 | tf_op jit(solution)/shard_map/ppermute | solution.py:191
  1.9 2.3 %collective-permute-start.3 = (f32[128,512]{1,0:T(8,128)}, f32[128,512]{1,0:T(8,128)}, u32[]{:S(2)}, u32[]{:S(2)}) collective-permute-start(f32[128,512]{1,0:T(8,128)} %w0.1), channel_id=1, source_target_pairs={{0,4},{2,6},{4,0},{6,2},{1,5},{3,7},{5,1},{7,3},{8,12},{10,14},{12... | collective-permute-start | bytes 786440 | tf_op jit(solution)/shard_map/ppermute | solution.py:191
  4.2 1.1 collective-permute-start.4
  5.3 0.0 collective-permute-start
  5.3 1.0 copy-done
  6.3 1.1 turn_kernel.1
  7.4 14.2 %all-to-all-start = ((f32[128,16,128]{2,1,0:T(8,128)}), f32[128,16,128]{2,1,0:T(8,128)S(1)}, u32[]{:S(2)}, u32[]{:S(2)}) async-start(f32[128,16,128]{2,1,0:T(8,128)} %bitcast.2), calls=%async_computation | async-start | bytes 2097152 | tf_op jit(solution)/shard_map/all_to_all | solution.py:195
  21.7 0.1 add_multiply_fusion
  21.7 0.1 iota_add_fusion
  21.8 0.1 add.54
  21.9 0.1 select_reduce_fusion
  22.0 0.1 convert_reduce_fusion.owners
  22.1 0.1 pad_add_fusion.1.where
  22.2 0.1 compare_select_fusion.6
  22.3 8.3 %collective-permute-done.3.w2 = f32[128,512]{1,0:T(8,128)} collective-permute-done((f32[128,512]{1,0:T(8,128)}, f32[128,512]{1,0:T(8,128)}, u32[]{:S(2)}, u32[]{:S(2)}) %collective-permute-start.3) | collective-permute-done | bytes 262176 | tf_op jit(solution)/shard_map/ppermute | solution.py:191
  30.6 4.0 %collective-permute-done.4.w3 = f32[128,512]{1,0:T(8,128)} collective-permute-done((f32[128,512]{1,0:T(8,128)}, f32[128,512]{1,0:T(8,128)}, u32[]{:S(2)}, u32[]{:S(2)}) %collective-permute-start.4) | collective-permute-done | bytes 262176 | tf_op jit(solution)/shard_map/ppermute | solution.py:191
  34.6 6.2 %beta_kernel.1 = (f32[16,128,128]{2,1,0:T(8,128)S(1)}, f32[16,128,128]{2,1,0:T(8,128)S(1)}) custom-call(s32[4]{0:T(128)S(1)} %pad_add_fusion.1.where, s32[64]{0:T(128)S(1)} %get-tuple-element.22.cols, s32[64]{0:T(128)S(1)} %get-tuple-element.21.slots, f32[128,512]{1,0:T(8,128)S(1)} %copy-done.1, f32[128,512]{1,0:T(8,128)} %collective-permute-done.2.w1, ...), custom_call_target="tpu_custom_call" | custom-call | flops 40000000000 | bytes 7340032 | tf_op jit(solution)/shard_map/beta_kernel/pallas_call | solution.py:174
  40.8 0.1 collective-permute-start.5
  40.9 2.6 %collective-permute-done.5.got_ref = f32[16,128,128]{2,1,0:T(8,128)S(1)} collective-permute-done((f32[16,128,128]{2,1,0:T(8,128)S(1)}, f32[16,128,128]{2,1,0:T(8,128)S(1)}, u32[]{:S(2)}, u32[]{:S(2)}) %collective-permute-start.5) | collective-permute-done | bytes 1048608 | tf_op jit(solution)/shard_map/ppermute | solution.py:156
  43.6 0.2 cores_kernel.1
  43.7 1.9 %collective-permute-start.6 = (f32[4,128,128]{2,1,0:T(8,128)S(1)}, f32[4,128,128]{2,1,0:T(8,128)S(1)}, u32[]{:S(2)}, u32[]{:S(2)}) collective-permute-start(f32[4,128,128]{2,1,0:T(8,128)S(1)} %get-tuple-element.16), channel_id=1, source_target_pairs={{2,0},{4,2},{6,4},{3,1},{5,3},{7,5},{10,8},{12,10},{14,12},{11,9},... | collective-permute-start | bytes 786440 | tf_op jit(solution)/shard_map/ppermute | solution.py:217
  45.6 3.9 %collective-permute-start.7 = (f32[4,128,128]{2,1,0:T(8,128)S(1)}, f32[4,128,128]{2,1,0:T(8,128)S(1)}, u32[]{:S(2)}, u32[]{:S(2)}) collective-permute-start(f32[4,128,128]{2,1,0:T(8,128)S(1)} %get-tuple-element.17), channel_id=1, source_target_pairs={{0,2},{2,4},{4,6},{1,3},{3,5},{5,7},{8,10},{10,12},{12,14},{9,11},... | collective-permute-start | bytes 786440 | tf_op jit(solution)/shard_map/ppermute | solution.py:218
  49.6 1.3 %collective-permute-start.8 = (f32[4,128,128]{2,1,0:T(8,128)S(1)}, f32[4,128,128]{2,1,0:T(8,128)S(1)}, u32[]{:S(2)}, u32[]{:S(2)}) collective-permute-start(f32[4,128,128]{2,1,0:T(8,128)S(1)} %get-tuple-element.18), channel_id=1, source_target_pairs={{0,4},{6,2},{1,5},{7,3},{8,12},{14,10},{9,13},{15,11},{16,20},{22,... | collective-permute-start | bytes 786440 | tf_op jit(solution)/shard_map/ppermute | solution.py:219
  50.9 10.5 %collective-permute-done.6.down_ref = f32[4,128,128]{2,1,0:T(8,128)S(1)} collective-permute-done((f32[4,128,128]{2,1,0:T(8,128)S(1)}, f32[4,128,128]{2,1,0:T(8,128)S(1)}, u32[]{:S(2)}, u32[]{:S(2)}) %collective-permute-start.6) | collective-permute-done | bytes 262176 | tf_op jit(solution)/shard_map/ppermute | solution.py:217
  61.4 0.0 collective-permute-done.7.up_ref
  61.4 0.0 collective-permute-done.8.edge_ref
  61.4 0.1 planes_kernel.1
  61.4 0.0 all-to-all-done
  61.5 5.7 %alpha_kernel.1 = f32[32,64,128]{2,1,0:T(8,128)S(1)} custom-call(s32[64]{0:T(128)S(1)} %get-tuple-element.22.cols, s32[64]{0:T(128)S(1)} %convert_reduce_fusion.owners, f32[32,64,128]{2,1,0:T(8,128)S(1)} %bitcast.9, f32[32,128,128]{2,1,0:T(8,128)S(1)} %copy-done.2, f32[32,128,128]{2,1,0:T(8,128)} %collective-permute-done.1.h1, ...), custom_call_target="tpu_custom_call" | custom-call | flops 40000000000 | bytes 7340032 | tf_op jit(solution)/shard_map/alpha_kernel/pallas_call | solution.py:174
  67.2 46.1 %all_to_all.18 = f32[128,16,128]{2,1,0:T(8,128)S(1)} all-to-all(f32[128,16,128]{2,1,0:T(8,128)S(1)} %bitcast.10), channel_id=1, replica_groups=mesh['y'=4,'h'=2,'x'=4,'z'=4,'c'=2] {'y','h','x','z'}, dimensions={0} | all-to-all | bytes 2097152 | tf_op jit(solution)/shard_map/all_to_all | solution.py:240
  113.3 0.8 final_kernel.1
  (12 shorter events, 0.0 us)
Async XLA Ops:
  0.0 34.6 %collective-permute-start.1 = (f32[32,128,128]{2,1,0:T(8,128)}, f32[32,128,128]{2,1,0:T(8,128)}, u32[]{:S(2)}, u32[]{:S(2)}) collective-permute-start(f32[32,128,128]{2,1,0:T(8,128)} %h0.3), channel_id=1, source_target_pairs={{0,1},{1,0},{2,3},{3,2},{4,5},{5,4},{6,7},{7,6},{8,9},{9,8},{10,11... | collective-permute-start | bytes 6291464 | tf_op jit(solution)/shard_map/ppermute | solution.py:156
  0.0 22.3 %collective-permute-start.2 = (f32[128,512]{1,0:T(8,128)}, f32[128,512]{1,0:T(8,128)}, u32[]{:S(2)}, u32[]{:S(2)}) collective-permute-start(f32[128,512]{1,0:T(8,128)} %w0.1), channel_id=1, source_target_pairs={{0,2},{2,4},{4,6},{6,0},{1,3},{3,5},{5,7},{7,1},{8,10},{10,12},{12... | collective-permute-start | bytes 786440 | tf_op jit(solution)/shard_map/ppermute | solution.py:191
  1.9 28.6 %collective-permute-start.3 = (f32[128,512]{1,0:T(8,128)}, f32[128,512]{1,0:T(8,128)}, u32[]{:S(2)}, u32[]{:S(2)}) collective-permute-start(f32[128,512]{1,0:T(8,128)} %w0.1), channel_id=1, source_target_pairs={{0,4},{2,6},{4,0},{6,2},{1,5},{3,7},{5,1},{7,3},{8,12},{10,14},{12... | collective-permute-start | bytes 786440 | tf_op jit(solution)/shard_map/ppermute | solution.py:191
  4.2 30.3 %collective-permute-start.4 = (f32[128,512]{1,0:T(8,128)}, f32[128,512]{1,0:T(8,128)}, u32[]{:S(2)}, u32[]{:S(2)}) collective-permute-start(f32[128,512]{1,0:T(8,128)} %w0.1), channel_id=1, source_target_pairs={{0,6},{2,0},{4,2},{6,4},{1,7},{3,1},{5,3},{7,5},{8,14},{10,8},{12,... | collective-permute-start | bytes 786440 | tf_op jit(solution)/shard_map/ppermute | solution.py:191
  5.3 16.9 %collective-permute-start = (s32[32]{0:T(128)}, s32[32]{0:T(128)S(1)}, u32[]{:S(2)}, u32[]{:S(2)}) collective-permute-start(s32[32]{0:T(128)} %param.7), channel_id=1, source_target_pairs={{0,1},{1,0},{2,3},{3,2},{4,5},{5,4},{6,7},{7,6},{8,9},{9,8},{10,11... | collective-permute-start | bytes 392 | tf_op jit(solution)/shard_map/ppermute | solution.py:156
  5.3 1.0 copy-start
  6.3 15.6 %copy-start.4 = (s32[32]{0:T(128)S(1)}, s32[32]{0:T(128)}, u32[]{:S(2)}) copy-start(s32[32]{0:T(128)} %param.6) | copy-start | bytes 388
  6.3 15.9 %copy-start.3 = (s32[32]{0:T(128)S(1)}, s32[32]{0:T(128)}, u32[]{:S(2)}) copy-start(s32[32]{0:T(128)} %param.7) | copy-start | bytes 388
  6.3 28.3 %copy-start.1 = (f32[128,512]{1,0:T(8,128)S(1)}, f32[128,512]{1,0:T(8,128)}, u32[]{:S(2)}) copy-start(f32[128,512]{1,0:T(8,128)} %w0.1) | copy-start | bytes 786436
  6.3 28.3 %copy-start.2 = (f32[32,128,128]{2,1,0:T(8,128)S(1)}, f32[32,128,128]{2,1,0:T(8,128)}, u32[]{:S(2)}) copy-start(f32[32,128,128]{2,1,0:T(8,128)} %h0.3) | copy-start | bytes 6291460
  7.4 54.0 %all-to-all-start = ((f32[128,16,128]{2,1,0:T(8,128)}), f32[128,16,128]{2,1,0:T(8,128)S(1)}, u32[]{:S(2)}, u32[]{:S(2)}) async-start(f32[128,16,128]{2,1,0:T(8,128)} %bitcast.2), calls=%async_computation | async-start | bytes 2097152 | tf_op jit(solution)/shard_map/all_to_all | solution.py:195
  40.8 2.7 %collective-permute-start.5 = (f32[16,128,128]{2,1,0:T(8,128)S(1)}, f32[16,128,128]{2,1,0:T(8,128)S(1)}, u32[]{:S(2)}, u32[]{:S(2)}) collective-permute-start(f32[16,128,128]{2,1,0:T(8,128)S(1)} %get-tuple-element.14), channel_id=1, source_target_pairs={{0,1},{1,0},{2,3},{3,2},{4,5},{5,4},{6,7},{7,6},{8,9},{9,8},{10,11... | collective-permute-start | bytes 3145736 | tf_op jit(solution)/shard_map/ppermute | solution.py:156
  43.7 17.7 %collective-permute-start.6 = (f32[4,128,128]{2,1,0:T(8,128)S(1)}, f32[4,128,128]{2,1,0:T(8,128)S(1)}, u32[]{:S(2)}, u32[]{:S(2)}) collective-permute-start(f32[4,128,128]{2,1,0:T(8,128)S(1)} %get-tuple-element.16), channel_id=1, source_target_pairs={{2,0},{4,2},{6,4},{3,1},{5,3},{7,5},{10,8},{12,10},{14,12},{11,9},... | collective-permute-start | bytes 786440 | tf_op jit(solution)/shard_map/ppermute | solution.py:217
  45.6 15.7 %collective-permute-start.7 = (f32[4,128,128]{2,1,0:T(8,128)S(1)}, f32[4,128,128]{2,1,0:T(8,128)S(1)}, u32[]{:S(2)}, u32[]{:S(2)}) collective-permute-start(f32[4,128,128]{2,1,0:T(8,128)S(1)} %get-tuple-element.17), channel_id=1, source_target_pairs={{0,2},{2,4},{4,6},{1,3},{3,5},{5,7},{8,10},{10,12},{12,14},{9,11},... | collective-permute-start | bytes 786440 | tf_op jit(solution)/shard_map/ppermute | solution.py:218
  49.6 11.8 %collective-permute-start.8 = (f32[4,128,128]{2,1,0:T(8,128)S(1)}, f32[4,128,128]{2,1,0:T(8,128)S(1)}, u32[]{:S(2)}, u32[]{:S(2)}) collective-permute-start(f32[4,128,128]{2,1,0:T(8,128)S(1)} %get-tuple-element.18), channel_id=1, source_target_pairs={{0,4},{6,2},{1,5},{7,3},{8,12},{14,10},{9,13},{15,11},{16,20},{22,... | collective-permute-start | bytes 786440 | tf_op jit(solution)/shard_map/ppermute | solution.py:219

commit v5 on v4

--- a/solution.py
+++ b/solution.py
@@ -103,7 +103,10 @@
     send_ref[12:] = jnp.where(mine, 0.0, edge)
 
 
-def alpha_kernel(cols, owners, a_ref, h0, h1, after, out_ref, acc, stack, hbuf, sem_h, sem_o):
+def alpha_kernel(
+    where, cols, owners, a_ref, h0, h1, after, o0, o1, o2, o3, acc, stack, hbuf, sem_h
+):
+    z = where[2]
     chunks = []
     for n in range(4):
         source = (h0, h1)[n // 2].at[pl.ds(16 * (n % 2), 16)]
@@ -114,9 +117,11 @@
 
     @pl.loop(0, 32)
     def _(j):
-        high, low = halves(a_ref[j])
-        stack[j, :64] = high
-        stack[j, 64:] = low
+        for k in range(4):
+            home = pl.multiple_of(16 * jnp.bitwise_and(z + k, 3), 16)
+            high, low = halves(a_ref[j, pl.ds(home, 16)])
+            stack[j, 16 * k : 16 * k + 16] = high
+            stack[j, 64 + 16 * k : 80 + 16 * k] = low
 
     for n, chunk in enumerate(chunks):
         chunk.wait()
@@ -130,30 +135,40 @@
             for owner, term in terms:
                 acc[owner] += term
 
-    copy = pltpu.make_async_copy(acc, out_ref, sem_o)
-    copy.start()
-    copy.wait()
-
-
-def cores_kernel(keep_ref, got_ref, own_ref, down_ref, up_ref, edge_ref):
+    for k, ref in enumerate((o0, o1, o2, o3)):
+        ref[...] = acc[pl.ds(4 * z, 20), 16 * k : 16 * k + 16]
+
+
+def strings_kernel(where, after, p0, p1, p2, p3, out_ref):
+    z = where[2]
+    out_ref[...] = jnp.zeros_like(out_ref)
+    for k, part in enumerate((p0, p1, p2, p3)):
+        out_ref[pl.ds(4 * jnp.bitwise_and(z - k + 4, 3), 20)] += part[...]
+
+
+def cores_kernel(keep_ref, got_ref, own_ref, down_ref, up_ref, edge_ref, token_ref):
+    token_ref[...] = jnp.zeros_like(token_ref)
     for n, ref in enumerate((own_ref, down_ref, up_ref, edge_ref)):
         ref[...] = keep_ref[4 * n : 4 * n + 4] + got_ref[4 * n : 4 * n + 4]
 
 
 def planes_kernel(own_ref, down_ref, up_ref, edge_ref, out_ref, token_ref):
+    token_ref[...] = jnp.zeros_like(token_ref)
     out_ref[...] = (own_ref[...] + down_ref[...]) + (up_ref[...] + edge_ref[...])
-    token_ref[...] = jnp.zeros_like(token_ref)
 
 
 def final_kernel(back_ref, beta_ref, out_ref):
     for t in range(4):
-        part = back_ref[8 * t : 8 * (t + 1)]
-        total = (part[:, 0] + part[:, 1]) + (part[:, 2] + part[:, 3])
-        out_ref[:, 128 * t : 128 * (t + 1)] = jnp.transpose(total.reshape(128, 128)) + beta_ref[t]
+        turned = jnp.transpose(back_ref[8 * t : 8 * (t + 1)].reshape(128, 128))
+        out_ref[:, 128 * t : 128 * (t + 1)] = turned + beta_ref[t]
 
 
 def swap(value):
     return lax.ppermute(value, "c", [(0, 1), (1, 0)])
+
+
+def shift(value, by):
+    return lax.ppermute(value, "z", [(i, (i + by) % 4) for i in range(4)])
 
 
 def tables(hcount, hcols, z, c):
@@ -187,9 +202,7 @@
     z, c = lax.axis_index("z"), lax.axis_index("c")
     where = jnp.stack([z, z, z, c]).astype(jnp.int32)
     swapped = swap(hblocks)
-    rows = [coeffs] + [
-        lax.ppermute(coeffs, "z", [(i, (i + k) % 4) for i in range(4)]) for k in (1, 2, 3)
-    ]
+    rows = [coeffs] + [shift(coeffs, k) for k in (1, 2, 3)]
     cols, owners, slots = tables(hcount, hcols, z, c)
     at = call(turn_kernel, shape(32, 4, 16, 128), [VMEM], coeffs)
     moved = lax.all_to_all(at.reshape(2048, 128), ROWS + ("z",), 0, 0, tiled=True)
@@ -211,36 +224,40 @@
         mib=24,
         work=(BUSY, 7 << 20),
     )
-    own, down, up, edge = call(
-        cores_kernel, (shape(4, 128, 128),) * 4, [VMEM] * 2, keep, swap(send)
+    own, down, up, edge, token = call(
+        cores_kernel,
+        (shape(4, 128, 128),) * 4 + (shape(8, 128),),
+        [VMEM] * 2,
+        keep, swap(send),
     )
     down = lax.ppermute(down, "z", [(1, 0), (2, 1), (3, 2)])
     up = lax.ppermute(up, "z", [(0, 1), (1, 2), (2, 3)])
     edge = lax.ppermute(edge, "z", [(0, 2), (3, 1)])
-    beta, token = call(
-        planes_kernel, (shape(4, 128, 128), shape(8, 128)), [VMEM] * 4, own, down, up, edge
-    )
-    out_a = call(
+    beta, done = call(
+        planes_kernel,
+        (shape(4, 128, 128), shape(8, 128)),
+        [VMEM] * 4,
+        own, down, up, edge,
+        work=(BUSY, 1 << 20),
+    )
+    parts = call(
         alpha_kernel,
-        shape(32, 64, 128),
-        [SMEM] * 2 + [VMEM] + [ANY] * 2 + [VMEM],
-        cols, owners, moved.reshape(32, 64, 128), hblocks, swapped, token,
+        (shape(20, 16, 128),) * 4,
+        [SMEM] * 3 + [VMEM] + [ANY] * 2 + [VMEM],
+        where, cols, owners, moved.reshape(32, 64, 128), hblocks, swapped, token,
         scratch=[
             pltpu.VMEM((32, 64, 128), F32),
             pltpu.VMEM((32, 128, 128), BF16),
             pltpu.VMEM((64, 128, 128), F32),
             pltpu.SemaphoreType.DMA((4,)),
-            pltpu.SemaphoreType.DMA,
         ],
         mib=24,
-        space=pl.BlockSpec(memory_space=pltpu.HBM),
         work=(BUSY, 7 << 20),
     )
-
-    back = lax.all_to_all(out_a.reshape(2048, 128), ROWS + ("z",), 0, 0, tiled=True)
-    return call(
-        final_kernel, shape(128, 512), [VMEM] * 2, back.reshape(32, 4, 16, 128), beta
-    )
+    parts = [parts[0]] + [shift(parts[k], k) for k in (1, 2, 3)]
+    total = call(strings_kernel, shape(32, 16, 128), [SMEM] + [VMEM] * 5, where, done, *parts)
+    back = lax.all_to_all(total, ROWS, 0, 0, tiled=True)
+    return call(final_kernel, shape(128, 512), [VMEM] * 2, back, beta)
 
 
 def solution(mesh):

time: 114 us -> 106 us (0.930)
  blocking collectives: 46.1 us -> 23.7 us
  starting transfers between devices: 26.8 us -> 32.9 us
  waiting for transfers between devices: 25.5 us -> 30.6 us
  Pallas kernels: 14.1 us -> 16.8 us
    all_to_all x1, blocking collectives: 46.1 us -> 23.7 us  [local(): back = lax.all_to_all(total, ROWS, 0, 0, tiled=True)]
    ppermute x3 -> x6, waiting for transfers between devices: 12.3 us -> 23.6 us  [shift(): return lax.ppermute(value, 'z', [(i, (i + by) % 4) for i in range(4)])]
    ppermute x1, waiting for transfers between devices: 10.5 us -> 0.01 us  [local(): down = lax.ppermute(down, 'z', [(1, 0), (2, 1), (3, 2)])]
    ppermute x3 -> x6, starting transfers between devices: 5.3 us -> 11.6 us  [shift(): return lax.ppermute(value, 'z', [(i, (i + by) % 4) for i in range(4)])]
    all_to_all x1, waiting for transfers between devices: 0.01 us -> 4.25 us  [local(): lax.all_to_all(at.reshape(2048, 128), ROWS + ('z',), 0, 0, tiled=True)]
    pallas_call x6 -> x7, Pallas kernels: 14.1 us -> 16.8 us  [call(): pl.pallas_call(kernel, out_shape=outs, in_specs=in_specs, out_specs=space...]
  transfers between devices with their start and end apart: 10 -> 13, of which waited for: 4 -> 7; matrix products, arithmetic and copies ran while one was open for 1% -> 1% of each run, Pallas kernels for 7% -> 14%
where the time goes in v5:
time: 106 us
  starting transfers between devices  32.9 us (31%)
  waiting for transfers between devices  30.6 us (29%)
  blocking collectives  23.7 us (22%)
  Pallas kernels  16.8 us (16%)
  local copies, waits for them, and re-layouts  1.08 us (1%)
    all_to_all x1, blocking collectives, local(): back = lax.all_to_all(total, ROWS, 0, 0, tiled=True)  23.7 us
    ppermute x6, waiting for transfers between devices, shift(): return lax.ppermute(value, 'z', [(i, (i + by) % 4) for i in range(4)])  23.6 us
    pallas_call x7, Pallas kernels, call(): pl.pallas_call(kernel, out_shape=outs, in_specs=in_specs, out_specs=space...  16.8 us
    all_to_all x1, starting transfers between devices, local(): lax.all_to_all(at.reshape(2048, 128), ROWS + ('z',), 0, 0, tiled=True)  14.1 us
    ppermute x6, starting transfers between devices, shift(): return lax.ppermute(value, 'z', [(i, (i + by) % 4) for i in range(4)])  11.6 us
    all_to_all x1, waiting for transfers between devices, local(): lax.all_to_all(at.reshape(2048, 128), ROWS + ('z',), 0, 0, tiled=True)  4.25 us
    ppermute x1, starting transfers between devices, local(): up = lax.ppermute(up, 'z', [(0, 1), (1, 2), (2, 3)])  3.92 us
    ppermute x3, waiting for transfers between devices, swap(): return lax.ppermute(value, 'c', [(0, 1), (1, 0)])  2.65 us
  transfers between devices with their start and end apart: 13, of which 7 were waited for; matrix products, arithmetic and copies ran while one was open for 1% of the time, Pallas kernels for 14%

profile of v5, /device:TPU:32, one launch (start us, length us, event | category | flops | bytes accessed | tf_op | source)
XLA Modules:
  0.0 105.7 jit_solution(5455644267518008225)
XLA Ops:
  0.0 1.9 %collective-permute-start.1 = (f32[128,512]{1,0:T(8,128)}, f32[128,512]{1,0:T(8,128)}, u32[]{:S(2)}, u32[]{:S(2)}) collective-permute-start(f32[128,512]{1,0:T(8,128)} %c_ref.1), channel_id=1, source_target_pairs={{0,2},{2,4},{4,6},{6,0},{1,3},{3,5},{5,7},{7,1},{8,10},{10,12},{12... | collective-permute-start | bytes 786440 | tf_op jit(solution)/shard_map/ppermute | solution.py:171
  1.9 2.3 %collective-permute-start.2 = (f32[128,512]{1,0:T(8,128)}, f32[128,512]{1,0:T(8,128)}, u32[]{:S(2)}, u32[]{:S(2)}) collective-permute-start(f32[128,512]{1,0:T(8,128)} %c_ref.1), channel_id=1, source_target_pairs={{0,4},{2,6},{4,0},{6,2},{1,5},{3,7},{5,1},{7,3},{8,12},{10,14},{12... | collective-permute-start | bytes 786440 | tf_op jit(solution)/shard_map/ppermute | solution.py:171
  4.2 1.1 %collective-permute-start.3 = (f32[128,512]{1,0:T(8,128)}, f32[128,512]{1,0:T(8,128)}, u32[]{:S(2)}, u32[]{:S(2)}) collective-permute-start(f32[128,512]{1,0:T(8,128)} %c_ref.1), channel_id=1, source_target_pairs={{0,6},{2,0},{4,2},{6,4},{1,7},{3,1},{5,3},{7,5},{8,14},{10,8},{12,... | collective-permute-start | bytes 786440 | tf_op jit(solution)/shard_map/ppermute | solution.py:171
  5.3 1.0 copy-done
  6.3 1.1 %turn_kernel.1 = f32[32,4,16,128]{3,2,1,0:T(8,128)} custom-call(f32[128,512]{1,0:T(8,128)S(1)} %copy-done), custom_call_target="tpu_custom_call" | custom-call | bytes 1048576 | tf_op jit(solution)/shard_map/turn_kernel/pallas_call | solution.py:189
  7.4 14.1 %all-to-all-start = ((f32[128,16,128]{2,1,0:T(8,128)}), f32[128,16,128]{2,1,0:T(8,128)S(1)}, u32[]{:S(2)}, u32[]{:S(2)}) async-start(f32[128,16,128]{2,1,0:T(8,128)} %bitcast.4), calls=%async_computation | async-start | bytes 2097152 | tf_op jit(solution)/shard_map/all_to_all | solution.py:208
  21.5 0.1 add_multiply_fusion
  21.7 0.1 add.55
  21.8 0.1 select_reduce_fusion
  21.9 0.1 convert_reduce_fusion.owners
  22.0 0.1 compare_select_fusion.6
  22.1 8.6 %collective-permute-done.2.w2 = f32[128,512]{1,0:T(8,128)} collective-permute-done((f32[128,512]{1,0:T(8,128)}, f32[128,512]{1,0:T(8,128)}, u32[]{:S(2)}, u32[]{:S(2)}) %collective-permute-start.2) | collective-permute-done | bytes 262176 | tf_op jit(solution)/shard_map/ppermute | solution.py:171
  30.7 3.9 %collective-permute-done.3.w3 = f32[128,512]{1,0:T(8,128)} collective-permute-done((f32[128,512]{1,0:T(8,128)}, f32[128,512]{1,0:T(8,128)}, u32[]{:S(2)}, u32[]{:S(2)}) %collective-permute-start.3) | collective-permute-done | bytes 262176 | tf_op jit(solution)/shard_map/ppermute | solution.py:171
  34.6 6.2 %beta_kernel.1 = (f32[16,128,128]{2,1,0:T(8,128)S(1)}, f32[16,128,128]{2,1,0:T(8,128)S(1)}) custom-call(s32[4]{0:T(128)S(1)} %pad_add_fusion.where, s32[64]{0:T(128)S(1)} %get-tuple-element.32.cols, s32[64]{0:T(128)S(1)} %get-tuple-element.31.slots, f32[128,512]{1,0:T(8,128)S(1)} %copy-done.1, f32[128,512]{1,0:T(8,128)} %collective-permute-done.1.w1, ...), custom_call_target="tpu_custom_call" | custom-call | flops 40000000000 | bytes 7340032 | tf_op jit(solution)/shard_map/beta_kernel/pallas_call | solution.py:189
  40.9 0.1 collective-permute-start.5
  41.0 2.6 %collective-permute-done.5.got_ref = f32[16,128,128]{2,1,0:T(8,128)S(1)} collective-permute-done((f32[16,128,128]{2,1,0:T(8,128)S(1)}, f32[16,128,128]{2,1,0:T(8,128)S(1)}, u32[]{:S(2)}, u32[]{:S(2)}) %collective-permute-start.5) | collective-permute-done | bytes 1048608 | tf_op jit(solution)/shard_map/ppermute | solution.py:167
  43.6 1.0 cores_kernel.1
  44.6 1.9 %collective-permute-start.6 = (f32[4,128,128]{2,1,0:T(8,128)}, f32[4,128,128]{2,1,0:T(8,128)}, u32[]{:S(2)}, u32[]{:S(2)}) collective-permute-start(f32[4,128,128]{2,1,0:T(8,128)} %get-tuple-element.21), channel_id=1, source_target_pairs={{2,0},{4,2},{6,4},{3,1},{5,3},{7,5},{10,8},{12,10},{14,12},{11,9},... | collective-permute-start | bytes 786440 | tf_op jit(solution)/shard_map/ppermute | solution.py:233
  46.5 3.9 %collective-permute-start.7 = (f32[4,128,128]{2,1,0:T(8,128)}, f32[4,128,128]{2,1,0:T(8,128)}, u32[]{:S(2)}, u32[]{:S(2)}) collective-permute-start(f32[4,128,128]{2,1,0:T(8,128)} %get-tuple-element.22), channel_id=1, source_target_pairs={{0,2},{2,4},{4,6},{1,3},{3,5},{5,7},{8,10},{10,12},{12,14},{9,11},... | collective-permute-start | bytes 786440 | tf_op jit(solution)/shard_map/ppermute | solution.py:234
  50.5 1.3 %collective-permute-start.8 = (f32[4,128,128]{2,1,0:T(8,128)}, f32[4,128,128]{2,1,0:T(8,128)}, u32[]{:S(2)}, u32[]{:S(2)}) collective-permute-start(f32[4,128,128]{2,1,0:T(8,128)} %get-tuple-element.23), channel_id=1, source_target_pairs={{0,4},{6,2},{1,5},{7,3},{8,12},{14,10},{9,13},{15,11},{16,20},{22,... | collective-permute-start | bytes 786440 | tf_op jit(solution)/shard_map/ppermute | solution.py:235
  51.8 4.2 %all-to-all-done = f32[128,16,128]{2,1,0:T(8,128)S(1)} async-done(((f32[128,16,128]{2,1,0:T(8,128)}), f32[128,16,128]{2,1,0:T(8,128)S(1)}, u32[]{:S(2)}, u32[]{:S(2)}) %all-to-all-start) | async-done | bytes 1048608 | tf_op jit(solution)/shard_map/all_to_all | solution.py:208
  56.0 5.8 %alpha_kernel.1 = (f32[20,16,128]{2,1,0:T(8,128)S(1)}, f32[20,16,128]{2,1,0:T(8,128)S(1)}, f32[20,16,128]{2,1,0:T(8,128)S(1)}, f32[20,16,128]{2,1,0:T(8,128)S(1)}) custom-call(s32[4]{0:T(128)S(1)} %pad_add_fusion.where, s32[64]{0:T(128)S(1)} %get-tuple-element.32.cols, s32[64]{0:T(128)S(1)} %convert_reduce_fusion.owners, f32[32,64,128]{2,1,0:T(8,128)S(1)} %bitcast.6, ...), custom_call_target="tpu_custom_call" | custom-call | flops 40000000000 | bytes 7340032 | tf_op jit(solution)/shard_map/alpha_kernel/pallas_call | solution.py:189
  61.9 3.8 %collective-permute-start.9 = (f32[20,16,128]{2,1,0:T(8,128)S(1)}, f32[20,16,128]{2,1,0:T(8,128)S(1)}, u32[]{:S(2)}, u32[]{:S(2)}) collective-permute-start(f32[20,16,128]{2,1,0:T(8,128)S(1)} %get-tuple-element.27), channel_id=1, source_target_pairs={{0,2},{2,4},{4,6},{6,0},{1,3},{3,5},{5,7},{7,1},{8,10},{10,12},{12... | collective-permute-start | bytes 491528 | tf_op jit(solution)/shard_map/ppermute | solution.py:171
  65.6 0.8 collective-permute-start.10
  66.4 1.8 %collective-permute-start.11 = (f32[20,16,128]{2,1,0:T(8,128)S(1)}, f32[20,16,128]{2,1,0:T(8,128)S(1)}, u32[]{:S(2)}, u32[]{:S(2)}) collective-permute-start(f32[20,16,128]{2,1,0:T(8,128)S(1)} %get-tuple-element.29), channel_id=1, source_target_pairs={{0,6},{2,0},{4,2},{6,4},{1,7},{3,1},{5,3},{7,5},{8,14},{10,8},{12,... | collective-permute-start | bytes 491528 | tf_op jit(solution)/shard_map/ppermute | solution.py:171
  68.2 1.2 %planes_kernel.1 = (f32[4,128,128]{2,1,0:T(8,128)S(1)}, f32[8,128]{1,0:T(8,128)S(1)}) custom-call(f32[4,128,128]{2,1,0:T(8,128)S(1)} %get-tuple-element.20.own_ref, f32[4,128,128]{2,1,0:T(8,128)} %collective-permute-done.6.down_ref, f32[4,128,128]{2,1,0:T(8,128)} %collective-permute-done.7.up_ref, f32[4,128,128]{2,1,0:T(8,128)} %collective-permute-done.8.edge_ref), custom_call_target="tpu_custom_call" | custom-call | flops 40000000000 | bytes 1048576 | tf_op jit(solution)/shard_map/planes_kernel/pallas_call | solution.py:189
  69.3 7.9 %collective-permute-done.9.p1 = f32[20,16,128]{2,1,0:T(8,128)S(1)} collective-permute-done((f32[20,16,128]{2,1,0:T(8,128)S(1)}, f32[20,16,128]{2,1,0:T(8,128)S(1)}, u32[]{:S(2)}, u32[]{:S(2)}) %collective-permute-start.9) | collective-permute-done | bytes 163872 | tf_op jit(solution)/shard_map/ppermute | solution.py:171
  77.2 2.5 %collective-permute-done.10.p2 = f32[20,16,128]{2,1,0:T(8,128)S(1)} collective-permute-done((f32[20,16,128]{2,1,0:T(8,128)S(1)}, f32[20,16,128]{2,1,0:T(8,128)S(1)}, u32[]{:S(2)}, u32[]{:S(2)}) %collective-permute-start.10) | collective-permute-done | bytes 163872 | tf_op jit(solution)/shard_map/ppermute | solution.py:171
  79.7 0.8 collective-permute-done.11.p3
  80.5 0.6 strings_kernel.1
  81.1 23.7 %all_to_all.14.back_ref = f32[32,16,128]{2,1,0:T(8,128)S(1)} all-to-all(f32[32,16,128]{2,1,0:T(8,128)S(1)} %strings_kernel.1), channel_id=1, replica_groups=mesh['y'=4,'h'=2,'x'=4,'z'=4,'c'=2] {'y','h','x'}, dimensions={0} | all-to-all | bytes 524288 | tf_op jit(solution)/shard_map/all_to_all | solution.py:259
  104.9 0.8 final_kernel.1
  (19 shorter events, 0.2 us)
Async XLA Ops:
  0.0 34.6 %collective-permute-start.4 = (f32[32,128,128]{2,1,0:T(8,128)}, f32[32,128,128]{2,1,0:T(8,128)}, u32[]{:S(2)}, u32[]{:S(2)}) collective-permute-start(f32[32,128,128]{2,1,0:T(8,128)} %h0.3), channel_id=1, source_target_pairs={{0,1},{1,0},{2,3},{3,2},{4,5},{5,4},{6,7},{7,6},{8,9},{9,8},{10,11... | collective-permute-start | bytes 6291464 | tf_op jit(solution)/shard_map/ppermute | solution.py:167
  0.0 22.1 %collective-permute-start.1 = (f32[128,512]{1,0:T(8,128)}, f32[128,512]{1,0:T(8,128)}, u32[]{:S(2)}, u32[]{:S(2)}) collective-permute-start(f32[128,512]{1,0:T(8,128)} %c_ref.1), channel_id=1, source_target_pairs={{0,2},{2,4},{4,6},{6,0},{1,3},{3,5},{5,7},{7,1},{8,10},{10,12},{12... | collective-permute-start | bytes 786440 | tf_op jit(solution)/shard_map/ppermute | solution.py:171
  1.9 28.8 %collective-permute-start.2 = (f32[128,512]{1,0:T(8,128)}, f32[128,512]{1,0:T(8,128)}, u32[]{:S(2)}, u32[]{:S(2)}) collective-permute-start(f32[128,512]{1,0:T(8,128)} %c_ref.1), channel_id=1, source_target_pairs={{0,4},{2,6},{4,0},{6,2},{1,5},{3,7},{5,1},{7,3},{8,12},{10,14},{12... | collective-permute-start | bytes 786440 | tf_op jit(solution)/shard_map/ppermute | solution.py:171
  4.2 30.4 %collective-permute-start.3 = (f32[128,512]{1,0:T(8,128)}, f32[128,512]{1,0:T(8,128)}, u32[]{:S(2)}, u32[]{:S(2)}) collective-permute-start(f32[128,512]{1,0:T(8,128)} %c_ref.1), channel_id=1, source_target_pairs={{0,6},{2,0},{4,2},{6,4},{1,7},{3,1},{5,3},{7,5},{8,14},{10,8},{12,... | collective-permute-start | bytes 786440 | tf_op jit(solution)/shard_map/ppermute | solution.py:171
  5.3 16.7 %collective-permute-start = (s32[32]{0:T(128)}, s32[32]{0:T(128)S(1)}, u32[]{:S(2)}, u32[]{:S(2)}) collective-permute-start(s32[32]{0:T(128)} %param.7), channel_id=1, source_target_pairs={{0,1},{1,0},{2,3},{3,2},{4,5},{5,4},{6,7},{7,6},{8,9},{9,8},{10,11... | collective-permute-start | bytes 392 | tf_op jit(solution)/shard_map/ppermute | solution.py:167
  5.3 1.0 copy-start
  6.3 15.5 %copy-start.4 = (s32[32]{0:T(128)S(1)}, s32[32]{0:T(128)}, u32[]{:S(2)}) copy-start(s32[32]{0:T(128)} %param.6) | copy-start | bytes 388
  6.3 15.7 %copy-start.3 = (s32[32]{0:T(128)S(1)}, s32[32]{0:T(128)}, u32[]{:S(2)}) copy-start(s32[32]{0:T(128)} %param.7) | copy-start | bytes 388
  6.3 28.3 %copy-start.1 = (f32[128,512]{1,0:T(8,128)S(1)}, f32[128,512]{1,0:T(8,128)}, u32[]{:S(2)}) copy-start(f32[128,512]{1,0:T(8,128)} %c_ref.1) | copy-start | bytes 786436
  6.3 28.3 %copy-start.2 = (f32[32,128,128]{2,1,0:T(8,128)S(1)}, f32[32,128,128]{2,1,0:T(8,128)}, u32[]{:S(2)}) copy-start(f32[32,128,128]{2,1,0:T(8,128)} %h0.3) | copy-start | bytes 6291460
  7.4 48.6 %all-to-all-start = ((f32[128,16,128]{2,1,0:T(8,128)}), f32[128,16,128]{2,1,0:T(8,128)S(1)}, u32[]{:S(2)}, u32[]{:S(2)}) async-start(f32[128,16,128]{2,1,0:T(8,128)} %bitcast.4), calls=%async_computation | async-start | bytes 2097152 | tf_op jit(solution)/shard_map/all_to_all | solution.py:208
  40.9 2.7 %collective-permute-start.5 = (f32[16,128,128]{2,1,0:T(8,128)S(1)}, f32[16,128,128]{2,1,0:T(8,128)S(1)}, u32[]{:S(2)}, u32[]{:S(2)}) collective-permute-start(f32[16,128,128]{2,1,0:T(8,128)S(1)} %get-tuple-element.19), channel_id=1, source_target_pairs={{0,1},{1,0},{2,3},{3,2},{4,5},{5,4},{6,7},{7,6},{8,9},{9,8},{10,11... | collective-permute-start | bytes 3145736 | tf_op jit(solution)/shard_map/ppermute | solution.py:167
  44.6 21.8 %collective-permute-start.6 = (f32[4,128,128]{2,1,0:T(8,128)}, f32[4,128,128]{2,1,0:T(8,128)}, u32[]{:S(2)}, u32[]{:S(2)}) collective-permute-start(f32[4,128,128]{2,1,0:T(8,128)} %get-tuple-element.21), channel_id=1, source_target_pairs={{2,0},{4,2},{6,4},{3,1},{5,3},{7,5},{10,8},{12,10},{14,12},{11,9},... | collective-permute-start | bytes 786440 | tf_op jit(solution)/shard_map/ppermute | solution.py:233
  46.5 21.6 %collective-permute-start.7 = (f32[4,128,128]{2,1,0:T(8,128)}, f32[4,128,128]{2,1,0:T(8,128)}, u32[]{:S(2)}, u32[]{:S(2)}) collective-permute-start(f32[4,128,128]{2,1,0:T(8,128)} %get-tuple-element.22), channel_id=1, source_target_pairs={{0,2},{2,4},{4,6},{1,3},{3,5},{5,7},{8,10},{10,12},{12,14},{9,11},... | collective-permute-start | bytes 786440 | tf_op jit(solution)/shard_map/ppermute | solution.py:234
  50.5 17.7 %collective-permute-start.8 = (f32[4,128,128]{2,1,0:T(8,128)}, f32[4,128,128]{2,1,0:T(8,128)}, u32[]{:S(2)}, u32[]{:S(2)}) collective-permute-start(f32[4,128,128]{2,1,0:T(8,128)} %get-tuple-element.23), channel_id=1, source_target_pairs={{0,4},{6,2},{1,5},{7,3},{8,12},{14,10},{9,13},{15,11},{16,20},{22,... | collective-permute-start | bytes 786440 | tf_op jit(solution)/shard_map/ppermute | solution.py:235
  61.9 15.4 %collective-permute-start.9 = (f32[20,16,128]{2,1,0:T(8,128)S(1)}, f32[20,16,128]{2,1,0:T(8,128)S(1)}, u32[]{:S(2)}, u32[]{:S(2)}) collective-permute-start(f32[20,16,128]{2,1,0:T(8,128)S(1)} %get-tuple-element.27), channel_id=1, source_target_pairs={{0,2},{2,4},{4,6},{6,0},{1,3},{3,5},{5,7},{7,1},{8,10},{10,12},{12... | collective-permute-start | bytes 491528 | tf_op jit(solution)/shard_map/ppermute | solution.py:171
  65.6 14.1 %collective-permute-start.10 = (f32[20,16,128]{2,1,0:T(8,128)S(1)}, f32[20,16,128]{2,1,0:T(8,128)S(1)}, u32[]{:S(2)}, u32[]{:S(2)}) collective-permute-start(f32[20,16,128]{2,1,0:T(8,128)S(1)} %get-tuple-element.28), channel_id=1, source_target_pairs={{0,4},{2,6},{4,0},{6,2},{1,5},{3,7},{5,1},{7,3},{8,12},{10,14},{12... | collective-permute-start | bytes 491528 | tf_op jit(solution)/shard_map/ppermute | solution.py:171
  66.4 14.1 %collective-permute-start.11 = (f32[20,16,128]{2,1,0:T(8,128)S(1)}, f32[20,16,128]{2,1,0:T(8,128)S(1)}, u32[]{:S(2)}, u32[]{:S(2)}) collective-permute-start(f32[20,16,128]{2,1,0:T(8,128)S(1)} %get-tuple-element.29), channel_id=1, source_target_pairs={{0,6},{2,0},{4,2},{6,4},{1,7},{3,1},{5,3},{7,5},{8,14},{10,8},{12,... | collective-permute-start | bytes 491528 | tf_op jit(solution)/shard_map/ppermute | solution.py:171

commit v6 on v5

--- a/solution.py
+++ b/solution.py
@@ -7,7 +7,7 @@
 from jax.sharding import PartitionSpec as P
 
 ROWS = ("y", "h", "x")
-ANY = pl.BlockSpec(memory_space=pl.ANY)
+HBM = pl.BlockSpec(memory_space=pltpu.HBM)
 VMEM = pl.BlockSpec(memory_space=pltpu.VMEM)
 SMEM = pl.BlockSpec(memory_space=pltpu.SMEM)
 F32 = jnp.float32
@@ -146,7 +146,7 @@
         out_ref[pl.ds(4 * jnp.bitwise_and(z - k + 4, 3), 20)] += part[...]
 
 
-def cores_kernel(keep_ref, got_ref, own_ref, down_ref, up_ref, edge_ref, token_ref):
+def cores_kernel(keep_ref, got_ref, after, own_ref, down_ref, up_ref, edge_ref, token_ref):
     token_ref[...] = jnp.zeros_like(token_ref)
     for n, ref in enumerate((own_ref, down_ref, up_ref, edge_ref)):
         ref[...] = keep_ref[4 * n : 4 * n + 4] + got_ref[4 * n : 4 * n + 4]
@@ -210,7 +210,7 @@
     keep, send = call(
         beta_kernel,
         (shape(16, 128, 128), shape(16, 128, 128)),
-        [SMEM] * 3 + [ANY] * 6,
+        [SMEM] * 3 + [HBM] * 6,
         where, cols, slots, *rows, hblocks, swapped,
         scratch=[
             pltpu.VMEM((4, 128, 512), F32),
@@ -227,8 +227,8 @@
     own, down, up, edge, token = call(
         cores_kernel,
         (shape(4, 128, 128),) * 4 + (shape(8, 128),),
-        [VMEM] * 2,
-        keep, swap(send),
+        [VMEM] * 2 + [HBM],
+        keep, swap(send), moved,
     )
     down = lax.ppermute(down, "z", [(1, 0), (2, 1), (3, 2)])
     up = lax.ppermute(up, "z", [(0, 1), (1, 2), (2, 3)])
@@ -243,7 +243,7 @@
     parts = call(
         alpha_kernel,
         (shape(20, 16, 128),) * 4,
-        [SMEM] * 3 + [VMEM] + [ANY] * 2 + [VMEM],
+        [SMEM] * 3 + [VMEM] + [HBM] * 2 + [VMEM],
         where, cols, owners, moved.reshape(32, 64, 128), hblocks, swapped, token,
         scratch=[
             pltpu.VMEM((32, 64, 128), F32),

time: 106 us -> 112 us (1.057)
  waiting for transfers between devices: 30.6 us -> 39.2 us
  blocking collectives: 23.7 us -> 21.2 us
  local copies, waits for them, and re-layouts: 1.08 us -> 2.67 us
    all_to_all x1, waiting for transfers between devices: 4.25 us -> 14.9 us  [local(): lax.all_to_all(at.reshape(2048, 128), ROWS + ('z',), 0, 0, tiled=True)]
    ppermute x3, waiting for transfers between devices: 2.65 us -> 0.01 us  [swap(): return lax.ppermute(value, 'c', [(0, 1), (1, 0)])]
    all_to_all x1, blocking collectives: 23.7 us -> 21.2 us  [local(): back = lax.all_to_all(total, ROWS, 0, 0, tiled=True)]
    unnamed x10 -> x12, local copies, waits for them, and re-layouts: 0.99 us -> 2.59 us
    all_to_all x1, starting transfers between devices: 14.1 us -> 12.8 us  [local(): lax.all_to_all(at.reshape(2048, 128), ROWS + ('z',), 0, 0, tiled=True)]
  transfers between devices with their start and end apart: 13 -> 13, of which waited for: 7 -> 4; matrix products, arithmetic and copies ran while one was open for 1% -> 1% of each run, Pallas kernels for 14% -> 13%
where the time goes in v6:
time: 112 us
  waiting for transfers between devices  39.2 us (35%)
  starting transfers between devices  32 us (29%)
  blocking collectives  21.2 us (19%)
  Pallas kernels  16.2 us (14%)
  local copies, waits for them, and re-layouts  2.67 us (2%)
    ppermute x6, waiting for transfers between devices, shift(): return lax.ppermute(value, 'z', [(i, (i + by) % 4) for i in range(4)])  24.2 us
    all_to_all x1, blocking collectives, local(): back = lax.all_to_all(total, ROWS, 0, 0, tiled=True)  21.2 us
    pallas_call x7, Pallas kernels, call(): pl.pallas_call(kernel, out_shape=outs, in_specs=in_specs, out_specs=space...  16.2 us
    all_to_all x1, waiting for transfers between devices, local(): lax.all_to_all(at.reshape(2048, 128), ROWS + ('z',), 0, 0, tiled=True)  14.9 us
    all_to_all x1, starting transfers between devices, local(): lax.all_to_all(at.reshape(2048, 128), ROWS + ('z',), 0, 0, tiled=True)  12.8 us
    ppermute x6, starting transfers between devices, shift(): return lax.ppermute(value, 'z', [(i, (i + by) % 4) for i in range(4)])  11.9 us
    ppermute x1, starting transfers between devices, local(): up = lax.ppermute(up, 'z', [(0, 1), (1, 2), (2, 3)])  3.03 us
    ppermute x1, starting transfers between devices, local(): down = lax.ppermute(down, 'z', [(1, 0), (2, 1), (3, 2)])  2.94 us
  transfers between devices with their start and end apart: 13, of which 4 were waited for; matrix products, arithmetic and copies ran while one was open for 1% of the time, Pallas kernels for 13%

profile of v6, /device:TPU:32, one launch (start us, length us, event | category | flops | bytes accessed | tf_op | source)
XLA Modules:
  0.0 111.8 jit_solution(16949943592705513442)
XLA Ops:
  0.0 1.8 %collective-permute-start.3 = (f32[128,512]{1,0:T(8,128)}, f32[128,512]{1,0:T(8,128)S(1)}, u32[]{:S(2)}, u32[]{:S(2)}) collective-permute-start(f32[128,512]{1,0:T(8,128)} %c_ref.1), channel_id=1, source_target_pairs={{0,6},{2,0},{4,2},{6,4},{1,7},{3,1},{5,3},{7,5},{8,14},{10,8},{12,... | collective-permute-start | bytes 786440 | tf_op jit(solution)/shard_map/ppermute | solution.py:171
  1.8 1.5 %collective-permute-start.2 = (f32[128,512]{1,0:T(8,128)}, f32[128,512]{1,0:T(8,128)S(1)}, u32[]{:S(2)}, u32[]{:S(2)}) collective-permute-start(f32[128,512]{1,0:T(8,128)} %c_ref.1), channel_id=1, source_target_pairs={{0,4},{2,6},{4,0},{6,2},{1,5},{3,7},{5,1},{7,3},{8,12},{10,14},{12... | collective-permute-start | bytes 786440 | tf_op jit(solution)/shard_map/ppermute | solution.py:171
  3.4 2.8 %collective-permute-start.1 = (f32[128,512]{1,0:T(8,128)}, f32[128,512]{1,0:T(8,128)S(1)}, u32[]{:S(2)}, u32[]{:S(2)}) collective-permute-start(f32[128,512]{1,0:T(8,128)} %c_ref.1), channel_id=1, source_target_pairs={{0,2},{2,4},{4,6},{6,0},{1,3},{3,5},{5,7},{7,1},{8,10},{10,12},{12... | collective-permute-start | bytes 786440 | tf_op jit(solution)/shard_map/ppermute | solution.py:171
  6.2 1.0 copy-done
  7.2 1.1 turn_kernel.1
  8.3 12.8 %all-to-all-start = ((f32[128,16,128]{2,1,0:T(8,128)}), f32[128,16,128]{2,1,0:T(8,128)S(1)}, u32[]{:S(2)}, u32[]{:S(2)}) async-start(f32[128,16,128]{2,1,0:T(8,128)} %bitcast.4), calls=%async_computation | async-start | bytes 2097152 | tf_op jit(solution)/shard_map/all_to_all | solution.py:208
  21.1 0.1 add_multiply_fusion
  21.1 0.1 iota_add_fusion
  21.2 0.1 add.55
  21.3 0.1 select_reduce_fusion
  21.4 0.1 convert_reduce_fusion.owners
  21.5 0.1 pad_add_fusion.where
  21.6 0.1 compare_select_fusion.6
  21.7 12.7 %collective-permute-done.1.w1 = f32[128,512]{1,0:T(8,128)S(1)} collective-permute-done((f32[128,512]{1,0:T(8,128)}, f32[128,512]{1,0:T(8,128)S(1)}, u32[]{:S(2)}, u32[]{:S(2)}) %collective-permute-start.1) | collective-permute-done | bytes 262176 | tf_op jit(solution)/shard_map/ppermute | solution.py:171
  34.4 1.6 %copy-done.2 = f32[32,128,128]{2,1,0:T(8,128)S(1)} copy-done((f32[32,128,128]{2,1,0:T(8,128)S(1)}, f32[32,128,128]{2,1,0:T(8,128)}, u32[]{:S(2)}) %copy-start.2) | copy-done | bytes 2097176
  36.0 7.6 %beta_kernel.1 = (f32[16,128,128]{2,1,0:T(8,128)S(1)}, f32[16,128,128]{2,1,0:T(8,128)}) custom-call(s32[4]{0:T(128)S(1)} %pad_add_fusion.where, s32[64]{0:T(128)S(1)} %get-tuple-element.32.cols, s32[64]{0:T(128)S(1)} %get-tuple-element.31.slots, f32[128,512]{1,0:T(8,128)S(1)} %copy-done.1, f32[128,512]{1,0:T(8,128)S(1)} %collective-permute-done.1.w1, ...), custom_call_target="tpu_custom_call" | custom-call | flops 40000000000 | bytes 7340032 | tf_op jit(solution)/shard_map/beta_kernel/pallas_call | solution.py:189
  43.6 0.1 collective-permute-start.5
  43.7 14.9 %all-to-all-done = f32[128,16,128]{2,1,0:T(8,128)S(1)} async-done(((f32[128,16,128]{2,1,0:T(8,128)}), f32[128,16,128]{2,1,0:T(8,128)S(1)}, u32[]{:S(2)}, u32[]{:S(2)}) %all-to-all-start) | async-done | bytes 1048608 | tf_op jit(solution)/shard_map/all_to_all | solution.py:208
  58.6 0.1 cores_kernel.1
  58.8 2.9 %collective-permute-start.6 = (f32[4,128,128]{2,1,0:T(8,128)S(1)}, f32[4,128,128]{2,1,0:T(8,128)S(1)}, u32[]{:S(2)}, u32[]{:S(2)}) collective-permute-start(f32[4,128,128]{2,1,0:T(8,128)S(1)} %get-tuple-element.21), channel_id=1, source_target_pairs={{2,0},{4,2},{6,4},{3,1},{5,3},{7,5},{10,8},{12,10},{14,12},{11,9},... | collective-permute-start | bytes 786440 | tf_op jit(solution)/shard_map/ppermute | solution.py:233
  61.7 3.0 %collective-permute-start.7 = (f32[4,128,128]{2,1,0:T(8,128)S(1)}, f32[4,128,128]{2,1,0:T(8,128)S(1)}, u32[]{:S(2)}, u32[]{:S(2)}) collective-permute-start(f32[4,128,128]{2,1,0:T(8,128)S(1)} %get-tuple-element.22), channel_id=1, source_target_pairs={{0,2},{2,4},{4,6},{1,3},{3,5},{5,7},{8,10},{10,12},{12,14},{9,11},... | collective-permute-start | bytes 786440 | tf_op jit(solution)/shard_map/ppermute | solution.py:234
  64.7 1.3 %collective-permute-start.8 = (f32[4,128,128]{2,1,0:T(8,128)S(1)}, f32[4,128,128]{2,1,0:T(8,128)S(1)}, u32[]{:S(2)}, u32[]{:S(2)}) collective-permute-start(f32[4,128,128]{2,1,0:T(8,128)S(1)} %get-tuple-element.23), channel_id=1, source_target_pairs={{0,4},{6,2},{1,5},{7,3},{8,12},{14,10},{9,13},{15,11},{16,20},{22,... | collective-permute-start | bytes 786440 | tf_op jit(solution)/shard_map/ppermute | solution.py:235
  66.1 5.8 %alpha_kernel.1 = (f32[20,16,128]{2,1,0:T(8,128)S(1)}, f32[20,16,128]{2,1,0:T(8,128)S(1)}, f32[20,16,128]{2,1,0:T(8,128)S(1)}, f32[20,16,128]{2,1,0:T(8,128)S(1)}) custom-call(s32[4]{0:T(128)S(1)} %pad_add_fusion.where, s32[64]{0:T(128)S(1)} %get-tuple-element.32.cols, s32[64]{0:T(128)S(1)} %convert_reduce_fusion.owners, f32[32,64,128]{2,1,0:T(8,128)S(1)} %bitcast.8, ...), custom_call_target="tpu_custom_call" | custom-call | flops 40000000000 | bytes 7340032 | tf_op jit(solution)/shard_map/alpha_kernel/pallas_call | solution.py:189
  71.9 0.1 collective-permute-start.9
  72.0 4.5 %collective-permute-start.10 = (f32[20,16,128]{2,1,0:T(8,128)S(1)}, f32[20,16,128]{2,1,0:T(8,128)S(1)}, u32[]{:S(2)}, u32[]{:S(2)}) collective-permute-start(f32[20,16,128]{2,1,0:T(8,128)S(1)} %get-tuple-element.28), channel_id=1, source_target_pairs={{0,4},{2,6},{4,0},{6,2},{1,5},{3,7},{5,1},{7,3},{8,12},{10,14},{12... | collective-permute-start | bytes 491528 | tf_op jit(solution)/shard_map/ppermute | solution.py:171
  76.4 1.1 collective-permute-start.11
  77.6 0.1 planes_kernel.1
  77.6 4.4 %collective-permute-done.9.p1 = f32[20,16,128]{2,1,0:T(8,128)S(1)} collective-permute-done((f32[20,16,128]{2,1,0:T(8,128)S(1)}, f32[20,16,128]{2,1,0:T(8,128)S(1)}, u32[]{:S(2)}, u32[]{:S(2)}) %collective-permute-start.9) | collective-permute-done | bytes 163872 | tf_op jit(solution)/shard_map/ppermute | solution.py:171
  82.0 7.1 %collective-permute-done.10.p2 = f32[20,16,128]{2,1,0:T(8,128)S(1)} collective-permute-done((f32[20,16,128]{2,1,0:T(8,128)S(1)}, f32[20,16,128]{2,1,0:T(8,128)S(1)}, u32[]{:S(2)}, u32[]{:S(2)}) %collective-permute-start.10) | collective-permute-done | bytes 163872 | tf_op jit(solution)/shard_map/ppermute | solution.py:171
  89.1 0.6 strings_kernel.1
  89.7 21.2 %all_to_all.16.back_ref = f32[32,16,128]{2,1,0:T(8,128)S(1)} all-to-all(f32[32,16,128]{2,1,0:T(8,128)S(1)} %strings_kernel.1), channel_id=1, replica_groups=mesh['y'=4,'h'=2,'x'=4,'z'=4,'c'=2] {'y','h','x'}, dimensions={0} | all-to-all | bytes 524288 | tf_op jit(solution)/shard_map/all_to_all | solution.py:259
  111.0 0.8 final_kernel.1
  (21 shorter events, 0.0 us)
Async XLA Ops:
  0.0 34.4 %collective-permute-start.4 = (f32[32,128,128]{2,1,0:T(8,128)}, f32[32,128,128]{2,1,0:T(8,128)}, u32[]{:S(2)}, u32[]{:S(2)}) collective-permute-start(f32[32,128,128]{2,1,0:T(8,128)} %h0.3), channel_id=1, source_target_pairs={{0,1},{1,0},{2,3},{3,2},{4,5},{5,4},{6,7},{7,6},{8,9},{9,8},{10,11... | collective-permute-start | bytes 6291464 | tf_op jit(solution)/shard_map/ppermute | solution.py:167
  0.0 21.7 %collective-permute-start.3 = (f32[128,512]{1,0:T(8,128)}, f32[128,512]{1,0:T(8,128)S(1)}, u32[]{:S(2)}, u32[]{:S(2)}) collective-permute-start(f32[128,512]{1,0:T(8,128)} %c_ref.1), channel_id=1, source_target_pairs={{0,6},{2,0},{4,2},{6,4},{1,7},{3,1},{5,3},{7,5},{8,14},{10,8},{12,... | collective-permute-start | bytes 786440 | tf_op jit(solution)/shard_map/ppermute | solution.py:171
  1.8 19.8 %collective-permute-start.2 = (f32[128,512]{1,0:T(8,128)}, f32[128,512]{1,0:T(8,128)S(1)}, u32[]{:S(2)}, u32[]{:S(2)}) collective-permute-start(f32[128,512]{1,0:T(8,128)} %c_ref.1), channel_id=1, source_target_pairs={{0,4},{2,6},{4,0},{6,2},{1,5},{3,7},{5,1},{7,3},{8,12},{10,14},{12... | collective-permute-start | bytes 786440 | tf_op jit(solution)/shard_map/ppermute | solution.py:171
  3.4 31.0 %collective-permute-start.1 = (f32[128,512]{1,0:T(8,128)}, f32[128,512]{1,0:T(8,128)S(1)}, u32[]{:S(2)}, u32[]{:S(2)}) collective-permute-start(f32[128,512]{1,0:T(8,128)} %c_ref.1), channel_id=1, source_target_pairs={{0,2},{2,4},{4,6},{6,0},{1,3},{3,5},{5,7},{7,1},{8,10},{10,12},{12... | collective-permute-start | bytes 786440 | tf_op jit(solution)/shard_map/ppermute | solution.py:171
  6.2 15.4 %collective-permute-start = (s32[32]{0:T(128)}, s32[32]{0:T(128)S(1)}, u32[]{:S(2)}, u32[]{:S(2)}) collective-permute-start(s32[32]{0:T(128)} %param.7), channel_id=1, source_target_pairs={{0,1},{1,0},{2,3},{3,2},{4,5},{5,4},{6,7},{7,6},{8,9},{9,8},{10,11... | collective-permute-start | bytes 392 | tf_op jit(solution)/shard_map/ppermute | solution.py:167
  6.2 1.0 copy-start
  7.2 14.1 %copy-start.5 = (s32[32]{0:T(128)S(1)}, s32[32]{0:T(128)}, u32[]{:S(2)}) copy-start(s32[32]{0:T(128)} %param.6) | copy-start | bytes 388
  7.2 14.4 %copy-start.4 = (s32[32]{0:T(128)S(1)}, s32[32]{0:T(128)}, u32[]{:S(2)}) copy-start(s32[32]{0:T(128)} %param.7) | copy-start | bytes 388
  7.2 27.2 %copy-start.1 = (f32[128,512]{1,0:T(8,128)S(1)}, f32[128,512]{1,0:T(8,128)}, u32[]{:S(2)}) copy-start(f32[128,512]{1,0:T(8,128)} %c_ref.1) | copy-start | bytes 786436
  8.3 50.3 %all-to-all-start = ((f32[128,16,128]{2,1,0:T(8,128)}), f32[128,16,128]{2,1,0:T(8,128)S(1)}, u32[]{:S(2)}, u32[]{:S(2)}) async-start(f32[128,16,128]{2,1,0:T(8,128)} %bitcast.4), calls=%async_computation | async-start | bytes 2097152 | tf_op jit(solution)/shard_map/all_to_all | solution.py:208
  34.4 1.6 %copy-start.2 = (f32[32,128,128]{2,1,0:T(8,128)S(1)}, f32[32,128,128]{2,1,0:T(8,128)}, u32[]{:S(2)}) copy-start(f32[32,128,128]{2,1,0:T(8,128)} %h0.3) | copy-start | bytes 6291460
  43.6 15.0 %collective-permute-start.5 = (f32[16,128,128]{2,1,0:T(8,128)}, f32[16,128,128]{2,1,0:T(8,128)S(1)}, u32[]{:S(2)}, u32[]{:S(2)}) collective-permute-start(f32[16,128,128]{2,1,0:T(8,128)} %get-tuple-element.19), channel_id=1, source_target_pairs={{0,1},{1,0},{2,3},{3,2},{4,5},{5,4},{6,7},{7,6},{8,9},{9,8},{10,11... | collective-permute-start | bytes 3145736 | tf_op jit(solution)/shard_map/ppermute | solution.py:167
  58.6 7.4 %copy-start.3 = (f32[32,128,128]{2,1,0:T(8,128)S(1)}, f32[32,128,128]{2,1,0:T(8,128)}, u32[]{:S(2)}) copy-start(f32[32,128,128]{2,1,0:T(8,128)} %h0.3) | copy-start | bytes 6291460
  58.8 17.7 %collective-permute-start.6 = (f32[4,128,128]{2,1,0:T(8,128)S(1)}, f32[4,128,128]{2,1,0:T(8,128)S(1)}, u32[]{:S(2)}, u32[]{:S(2)}) collective-permute-start(f32[4,128,128]{2,1,0:T(8,128)S(1)} %get-tuple-element.21), channel_id=1, source_target_pairs={{2,0},{4,2},{6,4},{3,1},{5,3},{7,5},{10,8},{12,10},{14,12},{11,9},... | collective-permute-start | bytes 786440 | tf_op jit(solution)/shard_map/ppermute | solution.py:233
  61.7 15.9 %collective-permute-start.7 = (f32[4,128,128]{2,1,0:T(8,128)S(1)}, f32[4,128,128]{2,1,0:T(8,128)S(1)}, u32[]{:S(2)}, u32[]{:S(2)}) collective-permute-start(f32[4,128,128]{2,1,0:T(8,128)S(1)} %get-tuple-element.22), channel_id=1, source_target_pairs={{0,2},{2,4},{4,6},{1,3},{3,5},{5,7},{8,10},{10,12},{12,14},{9,11},... | collective-permute-start | bytes 786440 | tf_op jit(solution)/shard_map/ppermute | solution.py:234
  64.7 12.8 %collective-permute-start.8 = (f32[4,128,128]{2,1,0:T(8,128)S(1)}, f32[4,128,128]{2,1,0:T(8,128)S(1)}, u32[]{:S(2)}, u32[]{:S(2)}) collective-permute-start(f32[4,128,128]{2,1,0:T(8,128)S(1)} %get-tuple-element.23), channel_id=1, source_target_pairs={{0,4},{6,2},{1,5},{7,3},{8,12},{14,10},{9,13},{15,11},{16,20},{22,... | collective-permute-start | bytes 786440 | tf_op jit(solution)/shard_map/ppermute | solution.py:235
  71.9 10.1 %collective-permute-start.9 = (f32[20,16,128]{2,1,0:T(8,128)S(1)}, f32[20,16,128]{2,1,0:T(8,128)S(1)}, u32[]{:S(2)}, u32[]{:S(2)}) collective-permute-start(f32[20,16,128]{2,1,0:T(8,128)S(1)} %get-tuple-element.27), channel_id=1, source_target_pairs={{0,2},{2,4},{4,6},{6,0},{1,3},{3,5},{5,7},{7,1},{8,10},{10,12},{12... | collective-permute-start | bytes 491528 | tf_op jit(solution)/shard_map/ppermute | solution.py:171
  72.0 17.1 %collective-permute-start.10 = (f32[20,16,128]{2,1,0:T(8,128)S(1)}, f32[20,16,128]{2,1,0:T(8,128)S(1)}, u32[]{:S(2)}, u32[]{:S(2)}) collective-permute-start(f32[20,16,128]{2,1,0:T(8,128)S(1)} %get-tuple-element.28), channel_id=1, source_target_pairs={{0,4},{2,6},{4,0},{6,2},{1,5},{3,7},{5,1},{7,3},{8,12},{10,14},{12... | collective-permute-start | bytes 491528 | tf_op jit(solution)/shard_map/ppermute | solution.py:171
  76.4 12.7 %collective-permute-start.11 = (f32[20,16,128]{2,1,0:T(8,128)S(1)}, f32[20,16,128]{2,1,0:T(8,128)S(1)}, u32[]{:S(2)}, u32[]{:S(2)}) collective-permute-start(f32[20,16,128]{2,1,0:T(8,128)S(1)} %get-tuple-element.29), channel_id=1, source_target_pairs={{0,6},{2,0},{4,2},{6,4},{1,7},{3,1},{5,3},{7,5},{8,14},{10,8},{12,... | collective-permute-start | bytes 491528 | tf_op jit(solution)/shard_map/ppermute | solution.py:171

commit v7 on v5

--- a/solution.py
+++ b/solution.py
@@ -7,13 +7,12 @@
 from jax.sharding import PartitionSpec as P
 
 ROWS = ("y", "h", "x")
-ANY = pl.BlockSpec(memory_space=pl.ANY)
+HBM = pl.BlockSpec(memory_space=pltpu.HBM)
 VMEM = pl.BlockSpec(memory_space=pltpu.VMEM)
 SMEM = pl.BlockSpec(memory_space=pltpu.SMEM)
 F32 = jnp.float32
 BF16 = jnp.bfloat16
 TRASH = 28
-CONTRACT = (((1,), (1,)), ((), ()))
 
 BUSY = 40 * 10**9
 
@@ -42,28 +41,41 @@
     return high, (value - high.astype(F32)).astype(BF16)
 
 
+def blocks_kernel(h0, h1, out_ref, hbuf, sem):
+    chunks = []
+    for n in range(8):
+        source = (h0, h1)[n // 4].at[pl.ds(8 * (n % 4), 8)]
+        chunks.append(pltpu.make_async_copy(source, hbuf.at[pl.ds(8 * n, 8)], sem.at[n]))
+    for chunk in chunks:
+        chunk.start()
+    for n, chunk in enumerate(chunks):
+        chunk.wait()
+
+        @pl.loop(0, 4)
+        def _(step, n=n):
+            for u in range(2):
+                at = 8 * n + 2 * step + u
+                high, low = halves(jnp.transpose(hbuf[at]))
+                out_ref[at, :, :128] = high
+                out_ref[at, :, 128:] = low
+
+
 def product(left, block):
-    high, low = halves(block)
     rows = left.shape[0] // 2
-    one = lax.dot_general(left, high, CONTRACT, preferred_element_type=F32)
-    two = lax.dot_general(left[:rows], low, CONTRACT, preferred_element_type=F32)
-    return one[:rows] + (one[rows:] + two)
+    both = jnp.dot(left, block, preferred_element_type=F32)
+    return both[:rows, :128] + (both[rows:, :128] + both[:rows, 128:])
 
 
 def beta_kernel(
-    where, cols, slots, w0, w1, w2, w3, h0, h1, keep_ref, send_ref,
-    wide, stack, hbuf, acc, list_ref, sem_w, sem_h,
+    where, cols, slots, w0, w1, w2, w3, blocks, keep_ref, send_ref,
+    wide, stack, acc, list_ref, sem_w,
 ):
     z, core = where[2], where[3]
     loads = [
         pltpu.make_async_copy(w, wide.at[k], sem_w.at[k]) for k, w in enumerate((w0, w1, w2, w3))
     ]
-    chunks = [
-        pltpu.make_async_copy(h, hbuf.at[pl.ds(32 * n, 32)], sem_h.at[n])
-        for n, h in enumerate((h0, h1))
-    ]
-    for copy in loads + chunks:
-        copy.start()
+    for load in loads:
+        load.start()
     acc[...] = jnp.zeros_like(acc)
 
     def note(n, count):
@@ -79,8 +91,6 @@
             high, low = halves(wide[k, :, 128 * t : 128 * (t + 1)])
             stack[home + t, :128] = high
             stack[home + t, 128:] = low
-    for chunk in chunks:
-        chunk.wait()
 
     @pl.loop(0, lax.shift_right_logical(count + 1, 1))
     def _(step):
@@ -90,7 +100,7 @@
             column = cols[n]
             left = stack[4 * lax.shift_right_logical(column, 3) + jnp.bitwise_and(column, 3)]
             slot = jnp.where(2 * step + u < count, slots[n], TRASH)
-            terms.append((slot, product(left, hbuf[n])))
+            terms.append((slot, product(left, blocks[n])))
         for slot, term in terms:
             acc[slot] += term
 
@@ -104,13 +114,13 @@
 
 
 def alpha_kernel(
-    where, cols, owners, a_ref, h0, h1, after, o0, o1, o2, o3, acc, stack, hbuf, sem_h
+    where, cols, owners, a_ref, source, after, o0, o1, o2, o3, acc, stack, blocks, sem
 ):
     z = where[2]
     chunks = []
-    for n in range(4):
-        source = (h0, h1)[n // 2].at[pl.ds(16 * (n % 2), 16)]
-        chunks.append(pltpu.make_async_copy(source, hbuf.at[pl.ds(16 * n, 16)], sem_h.at[n]))
+    for n in range(8):
+        span = pl.ds(8 * n, 8)
+        chunks.append(pltpu.make_async_copy(source.at[span], blocks.at[span], sem.at[n]))
     for chunk in chunks:
         chunk.start()
     acc[...] = jnp.zeros_like(acc)
@@ -126,12 +136,12 @@
     for n, chunk in enumerate(chunks):
         chunk.wait()
 
-        @pl.loop(0, 4)
+        @pl.loop(0, 2)
         def _(step, n=n):
             terms = []
             for u in range(4):
-                spot = 16 * n + 4 * step + u
-                terms.append((owners[spot], product(stack[cols[spot]], hbuf[spot])))
+                spot = 8 * n + 4 * step + u
+                terms.append((owners[spot], product(stack[cols[spot]], blocks[spot])))
             for owner, term in terms:
                 acc[owner] += term
 
@@ -201,25 +211,31 @@
 def local(coeffs, hblocks, hcount, hcols):
     z, c = lax.axis_index("z"), lax.axis_index("c")
     where = jnp.stack([z, z, z, c]).astype(jnp.int32)
-    swapped = swap(hblocks)
     rows = [coeffs] + [shift(coeffs, k) for k in (1, 2, 3)]
     cols, owners, slots = tables(hcount, hcols, z, c)
     at = call(turn_kernel, shape(32, 4, 16, 128), [VMEM], coeffs)
     moved = lax.all_to_all(at.reshape(2048, 128), ROWS + ("z",), 0, 0, tiled=True)
 
+    blocks = call(
+        blocks_kernel,
+        shape(64, 128, 256, kind=BF16),
+        [HBM] * 2,
+        hblocks, swap(hblocks),
+        scratch=[pltpu.VMEM((64, 128, 128), F32), pltpu.SemaphoreType.DMA((8,))],
+        mib=24,
+        work=(0, 8 << 20),
+    )
     keep, send = call(
         beta_kernel,
         (shape(16, 128, 128), shape(16, 128, 128)),
-        [SMEM] * 3 + [ANY] * 6,
-        where, cols, slots, *rows, hblocks, swapped,
+        [SMEM] * 3 + [HBM] * 4 + [VMEM],
+        where, cols, slots, *rows, blocks,
         scratch=[
             pltpu.VMEM((4, 128, 512), F32),
             pltpu.VMEM((16, 256, 128), BF16),
-            pltpu.VMEM((64, 128, 128), F32),
             pltpu.VMEM((TRASH + 1, 128, 128), F32),
             pltpu.SMEM((72,), jnp.int32),
             pltpu.SemaphoreType.DMA((4,)),
-            pltpu.SemaphoreType.DMA((2,)),
         ],
         mib=24,
         work=(BUSY, 7 << 20),
@@ -230,9 +246,9 @@
         [VMEM] * 2,
         keep, swap(send),
     )
-    down = lax.ppermute(down, "z", [(1, 0), (2, 1), (3, 2)])
-    up = lax.ppermute(up, "z", [(0, 1), (1, 2), (2, 3)])
-    edge = lax.ppermute(edge, "z", [(0, 2), (3, 1)])
+    down = lax.ppermute(down, ("z", "c"), [(3, 1), (4, 2), (5, 3), (6, 4), (7, 5)])
+    up = lax.ppermute(up, ("z", "c"), [(0, 2), (1, 3), (2, 4), (3, 5), (4, 6)])
+    edge = lax.ppermute(edge, ("z", "c"), [(0, 4), (7, 3)])
     beta, done = call(
         planes_kernel,
         (shape(4, 128, 128), shape(8, 128)),
@@ -243,13 +259,13 @@
     parts = call(
         alpha_kernel,
         (shape(20, 16, 128),) * 4,
-        [SMEM] * 3 + [VMEM] + [ANY] * 2 + [VMEM],
-        where, cols, owners, moved.reshape(32, 64, 128), hblocks, swapped, token,
+        [SMEM] * 3 + [VMEM, HBM, VMEM],
+        where, cols, owners, moved.reshape(32, 64, 128), blocks, token,
         scratch=[
             pltpu.VMEM((32, 64, 128), F32),
             pltpu.VMEM((32, 128, 128), BF16),
-            pltpu.VMEM((64, 128, 128), F32),
-            pltpu.SemaphoreType.DMA((4,)),
+            pltpu.VMEM((64, 128, 256), BF16),
+            pltpu.SemaphoreType.DMA((8,)),
         ],
         mib=24,
         work=(BUSY, 7 << 20),

time: 106 us -> 106 us (level)
  local copies, waits for them, and re-layouts: 1.08 us -> 3.27 us
  blocking collectives: 23.7 us -> 21.8 us
    ppermute x6, waiting for transfers between devices: 23.6 us -> 21 us  [shift(): return lax.ppermute(value, 'z', [(i, (i + by) % 4) for i in range(4)])]
    unnamed x10 -> x14, local copies, waits for them, and re-layouts: 0.99 us -> 3.19 us
    all_to_all x1, waiting for transfers between devices: 4.25 us -> 6.34 us  [local(): lax.all_to_all(at.reshape(2048, 128), ROWS + ('z',), 0, 0, tiled=True)]
    all_to_all x1, blocking collectives: 23.7 us -> 21.8 us  [local(): back = lax.all_to_all(total, ROWS, 0, 0, tiled=True)]
    pallas_call x7 -> x8, Pallas kernels: 16.8 us -> 17 us  [call(): pl.pallas_call(kernel, out_shape=outs, in_specs=in_specs, out_specs=space...]
  transfers between devices with their start and end apart: 13 -> 13, of which waited for: 7 -> 7; matrix products, arithmetic and copies ran while one was open for 1% -> 1% of each run, Pallas kernels for 14% -> 15%
where the time goes in v7:
time: 106 us; the launch traced here: 105 us
  starting transfers between devices  32.4 us (31%)
  waiting for transfers between devices  30 us (28%)
  blocking collectives  21.8 us (21%)
  Pallas kernels  17 us (16%)
  local copies, waits for them, and re-layouts  3.27 us (3%)
    all_to_all x1, blocking collectives, local(): back = lax.all_to_all(total, ROWS, 0, 0, tiled=True)  21.8 us
    ppermute x6, waiting for transfers between devices, shift(): return lax.ppermute(value, 'z', [(i, (i + by) % 4) for i in range(4)])  21 us
    pallas_call x8, Pallas kernels, call(): pl.pallas_call(kernel, out_shape=outs, in_specs=in_specs, out_specs=space...  17 us
    all_to_all x1, starting transfers between devices, local(): lax.all_to_all(at.reshape(2048, 128), ROWS + ('z',), 0, 0, tiled=True)  14.1 us
    ppermute x6, starting transfers between devices, shift(): return lax.ppermute(value, 'z', [(i, (i + by) % 4) for i in range(4)])  11.7 us
    all_to_all x1, waiting for transfers between devices, local(): lax.all_to_all(at.reshape(2048, 128), ROWS + ('z',), 0, 0, tiled=True)  6.34 us
    ppermute x1, starting transfers between devices, local(): up = lax.ppermute(up, ('z', 'c'), [(0, 2), (1, 3), (2, 4), (3, 5), (4, 6)])  4.55 us
    unnamed x14, local copies, waits for them, and re-layouts  3.19 us
  transfers between devices with their start and end apart: 13, of which 7 were waited for; matrix products, arithmetic and copies ran while one was open for 1% of the time, Pallas kernels for 15%

profile of v7, /device:TPU:32, one launch (start us, length us, event | category | flops | bytes accessed | tf_op | source)
XLA Modules:
  0.0 105.1 jit_solution(7346740682383667108)
XLA Ops:
  0.0 2.0 %collective-permute-start.1 = (f32[128,512]{1,0:T(8,128)}, f32[128,512]{1,0:T(8,128)S(1)}, u32[]{:S(2)}, u32[]{:S(2)}) collective-permute-start(f32[128,512]{1,0:T(8,128)} %c_ref.1), channel_id=1, source_target_pairs={{0,2},{2,4},{4,6},{6,0},{1,3},{3,5},{5,7},{7,1},{8,10},{10,12},{12... | collective-permute-start | bytes 786440 | tf_op jit(solution)/shard_map/ppermute | solution.py:181
  2.0 2.2 %collective-permute-start.2 = (f32[128,512]{1,0:T(8,128)}, f32[128,512]{1,0:T(8,128)}, u32[]{:S(2)}, u32[]{:S(2)}) collective-permute-start(f32[128,512]{1,0:T(8,128)} %c_ref.1), channel_id=1, source_target_pairs={{0,4},{2,6},{4,0},{6,2},{1,5},{3,7},{5,1},{7,3},{8,12},{10,14},{12... | collective-permute-start | bytes 786440 | tf_op jit(solution)/shard_map/ppermute | solution.py:181
  4.2 1.2 %collective-permute-start.3 = (f32[128,512]{1,0:T(8,128)}, f32[128,512]{1,0:T(8,128)}, u32[]{:S(2)}, u32[]{:S(2)}) collective-permute-start(f32[128,512]{1,0:T(8,128)} %c_ref.1), channel_id=1, source_target_pairs={{0,6},{2,0},{4,2},{6,4},{1,7},{3,1},{5,3},{7,5},{8,14},{10,8},{12,... | collective-permute-start | bytes 786440 | tf_op jit(solution)/shard_map/ppermute | solution.py:181
  5.4 1.0 copy-done.3
  6.4 1.1 %turn_kernel.1 = f32[32,4,16,128]{3,2,1,0:T(8,128)} custom-call(f32[128,512]{1,0:T(8,128)S(1)} %copy-done.3), custom_call_target="tpu_custom_call" | custom-call | bytes 1048576 | tf_op jit(solution)/shard_map/turn_kernel/pallas_call | solution.py:199
  7.5 14.1 %all-to-all-start = ((f32[128,16,128]{2,1,0:T(8,128)}), f32[128,16,128]{2,1,0:T(8,128)S(1)}, u32[]{:S(2)}, u32[]{:S(2)}) async-start(f32[128,16,128]{2,1,0:T(8,128)} %bitcast.4), calls=%async_computation | async-start | bytes 2097152 | tf_op jit(solution)/shard_map/all_to_all | solution.py:217
  21.8 0.1 add.55
  21.8 0.1 select_reduce_fusion
  21.9 0.1 convert_reduce_fusion.owners
  22.1 0.1 compare_select_fusion.6
  22.2 3.6 %blocks_kernel.1.blocks.source = bf16[64,128,256]{2,1,0:T(8,128)(2,1)S(1)} custom-call(f32[32,128,128]{2,1,0:T(8,128)S(1)} %copy-done.2, f32[32,128,128]{2,1,0:T(8,128)} %collective-permute-done.4.h1), custom_call_target="tpu_custom_call" | custom-call | bytes 8388608 | tf_op jit(solution)/shard_map/blocks_kernel/pallas_call | solution.py:199
  25.8 4.9 %collective-permute-done.2.w2 = f32[128,512]{1,0:T(8,128)} collective-permute-done((f32[128,512]{1,0:T(8,128)}, f32[128,512]{1,0:T(8,128)}, u32[]{:S(2)}, u32[]{:S(2)}) %collective-permute-start.2) | collective-permute-done | bytes 262176 | tf_op jit(solution)/shard_map/ppermute | solution.py:181
  30.8 3.8 %collective-permute-done.3.w3 = f32[128,512]{1,0:T(8,128)} collective-permute-done((f32[128,512]{1,0:T(8,128)}, f32[128,512]{1,0:T(8,128)}, u32[]{:S(2)}, u32[]{:S(2)}) %collective-permute-start.3) | collective-permute-done | bytes 262176 | tf_op jit(solution)/shard_map/ppermute | solution.py:181
  34.6 5.6 %beta_kernel.1 = (f32[16,128,128]{2,1,0:T(8,128)S(1)}, f32[16,128,128]{2,1,0:T(8,128)S(1)}) custom-call(s32[4]{0:T(128)S(1)} %pad_add_fusion.where, s32[64]{0:T(128)S(1)} %get-tuple-element.32.cols, s32[64]{0:T(128)S(1)} %get-tuple-element.31.slots, f32[128,512]{1,0:T(8,128)S(1)} %copy-done.4, f32[128,512]{1,0:T(8,128)S(1)} %collective-permute-done.1.w1, ...), custom_call_target="tpu_custom_call" | custom-call | flops 40000000000 | bytes 7340032 | tf_op jit(solution)/shard_map/beta_kernel/pallas_call | solution.py:199
  40.3 0.1 collective-permute-start.5
  40.4 2.6 %collective-permute-done.5.got_ref = f32[16,128,128]{2,1,0:T(8,128)S(1)} collective-permute-done((f32[16,128,128]{2,1,0:T(8,128)S(1)}, f32[16,128,128]{2,1,0:T(8,128)S(1)}, u32[]{:S(2)}, u32[]{:S(2)}) %collective-permute-start.5) | collective-permute-done | bytes 1048608 | tf_op jit(solution)/shard_map/ppermute | solution.py:177
  43.0 0.2 cores_kernel.1
  43.2 1.3 %collective-permute-start.6 = (f32[4,128,128]{2,1,0:T(8,128)S(1)}, f32[4,128,128]{2,1,0:T(8,128)S(1)}, u32[]{:S(2)}, u32[]{:S(2)}) collective-permute-start(f32[4,128,128]{2,1,0:T(8,128)S(1)} %get-tuple-element.21), channel_id=1, source_target_pairs={{3,1},{4,2},{5,3},{6,4},{7,5},{11,9},{12,10},{13,11},{14,12},{15,1... | collective-permute-start | bytes 786440 | tf_op jit(solution)/shard_map/ppermute | solution.py:249
  44.5 4.6 %collective-permute-start.7 = (f32[4,128,128]{2,1,0:T(8,128)S(1)}, f32[4,128,128]{2,1,0:T(8,128)S(1)}, u32[]{:S(2)}, u32[]{:S(2)}) collective-permute-start(f32[4,128,128]{2,1,0:T(8,128)S(1)} %get-tuple-element.22), channel_id=1, source_target_pairs={{0,2},{1,3},{2,4},{3,5},{4,6},{8,10},{9,11},{10,12},{11,13},{12,14... | collective-permute-start | bytes 786440 | tf_op jit(solution)/shard_map/ppermute | solution.py:250
  49.0 0.7 collective-permute-start.8
  49.7 6.3 %all-to-all-done = f32[128,16,128]{2,1,0:T(8,128)S(1)} async-done(((f32[128,16,128]{2,1,0:T(8,128)}), f32[128,16,128]{2,1,0:T(8,128)S(1)}, u32[]{:S(2)}, u32[]{:S(2)}) %all-to-all-start) | async-done | bytes 1048608 | tf_op jit(solution)/shard_map/all_to_all | solution.py:217
  56.1 2.2 %copy-done.1 = bf16[64,128,256]{2,1,0:T(8,128)(2,1)S(1)} copy-done((bf16[64,128,256]{2,1,0:T(8,128)(2,1)S(1)}, bf16[64,128,256]{2,1,0:T(8,128)(2,1)}, u32[]{:S(2)}) %copy-start.1) | copy-done | bytes 4194328
  58.2 5.0 %alpha_kernel.1 = (f32[20,16,128]{2,1,0:T(8,128)S(1)}, f32[20,16,128]{2,1,0:T(8,128)S(1)}, f32[20,16,128]{2,1,0:T(8,128)S(1)}, f32[20,16,128]{2,1,0:T(8,128)S(1)}) custom-call(s32[4]{0:T(128)S(1)} %pad_add_fusion.where, s32[64]{0:T(128)S(1)} %get-tuple-element.32.cols, s32[64]{0:T(128)S(1)} %convert_reduce_fusion.owners, f32[32,64,128]{2,1,0:T(8,128)S(1)} %bitcast.6, ...), custom_call_target="tpu_custom_call" | custom-call | flops 40000000000 | bytes 7340032 | tf_op jit(solution)/shard_map/alpha_kernel/pallas_call | solution.py:199
  63.3 3.6 %collective-permute-start.9 = (f32[20,16,128]{2,1,0:T(8,128)S(1)}, f32[20,16,128]{2,1,0:T(8,128)S(1)}, u32[]{:S(2)}, u32[]{:S(2)}) collective-permute-start(f32[20,16,128]{2,1,0:T(8,128)S(1)} %get-tuple-element.27), channel_id=1, source_target_pairs={{0,2},{2,4},{4,6},{6,0},{1,3},{3,5},{5,7},{7,1},{8,10},{10,12},{12... | collective-permute-start | bytes 491528 | tf_op jit(solution)/shard_map/ppermute | solution.py:181
  66.9 0.9 collective-permute-start.10
  67.8 1.8 %collective-permute-start.11 = (f32[20,16,128]{2,1,0:T(8,128)S(1)}, f32[20,16,128]{2,1,0:T(8,128)S(1)}, u32[]{:S(2)}, u32[]{:S(2)}) collective-permute-start(f32[20,16,128]{2,1,0:T(8,128)S(1)} %get-tuple-element.29), channel_id=1, source_target_pairs={{0,6},{2,0},{4,2},{6,4},{1,7},{3,1},{5,3},{7,5},{8,14},{10,8},{12,... | collective-permute-start | bytes 491528 | tf_op jit(solution)/shard_map/ppermute | solution.py:181
  69.7 8.8 %collective-permute-done.9.p1 = f32[20,16,128]{2,1,0:T(8,128)S(1)} collective-permute-done((f32[20,16,128]{2,1,0:T(8,128)S(1)}, f32[20,16,128]{2,1,0:T(8,128)S(1)}, u32[]{:S(2)}, u32[]{:S(2)}) %collective-permute-start.9) | collective-permute-done | bytes 163872 | tf_op jit(solution)/shard_map/ppermute | solution.py:181
  78.5 2.6 %collective-permute-done.10.p2 = f32[20,16,128]{2,1,0:T(8,128)S(1)} collective-permute-done((f32[20,16,128]{2,1,0:T(8,128)S(1)}, f32[20,16,128]{2,1,0:T(8,128)S(1)}, u32[]{:S(2)}, u32[]{:S(2)}) %collective-permute-start.10) | collective-permute-done | bytes 163872 | tf_op jit(solution)/shard_map/ppermute | solution.py:181
  81.1 0.8 collective-permute-done.11.p3
  81.9 0.6 strings_kernel.1
  82.5 21.8 %all_to_all.14.back_ref = f32[32,16,128]{2,1,0:T(8,128)S(1)} all-to-all(f32[32,16,128]{2,1,0:T(8,128)S(1)} %strings_kernel.1), channel_id=1, replica_groups=mesh['y'=4,'h'=2,'x'=4,'z'=4,'c'=2] {'y','h','x'}, dimensions={0} | all-to-all | bytes 524288 | tf_op jit(solution)/shard_map/all_to_all | solution.py:275
  104.3 0.8 final_kernel.1
  (24 shorter events, 0.3 us)
Async XLA Ops:
  0.0 22.2 %copy-start.2 = (f32[32,128,128]{2,1,0:T(8,128)S(1)}, f32[32,128,128]{2,1,0:T(8,128)}, u32[]{:S(2)}) copy-start(f32[32,128,128]{2,1,0:T(8,128)} %h0.1) | copy-start | bytes 6291460
  0.0 22.2 %collective-permute-start.4 = (f32[32,128,128]{2,1,0:T(8,128)}, f32[32,128,128]{2,1,0:T(8,128)}, u32[]{:S(2)}, u32[]{:S(2)}) collective-permute-start(f32[32,128,128]{2,1,0:T(8,128)} %h0.1), channel_id=1, source_target_pairs={{0,1},{1,0},{2,3},{3,2},{4,5},{5,4},{6,7},{7,6},{8,9},{9,8},{10,11... | collective-permute-start | bytes 6291464 | tf_op jit(solution)/shard_map/ppermute | solution.py:177
  0.0 25.8 %collective-permute-start.1 = (f32[128,512]{1,0:T(8,128)}, f32[128,512]{1,0:T(8,128)S(1)}, u32[]{:S(2)}, u32[]{:S(2)}) collective-permute-start(f32[128,512]{1,0:T(8,128)} %c_ref.1), channel_id=1, source_target_pairs={{0,2},{2,4},{4,6},{6,0},{1,3},{3,5},{5,7},{7,1},{8,10},{10,12},{12... | collective-permute-start | bytes 786440 | tf_op jit(solution)/shard_map/ppermute | solution.py:181
  2.0 28.8 %collective-permute-start.2 = (f32[128,512]{1,0:T(8,128)}, f32[128,512]{1,0:T(8,128)}, u32[]{:S(2)}, u32[]{:S(2)}) collective-permute-start(f32[128,512]{1,0:T(8,128)} %c_ref.1), channel_id=1, source_target_pairs={{0,4},{2,6},{4,0},{6,2},{1,5},{3,7},{5,1},{7,3},{8,12},{10,14},{12... | collective-permute-start | bytes 786440 | tf_op jit(solution)/shard_map/ppermute | solution.py:181
  4.2 30.4 %collective-permute-start.3 = (f32[128,512]{1,0:T(8,128)}, f32[128,512]{1,0:T(8,128)}, u32[]{:S(2)}, u32[]{:S(2)}) collective-permute-start(f32[128,512]{1,0:T(8,128)} %c_ref.1), channel_id=1, source_target_pairs={{0,6},{2,0},{4,2},{6,4},{1,7},{3,1},{5,3},{7,5},{8,14},{10,8},{12,... | collective-permute-start | bytes 786440 | tf_op jit(solution)/shard_map/ppermute | solution.py:181
  5.4 16.7 %collective-permute-start = (s32[32]{0:T(128)}, s32[32]{0:T(128)S(1)}, u32[]{:S(2)}, u32[]{:S(2)}) collective-permute-start(s32[32]{0:T(128)} %param.7), channel_id=1, source_target_pairs={{0,1},{1,0},{2,3},{3,2},{4,5},{5,4},{6,7},{7,6},{8,9},{9,8},{10,11... | collective-permute-start | bytes 392 | tf_op jit(solution)/shard_map/ppermute | solution.py:177
  5.4 1.0 copy-start.3
  6.4 15.5 %copy-start.6 = (s32[32]{0:T(128)S(1)}, s32[32]{0:T(128)}, u32[]{:S(2)}) copy-start(s32[32]{0:T(128)} %param.6) | copy-start | bytes 388
  6.4 15.7 %copy-start.5 = (s32[32]{0:T(128)S(1)}, s32[32]{0:T(128)}, u32[]{:S(2)}) copy-start(s32[32]{0:T(128)} %param.7) | copy-start | bytes 388
  7.5 48.6 %all-to-all-start = ((f32[128,16,128]{2,1,0:T(8,128)}), f32[128,16,128]{2,1,0:T(8,128)S(1)}, u32[]{:S(2)}, u32[]{:S(2)}) async-start(f32[128,16,128]{2,1,0:T(8,128)} %bitcast.4), calls=%async_computation | async-start | bytes 2097152 | tf_op jit(solution)/shard_map/all_to_all | solution.py:217
  22.2 12.4 %copy-start.4 = (f32[128,512]{1,0:T(8,128)S(1)}, f32[128,512]{1,0:T(8,128)}, u32[]{:S(2)}) copy-start(f32[128,512]{1,0:T(8,128)} %c_ref.1) | copy-start | bytes 786436
  25.8 14.4 %copy-start = (bf16[64,128,256]{2,1,0:T(8,128)(2,1)}, bf16[64,128,256]{2,1,0:T(8,128)(2,1)S(1)}, u32[]{:S(2)}) copy-start(bf16[64,128,256]{2,1,0:T(8,128)(2,1)S(1)} %blocks_kernel.1.blocks.source) | copy-start | bytes 12582916
  40.3 2.7 %collective-permute-start.5 = (f32[16,128,128]{2,1,0:T(8,128)S(1)}, f32[16,128,128]{2,1,0:T(8,128)S(1)}, u32[]{:S(2)}, u32[]{:S(2)}) collective-permute-start(f32[16,128,128]{2,1,0:T(8,128)S(1)} %get-tuple-element.19), channel_id=1, source_target_pairs={{0,1},{1,0},{2,3},{3,2},{4,5},{5,4},{6,7},{7,6},{8,9},{9,8},{10,11... | collective-permute-start | bytes 3145736 | tf_op jit(solution)/shard_map/ppermute | solution.py:177
  43.2 24.6 %collective-permute-start.6 = (f32[4,128,128]{2,1,0:T(8,128)S(1)}, f32[4,128,128]{2,1,0:T(8,128)S(1)}, u32[]{:S(2)}, u32[]{:S(2)}) collective-permute-start(f32[4,128,128]{2,1,0:T(8,128)S(1)} %get-tuple-element.21), channel_id=1, source_target_pairs={{3,1},{4,2},{5,3},{6,4},{7,5},{11,9},{12,10},{13,11},{14,12},{15,1... | collective-permute-start | bytes 786440 | tf_op jit(solution)/shard_map/ppermute | solution.py:249
  44.5 25.1 %collective-permute-start.7 = (f32[4,128,128]{2,1,0:T(8,128)S(1)}, f32[4,128,128]{2,1,0:T(8,128)S(1)}, u32[]{:S(2)}, u32[]{:S(2)}) collective-permute-start(f32[4,128,128]{2,1,0:T(8,128)S(1)} %get-tuple-element.22), channel_id=1, source_target_pairs={{0,2},{1,3},{2,4},{3,5},{4,6},{8,10},{9,11},{10,12},{11,13},{12,14... | collective-permute-start | bytes 786440 | tf_op jit(solution)/shard_map/ppermute | solution.py:250
  49.0 20.6 %collective-permute-start.8 = (f32[4,128,128]{2,1,0:T(8,128)S(1)}, f32[4,128,128]{2,1,0:T(8,128)S(1)}, u32[]{:S(2)}, u32[]{:S(2)}) collective-permute-start(f32[4,128,128]{2,1,0:T(8,128)S(1)} %get-tuple-element.23), channel_id=1, source_target_pairs={{0,4},{7,3},{8,12},{15,11},{16,20},{23,19},{24,28},{31,27},{32,36}... | collective-permute-start | bytes 786440 | tf_op jit(solution)/shard_map/ppermute | solution.py:251
  56.1 2.2 %copy-start.1 = (bf16[64,128,256]{2,1,0:T(8,128)(2,1)S(1)}, bf16[64,128,256]{2,1,0:T(8,128)(2,1)}, u32[]{:S(2)}) copy-start(bf16[64,128,256]{2,1,0:T(8,128)(2,1)} %copy-done) | copy-start | bytes 12582916
  63.3 15.2 %collective-permute-start.9 = (f32[20,16,128]{2,1,0:T(8,128)S(1)}, f32[20,16,128]{2,1,0:T(8,128)S(1)}, u32[]{:S(2)}, u32[]{:S(2)}) collective-permute-start(f32[20,16,128]{2,1,0:T(8,128)S(1)} %get-tuple-element.27), channel_id=1, source_target_pairs={{0,2},{2,4},{4,6},{6,0},{1,3},{3,5},{5,7},{7,1},{8,10},{10,12},{12... | collective-permute-start | bytes 491528 | tf_op jit(solution)/shard_map/ppermute | solution.py:181
  66.9 14.2 %collective-permute-start.10 = (f32[20,16,128]{2,1,0:T(8,128)S(1)}, f32[20,16,128]{2,1,0:T(8,128)S(1)}, u32[]{:S(2)}, u32[]{:S(2)}) collective-permute-start(f32[20,16,128]{2,1,0:T(8,128)S(1)} %get-tuple-element.28), channel_id=1, source_target_pairs={{0,4},{2,6},{4,0},{6,2},{1,5},{3,7},{5,1},{7,3},{8,12},{10,14},{12... | collective-permute-start | bytes 491528 | tf_op jit(solution)/shard_map/ppermute | solution.py:181
  67.8 14.0 %collective-permute-start.11 = (f32[20,16,128]{2,1,0:T(8,128)S(1)}, f32[20,16,128]{2,1,0:T(8,128)S(1)}, u32[]{:S(2)}, u32[]{:S(2)}) collective-permute-start(f32[20,16,128]{2,1,0:T(8,128)S(1)} %get-tuple-element.29), channel_id=1, source_target_pairs={{0,6},{2,0},{4,2},{6,4},{1,7},{3,1},{5,3},{7,5},{8,14},{10,8},{12,... | collective-permute-start | bytes 491528 | tf_op jit(solution)/shard_map/ppermute | solution.py:181

commit v8 on v7

--- a/solution.py
+++ b/solution.py
@@ -29,9 +29,16 @@
     return jax.ShapeDtypeStruct(dims, kind)
 
 
-def turn_kernel(c_ref, at_ref):
+def turn_kernel(c_ref, at_ref, buf, sem):
+    loads = []
     for t in range(4):
-        turned = jnp.transpose(c_ref[:, 128 * t : 128 * (t + 1)]).reshape(8, 16, 128)
+        span = pl.ds(128 * t, 128)
+        loads.append(pltpu.make_async_copy(c_ref.at[:, span], buf.at[t], sem.at[t]))
+    for load in loads:
+        load.start()
+    for t, load in enumerate(loads):
+        load.wait()
+        turned = jnp.transpose(buf[t]).reshape(8, 16, 128)
         for plane in range(4):
             at_ref[8 * t : 8 * (t + 1), plane] = turned
 
@@ -213,7 +220,13 @@
     where = jnp.stack([z, z, z, c]).astype(jnp.int32)
     rows = [coeffs] + [shift(coeffs, k) for k in (1, 2, 3)]
     cols, owners, slots = tables(hcount, hcols, z, c)
-    at = call(turn_kernel, shape(32, 4, 16, 128), [VMEM], coeffs)
+    at = call(
+        turn_kernel,
+        shape(32, 4, 16, 128),
+        [HBM],
+        pltpu.with_memory_space_constraint(coeffs, pltpu.HBM),
+        scratch=[pltpu.VMEM((4, 128, 128), F32), pltpu.SemaphoreType.DMA((4,))],
+    )
     moved = lax.all_to_all(at.reshape(2048, 128), ROWS + ("z",), 0, 0, tiled=True)
 
     blocks = call(
@@ -260,7 +273,8 @@
         alpha_kernel,
         (shape(20, 16, 128),) * 4,
         [SMEM] * 3 + [VMEM, HBM, VMEM],
-        where, cols, owners, moved.reshape(32, 64, 128), blocks, token,
+        where, cols, owners, moved.reshape(32, 64, 128),
+        pltpu.with_memory_space_constraint(blocks, pltpu.HBM), token,
         scratch=[
             pltpu.VMEM((32, 64, 128), F32),
             pltpu.VMEM((32, 128, 128), BF16),

time: 106 us -> 106 us (level)
  local copies, waits for them, and re-layouts: 3.27 us -> 0.11 us
  blocking collectives: 21.8 us -> 23.7 us
  Pallas kernels: 17 us -> 18.7 us
    unnamed x14 -> x10, local copies, waits for them, and re-layouts: 3.19 us -> 0.02 us
    all_to_all x1, blocking collectives: 21.8 us -> 23.7 us  [local(): back = lax.all_to_all(total, ROWS, 0, 0, tiled=True)]
    pallas_call x8, Pallas kernels: 17 us -> 18.7 us  [call(): pl.pallas_call(kernel, out_shape=outs, in_specs=in_specs, out_specs=space...]
  transfers between devices with their start and end apart: 13 -> 13, of which waited for: 7 -> 7; matrix products, arithmetic and copies ran while one was open for 1% -> 1% of each run, Pallas kernels for 15% -> 16%
where the time goes in v8:
time: 106 us; the launch traced here: 105 us
  starting transfers between devices  32.5 us (31%)
  waiting for transfers between devices  29.6 us (28%)
  blocking collectives  23.7 us (22%)
  Pallas kernels  18.7 us (18%)
    all_to_all x1, blocking collectives, local(): back = lax.all_to_all(total, ROWS, 0, 0, tiled=True)  23.7 us
    ppermute x6, waiting for transfers between devices, shift(): return lax.ppermute(value, 'z', [(i, (i + by) % 4) for i in range(4)])  20.2 us
    pallas_call x8, Pallas kernels, call(): pl.pallas_call(kernel, out_shape=outs, in_specs=in_specs, out_specs=space...  18.7 us
    all_to_all x1, starting transfers between devices, local(): lax.all_to_all(at.reshape(2048, 128), ROWS + ('z',), 0, 0, tiled=True)  14.1 us
    ppermute x6, starting transfers between devices, shift(): return lax.ppermute(value, 'z', [(i, (i + by) % 4) for i in range(4)])  11.7 us
    all_to_all x1, waiting for transfers between devices, local(): lax.all_to_all(at.reshape(2048, 128), ROWS + ('z',), 0, 0, tiled=True)  6.7 us
    ppermute x1, starting transfers between devices, local(): up = lax.ppermute(up, ('z', 'c'), [(0, 2), (1, 3), (2, 4), (3, 5), (4, 6)])  4.55 us
    ppermute x3, waiting for transfers between devices, swap(): return lax.ppermute(value, 'c', [(0, 1), (1, 0)])  2.65 us
  transfers between devices with their start and end apart: 13, of which 7 were waited for; matrix products, arithmetic and copies ran while one was open for 1% of the time, Pallas kernels for 16%

profile of v8, /device:TPU:32, one launch (start us, length us, event | category | flops | bytes accessed | tf_op | source)
XLA Modules:
  0.0 105.2 jit_solution(15786021965728502264)
XLA Ops:
  0.0 0.1 collective-permute-start.4
  0.1 2.0 %collective-permute-start.1 = (f32[128,512]{1,0:T(8,128)}, f32[128,512]{1,0:T(8,128)S(1)}, u32[]{:S(2)}, u32[]{:S(2)}) collective-permute-start(f32[128,512]{1,0:T(8,128)} %c_ref.1), channel_id=1, source_target_pairs={{0,2},{2,4},{4,6},{6,0},{1,3},{3,5},{5,7},{7,1},{8,10},{10,12},{12... | collective-permute-start | bytes 786440 | tf_op jit(solution)/shard_map/ppermute | solution.py:188
  2.1 2.2 %collective-permute-start.2 = (f32[128,512]{1,0:T(8,128)}, f32[128,512]{1,0:T(8,128)}, u32[]{:S(2)}, u32[]{:S(2)}) collective-permute-start(f32[128,512]{1,0:T(8,128)} %c_ref.1), channel_id=1, source_target_pairs={{0,4},{2,6},{4,0},{6,2},{1,5},{3,7},{5,1},{7,3},{8,12},{10,14},{12... | collective-permute-start | bytes 786440 | tf_op jit(solution)/shard_map/ppermute | solution.py:188
  4.3 1.2 %collective-permute-start.3 = (f32[128,512]{1,0:T(8,128)}, f32[128,512]{1,0:T(8,128)}, u32[]{:S(2)}, u32[]{:S(2)}) collective-permute-start(f32[128,512]{1,0:T(8,128)} %c_ref.1), channel_id=1, source_target_pairs={{0,6},{2,0},{4,2},{6,4},{1,7},{3,1},{5,3},{7,5},{8,14},{10,8},{12,... | collective-permute-start | bytes 786440 | tf_op jit(solution)/shard_map/ppermute | solution.py:188
  5.5 2.3 %turn_kernel.1 = f32[32,4,16,128]{3,2,1,0:T(8,128)} custom-call(f32[128,512]{1,0:T(8,128)} %c_ref.1), custom_call_target="tpu_custom_call" | custom-call | bytes 1048576 | tf_op jit(solution)/shard_map/turn_kernel/pallas_call | solution.py:206
  7.8 14.1 %all-to-all-start = ((f32[128,16,128]{2,1,0:T(8,128)}), f32[128,16,128]{2,1,0:T(8,128)S(1)}, u32[]{:S(2)}, u32[]{:S(2)}) async-start(f32[128,16,128]{2,1,0:T(8,128)} %bitcast.4), calls=%async_computation | async-start | bytes 2097152 | tf_op jit(solution)/shard_map/all_to_all | solution.py:230
  22.1 0.1 add.55
  22.2 0.1 select_reduce_fusion
  22.2 0.1 convert_reduce_fusion.owners
  22.3 0.1 pad_add_fusion.where
  22.4 0.1 compare_select_fusion.6
  22.5 3.6 %blocks_kernel.1.blocks.source = bf16[64,128,256]{2,1,0:T(8,128)(2,1)S(1)} custom-call(f32[32,128,128]{2,1,0:T(8,128)S(1)} %copy-done.1, f32[32,128,128]{2,1,0:T(8,128)} %collective-permute-done.4.h1), custom_call_target="tpu_custom_call" | custom-call | bytes 8388608 | tf_op jit(solution)/shard_map/blocks_kernel/pallas_call | solution.py:206
  26.2 4.5 %collective-permute-done.2.w2 = f32[128,512]{1,0:T(8,128)} collective-permute-done((f32[128,512]{1,0:T(8,128)}, f32[128,512]{1,0:T(8,128)}, u32[]{:S(2)}, u32[]{:S(2)}) %collective-permute-start.2) | collective-permute-done | bytes 262176 | tf_op jit(solution)/shard_map/ppermute | solution.py:188
  30.7 3.5 %collective-permute-done.3.w3 = f32[128,512]{1,0:T(8,128)} collective-permute-done((f32[128,512]{1,0:T(8,128)}, f32[128,512]{1,0:T(8,128)}, u32[]{:S(2)}, u32[]{:S(2)}) %collective-permute-start.3) | collective-permute-done | bytes 262176 | tf_op jit(solution)/shard_map/ppermute | solution.py:188
  34.2 5.8 %beta_kernel.1 = (f32[16,128,128]{2,1,0:T(8,128)S(1)}, f32[16,128,128]{2,1,0:T(8,128)S(1)}) custom-call(s32[4]{0:T(128)S(1)} %pad_add_fusion.where, s32[64]{0:T(128)S(1)} %get-tuple-element.32.cols, s32[64]{0:T(128)S(1)} %get-tuple-element.31.slots, f32[128,512]{1,0:T(8,128)S(1)} %copy-done.2, f32[128,512]{1,0:T(8,128)S(1)} %collective-permute-done.1.w1, ...), custom_call_target="tpu_custom_call" | custom-call | flops 40000000000 | bytes 7340032 | tf_op jit(solution)/shard_map/beta_kernel/pallas_call | solution.py:206
  40.0 0.1 collective-permute-start.5
  40.1 2.6 %collective-permute-done.5.got_ref = f32[16,128,128]{2,1,0:T(8,128)S(1)} collective-permute-done((f32[16,128,128]{2,1,0:T(8,128)S(1)}, f32[16,128,128]{2,1,0:T(8,128)S(1)}, u32[]{:S(2)}, u32[]{:S(2)}) %collective-permute-start.5) | collective-permute-done | bytes 1048608 | tf_op jit(solution)/shard_map/ppermute | solution.py:184
  42.8 0.2 cores_kernel.1
  42.9 1.3 %collective-permute-start.6 = (f32[4,128,128]{2,1,0:T(8,128)S(1)}, f32[4,128,128]{2,1,0:T(8,128)S(1)}, u32[]{:S(2)}, u32[]{:S(2)}) collective-permute-start(f32[4,128,128]{2,1,0:T(8,128)S(1)} %get-tuple-element.21), channel_id=1, source_target_pairs={{3,1},{4,2},{5,3},{6,4},{7,5},{11,9},{12,10},{13,11},{14,12},{15,1... | collective-permute-start | bytes 786440 | tf_op jit(solution)/shard_map/ppermute | solution.py:262
  44.2 4.6 %collective-permute-start.7 = (f32[4,128,128]{2,1,0:T(8,128)S(1)}, f32[4,128,128]{2,1,0:T(8,128)S(1)}, u32[]{:S(2)}, u32[]{:S(2)}) collective-permute-start(f32[4,128,128]{2,1,0:T(8,128)S(1)} %get-tuple-element.22), channel_id=1, source_target_pairs={{0,2},{1,3},{2,4},{3,5},{4,6},{8,10},{9,11},{10,12},{11,13},{12,14... | collective-permute-start | bytes 786440 | tf_op jit(solution)/shard_map/ppermute | solution.py:263
  48.8 0.7 collective-permute-start.8
  49.5 6.7 %all-to-all-done = f32[128,16,128]{2,1,0:T(8,128)S(1)} async-done(((f32[128,16,128]{2,1,0:T(8,128)}), f32[128,16,128]{2,1,0:T(8,128)S(1)}, u32[]{:S(2)}, u32[]{:S(2)}) %all-to-all-start) | async-done | bytes 1048608 | tf_op jit(solution)/shard_map/all_to_all | solution.py:230
  56.2 5.3 %alpha_kernel.1 = (f32[20,16,128]{2,1,0:T(8,128)S(1)}, f32[20,16,128]{2,1,0:T(8,128)S(1)}, f32[20,16,128]{2,1,0:T(8,128)S(1)}, f32[20,16,128]{2,1,0:T(8,128)S(1)}) custom-call(s32[4]{0:T(128)S(1)} %pad_add_fusion.where, s32[64]{0:T(128)S(1)} %get-tuple-element.32.cols, s32[64]{0:T(128)S(1)} %convert_reduce_fusion.owners, f32[32,64,128]{2,1,0:T(8,128)S(1)} %bitcast.6, ...), custom_call_target="tpu_custom_call" | custom-call | flops 40000000000 | bytes 7340032 | tf_op jit(solution)/shard_map/alpha_kernel/pallas_call | solution.py:206
  61.5 3.7 %collective-permute-start.9 = (f32[20,16,128]{2,1,0:T(8,128)S(1)}, f32[20,16,128]{2,1,0:T(8,128)S(1)}, u32[]{:S(2)}, u32[]{:S(2)}) collective-permute-start(f32[20,16,128]{2,1,0:T(8,128)S(1)} %get-tuple-element.27), channel_id=1, source_target_pairs={{0,2},{2,4},{4,6},{6,0},{1,3},{3,5},{5,7},{7,1},{8,10},{10,12},{12... | collective-permute-start | bytes 491528 | tf_op jit(solution)/shard_map/ppermute | solution.py:188
  65.2 0.8 collective-permute-start.10
  66.0 1.8 %collective-permute-start.11 = (f32[20,16,128]{2,1,0:T(8,128)S(1)}, f32[20,16,128]{2,1,0:T(8,128)S(1)}, u32[]{:S(2)}, u32[]{:S(2)}) collective-permute-start(f32[20,16,128]{2,1,0:T(8,128)S(1)} %get-tuple-element.29), channel_id=1, source_target_pairs={{0,6},{2,0},{4,2},{6,4},{1,7},{3,1},{5,3},{7,5},{8,14},{10,8},{12,... | collective-permute-start | bytes 491528 | tf_op jit(solution)/shard_map/ppermute | solution.py:188
  67.9 9.0 %collective-permute-done.9.p1 = f32[20,16,128]{2,1,0:T(8,128)S(1)} collective-permute-done((f32[20,16,128]{2,1,0:T(8,128)S(1)}, f32[20,16,128]{2,1,0:T(8,128)S(1)}, u32[]{:S(2)}, u32[]{:S(2)}) %collective-permute-start.9) | collective-permute-done | bytes 163872 | tf_op jit(solution)/shard_map/ppermute | solution.py:188
  76.9 2.5 %collective-permute-done.10.p2 = f32[20,16,128]{2,1,0:T(8,128)S(1)} collective-permute-done((f32[20,16,128]{2,1,0:T(8,128)S(1)}, f32[20,16,128]{2,1,0:T(8,128)S(1)}, u32[]{:S(2)}, u32[]{:S(2)}) %collective-permute-start.10) | collective-permute-done | bytes 163872 | tf_op jit(solution)/shard_map/ppermute | solution.py:188
  79.3 0.8 collective-permute-done.11.p3
  80.1 0.6 strings_kernel.1
  80.7 23.7 %all_to_all.14.back_ref = f32[32,16,128]{2,1,0:T(8,128)S(1)} all-to-all(f32[32,16,128]{2,1,0:T(8,128)S(1)} %strings_kernel.1), channel_id=1, replica_groups=mesh['y'=4,'h'=2,'x'=4,'z'=4,'c'=2] {'y','h','x'}, dimensions={0} | all-to-all | bytes 524288 | tf_op jit(solution)/shard_map/all_to_all | solution.py:289
  104.4 0.8 final_kernel.1
  (20 shorter events, 0.2 us)
Async XLA Ops:
  0.0 22.5 %copy-start.1 = (f32[32,128,128]{2,1,0:T(8,128)S(1)}, f32[32,128,128]{2,1,0:T(8,128)}, u32[]{:S(2)}) copy-start(f32[32,128,128]{2,1,0:T(8,128)} %h0.1) | copy-start | bytes 6291460
  0.0 22.4 %copy-start.3 = (s32[32]{0:T(128)S(1)}, s32[32]{0:T(128)}, u32[]{:S(2)}) copy-start(s32[32]{0:T(128)} %param.7) | copy-start | bytes 388
  0.0 22.1 %copy-start.4 = (s32[32]{0:T(128)S(1)}, s32[32]{0:T(128)}, u32[]{:S(2)}) copy-start(s32[32]{0:T(128)} %param.6) | copy-start | bytes 388
  0.0 22.5 %collective-permute-start.4 = (f32[32,128,128]{2,1,0:T(8,128)}, f32[32,128,128]{2,1,0:T(8,128)}, u32[]{:S(2)}, u32[]{:S(2)}) collective-permute-start(f32[32,128,128]{2,1,0:T(8,128)} %h0.1), channel_id=1, source_target_pairs={{0,1},{1,0},{2,3},{3,2},{4,5},{5,4},{6,7},{7,6},{8,9},{9,8},{10,11... | collective-permute-start | bytes 6291464 | tf_op jit(solution)/shard_map/ppermute | solution.py:184
  0.1 26.0 %collective-permute-start.1 = (f32[128,512]{1,0:T(8,128)}, f32[128,512]{1,0:T(8,128)S(1)}, u32[]{:S(2)}, u32[]{:S(2)}) collective-permute-start(f32[128,512]{1,0:T(8,128)} %c_ref.1), channel_id=1, source_target_pairs={{0,2},{2,4},{4,6},{6,0},{1,3},{3,5},{5,7},{7,1},{8,10},{10,12},{12... | collective-permute-start | bytes 786440 | tf_op jit(solution)/shard_map/ppermute | solution.py:188
  2.1 28.6 %collective-permute-start.2 = (f32[128,512]{1,0:T(8,128)}, f32[128,512]{1,0:T(8,128)}, u32[]{:S(2)}, u32[]{:S(2)}) collective-permute-start(f32[128,512]{1,0:T(8,128)} %c_ref.1), channel_id=1, source_target_pairs={{0,4},{2,6},{4,0},{6,2},{1,5},{3,7},{5,1},{7,3},{8,12},{10,14},{12... | collective-permute-start | bytes 786440 | tf_op jit(solution)/shard_map/ppermute | solution.py:188
  4.3 29.9 %collective-permute-start.3 = (f32[128,512]{1,0:T(8,128)}, f32[128,512]{1,0:T(8,128)}, u32[]{:S(2)}, u32[]{:S(2)}) collective-permute-start(f32[128,512]{1,0:T(8,128)} %c_ref.1), channel_id=1, source_target_pairs={{0,6},{2,0},{4,2},{6,4},{1,7},{3,1},{5,3},{7,5},{8,14},{10,8},{12,... | collective-permute-start | bytes 786440 | tf_op jit(solution)/shard_map/ppermute | solution.py:188
  5.5 16.9 %collective-permute-start = (s32[32]{0:T(128)}, s32[32]{0:T(128)S(1)}, u32[]{:S(2)}, u32[]{:S(2)}) collective-permute-start(s32[32]{0:T(128)} %param.7), channel_id=1, source_target_pairs={{0,1},{1,0},{2,3},{3,2},{4,5},{5,4},{6,7},{7,6},{8,9},{9,8},{10,11... | collective-permute-start | bytes 392 | tf_op jit(solution)/shard_map/ppermute | solution.py:184
  7.8 48.4 %all-to-all-start = ((f32[128,16,128]{2,1,0:T(8,128)}), f32[128,16,128]{2,1,0:T(8,128)S(1)}, u32[]{:S(2)}, u32[]{:S(2)}) async-start(f32[128,16,128]{2,1,0:T(8,128)} %bitcast.4), calls=%async_computation | async-start | bytes 2097152 | tf_op jit(solution)/shard_map/all_to_all | solution.py:230
  22.5 11.7 %copy-start.2 = (f32[128,512]{1,0:T(8,128)S(1)}, f32[128,512]{1,0:T(8,128)}, u32[]{:S(2)}) copy-start(f32[128,512]{1,0:T(8,128)} %c_ref.1) | copy-start | bytes 786436
  26.1 13.9 %copy-start = (bf16[64,128,256]{2,1,0:T(8,128)(2,1)}, bf16[64,128,256]{2,1,0:T(8,128)(2,1)S(1)}, u32[]{:S(2)}) copy-start(bf16[64,128,256]{2,1,0:T(8,128)(2,1)S(1)} %blocks_kernel.1.blocks.source) | copy-start | bytes 12582916
  40.0 2.7 %collective-permute-start.5 = (f32[16,128,128]{2,1,0:T(8,128)S(1)}, f32[16,128,128]{2,1,0:T(8,128)S(1)}, u32[]{:S(2)}, u32[]{:S(2)}) collective-permute-start(f32[16,128,128]{2,1,0:T(8,128)S(1)} %get-tuple-element.19), channel_id=1, source_target_pairs={{0,1},{1,0},{2,3},{3,2},{4,5},{5,4},{6,7},{7,6},{8,9},{9,8},{10,11... | collective-permute-start | bytes 3145736 | tf_op jit(solution)/shard_map/ppermute | solution.py:184
  42.9 23.1 %collective-permute-start.6 = (f32[4,128,128]{2,1,0:T(8,128)S(1)}, f32[4,128,128]{2,1,0:T(8,128)S(1)}, u32[]{:S(2)}, u32[]{:S(2)}) collective-permute-start(f32[4,128,128]{2,1,0:T(8,128)S(1)} %get-tuple-element.21), channel_id=1, source_target_pairs={{3,1},{4,2},{5,3},{6,4},{7,5},{11,9},{12,10},{13,11},{14,12},{15,1... | collective-permute-start | bytes 786440 | tf_op jit(solution)/shard_map/ppermute | solution.py:262
  44.2 23.6 %collective-permute-start.7 = (f32[4,128,128]{2,1,0:T(8,128)S(1)}, f32[4,128,128]{2,1,0:T(8,128)S(1)}, u32[]{:S(2)}, u32[]{:S(2)}) collective-permute-start(f32[4,128,128]{2,1,0:T(8,128)S(1)} %get-tuple-element.22), channel_id=1, source_target_pairs={{0,2},{1,3},{2,4},{3,5},{4,6},{8,10},{9,11},{10,12},{11,13},{12,14... | collective-permute-start | bytes 786440 | tf_op jit(solution)/shard_map/ppermute | solution.py:263
  48.8 19.0 %collective-permute-start.8 = (f32[4,128,128]{2,1,0:T(8,128)S(1)}, f32[4,128,128]{2,1,0:T(8,128)S(1)}, u32[]{:S(2)}, u32[]{:S(2)}) collective-permute-start(f32[4,128,128]{2,1,0:T(8,128)S(1)} %get-tuple-element.23), channel_id=1, source_target_pairs={{0,4},{7,3},{8,12},{15,11},{16,20},{23,19},{24,28},{31,27},{32,36}... | collective-permute-start | bytes 786440 | tf_op jit(solution)/shard_map/ppermute | solution.py:264
  61.5 15.4 %collective-permute-start.9 = (f32[20,16,128]{2,1,0:T(8,128)S(1)}, f32[20,16,128]{2,1,0:T(8,128)S(1)}, u32[]{:S(2)}, u32[]{:S(2)}) collective-permute-start(f32[20,16,128]{2,1,0:T(8,128)S(1)} %get-tuple-element.27), channel_id=1, source_target_pairs={{0,2},{2,4},{4,6},{6,0},{1,3},{3,5},{5,7},{7,1},{8,10},{10,12},{12... | collective-permute-start | bytes 491528 | tf_op jit(solution)/shard_map/ppermute | solution.py:188
  65.2 14.1 %collective-permute-start.10 = (f32[20,16,128]{2,1,0:T(8,128)S(1)}, f32[20,16,128]{2,1,0:T(8,128)S(1)}, u32[]{:S(2)}, u32[]{:S(2)}) collective-permute-start(f32[20,16,128]{2,1,0:T(8,128)S(1)} %get-tuple-element.28), channel_id=1, source_target_pairs={{0,4},{2,6},{4,0},{6,2},{1,5},{3,7},{5,1},{7,3},{8,12},{10,14},{12... | collective-permute-start | bytes 491528 | tf_op jit(solution)/shard_map/ppermute | solution.py:188
  66.0 14.1 %collective-permute-start.11 = (f32[20,16,128]{2,1,0:T(8,128)S(1)}, f32[20,16,128]{2,1,0:T(8,128)S(1)}, u32[]{:S(2)}, u32[]{:S(2)}) collective-permute-start(f32[20,16,128]{2,1,0:T(8,128)S(1)} %get-tuple-element.29), channel_id=1, source_target_pairs={{0,6},{2,0},{4,2},{6,4},{1,7},{3,1},{5,3},{7,5},{8,14},{10,8},{12,... | collective-permute-start | bytes 491528 | tf_op jit(solution)/shard_map/ppermute | solution.py:188

commit v9 on v8

--- a/solution.py
+++ b/solution.py
@@ -74,12 +74,20 @@
 
 
 def beta_kernel(
-    where, cols, slots, w0, w1, w2, w3, blocks, keep_ref, send_ref,
+    where, cols, slots, w0, w1, w2, w3, w4, blocks, keep_ref, send_ref,
     wide, stack, acc, list_ref, sem_w,
 ):
     z, core = where[2], where[3]
+    homes = (
+        z,
+        jnp.where(z > 0, z - 1, 4),
+        jnp.bitwise_xor(z, 2),
+        jnp.where(z < 3, z + 1, 4),
+        jnp.where(z == 0, 3, jnp.where(z == 3, 0, 4)),
+    )
     loads = [
-        pltpu.make_async_copy(w, wide.at[k], sem_w.at[k]) for k, w in enumerate((w0, w1, w2, w3))
+        pltpu.make_async_copy(w, wide.at[k], sem_w.at[k])
+        for k, w in enumerate((w0, w1, w2, w3, w4))
     ]
     for load in loads:
         load.start()
@@ -92,7 +100,7 @@
     count = lax.fori_loop(0, 64, note, 0)
     list_ref[count] = 0
     for k, load in enumerate(loads):
-        home = 4 * jnp.bitwise_and(z - k + 4, 3)
+        home = 4 * homes[k]
         load.wait()
         for t in range(4):
             high, low = halves(wide[k, :, 128 * t : 128 * (t + 1)])
@@ -143,11 +151,9 @@
     for n, chunk in enumerate(chunks):
         chunk.wait()
 
-        @pl.loop(0, 2)
-        def _(step, n=n):
+        for first in (8 * n, 8 * n + 4):
             terms = []
-            for u in range(4):
-                spot = 8 * n + 4 * step + u
+            for spot in range(first, first + 4):
                 terms.append((owners[spot], product(stack[cols[spot]], blocks[spot])))
             for owner, term in terms:
                 acc[owner] += term
@@ -218,7 +224,10 @@
 def local(coeffs, hblocks, hcount, hcols):
     z, c = lax.axis_index("z"), lax.axis_index("c")
     where = jnp.stack([z, z, z, c]).astype(jnp.int32)
-    rows = [coeffs] + [shift(coeffs, k) for k in (1, 2, 3)]
+    below = lax.ppermute(coeffs, "z", [(0, 1), (1, 2), (2, 3)])
+    across = shift(coeffs, 2)
+    above = lax.ppermute(coeffs, "z", [(1, 0), (2, 1), (3, 2)])
+    rows = [coeffs, below, across, above, lax.ppermute(across, "z", [(1, 0), (2, 3)])]
     cols, owners, slots = tables(hcount, hcols, z, c)
     at = call(
         turn_kernel,
@@ -241,14 +250,14 @@
     keep, send = call(
         beta_kernel,
         (shape(16, 128, 128), shape(16, 128, 128)),
-        [SMEM] * 3 + [HBM] * 4 + [VMEM],
+        [SMEM] * 3 + [HBM] * 5 + [VMEM],
         where, cols, slots, *rows, blocks,
         scratch=[
-            pltpu.VMEM((4, 128, 512), F32),
-            pltpu.VMEM((16, 256, 128), BF16),
+            pltpu.VMEM((5, 128, 512), F32),
+            pltpu.VMEM((20, 256, 128), BF16),
             pltpu.VMEM((TRASH + 1, 128, 128), F32),
             pltpu.SMEM((72,), jnp.int32),
-            pltpu.SemaphoreType.DMA((4,)),
+            pltpu.SemaphoreType.DMA((5,)),
         ],
         mib=24,
         work=(BUSY, 7 << 20),

time: 106 us -> 120 us (1.13)
  waiting for transfers between devices: 29.6 us -> 36.1 us
  starting transfers between devices: 32.5 us -> 37.9 us
  blocking collectives: 23.7 us -> 27.2 us
    ppermute x0 -> x3, waiting for transfers between devices: none -> 20.8 us  [the longest x1 20.8 us: local(): lax.ppermute(across, 'z', [(1, 0), (2, 3)])]
    ppermute x0 -> x3, starting transfers between devices: none -> 11.3 us  [the longest x1 4.54 us: local(): above = lax.ppermute(coeffs, 'z', [(1, 0), (2, 1), (3, 2)])]
    ppermute x6 -> x4, waiting for transfers between devices: 20.2 us -> 12.6 us  [shift(): return lax.ppermute(value, 'z', [(i, (i + by) % 4) for i in range(4)])]
    all_to_all x1, waiting for transfers between devices: 6.7 us -> 0.01 us  [local(): lax.all_to_all(at.reshape(2048, 128), ROWS + ('z',), 0, 0, tiled=True)]
    ppermute x6 -> x4, starting transfers between devices: 11.7 us -> 6.99 us  [shift(): return lax.ppermute(value, 'z', [(i, (i + by) % 4) for i in range(4)])]
    all_to_all x1, blocking collectives: 23.7 us -> 27.2 us  [local(): back = lax.all_to_all(total, ROWS, 0, 0, tiled=True)]
    all_to_all x1, starting transfers between devices: 14.1 us -> 12.8 us  [local(): lax.all_to_all(at.reshape(2048, 128), ROWS + ('z',), 0, 0, tiled=True)]
    pallas_call x8, Pallas kernels: 18.7 us -> 17.5 us  [call(): pl.pallas_call(kernel, out_shape=outs, in_specs=in_specs, out_specs=space...]
  transfers between devices with their start and end apart: 13 -> 14, of which waited for: 7 -> 5; matrix products, arithmetic and copies ran while one was open for 1% -> 0% of each run, Pallas kernels for 16% -> 13%
where the time goes in v9:
time: 120 us
  starting transfers between devices  37.9 us (32%)
  waiting for transfers between devices  36.1 us (30%)
  blocking collectives  27.2 us (23%)
  Pallas kernels  17.5 us (15%)
    all_to_all x1, blocking collectives, local(): back = lax.all_to_all(total, ROWS, 0, 0, tiled=True)  27.2 us
    ppermute x1, waiting for transfers between devices, local(): lax.ppermute(across, 'z', [(1, 0), (2, 3)])  20.8 us
    pallas_call x8, Pallas kernels, call(): pl.pallas_call(kernel, out_shape=outs, in_specs=in_specs, out_specs=space...  17.5 us
    all_to_all x1, starting transfers between devices, local(): lax.all_to_all(at.reshape(2048, 128), ROWS + ('z',), 0, 0, tiled=True)  12.8 us
    ppermute x4, waiting for transfers between devices, shift(): return lax.ppermute(value, 'z', [(i, (i + by) % 4) for i in range(4)])  12.6 us
    ppermute x4, starting transfers between devices, shift(): return lax.ppermute(value, 'z', [(i, (i + by) % 4) for i in range(4)])  6.99 us
    ppermute x1, starting transfers between devices, local(): up = lax.ppermute(up, ('z', 'c'), [(0, 2), (1, 3), (2, 4), (3, 5), (4, 6)])  4.55 us
    ppermute x1, starting transfers between devices, local(): above = lax.ppermute(coeffs, 'z', [(1, 0), (2, 1), (3, 2)])  4.54 us
  transfers between devices with their start and end apart: 14, of which 5 were waited for; matrix products, arithmetic and copies ran while one was open for 0% of the time, Pallas kernels for 13%

profile of v9, /device:TPU:32, one launch (start us, length us, event | category | flops | bytes accessed | tf_op | source)
XLA Modules:
  0.0 119.5 jit_solution(1403989080713215357)
XLA Ops:
  0.0 0.1 collective-permute-start.5
  0.1 4.0 %collective-permute-start.1 = (f32[128,512]{1,0:T(8,128)}, f32[128,512]{1,0:T(8,128)S(1)}, u32[]{:S(2)}, u32[]{:S(2)}) collective-permute-start(f32[128,512]{1,0:T(8,128)} %c_ref.1), channel_id=1, source_target_pairs={{0,2},{2,4},{4,6},{1,3},{3,5},{5,7},{8,10},{10,12},{12,14},{9,11},... | collective-permute-start | bytes 786440 | tf_op jit(solution)/shard_map/ppermute | solution.py:227
  4.1 0.8 collective-permute-start.2
  4.9 4.5 %collective-permute-start.3 = (f32[128,512]{1,0:T(8,128)}, f32[128,512]{1,0:T(8,128)}, u32[]{:S(2)}, u32[]{:S(2)}) collective-permute-start(f32[128,512]{1,0:T(8,128)} %c_ref.1), channel_id=1, source_target_pairs={{2,0},{4,2},{6,4},{3,1},{5,3},{7,5},{10,8},{12,10},{14,12},{11,9},... | collective-permute-start | bytes 786440 | tf_op jit(solution)/shard_map/ppermute | solution.py:229
  9.5 0.1 collective-permute-start
  9.6 2.3 %turn_kernel.1 = f32[32,4,16,128]{3,2,1,0:T(8,128)} custom-call(f32[128,512]{1,0:T(8,128)} %c_ref.1), custom_call_target="tpu_custom_call" | custom-call | bytes 1048576 | tf_op jit(solution)/shard_map/turn_kernel/pallas_call | solution.py:212
  11.8 12.8 %all-to-all-start = ((f32[128,16,128]{2,1,0:T(8,128)}), f32[128,16,128]{2,1,0:T(8,128)S(1)}, u32[]{:S(2)}, u32[]{:S(2)}) async-start(f32[128,16,128]{2,1,0:T(8,128)} %bitcast.4), calls=%async_computation | async-start | bytes 2097152 | tf_op jit(solution)/shard_map/all_to_all | solution.py:239
  24.6 0.1 add_multiply_fusion
  24.8 0.1 add.55
  24.8 0.1 select_reduce_fusion
  24.9 0.1 convert_reduce_fusion.owners
  25.0 2.8 %collective-permute-start.4 = (f32[128,512]{1,0:T(8,128)}, f32[128,512]{1,0:T(8,128)S(1)}, u32[]{:S(2)}, u32[]{:S(2)}) collective-permute-start(f32[128,512]{1,0:T(8,128)} %collective-permute-done.2.w2), channel_id=1, source_target_pairs={{2,0},{4,6},{3,1},{5,7},{10,8},{12,14},{11,9},{13,15},{18,16},{20,... | collective-permute-start | bytes 786440 | tf_op jit(solution)/shard_map/ppermute | solution.py:230
  27.8 0.1 pad_add_fusion.where
  27.9 0.1 compare_select_fusion.6
  28.1 3.6 %blocks_kernel.1.blocks.source = bf16[64,128,256]{2,1,0:T(8,128)(2,1)S(1)} custom-call(f32[32,128,128]{2,1,0:T(8,128)S(1)} %copy-done.1, f32[32,128,128]{2,1,0:T(8,128)} %collective-permute-done.5.h1), custom_call_target="tpu_custom_call" | custom-call | bytes 8388608 | tf_op jit(solution)/shard_map/blocks_kernel/pallas_call | solution.py:212
  31.7 20.8 %collective-permute-done.4.w4 = f32[128,512]{1,0:T(8,128)S(1)} collective-permute-done((f32[128,512]{1,0:T(8,128)}, f32[128,512]{1,0:T(8,128)S(1)}, u32[]{:S(2)}, u32[]{:S(2)}) %collective-permute-start.4) | collective-permute-done | bytes 262176 | tf_op jit(solution)/shard_map/ppermute | solution.py:230
  52.5 5.9 %beta_kernel.1 = (f32[16,128,128]{2,1,0:T(8,128)S(1)}, f32[16,128,128]{2,1,0:T(8,128)S(1)}) custom-call(s32[4]{0:T(128)S(1)} %pad_add_fusion.where, s32[64]{0:T(128)S(1)} %get-tuple-element.32.cols, s32[64]{0:T(128)S(1)} %get-tuple-element.31.slots, f32[128,512]{1,0:T(8,128)S(1)} %copy-done.2, f32[128,512]{1,0:T(8,128)S(1)} %collective-permute-done.1.w1, ...), custom_call_target="tpu_custom_call" | custom-call | flops 40000000000 | bytes 7340032 | tf_op jit(solution)/shard_map/beta_kernel/pallas_call | solution.py:212
  58.4 0.1 collective-permute-start.6
  58.5 2.6 %collective-permute-done.6.got_ref = f32[16,128,128]{2,1,0:T(8,128)S(1)} collective-permute-done((f32[16,128,128]{2,1,0:T(8,128)S(1)}, f32[16,128,128]{2,1,0:T(8,128)S(1)}, u32[]{:S(2)}, u32[]{:S(2)}) %collective-permute-start.6) | collective-permute-done | bytes 1048608 | tf_op jit(solution)/shard_map/ppermute | solution.py:190
  61.1 0.2 cores_kernel.1
  61.3 1.3 %collective-permute-start.7 = (f32[4,128,128]{2,1,0:T(8,128)S(1)}, f32[4,128,128]{2,1,0:T(8,128)S(1)}, u32[]{:S(2)}, u32[]{:S(2)}) collective-permute-start(f32[4,128,128]{2,1,0:T(8,128)S(1)} %get-tuple-element.21), channel_id=1, source_target_pairs={{3,1},{4,2},{5,3},{6,4},{7,5},{11,9},{12,10},{13,11},{14,12},{15,1... | collective-permute-start | bytes 786440 | tf_op jit(solution)/shard_map/ppermute | solution.py:271
  62.6 4.6 %collective-permute-start.8 = (f32[4,128,128]{2,1,0:T(8,128)S(1)}, f32[4,128,128]{2,1,0:T(8,128)S(1)}, u32[]{:S(2)}, u32[]{:S(2)}) collective-permute-start(f32[4,128,128]{2,1,0:T(8,128)S(1)} %get-tuple-element.22), channel_id=1, source_target_pairs={{0,2},{1,3},{2,4},{3,5},{4,6},{8,10},{9,11},{10,12},{11,13},{12,14... | collective-permute-start | bytes 786440 | tf_op jit(solution)/shard_map/ppermute | solution.py:272
  67.1 0.7 collective-permute-start.9
  67.8 4.1 %alpha_kernel.1 = (f32[20,16,128]{2,1,0:T(8,128)S(1)}, f32[20,16,128]{2,1,0:T(8,128)S(1)}, f32[20,16,128]{2,1,0:T(8,128)S(1)}, f32[20,16,128]{2,1,0:T(8,128)S(1)}) custom-call(s32[4]{0:T(128)S(1)} %pad_add_fusion.where, s32[64]{0:T(128)S(1)} %get-tuple-element.32.cols, s32[64]{0:T(128)S(1)} %convert_reduce_fusion.owners, f32[32,64,128]{2,1,0:T(8,128)S(1)} %bitcast.6, ...), custom_call_target="tpu_custom_call" | custom-call | flops 40000000000 | bytes 7340032 | tf_op jit(solution)/shard_map/alpha_kernel/pallas_call | solution.py:212
  71.9 1.7 %collective-permute-start.10 = (f32[20,16,128]{2,1,0:T(8,128)S(1)}, f32[20,16,128]{2,1,0:T(8,128)S(1)}, u32[]{:S(2)}, u32[]{:S(2)}) collective-permute-start(f32[20,16,128]{2,1,0:T(8,128)S(1)} %get-tuple-element.27), channel_id=1, source_target_pairs={{0,2},{2,4},{4,6},{6,0},{1,3},{3,5},{5,7},{7,1},{8,10},{10,12},{12... | collective-permute-start | bytes 491528 | tf_op jit(solution)/shard_map/ppermute | solution.py:194
  73.6 4.4 %collective-permute-start.11 = (f32[20,16,128]{2,1,0:T(8,128)S(1)}, f32[20,16,128]{2,1,0:T(8,128)S(1)}, u32[]{:S(2)}, u32[]{:S(2)}) collective-permute-start(f32[20,16,128]{2,1,0:T(8,128)S(1)} %get-tuple-element.28), channel_id=1, source_target_pairs={{0,4},{2,6},{4,0},{6,2},{1,5},{3,7},{5,1},{7,3},{8,12},{10,14},{12... | collective-permute-start | bytes 491528 | tf_op jit(solution)/shard_map/ppermute | solution.py:194
  78.2 8.8 %collective-permute-done.10.p1 = f32[20,16,128]{2,1,0:T(8,128)S(1)} collective-permute-done((f32[20,16,128]{2,1,0:T(8,128)S(1)}, f32[20,16,128]{2,1,0:T(8,128)S(1)}, u32[]{:S(2)}, u32[]{:S(2)}) %collective-permute-start.10) | collective-permute-done | bytes 163872 | tf_op jit(solution)/shard_map/ppermute | solution.py:194
  87.0 3.0 %collective-permute-done.11.p2 = f32[20,16,128]{2,1,0:T(8,128)S(1)} collective-permute-done((f32[20,16,128]{2,1,0:T(8,128)S(1)}, f32[20,16,128]{2,1,0:T(8,128)S(1)}, u32[]{:S(2)}, u32[]{:S(2)}) %collective-permute-start.11) | collective-permute-done | bytes 163872 | tf_op jit(solution)/shard_map/ppermute | solution.py:194
  90.0 0.8 collective-permute-done.12.p3
  90.8 0.6 strings_kernel.1
  91.4 27.2 %all_to_all.14.back_ref = f32[32,16,128]{2,1,0:T(8,128)S(1)} all-to-all(f32[32,16,128]{2,1,0:T(8,128)S(1)} %strings_kernel.1), channel_id=1, replica_groups=mesh['y'=4,'h'=2,'x'=4,'z'=4,'c'=2] {'y','h','x'}, dimensions={0} | all-to-all | bytes 524288 | tf_op jit(solution)/shard_map/all_to_all | solution.py:298
  118.7 0.8 final_kernel.1
  (22 shorter events, 0.2 us)
Async XLA Ops:
  0.0 28.1 %copy-start.1 = (f32[32,128,128]{2,1,0:T(8,128)S(1)}, f32[32,128,128]{2,1,0:T(8,128)}, u32[]{:S(2)}) copy-start(f32[32,128,128]{2,1,0:T(8,128)} %h0.1) | copy-start | bytes 6291460
  0.0 27.9 %copy-start.3 = (s32[32]{0:T(128)S(1)}, s32[32]{0:T(128)}, u32[]{:S(2)}) copy-start(s32[32]{0:T(128)} %param.7) | copy-start | bytes 388
  0.0 24.8 %copy-start.4 = (s32[32]{0:T(128)S(1)}, s32[32]{0:T(128)}, u32[]{:S(2)}) copy-start(s32[32]{0:T(128)} %param.6) | copy-start | bytes 388
  0.0 28.0 %collective-permute-start.5 = (f32[32,128,128]{2,1,0:T(8,128)}, f32[32,128,128]{2,1,0:T(8,128)}, u32[]{:S(2)}, u32[]{:S(2)}) collective-permute-start(f32[32,128,128]{2,1,0:T(8,128)} %h0.1), channel_id=1, source_target_pairs={{0,1},{1,0},{2,3},{3,2},{4,5},{5,4},{6,7},{7,6},{8,9},{9,8},{10,11... | collective-permute-start | bytes 6291464 | tf_op jit(solution)/shard_map/ppermute | solution.py:190
  0.1 31.6 %collective-permute-start.1 = (f32[128,512]{1,0:T(8,128)}, f32[128,512]{1,0:T(8,128)S(1)}, u32[]{:S(2)}, u32[]{:S(2)}) collective-permute-start(f32[128,512]{1,0:T(8,128)} %c_ref.1), channel_id=1, source_target_pairs={{0,2},{2,4},{4,6},{1,3},{3,5},{5,7},{8,10},{10,12},{12,14},{9,11},... | collective-permute-start | bytes 786440 | tf_op jit(solution)/shard_map/ppermute | solution.py:227
  4.1 20.9 %collective-permute-start.2 = (f32[128,512]{1,0:T(8,128)}, f32[128,512]{1,0:T(8,128)}, u32[]{:S(2)}, u32[]{:S(2)}) collective-permute-start(f32[128,512]{1,0:T(8,128)} %c_ref.1), channel_id=1, source_target_pairs={{0,4},{2,6},{4,0},{6,2},{1,5},{3,7},{5,1},{7,3},{8,12},{10,14},{12... | collective-permute-start | bytes 786440 | tf_op jit(solution)/shard_map/ppermute | solution.py:194
  4.9 26.8 %collective-permute-start.3 = (f32[128,512]{1,0:T(8,128)}, f32[128,512]{1,0:T(8,128)}, u32[]{:S(2)}, u32[]{:S(2)}) collective-permute-start(f32[128,512]{1,0:T(8,128)} %c_ref.1), channel_id=1, source_target_pairs={{2,0},{4,2},{6,4},{3,1},{5,3},{7,5},{10,8},{12,10},{14,12},{11,9},... | collective-permute-start | bytes 786440 | tf_op jit(solution)/shard_map/ppermute | solution.py:229
  9.5 18.5 %collective-permute-start = (s32[32]{0:T(128)}, s32[32]{0:T(128)S(1)}, u32[]{:S(2)}, u32[]{:S(2)}) collective-permute-start(s32[32]{0:T(128)} %param.7), channel_id=1, source_target_pairs={{0,1},{1,0},{2,3},{3,2},{4,5},{5,4},{6,7},{7,6},{8,9},{9,8},{10,11... | collective-permute-start | bytes 392 | tf_op jit(solution)/shard_map/ppermute | solution.py:190
  11.8 56.0 %all-to-all-start = ((f32[128,16,128]{2,1,0:T(8,128)}), f32[128,16,128]{2,1,0:T(8,128)S(1)}, u32[]{:S(2)}, u32[]{:S(2)}) async-start(f32[128,16,128]{2,1,0:T(8,128)} %bitcast.4), calls=%async_computation | async-start | bytes 2097152 | tf_op jit(solution)/shard_map/all_to_all | solution.py:239
  25.0 27.4 %collective-permute-start.4 = (f32[128,512]{1,0:T(8,128)}, f32[128,512]{1,0:T(8,128)S(1)}, u32[]{:S(2)}, u32[]{:S(2)}) collective-permute-start(f32[128,512]{1,0:T(8,128)} %collective-permute-done.2.w2), channel_id=1, source_target_pairs={{2,0},{4,6},{3,1},{5,7},{10,8},{12,14},{11,9},{13,15},{18,16},{20,... | collective-permute-start | bytes 786440 | tf_op jit(solution)/shard_map/ppermute | solution.py:230
  28.0 24.4 %copy-start.2 = (f32[128,512]{1,0:T(8,128)S(1)}, f32[128,512]{1,0:T(8,128)}, u32[]{:S(2)}) copy-start(f32[128,512]{1,0:T(8,128)} %c_ref.1) | copy-start | bytes 786436
  31.7 26.7 %copy-start = (bf16[64,128,256]{2,1,0:T(8,128)(2,1)}, bf16[64,128,256]{2,1,0:T(8,128)(2,1)S(1)}, u32[]{:S(2)}) copy-start(bf16[64,128,256]{2,1,0:T(8,128)(2,1)S(1)} %blocks_kernel.1.blocks.source) | copy-start | bytes 12582916
  58.4 2.7 %collective-permute-start.6 = (f32[16,128,128]{2,1,0:T(8,128)S(1)}, f32[16,128,128]{2,1,0:T(8,128)S(1)}, u32[]{:S(2)}, u32[]{:S(2)}) collective-permute-start(f32[16,128,128]{2,1,0:T(8,128)S(1)} %get-tuple-element.19), channel_id=1, source_target_pairs={{0,1},{1,0},{2,3},{3,2},{4,5},{5,4},{6,7},{7,6},{8,9},{9,8},{10,11... | collective-permute-start | bytes 3145736 | tf_op jit(solution)/shard_map/ppermute | solution.py:190
  61.3 16.8 %collective-permute-start.7 = (f32[4,128,128]{2,1,0:T(8,128)S(1)}, f32[4,128,128]{2,1,0:T(8,128)S(1)}, u32[]{:S(2)}, u32[]{:S(2)}) collective-permute-start(f32[4,128,128]{2,1,0:T(8,128)S(1)} %get-tuple-element.21), channel_id=1, source_target_pairs={{3,1},{4,2},{5,3},{6,4},{7,5},{11,9},{12,10},{13,11},{14,12},{15,1... | collective-permute-start | bytes 786440 | tf_op jit(solution)/shard_map/ppermute | solution.py:271
  62.6 15.5 %collective-permute-start.8 = (f32[4,128,128]{2,1,0:T(8,128)S(1)}, f32[4,128,128]{2,1,0:T(8,128)S(1)}, u32[]{:S(2)}, u32[]{:S(2)}) collective-permute-start(f32[4,128,128]{2,1,0:T(8,128)S(1)} %get-tuple-element.22), channel_id=1, source_target_pairs={{0,2},{1,3},{2,4},{3,5},{4,6},{8,10},{9,11},{10,12},{11,13},{12,14... | collective-permute-start | bytes 786440 | tf_op jit(solution)/shard_map/ppermute | solution.py:272
  67.1 11.0 %collective-permute-start.9 = (f32[4,128,128]{2,1,0:T(8,128)S(1)}, f32[4,128,128]{2,1,0:T(8,128)S(1)}, u32[]{:S(2)}, u32[]{:S(2)}) collective-permute-start(f32[4,128,128]{2,1,0:T(8,128)S(1)} %get-tuple-element.23), channel_id=1, source_target_pairs={{0,4},{7,3},{8,12},{15,11},{16,20},{23,19},{24,28},{31,27},{32,36}... | collective-permute-start | bytes 786440 | tf_op jit(solution)/shard_map/ppermute | solution.py:273
  71.9 15.0 %collective-permute-start.10 = (f32[20,16,128]{2,1,0:T(8,128)S(1)}, f32[20,16,128]{2,1,0:T(8,128)S(1)}, u32[]{:S(2)}, u32[]{:S(2)}) collective-permute-start(f32[20,16,128]{2,1,0:T(8,128)S(1)} %get-tuple-element.27), channel_id=1, source_target_pairs={{0,2},{2,4},{4,6},{6,0},{1,3},{3,5},{5,7},{7,1},{8,10},{10,12},{12... | collective-permute-start | bytes 491528 | tf_op jit(solution)/shard_map/ppermute | solution.py:194
  73.6 16.3 %collective-permute-start.11 = (f32[20,16,128]{2,1,0:T(8,128)S(1)}, f32[20,16,128]{2,1,0:T(8,128)S(1)}, u32[]{:S(2)}, u32[]{:S(2)}) collective-permute-start(f32[20,16,128]{2,1,0:T(8,128)S(1)} %get-tuple-element.28), channel_id=1, source_target_pairs={{0,4},{2,6},{4,0},{6,2},{1,5},{3,7},{5,1},{7,3},{8,12},{10,14},{12... | collective-permute-start | bytes 491528 | tf_op jit(solution)/shard_map/ppermute | solution.py:194
  78.1 12.7 %collective-permute-start.12 = (f32[20,16,128]{2,1,0:T(8,128)S(1)}, f32[20,16,128]{2,1,0:T(8,128)S(1)}, u32[]{:S(2)}, u32[]{:S(2)}) collective-permute-start(f32[20,16,128]{2,1,0:T(8,128)S(1)} %get-tuple-element.29), channel_id=1, source_target_pairs={{0,6},{2,0},{4,2},{6,4},{1,7},{3,1},{5,3},{7,5},{8,14},{10,8},{12,... | collective-permute-start | bytes 491528 | tf_op jit(solution)/shard_map/ppermute | solution.py:194

commit v10 on v8

--- a/solution.py
+++ b/solution.py
@@ -29,18 +29,23 @@
     return jax.ShapeDtypeStruct(dims, kind)
 
 
-def turn_kernel(c_ref, at_ref, buf, sem):
-    loads = []
+def turn_kernel(c_ref, at_ref, buf, turned, sem, out_sem):
+    loads, stores = [], []
     for t in range(4):
         span = pl.ds(128 * t, 128)
         loads.append(pltpu.make_async_copy(c_ref.at[:, span], buf.at[t], sem.at[t]))
+        for plane in range(4):
+            home = at_ref.at[pl.ds(8 * t, 8), plane]
+            stores.append(pltpu.make_async_copy(turned.at[t], home, out_sem.at[t, plane]))
     for load in loads:
         load.start()
     for t, load in enumerate(loads):
         load.wait()
-        turned = jnp.transpose(buf[t]).reshape(8, 16, 128)
-        for plane in range(4):
-            at_ref[8 * t : 8 * (t + 1), plane] = turned
+        turned[t] = jnp.transpose(buf[t]).reshape(8, 16, 128)
+        for store in stores[4 * t : 4 * t + 4]:
+            store.start()
+    for store in stores:
+        store.wait()
 
 
 def halves(value):
@@ -143,11 +148,9 @@
     for n, chunk in enumerate(chunks):
         chunk.wait()
 
-        @pl.loop(0, 2)
-        def _(step, n=n):
+        for first in (8 * n, 8 * n + 4):
             terms = []
-            for u in range(4):
-                spot = 8 * n + 4 * step + u
+            for spot in range(first, first + 4):
                 terms.append((owners[spot], product(stack[cols[spot]], blocks[spot])))
             for owner, term in terms:
                 acc[owner] += term
@@ -225,7 +228,13 @@
         shape(32, 4, 16, 128),
         [HBM],
         pltpu.with_memory_space_constraint(coeffs, pltpu.HBM),
-        scratch=[pltpu.VMEM((4, 128, 128), F32), pltpu.SemaphoreType.DMA((4,))],
+        scratch=[
+            pltpu.VMEM((4, 128, 128), F32),
+            pltpu.VMEM((4, 8, 16, 128), F32),
+            pltpu.SemaphoreType.DMA((4,)),
+            pltpu.SemaphoreType.DMA((4, 4)),
+        ],
+        space=HBM,
     )
     moved = lax.all_to_all(at.reshape(2048, 128), ROWS + ("z",), 0, 0, tiled=True)
 

time: 106 us -> 104 us (0.981)
  Pallas kernels: 18.7 us -> 16.9 us
    pallas_call x8, Pallas kernels: 18.7 us -> 16.9 us  [call(): pl.pallas_call(kernel, out_shape=outs, in_specs=in_specs, out_specs=space...]
  transfers between devices with their start and end apart: 13 -> 13, of which waited for: 7 -> 7; matrix products, arithmetic and copies ran while one was open for 1% -> 1% of each run, Pallas kernels for 16% -> 15%
where the time goes in v10:
time: 104 us; the launch traced here: 103 us
  starting transfers between devices  32.5 us (31%)
  waiting for transfers between devices  30.1 us (29%)
  blocking collectives  23 us (22%)
  Pallas kernels  16.9 us (16%)
    all_to_all x1, blocking collectives, local(): back = lax.all_to_all(total, ROWS, 0, 0, tiled=True)  23 us
    ppermute x6, waiting for transfers between devices, shift(): return lax.ppermute(value, 'z', [(i, (i + by) % 4) for i in range(4)])  20.6 us
    pallas_call x8, Pallas kernels, call(): pl.pallas_call(kernel, out_shape=outs, in_specs=in_specs, out_specs=space...  16.9 us
    all_to_all x1, starting transfers between devices, local(): lax.all_to_all(at.reshape(2048, 128), ROWS + ('z',), 0, 0, tiled=True)  14.1 us
    ppermute x6, starting transfers between devices, shift(): return lax.ppermute(value, 'z', [(i, (i + by) % 4) for i in range(4)])  11.7 us
    all_to_all x1, waiting for transfers between devices, local(): lax.all_to_all(at.reshape(2048, 128), ROWS + ('z',), 0, 0, tiled=True)  6.85 us
    ppermute x1, starting transfers between devices, local(): up = lax.ppermute(up, ('z', 'c'), [(0, 2), (1, 3), (2, 4), (3, 5), (4, 6)])  4.55 us
    ppermute x3, waiting for transfers between devices, swap(): return lax.ppermute(value, 'c', [(0, 1), (1, 0)])  2.65 us
  transfers between devices with their start and end apart: 13, of which 7 were waited for; matrix products, arithmetic and copies ran while one was open for 1% of the time, Pallas kernels for 15%

profile of v10, /device:TPU:32, one launch (start us, length us, event | category | flops | bytes accessed | tf_op | source)
XLA Modules:
  0.0 103.3 jit_solution(1244059923077187923)
XLA Ops:
  0.0 0.1 collective-permute-start.4
  0.1 2.0 %collective-permute-start.1 = (f32[128,512]{1,0:T(8,128)}, f32[128,512]{1,0:T(8,128)S(1)}, u32[]{:S(2)}, u32[]{:S(2)}) collective-permute-start(f32[128,512]{1,0:T(8,128)} %c_ref.1), channel_id=1, source_target_pairs={{0,2},{2,4},{4,6},{6,0},{1,3},{3,5},{5,7},{7,1},{8,10},{10,12},{12... | collective-permute-start | bytes 786440 | tf_op jit(solution)/shard_map/ppermute | solution.py:191
  2.1 2.2 %collective-permute-start.2 = (f32[128,512]{1,0:T(8,128)}, f32[128,512]{1,0:T(8,128)}, u32[]{:S(2)}, u32[]{:S(2)}) collective-permute-start(f32[128,512]{1,0:T(8,128)} %c_ref.1), channel_id=1, source_target_pairs={{0,4},{2,6},{4,0},{6,2},{1,5},{3,7},{5,1},{7,3},{8,12},{10,14},{12... | collective-permute-start | bytes 786440 | tf_op jit(solution)/shard_map/ppermute | solution.py:191
  4.3 1.2 %collective-permute-start.3 = (f32[128,512]{1,0:T(8,128)}, f32[128,512]{1,0:T(8,128)}, u32[]{:S(2)}, u32[]{:S(2)}) collective-permute-start(f32[128,512]{1,0:T(8,128)} %c_ref.1), channel_id=1, source_target_pairs={{0,6},{2,0},{4,2},{6,4},{1,7},{3,1},{5,3},{7,5},{8,14},{10,8},{12,... | collective-permute-start | bytes 786440 | tf_op jit(solution)/shard_map/ppermute | solution.py:191
  5.5 2.2 %turn_kernel.1 = f32[32,4,16,128]{3,2,1,0:T(8,128)} custom-call(f32[128,512]{1,0:T(8,128)} %c_ref.1), custom_call_target="tpu_custom_call" | custom-call | bytes 1048576 | tf_op jit(solution)/shard_map/turn_kernel/pallas_call | solution.py:209
  7.7 14.1 %all-to-all-start = ((f32[128,16,128]{2,1,0:T(8,128)}), f32[128,16,128]{2,1,0:T(8,128)S(1)}, u32[]{:S(2)}, u32[]{:S(2)}) async-start(f32[128,16,128]{2,1,0:T(8,128)} %bitcast.4), calls=%async_computation | async-start | bytes 2097152 | tf_op jit(solution)/shard_map/all_to_all | solution.py:239
  21.8 0.1 add_multiply_fusion
  21.9 0.1 add.55
  22.0 0.1 select_reduce_fusion
  22.1 0.1 convert_reduce_fusion.owners
  22.3 0.1 compare_select_fusion.6
  22.4 3.6 %blocks_kernel.1.blocks.source = bf16[64,128,256]{2,1,0:T(8,128)(2,1)S(1)} custom-call(f32[32,128,128]{2,1,0:T(8,128)S(1)} %copy-done.1, f32[32,128,128]{2,1,0:T(8,128)} %collective-permute-done.4.h1), custom_call_target="tpu_custom_call" | custom-call | bytes 8388608 | tf_op jit(solution)/shard_map/blocks_kernel/pallas_call | solution.py:209
  26.0 4.8 %collective-permute-done.2.w2 = f32[128,512]{1,0:T(8,128)} collective-permute-done((f32[128,512]{1,0:T(8,128)}, f32[128,512]{1,0:T(8,128)}, u32[]{:S(2)}, u32[]{:S(2)}) %collective-permute-start.2) | collective-permute-done | bytes 262176 | tf_op jit(solution)/shard_map/ppermute | solution.py:191
  30.8 3.6 %collective-permute-done.3.w3 = f32[128,512]{1,0:T(8,128)} collective-permute-done((f32[128,512]{1,0:T(8,128)}, f32[128,512]{1,0:T(8,128)}, u32[]{:S(2)}, u32[]{:S(2)}) %collective-permute-start.3) | collective-permute-done | bytes 262176 | tf_op jit(solution)/shard_map/ppermute | solution.py:191
  34.4 5.4 %beta_kernel.1 = (f32[16,128,128]{2,1,0:T(8,128)S(1)}, f32[16,128,128]{2,1,0:T(8,128)S(1)}) custom-call(s32[4]{0:T(128)S(1)} %pad_add_fusion.where, s32[64]{0:T(128)S(1)} %get-tuple-element.32.cols, s32[64]{0:T(128)S(1)} %get-tuple-element.31.slots, f32[128,512]{1,0:T(8,128)S(1)} %copy-done.2, f32[128,512]{1,0:T(8,128)S(1)} %collective-permute-done.1.w1, ...), custom_call_target="tpu_custom_call" | custom-call | flops 40000000000 | bytes 7340032 | tf_op jit(solution)/shard_map/beta_kernel/pallas_call | solution.py:209
  39.9 0.1 collective-permute-start.5
  40.0 2.6 %collective-permute-done.5.got_ref = f32[16,128,128]{2,1,0:T(8,128)S(1)} collective-permute-done((f32[16,128,128]{2,1,0:T(8,128)S(1)}, f32[16,128,128]{2,1,0:T(8,128)S(1)}, u32[]{:S(2)}, u32[]{:S(2)}) %collective-permute-start.5) | collective-permute-done | bytes 1048608 | tf_op jit(solution)/shard_map/ppermute | solution.py:187
  42.6 0.2 cores_kernel.1
  42.8 1.3 %collective-permute-start.6 = (f32[4,128,128]{2,1,0:T(8,128)S(1)}, f32[4,128,128]{2,1,0:T(8,128)S(1)}, u32[]{:S(2)}, u32[]{:S(2)}) collective-permute-start(f32[4,128,128]{2,1,0:T(8,128)S(1)} %get-tuple-element.21), channel_id=1, source_target_pairs={{3,1},{4,2},{5,3},{6,4},{7,5},{11,9},{12,10},{13,11},{14,12},{15,1... | collective-permute-start | bytes 786440 | tf_op jit(solution)/shard_map/ppermute | solution.py:271
  44.1 4.6 %collective-permute-start.7 = (f32[4,128,128]{2,1,0:T(8,128)S(1)}, f32[4,128,128]{2,1,0:T(8,128)S(1)}, u32[]{:S(2)}, u32[]{:S(2)}) collective-permute-start(f32[4,128,128]{2,1,0:T(8,128)S(1)} %get-tuple-element.22), channel_id=1, source_target_pairs={{0,2},{1,3},{2,4},{3,5},{4,6},{8,10},{9,11},{10,12},{11,13},{12,14... | collective-permute-start | bytes 786440 | tf_op jit(solution)/shard_map/ppermute | solution.py:272
  48.6 0.7 collective-permute-start.8
  49.3 6.9 %all-to-all-done = f32[128,16,128]{2,1,0:T(8,128)S(1)} async-done(((f32[128,16,128]{2,1,0:T(8,128)}), f32[128,16,128]{2,1,0:T(8,128)S(1)}, u32[]{:S(2)}, u32[]{:S(2)}) %all-to-all-start) | async-done | bytes 1048608 | tf_op jit(solution)/shard_map/all_to_all | solution.py:239
  56.2 4.1 %alpha_kernel.1 = (f32[20,16,128]{2,1,0:T(8,128)S(1)}, f32[20,16,128]{2,1,0:T(8,128)S(1)}, f32[20,16,128]{2,1,0:T(8,128)S(1)}, f32[20,16,128]{2,1,0:T(8,128)S(1)}) custom-call(s32[4]{0:T(128)S(1)} %pad_add_fusion.where, s32[64]{0:T(128)S(1)} %get-tuple-element.32.cols, s32[64]{0:T(128)S(1)} %convert_reduce_fusion.owners, f32[32,64,128]{2,1,0:T(8,128)S(1)} %bitcast.6, ...), custom_call_target="tpu_custom_call" | custom-call | flops 40000000000 | bytes 7340032 | tf_op jit(solution)/shard_map/alpha_kernel/pallas_call | solution.py:209
  60.2 3.6 %collective-permute-start.9 = (f32[20,16,128]{2,1,0:T(8,128)S(1)}, f32[20,16,128]{2,1,0:T(8,128)S(1)}, u32[]{:S(2)}, u32[]{:S(2)}) collective-permute-start(f32[20,16,128]{2,1,0:T(8,128)S(1)} %get-tuple-element.27), channel_id=1, source_target_pairs={{0,2},{2,4},{4,6},{6,0},{1,3},{3,5},{5,7},{7,1},{8,10},{10,12},{12... | collective-permute-start | bytes 491528 | tf_op jit(solution)/shard_map/ppermute | solution.py:191
  63.9 0.9 collective-permute-start.10
  64.8 1.8 %collective-permute-start.11 = (f32[20,16,128]{2,1,0:T(8,128)S(1)}, f32[20,16,128]{2,1,0:T(8,128)S(1)}, u32[]{:S(2)}, u32[]{:S(2)}) collective-permute-start(f32[20,16,128]{2,1,0:T(8,128)S(1)} %get-tuple-element.29), channel_id=1, source_target_pairs={{0,6},{2,0},{4,2},{6,4},{1,7},{3,1},{5,3},{7,5},{8,14},{10,8},{12,... | collective-permute-start | bytes 491528 | tf_op jit(solution)/shard_map/ppermute | solution.py:191
  66.6 8.9 %collective-permute-done.9.p1 = f32[20,16,128]{2,1,0:T(8,128)S(1)} collective-permute-done((f32[20,16,128]{2,1,0:T(8,128)S(1)}, f32[20,16,128]{2,1,0:T(8,128)S(1)}, u32[]{:S(2)}, u32[]{:S(2)}) %collective-permute-start.9) | collective-permute-done | bytes 163872 | tf_op jit(solution)/shard_map/ppermute | solution.py:191
  75.5 2.5 %collective-permute-done.10.p2 = f32[20,16,128]{2,1,0:T(8,128)S(1)} collective-permute-done((f32[20,16,128]{2,1,0:T(8,128)S(1)}, f32[20,16,128]{2,1,0:T(8,128)S(1)}, u32[]{:S(2)}, u32[]{:S(2)}) %collective-permute-start.10) | collective-permute-done | bytes 163872 | tf_op jit(solution)/shard_map/ppermute | solution.py:191
  78.0 0.8 collective-permute-done.11.p3
  78.9 0.6 strings_kernel.1
  79.5 23.0 %all_to_all.14.back_ref = f32[32,16,128]{2,1,0:T(8,128)S(1)} all-to-all(f32[32,16,128]{2,1,0:T(8,128)S(1)} %strings_kernel.1), channel_id=1, replica_groups=mesh['y'=4,'h'=2,'x'=4,'z'=4,'c'=2] {'y','h','x'}, dimensions={0} | all-to-all | bytes 524288 | tf_op jit(solution)/shard_map/all_to_all | solution.py:298
  102.5 0.8 final_kernel.1
  (20 shorter events, 0.2 us)
Async XLA Ops:
  0.0 22.4 %copy-start.1 = (f32[32,128,128]{2,1,0:T(8,128)S(1)}, f32[32,128,128]{2,1,0:T(8,128)}, u32[]{:S(2)}) copy-start(f32[32,128,128]{2,1,0:T(8,128)} %h0.1) | copy-start | bytes 6291460
  0.0 22.3 %copy-start.3 = (s32[32]{0:T(128)S(1)}, s32[32]{0:T(128)}, u32[]{:S(2)}) copy-start(s32[32]{0:T(128)} %param.7) | copy-start | bytes 388
  0.0 22.0 %copy-start.4 = (s32[32]{0:T(128)S(1)}, s32[32]{0:T(128)}, u32[]{:S(2)}) copy-start(s32[32]{0:T(128)} %param.6) | copy-start | bytes 388
  0.0 22.4 %collective-permute-start.4 = (f32[32,128,128]{2,1,0:T(8,128)}, f32[32,128,128]{2,1,0:T(8,128)}, u32[]{:S(2)}, u32[]{:S(2)}) collective-permute-start(f32[32,128,128]{2,1,0:T(8,128)} %h0.1), channel_id=1, source_target_pairs={{0,1},{1,0},{2,3},{3,2},{4,5},{5,4},{6,7},{7,6},{8,9},{9,8},{10,11... | collective-permute-start | bytes 6291464 | tf_op jit(solution)/shard_map/ppermute | solution.py:187
  0.1 25.9 %collective-permute-start.1 = (f32[128,512]{1,0:T(8,128)}, f32[128,512]{1,0:T(8,128)S(1)}, u32[]{:S(2)}, u32[]{:S(2)}) collective-permute-start(f32[128,512]{1,0:T(8,128)} %c_ref.1), channel_id=1, source_target_pairs={{0,2},{2,4},{4,6},{6,0},{1,3},{3,5},{5,7},{7,1},{8,10},{10,12},{12... | collective-permute-start | bytes 786440 | tf_op jit(solution)/shard_map/ppermute | solution.py:191
  2.1 28.7 %collective-permute-start.2 = (f32[128,512]{1,0:T(8,128)}, f32[128,512]{1,0:T(8,128)}, u32[]{:S(2)}, u32[]{:S(2)}) collective-permute-start(f32[128,512]{1,0:T(8,128)} %c_ref.1), channel_id=1, source_target_pairs={{0,4},{2,6},{4,0},{6,2},{1,5},{3,7},{5,1},{7,3},{8,12},{10,14},{12... | collective-permute-start | bytes 786440 | tf_op jit(solution)/shard_map/ppermute | solution.py:191
  4.3 30.1 %collective-permute-start.3 = (f32[128,512]{1,0:T(8,128)}, f32[128,512]{1,0:T(8,128)}, u32[]{:S(2)}, u32[]{:S(2)}) collective-permute-start(f32[128,512]{1,0:T(8,128)} %c_ref.1), channel_id=1, source_target_pairs={{0,6},{2,0},{4,2},{6,4},{1,7},{3,1},{5,3},{7,5},{8,14},{10,8},{12,... | collective-permute-start | bytes 786440 | tf_op jit(solution)/shard_map/ppermute | solution.py:191
  5.5 16.8 %collective-permute-start = (s32[32]{0:T(128)}, s32[32]{0:T(128)S(1)}, u32[]{:S(2)}, u32[]{:S(2)}) collective-permute-start(s32[32]{0:T(128)} %param.7), channel_id=1, source_target_pairs={{0,1},{1,0},{2,3},{3,2},{4,5},{5,4},{6,7},{7,6},{8,9},{9,8},{10,11... | collective-permute-start | bytes 392 | tf_op jit(solution)/shard_map/ppermute | solution.py:187
  7.7 48.5 %all-to-all-start = ((f32[128,16,128]{2,1,0:T(8,128)}), f32[128,16,128]{2,1,0:T(8,128)S(1)}, u32[]{:S(2)}, u32[]{:S(2)}) async-start(f32[128,16,128]{2,1,0:T(8,128)} %bitcast.4), calls=%async_computation | async-start | bytes 2097152 | tf_op jit(solution)/shard_map/all_to_all | solution.py:239
  22.4 12.1 %copy-start.2 = (f32[128,512]{1,0:T(8,128)S(1)}, f32[128,512]{1,0:T(8,128)}, u32[]{:S(2)}) copy-start(f32[128,512]{1,0:T(8,128)} %c_ref.1) | copy-start | bytes 786436
  26.0 13.8 %copy-start = (bf16[64,128,256]{2,1,0:T(8,128)(2,1)}, bf16[64,128,256]{2,1,0:T(8,128)(2,1)S(1)}, u32[]{:S(2)}) copy-start(bf16[64,128,256]{2,1,0:T(8,128)(2,1)S(1)} %blocks_kernel.1.blocks.source) | copy-start | bytes 12582916
  39.9 2.7 %collective-permute-start.5 = (f32[16,128,128]{2,1,0:T(8,128)S(1)}, f32[16,128,128]{2,1,0:T(8,128)S(1)}, u32[]{:S(2)}, u32[]{:S(2)}) collective-permute-start(f32[16,128,128]{2,1,0:T(8,128)S(1)} %get-tuple-element.19), channel_id=1, source_target_pairs={{0,1},{1,0},{2,3},{3,2},{4,5},{5,4},{6,7},{7,6},{8,9},{9,8},{10,11... | collective-permute-start | bytes 3145736 | tf_op jit(solution)/shard_map/ppermute | solution.py:187
  42.8 22.0 %collective-permute-start.6 = (f32[4,128,128]{2,1,0:T(8,128)S(1)}, f32[4,128,128]{2,1,0:T(8,128)S(1)}, u32[]{:S(2)}, u32[]{:S(2)}) collective-permute-start(f32[4,128,128]{2,1,0:T(8,128)S(1)} %get-tuple-element.21), channel_id=1, source_target_pairs={{3,1},{4,2},{5,3},{6,4},{7,5},{11,9},{12,10},{13,11},{14,12},{15,1... | collective-permute-start | bytes 786440 | tf_op jit(solution)/shard_map/ppermute | solution.py:271
  44.1 22.5 %collective-permute-start.7 = (f32[4,128,128]{2,1,0:T(8,128)S(1)}, f32[4,128,128]{2,1,0:T(8,128)S(1)}, u32[]{:S(2)}, u32[]{:S(2)}) collective-permute-start(f32[4,128,128]{2,1,0:T(8,128)S(1)} %get-tuple-element.22), channel_id=1, source_target_pairs={{0,2},{1,3},{2,4},{3,5},{4,6},{8,10},{9,11},{10,12},{11,13},{12,14... | collective-permute-start | bytes 786440 | tf_op jit(solution)/shard_map/ppermute | solution.py:272
  48.6 17.9 %collective-permute-start.8 = (f32[4,128,128]{2,1,0:T(8,128)S(1)}, f32[4,128,128]{2,1,0:T(8,128)S(1)}, u32[]{:S(2)}, u32[]{:S(2)}) collective-permute-start(f32[4,128,128]{2,1,0:T(8,128)S(1)} %get-tuple-element.23), channel_id=1, source_target_pairs={{0,4},{7,3},{8,12},{15,11},{16,20},{23,19},{24,28},{31,27},{32,36}... | collective-permute-start | bytes 786440 | tf_op jit(solution)/shard_map/ppermute | solution.py:273
  60.2 15.2 %collective-permute-start.9 = (f32[20,16,128]{2,1,0:T(8,128)S(1)}, f32[20,16,128]{2,1,0:T(8,128)S(1)}, u32[]{:S(2)}, u32[]{:S(2)}) collective-permute-start(f32[20,16,128]{2,1,0:T(8,128)S(1)} %get-tuple-element.27), channel_id=1, source_target_pairs={{0,2},{2,4},{4,6},{6,0},{1,3},{3,5},{5,7},{7,1},{8,10},{10,12},{12... | collective-permute-start | bytes 491528 | tf_op jit(solution)/shard_map/ppermute | solution.py:191
  63.9 14.2 %collective-permute-start.10 = (f32[20,16,128]{2,1,0:T(8,128)S(1)}, f32[20,16,128]{2,1,0:T(8,128)S(1)}, u32[]{:S(2)}, u32[]{:S(2)}) collective-permute-start(f32[20,16,128]{2,1,0:T(8,128)S(1)} %get-tuple-element.28), channel_id=1, source_target_pairs={{0,4},{2,6},{4,0},{6,2},{1,5},{3,7},{5,1},{7,3},{8,12},{10,14},{12... | collective-permute-start | bytes 491528 | tf_op jit(solution)/shard_map/ppermute | solution.py:191
  64.8 14.1 %collective-permute-start.11 = (f32[20,16,128]{2,1,0:T(8,128)S(1)}, f32[20,16,128]{2,1,0:T(8,128)S(1)}, u32[]{:S(2)}, u32[]{:S(2)}) collective-permute-start(f32[20,16,128]{2,1,0:T(8,128)S(1)} %get-tuple-element.29), channel_id=1, source_target_pairs={{0,6},{2,0},{4,2},{6,4},{1,7},{3,1},{5,3},{7,5},{8,14},{10,8},{12,... | collective-permute-start | bytes 491528 | tf_op jit(solution)/shard_map/ppermute | solution.py:191

commit v11 on v10

--- a/solution.py
+++ b/solution.py
@@ -130,8 +130,8 @@
 ):
     z = where[2]
     chunks = []
-    for n in range(8):
-        span = pl.ds(8 * n, 8)
+    for n in range(4):
+        span = pl.ds(16 * n, 16)
         chunks.append(pltpu.make_async_copy(source.at[span], blocks.at[span], sem.at[n]))
     for chunk in chunks:
         chunk.start()
@@ -148,7 +148,7 @@
     for n, chunk in enumerate(chunks):
         chunk.wait()
 
-        for first in (8 * n, 8 * n + 4):
+        for first in range(16 * n, 16 * n + 16, 4):
             terms = []
             for spot in range(first, first + 4):
                 terms.append((owners[spot], product(stack[cols[spot]], blocks[spot])))
@@ -288,12 +288,13 @@
             pltpu.VMEM((32, 64, 128), F32),
             pltpu.VMEM((32, 128, 128), BF16),
             pltpu.VMEM((64, 128, 256), BF16),
-            pltpu.SemaphoreType.DMA((8,)),
+            pltpu.SemaphoreType.DMA((4,)),
         ],
         mib=24,
         work=(BUSY, 7 << 20),
     )
-    parts = [parts[0]] + [shift(parts[k], k) for k in (1, 2, 3)]
+    far = shift(parts[2], 2)
+    parts = [parts[0], shift(parts[1], 1), far, shift(parts[3], 3)]
     total = call(strings_kernel, shape(32, 16, 128), [SMEM] + [VMEM] * 5, where, done, *parts)
     back = lax.all_to_all(total, ROWS, 0, 0, tiled=True)
     return call(final_kernel, shape(128, 512), [VMEM] * 2, back, beta)

time: 104 us -> 103 us (level)
  no operation moved by 1% of the time
where the time goes in v11:
time: 103 us; the launch traced here: 102 us
  starting transfers between devices  32.5 us (32%)
  waiting for transfers between devices  29.5 us (29%)
  blocking collectives  22.4 us (22%)
  Pallas kernels  17.1 us (17%)
    all_to_all x1, blocking collectives, local(): back = lax.all_to_all(total, ROWS, 0, 0, tiled=True)  22.4 us
    ppermute x6, waiting for transfers between devices, shift(): return lax.ppermute(value, 'z', [(i, (i + by) % 4) for i in range(4)])  20.6 us
    pallas_call x8, Pallas kernels, call(): pl.pallas_call(kernel, out_shape=outs, in_specs=in_specs, out_specs=space...  17.1 us
    all_to_all x1, starting transfers between devices, local(): lax.all_to_all(at.reshape(2048, 128), ROWS + ('z',), 0, 0, tiled=True)  14.1 us
    ppermute x6, starting transfers between devices, shift(): return lax.ppermute(value, 'z', [(i, (i + by) % 4) for i in range(4)])  11.7 us
    all_to_all x1, waiting for transfers between devices, local(): lax.all_to_all(at.reshape(2048, 128), ROWS + ('z',), 0, 0, tiled=True)  6.18 us
    ppermute x1, starting transfers between devices, local(): up = lax.ppermute(up, ('z', 'c'), [(0, 2), (1, 3), (2, 4), (3, 5), (4, 6)])  4.55 us
    ppermute x3, waiting for transfers between devices, swap(): return lax.ppermute(value, 'c', [(0, 1), (1, 0)])  2.65 us
  transfers between devices with their start and end apart: 13, of which 7 were waited for; matrix products, arithmetic and copies ran while one was open for 1% of the time, Pallas kernels for 15%

profile of v11, /device:TPU:32, one launch (start us, length us, event | category | flops | bytes accessed | tf_op | source)
XLA Modules:
  0.0 102.2 jit_solution(9464079005896875084)
XLA Ops:
  0.0 0.1 collective-permute-start.4
  0.1 2.0 %collective-permute-start.1 = (f32[128,512]{1,0:T(8,128)}, f32[128,512]{1,0:T(8,128)S(1)}, u32[]{:S(2)}, u32[]{:S(2)}) collective-permute-start(f32[128,512]{1,0:T(8,128)} %c_ref.1), channel_id=1, source_target_pairs={{0,2},{2,4},{4,6},{6,0},{1,3},{3,5},{5,7},{7,1},{8,10},{10,12},{12... | collective-permute-start | bytes 786440 | tf_op jit(solution)/shard_map/ppermute | solution.py:191
  2.1 2.2 %collective-permute-start.2 = (f32[128,512]{1,0:T(8,128)}, f32[128,512]{1,0:T(8,128)}, u32[]{:S(2)}, u32[]{:S(2)}) collective-permute-start(f32[128,512]{1,0:T(8,128)} %c_ref.1), channel_id=1, source_target_pairs={{0,4},{2,6},{4,0},{6,2},{1,5},{3,7},{5,1},{7,3},{8,12},{10,14},{12... | collective-permute-start | bytes 786440 | tf_op jit(solution)/shard_map/ppermute | solution.py:191
  4.3 1.2 %collective-permute-start.3 = (f32[128,512]{1,0:T(8,128)}, f32[128,512]{1,0:T(8,128)}, u32[]{:S(2)}, u32[]{:S(2)}) collective-permute-start(f32[128,512]{1,0:T(8,128)} %c_ref.1), channel_id=1, source_target_pairs={{0,6},{2,0},{4,2},{6,4},{1,7},{3,1},{5,3},{7,5},{8,14},{10,8},{12,... | collective-permute-start | bytes 786440 | tf_op jit(solution)/shard_map/ppermute | solution.py:191
  5.5 2.2 %turn_kernel.1 = f32[32,4,16,128]{3,2,1,0:T(8,128)} custom-call(f32[128,512]{1,0:T(8,128)} %c_ref.1), custom_call_target="tpu_custom_call" | custom-call | bytes 1048576 | tf_op jit(solution)/shard_map/turn_kernel/pallas_call | solution.py:209
  7.7 14.1 %all-to-all-start = ((f32[128,16,128]{2,1,0:T(8,128)}), f32[128,16,128]{2,1,0:T(8,128)S(1)}, u32[]{:S(2)}, u32[]{:S(2)}) async-start(f32[128,16,128]{2,1,0:T(8,128)} %bitcast.4), calls=%async_computation | async-start | bytes 2097152 | tf_op jit(solution)/shard_map/all_to_all | solution.py:239
  21.8 0.1 add_multiply_fusion
  21.9 0.1 add.55
  22.0 0.1 select_reduce_fusion
  22.1 0.1 convert_reduce_fusion.owners
  22.3 0.1 compare_select_fusion.6
  22.4 3.6 %blocks_kernel.1.blocks.source = bf16[64,128,256]{2,1,0:T(8,128)(2,1)S(1)} custom-call(f32[32,128,128]{2,1,0:T(8,128)S(1)} %copy-done.1, f32[32,128,128]{2,1,0:T(8,128)} %collective-permute-done.4.h1), custom_call_target="tpu_custom_call" | custom-call | bytes 8388608 | tf_op jit(solution)/shard_map/blocks_kernel/pallas_call | solution.py:209
  26.0 4.8 %collective-permute-done.2.w2 = f32[128,512]{1,0:T(8,128)} collective-permute-done((f32[128,512]{1,0:T(8,128)}, f32[128,512]{1,0:T(8,128)}, u32[]{:S(2)}, u32[]{:S(2)}) %collective-permute-start.2) | collective-permute-done | bytes 262176 | tf_op jit(solution)/shard_map/ppermute | solution.py:191
  30.8 3.6 %collective-permute-done.3.w3 = f32[128,512]{1,0:T(8,128)} collective-permute-done((f32[128,512]{1,0:T(8,128)}, f32[128,512]{1,0:T(8,128)}, u32[]{:S(2)}, u32[]{:S(2)}) %collective-permute-start.3) | collective-permute-done | bytes 262176 | tf_op jit(solution)/shard_map/ppermute | solution.py:191
  34.4 6.1 %beta_kernel.1 = (f32[16,128,128]{2,1,0:T(8,128)S(1)}, f32[16,128,128]{2,1,0:T(8,128)S(1)}) custom-call(s32[4]{0:T(128)S(1)} %pad_add_fusion.where, s32[64]{0:T(128)S(1)} %get-tuple-element.32.cols, s32[64]{0:T(128)S(1)} %get-tuple-element.31.slots, f32[128,512]{1,0:T(8,128)S(1)} %copy-done.2, f32[128,512]{1,0:T(8,128)S(1)} %collective-permute-done.1.w1, ...), custom_call_target="tpu_custom_call" | custom-call | flops 40000000000 | bytes 7340032 | tf_op jit(solution)/shard_map/beta_kernel/pallas_call | solution.py:209
  40.5 0.1 collective-permute-start.5
  40.6 2.6 %collective-permute-done.5.got_ref = f32[16,128,128]{2,1,0:T(8,128)S(1)} collective-permute-done((f32[16,128,128]{2,1,0:T(8,128)S(1)}, f32[16,128,128]{2,1,0:T(8,128)S(1)}, u32[]{:S(2)}, u32[]{:S(2)}) %collective-permute-start.5) | collective-permute-done | bytes 1048608 | tf_op jit(solution)/shard_map/ppermute | solution.py:187
  43.3 0.2 cores_kernel.1
  43.4 1.3 %collective-permute-start.6 = (f32[4,128,128]{2,1,0:T(8,128)S(1)}, f32[4,128,128]{2,1,0:T(8,128)S(1)}, u32[]{:S(2)}, u32[]{:S(2)}) collective-permute-start(f32[4,128,128]{2,1,0:T(8,128)S(1)} %get-tuple-element.21), channel_id=1, source_target_pairs={{3,1},{4,2},{5,3},{6,4},{7,5},{11,9},{12,10},{13,11},{14,12},{15,1... | collective-permute-start | bytes 786440 | tf_op jit(solution)/shard_map/ppermute | solution.py:271
  44.7 4.6 %collective-permute-start.7 = (f32[4,128,128]{2,1,0:T(8,128)S(1)}, f32[4,128,128]{2,1,0:T(8,128)S(1)}, u32[]{:S(2)}, u32[]{:S(2)}) collective-permute-start(f32[4,128,128]{2,1,0:T(8,128)S(1)} %get-tuple-element.22), channel_id=1, source_target_pairs={{0,2},{1,3},{2,4},{3,5},{4,6},{8,10},{9,11},{10,12},{11,13},{12,14... | collective-permute-start | bytes 786440 | tf_op jit(solution)/shard_map/ppermute | solution.py:272
  49.3 0.7 collective-permute-start.8
  50.0 6.2 %all-to-all-done = f32[128,16,128]{2,1,0:T(8,128)S(1)} async-done(((f32[128,16,128]{2,1,0:T(8,128)}), f32[128,16,128]{2,1,0:T(8,128)S(1)}, u32[]{:S(2)}, u32[]{:S(2)}) %all-to-all-start) | async-done | bytes 1048608 | tf_op jit(solution)/shard_map/all_to_all | solution.py:239
  56.2 3.6 %alpha_kernel.1 = (f32[20,16,128]{2,1,0:T(8,128)S(1)}, f32[20,16,128]{2,1,0:T(8,128)S(1)}, f32[20,16,128]{2,1,0:T(8,128)S(1)}, f32[20,16,128]{2,1,0:T(8,128)S(1)}) custom-call(s32[4]{0:T(128)S(1)} %pad_add_fusion.where, s32[64]{0:T(128)S(1)} %get-tuple-element.32.cols, s32[64]{0:T(128)S(1)} %convert_reduce_fusion.owners, f32[32,64,128]{2,1,0:T(8,128)S(1)} %bitcast.6, ...), custom_call_target="tpu_custom_call" | custom-call | flops 40000000000 | bytes 7340032 | tf_op jit(solution)/shard_map/alpha_kernel/pallas_call | solution.py:209
  59.8 3.7 %collective-permute-start.9 = (f32[20,16,128]{2,1,0:T(8,128)S(1)}, f32[20,16,128]{2,1,0:T(8,128)S(1)}, u32[]{:S(2)}, u32[]{:S(2)}) collective-permute-start(f32[20,16,128]{2,1,0:T(8,128)S(1)} %get-tuple-element.27), channel_id=1, source_target_pairs={{0,2},{2,4},{4,6},{6,0},{1,3},{3,5},{5,7},{7,1},{8,10},{10,12},{12... | collective-permute-start | bytes 491528 | tf_op jit(solution)/shard_map/ppermute | solution.py:191
  63.5 0.8 collective-permute-start.10
  64.3 1.8 %collective-permute-start.11 = (f32[20,16,128]{2,1,0:T(8,128)S(1)}, f32[20,16,128]{2,1,0:T(8,128)S(1)}, u32[]{:S(2)}, u32[]{:S(2)}) collective-permute-start(f32[20,16,128]{2,1,0:T(8,128)S(1)} %get-tuple-element.29), channel_id=1, source_target_pairs={{0,6},{2,0},{4,2},{6,4},{1,7},{3,1},{5,3},{7,5},{8,14},{10,8},{12,... | collective-permute-start | bytes 491528 | tf_op jit(solution)/shard_map/ppermute | solution.py:191
  66.2 9.0 %collective-permute-done.9.p1 = f32[20,16,128]{2,1,0:T(8,128)S(1)} collective-permute-done((f32[20,16,128]{2,1,0:T(8,128)S(1)}, f32[20,16,128]{2,1,0:T(8,128)S(1)}, u32[]{:S(2)}, u32[]{:S(2)}) %collective-permute-start.9) | collective-permute-done | bytes 163872 | tf_op jit(solution)/shard_map/ppermute | solution.py:191
  75.1 2.5 %collective-permute-done.10.p2 = f32[20,16,128]{2,1,0:T(8,128)S(1)} collective-permute-done((f32[20,16,128]{2,1,0:T(8,128)S(1)}, f32[20,16,128]{2,1,0:T(8,128)S(1)}, u32[]{:S(2)}, u32[]{:S(2)}) %collective-permute-start.10) | collective-permute-done | bytes 163872 | tf_op jit(solution)/shard_map/ppermute | solution.py:191
  77.6 0.8 collective-permute-done.11.p3
  78.4 0.6 strings_kernel.1
  79.0 22.4 %all_to_all.14.back_ref = f32[32,16,128]{2,1,0:T(8,128)S(1)} all-to-all(f32[32,16,128]{2,1,0:T(8,128)S(1)} %strings_kernel.1), channel_id=1, replica_groups=mesh['y'=4,'h'=2,'x'=4,'z'=4,'c'=2] {'y','h','x'}, dimensions={0} | all-to-all | bytes 524288 | tf_op jit(solution)/shard_map/all_to_all | solution.py:299
  101.4 0.8 final_kernel.1
  (20 shorter events, 0.2 us)
Async XLA Ops:
  0.0 22.4 %copy-start.1 = (f32[32,128,128]{2,1,0:T(8,128)S(1)}, f32[32,128,128]{2,1,0:T(8,128)}, u32[]{:S(2)}) copy-start(f32[32,128,128]{2,1,0:T(8,128)} %h0.1) | copy-start | bytes 6291460
  0.0 22.3 %copy-start.3 = (s32[32]{0:T(128)S(1)}, s32[32]{0:T(128)}, u32[]{:S(2)}) copy-start(s32[32]{0:T(128)} %param.7) | copy-start | bytes 388
  0.0 22.0 %copy-start.4 = (s32[32]{0:T(128)S(1)}, s32[32]{0:T(128)}, u32[]{:S(2)}) copy-start(s32[32]{0:T(128)} %param.6) | copy-start | bytes 388
  0.0 22.4 %collective-permute-start.4 = (f32[32,128,128]{2,1,0:T(8,128)}, f32[32,128,128]{2,1,0:T(8,128)}, u32[]{:S(2)}, u32[]{:S(2)}) collective-permute-start(f32[32,128,128]{2,1,0:T(8,128)} %h0.1), channel_id=1, source_target_pairs={{0,1},{1,0},{2,3},{3,2},{4,5},{5,4},{6,7},{7,6},{8,9},{9,8},{10,11... | collective-permute-start | bytes 6291464 | tf_op jit(solution)/shard_map/ppermute | solution.py:187
  0.1 25.9 %collective-permute-start.1 = (f32[128,512]{1,0:T(8,128)}, f32[128,512]{1,0:T(8,128)S(1)}, u32[]{:S(2)}, u32[]{:S(2)}) collective-permute-start(f32[128,512]{1,0:T(8,128)} %c_ref.1), channel_id=1, source_target_pairs={{0,2},{2,4},{4,6},{6,0},{1,3},{3,5},{5,7},{7,1},{8,10},{10,12},{12... | collective-permute-start | bytes 786440 | tf_op jit(solution)/shard_map/ppermute | solution.py:191
  2.1 28.7 %collective-permute-start.2 = (f32[128,512]{1,0:T(8,128)}, f32[128,512]{1,0:T(8,128)}, u32[]{:S(2)}, u32[]{:S(2)}) collective-permute-start(f32[128,512]{1,0:T(8,128)} %c_ref.1), channel_id=1, source_target_pairs={{0,4},{2,6},{4,0},{6,2},{1,5},{3,7},{5,1},{7,3},{8,12},{10,14},{12... | collective-permute-start | bytes 786440 | tf_op jit(solution)/shard_map/ppermute | solution.py:191
  4.3 30.1 %collective-permute-start.3 = (f32[128,512]{1,0:T(8,128)}, f32[128,512]{1,0:T(8,128)}, u32[]{:S(2)}, u32[]{:S(2)}) collective-permute-start(f32[128,512]{1,0:T(8,128)} %c_ref.1), channel_id=1, source_target_pairs={{0,6},{2,0},{4,2},{6,4},{1,7},{3,1},{5,3},{7,5},{8,14},{10,8},{12,... | collective-permute-start | bytes 786440 | tf_op jit(solution)/shard_map/ppermute | solution.py:191
  5.5 16.8 %collective-permute-start = (s32[32]{0:T(128)}, s32[32]{0:T(128)S(1)}, u32[]{:S(2)}, u32[]{:S(2)}) collective-permute-start(s32[32]{0:T(128)} %param.7), channel_id=1, source_target_pairs={{0,1},{1,0},{2,3},{3,2},{4,5},{5,4},{6,7},{7,6},{8,9},{9,8},{10,11... | collective-permute-start | bytes 392 | tf_op jit(solution)/shard_map/ppermute | solution.py:187
  7.7 48.5 %all-to-all-start = ((f32[128,16,128]{2,1,0:T(8,128)}), f32[128,16,128]{2,1,0:T(8,128)S(1)}, u32[]{:S(2)}, u32[]{:S(2)}) async-start(f32[128,16,128]{2,1,0:T(8,128)} %bitcast.4), calls=%async_computation | async-start | bytes 2097152 | tf_op jit(solution)/shard_map/all_to_all | solution.py:239
  22.4 12.1 %copy-start.2 = (f32[128,512]{1,0:T(8,128)S(1)}, f32[128,512]{1,0:T(8,128)}, u32[]{:S(2)}) copy-start(f32[128,512]{1,0:T(8,128)} %c_ref.1) | copy-start | bytes 786436
  26.0 14.5 %copy-start = (bf16[64,128,256]{2,1,0:T(8,128)(2,1)}, bf16[64,128,256]{2,1,0:T(8,128)(2,1)S(1)}, u32[]{:S(2)}) copy-start(bf16[64,128,256]{2,1,0:T(8,128)(2,1)S(1)} %blocks_kernel.1.blocks.source) | copy-start | bytes 12582916
  40.5 2.7 %collective-permute-start.5 = (f32[16,128,128]{2,1,0:T(8,128)S(1)}, f32[16,128,128]{2,1,0:T(8,128)S(1)}, u32[]{:S(2)}, u32[]{:S(2)}) collective-permute-start(f32[16,128,128]{2,1,0:T(8,128)S(1)} %get-tuple-element.19), channel_id=1, source_target_pairs={{0,1},{1,0},{2,3},{3,2},{4,5},{5,4},{6,7},{7,6},{8,9},{9,8},{10,11... | collective-permute-start | bytes 3145736 | tf_op jit(solution)/shard_map/ppermute | solution.py:187
  43.4 20.8 %collective-permute-start.6 = (f32[4,128,128]{2,1,0:T(8,128)S(1)}, f32[4,128,128]{2,1,0:T(8,128)S(1)}, u32[]{:S(2)}, u32[]{:S(2)}) collective-permute-start(f32[4,128,128]{2,1,0:T(8,128)S(1)} %get-tuple-element.21), channel_id=1, source_target_pairs={{3,1},{4,2},{5,3},{6,4},{7,5},{11,9},{12,10},{13,11},{14,12},{15,1... | collective-permute-start | bytes 786440 | tf_op jit(solution)/shard_map/ppermute | solution.py:271
  44.7 21.3 %collective-permute-start.7 = (f32[4,128,128]{2,1,0:T(8,128)S(1)}, f32[4,128,128]{2,1,0:T(8,128)S(1)}, u32[]{:S(2)}, u32[]{:S(2)}) collective-permute-start(f32[4,128,128]{2,1,0:T(8,128)S(1)} %get-tuple-element.22), channel_id=1, source_target_pairs={{0,2},{1,3},{2,4},{3,5},{4,6},{8,10},{9,11},{10,12},{11,13},{12,14... | collective-permute-start | bytes 786440 | tf_op jit(solution)/shard_map/ppermute | solution.py:272
  49.3 16.8 %collective-permute-start.8 = (f32[4,128,128]{2,1,0:T(8,128)S(1)}, f32[4,128,128]{2,1,0:T(8,128)S(1)}, u32[]{:S(2)}, u32[]{:S(2)}) collective-permute-start(f32[4,128,128]{2,1,0:T(8,128)S(1)} %get-tuple-element.23), channel_id=1, source_target_pairs={{0,4},{7,3},{8,12},{15,11},{16,20},{23,19},{24,28},{31,27},{32,36}... | collective-permute-start | bytes 786440 | tf_op jit(solution)/shard_map/ppermute | solution.py:273
  59.8 15.4 %collective-permute-start.9 = (f32[20,16,128]{2,1,0:T(8,128)S(1)}, f32[20,16,128]{2,1,0:T(8,128)S(1)}, u32[]{:S(2)}, u32[]{:S(2)}) collective-permute-start(f32[20,16,128]{2,1,0:T(8,128)S(1)} %get-tuple-element.27), channel_id=1, source_target_pairs={{0,2},{2,4},{4,6},{6,0},{1,3},{3,5},{5,7},{7,1},{8,10},{10,12},{12... | collective-permute-start | bytes 491528 | tf_op jit(solution)/shard_map/ppermute | solution.py:191
  63.5 14.1 %collective-permute-start.10 = (f32[20,16,128]{2,1,0:T(8,128)S(1)}, f32[20,16,128]{2,1,0:T(8,128)S(1)}, u32[]{:S(2)}, u32[]{:S(2)}) collective-permute-start(f32[20,16,128]{2,1,0:T(8,128)S(1)} %get-tuple-element.28), channel_id=1, source_target_pairs={{0,4},{2,6},{4,0},{6,2},{1,5},{3,7},{5,1},{7,3},{8,12},{10,14},{12... | collective-permute-start | bytes 491528 | tf_op jit(solution)/shard_map/ppermute | solution.py:191
  64.3 14.1 %collective-permute-start.11 = (f32[20,16,128]{2,1,0:T(8,128)S(1)}, f32[20,16,128]{2,1,0:T(8,128)S(1)}, u32[]{:S(2)}, u32[]{:S(2)}) collective-permute-start(f32[20,16,128]{2,1,0:T(8,128)S(1)} %get-tuple-element.29), channel_id=1, source_target_pairs={{0,6},{2,0},{4,2},{6,4},{1,7},{3,1},{5,3},{7,5},{8,14},{10,8},{12,... | collective-permute-start | bytes 491528 | tf_op jit(solution)/shard_map/ppermute | solution.py:191

commit v12 on v11

--- a/solution.py
+++ b/solution.py
@@ -95,7 +95,8 @@
         return count + jnp.where(slots[n] < TRASH, 1, 0)
 
     count = lax.fori_loop(0, 64, note, 0)
-    list_ref[count] = 0
+    for u in range(3):
+        list_ref[count + u] = 0
     for k, load in enumerate(loads):
         home = 4 * jnp.bitwise_and(z - k + 4, 3)
         load.wait()
@@ -104,14 +105,14 @@
             stack[home + t, :128] = high
             stack[home + t, 128:] = low
 
-    @pl.loop(0, lax.shift_right_logical(count + 1, 1))
+    @pl.loop(0, lax.shift_right_logical(count + 3, 2))
     def _(step):
         terms = []
-        for u in range(2):
-            n = list_ref[2 * step + u]
+        for u in range(4):
+            n = list_ref[4 * step + u]
             column = cols[n]
             left = stack[4 * lax.shift_right_logical(column, 3) + jnp.bitwise_and(column, 3)]
-            slot = jnp.where(2 * step + u < count, slots[n], TRASH)
+            slot = jnp.where(4 * step + u < count, slots[n], TRASH)
             terms.append((slot, product(left, blocks[n])))
         for slot, term in terms:
             acc[slot] += term
@@ -137,13 +138,14 @@
         chunk.start()
     acc[...] = jnp.zeros_like(acc)
 
-    @pl.loop(0, 32)
-    def _(j):
+    @pl.loop(0, 8)
+    def _(step):
         for k in range(4):
             home = pl.multiple_of(16 * jnp.bitwise_and(z + k, 3), 16)
-            high, low = halves(a_ref[j, pl.ds(home, 16)])
-            stack[j, 16 * k : 16 * k + 16] = high
-            stack[j, 64 + 16 * k : 80 + 16 * k] = low
+            for j in range(4):
+                high, low = halves(a_ref[4 * step + j, pl.ds(home, 16)])
+                stack[4 * step + j, 16 * k : 16 * k + 16] = high
+                stack[4 * step + j, 64 + 16 * k : 80 + 16 * k] = low
 
     for n, chunk in enumerate(chunks):
         chunk.wait()

time: 103 us -> 103 us (level)
  Pallas kernels: 17.1 us -> 15.5 us
  waiting for transfers between devices: 29.5 us -> 31.1 us
    pallas_call x8, Pallas kernels: 17.1 us -> 15.5 us  [call(): pl.pallas_call(kernel, out_shape=outs, in_specs=in_specs, out_specs=space...]
    all_to_all x1, waiting for transfers between devices: 6.18 us -> 7.78 us  [local(): lax.all_to_all(at.reshape(2048, 128), ROWS + ('z',), 0, 0, tiled=True)]
  transfers between devices with their start and end apart: 13 -> 13, of which waited for: 7 -> 7; matrix products, arithmetic and copies ran while one was open for 1% -> 1% of each run, Pallas kernels for 15% -> 14%
where the time goes in v12:
time: 103 us; the launch traced here: 102 us
  starting transfers between devices  32.5 us (32%)
  waiting for transfers between devices  31.1 us (30%)
  blocking collectives  22.4 us (22%)
  Pallas kernels  15.5 us (15%)
    all_to_all x1, blocking collectives, local(): back = lax.all_to_all(total, ROWS, 0, 0, tiled=True)  22.4 us
    ppermute x6, waiting for transfers between devices, shift(): return lax.ppermute(value, 'z', [(i, (i + by) % 4) for i in range(4)])  20.6 us
    pallas_call x8, Pallas kernels, call(): pl.pallas_call(kernel, out_shape=outs, in_specs=in_specs, out_specs=space...  15.5 us
    all_to_all x1, starting transfers between devices, local(): lax.all_to_all(at.reshape(2048, 128), ROWS + ('z',), 0, 0, tiled=True)  14.1 us
    ppermute x6, starting transfers between devices, shift(): return lax.ppermute(value, 'z', [(i, (i + by) % 4) for i in range(4)])  11.7 us
    all_to_all x1, waiting for transfers between devices, local(): lax.all_to_all(at.reshape(2048, 128), ROWS + ('z',), 0, 0, tiled=True)  7.78 us
    ppermute x1, starting transfers between devices, local(): up = lax.ppermute(up, ('z', 'c'), [(0, 2), (1, 3), (2, 4), (3, 5), (4, 6)])  4.55 us
    ppermute x3, waiting for transfers between devices, swap(): return lax.ppermute(value, 'c', [(0, 1), (1, 0)])  2.65 us
  transfers between devices with their start and end apart: 13, of which 7 were waited for; matrix products, arithmetic and copies ran while one was open for 1% of the time, Pallas kernels for 14%

profile of v12, /device:TPU:32, one launch (start us, length us, event | category | flops | bytes accessed | tf_op | source)
XLA Modules:
  0.0 102.3 jit_solution(11422505775114386054)
XLA Ops:
  0.0 0.1 collective-permute-start.4
  0.1 2.0 %collective-permute-start.1 = (f32[128,512]{1,0:T(8,128)}, f32[128,512]{1,0:T(8,128)S(1)}, u32[]{:S(2)}, u32[]{:S(2)}) collective-permute-start(f32[128,512]{1,0:T(8,128)} %c_ref.1), channel_id=1, source_target_pairs={{0,2},{2,4},{4,6},{6,0},{1,3},{3,5},{5,7},{7,1},{8,10},{10,12},{12... | collective-permute-start | bytes 786440 | tf_op jit(solution)/shard_map/ppermute | solution.py:193
  2.1 2.2 %collective-permute-start.2 = (f32[128,512]{1,0:T(8,128)}, f32[128,512]{1,0:T(8,128)}, u32[]{:S(2)}, u32[]{:S(2)}) collective-permute-start(f32[128,512]{1,0:T(8,128)} %c_ref.1), channel_id=1, source_target_pairs={{0,4},{2,6},{4,0},{6,2},{1,5},{3,7},{5,1},{7,3},{8,12},{10,14},{12... | collective-permute-start | bytes 786440 | tf_op jit(solution)/shard_map/ppermute | solution.py:193
  4.3 1.2 %collective-permute-start.3 = (f32[128,512]{1,0:T(8,128)}, f32[128,512]{1,0:T(8,128)}, u32[]{:S(2)}, u32[]{:S(2)}) collective-permute-start(f32[128,512]{1,0:T(8,128)} %c_ref.1), channel_id=1, source_target_pairs={{0,6},{2,0},{4,2},{6,4},{1,7},{3,1},{5,3},{7,5},{8,14},{10,8},{12,... | collective-permute-start | bytes 786440 | tf_op jit(solution)/shard_map/ppermute | solution.py:193
  5.5 2.2 %turn_kernel.1 = f32[32,4,16,128]{3,2,1,0:T(8,128)} custom-call(f32[128,512]{1,0:T(8,128)} %c_ref.1), custom_call_target="tpu_custom_call" | custom-call | bytes 1048576 | tf_op jit(solution)/shard_map/turn_kernel/pallas_call | solution.py:211
  7.7 14.1 %all-to-all-start = ((f32[128,16,128]{2,1,0:T(8,128)}), f32[128,16,128]{2,1,0:T(8,128)S(1)}, u32[]{:S(2)}, u32[]{:S(2)}) async-start(f32[128,16,128]{2,1,0:T(8,128)} %bitcast.4), calls=%async_computation | async-start | bytes 2097152 | tf_op jit(solution)/shard_map/all_to_all | solution.py:241
  21.8 0.1 add_multiply_fusion
  21.9 0.1 add.55
  22.0 0.1 select_reduce_fusion
  22.1 0.1 convert_reduce_fusion.owners
  22.3 0.1 compare_select_fusion.6
  22.4 3.6 %blocks_kernel.1.blocks.source = bf16[64,128,256]{2,1,0:T(8,128)(2,1)S(1)} custom-call(f32[32,128,128]{2,1,0:T(8,128)S(1)} %copy-done.1, f32[32,128,128]{2,1,0:T(8,128)} %collective-permute-done.4.h1), custom_call_target="tpu_custom_call" | custom-call | bytes 8388608 | tf_op jit(solution)/shard_map/blocks_kernel/pallas_call | solution.py:211
  26.0 4.8 %collective-permute-done.2.w2 = f32[128,512]{1,0:T(8,128)} collective-permute-done((f32[128,512]{1,0:T(8,128)}, f32[128,512]{1,0:T(8,128)}, u32[]{:S(2)}, u32[]{:S(2)}) %collective-permute-start.2) | collective-permute-done | bytes 262176 | tf_op jit(solution)/shard_map/ppermute | solution.py:193
  30.8 3.6 %collective-permute-done.3.w3 = f32[128,512]{1,0:T(8,128)} collective-permute-done((f32[128,512]{1,0:T(8,128)}, f32[128,512]{1,0:T(8,128)}, u32[]{:S(2)}, u32[]{:S(2)}) %collective-permute-start.3) | collective-permute-done | bytes 262176 | tf_op jit(solution)/shard_map/ppermute | solution.py:193
  34.4 4.5 %beta_kernel.1 = (f32[16,128,128]{2,1,0:T(8,128)S(1)}, f32[16,128,128]{2,1,0:T(8,128)S(1)}) custom-call(s32[4]{0:T(128)S(1)} %pad_add_fusion.where, s32[64]{0:T(128)S(1)} %get-tuple-element.32.cols, s32[64]{0:T(128)S(1)} %get-tuple-element.31.slots, f32[128,512]{1,0:T(8,128)S(1)} %copy-done.2, f32[128,512]{1,0:T(8,128)S(1)} %collective-permute-done.1.w1, ...), custom_call_target="tpu_custom_call" | custom-call | flops 40000000000 | bytes 7340032 | tf_op jit(solution)/shard_map/beta_kernel/pallas_call | solution.py:211
  38.9 0.1 collective-permute-start.5
  39.0 2.6 %collective-permute-done.5.got_ref = f32[16,128,128]{2,1,0:T(8,128)S(1)} collective-permute-done((f32[16,128,128]{2,1,0:T(8,128)S(1)}, f32[16,128,128]{2,1,0:T(8,128)S(1)}, u32[]{:S(2)}, u32[]{:S(2)}) %collective-permute-start.5) | collective-permute-done | bytes 1048608 | tf_op jit(solution)/shard_map/ppermute | solution.py:189
  41.7 0.2 cores_kernel.1
  41.9 1.3 %collective-permute-start.6 = (f32[4,128,128]{2,1,0:T(8,128)S(1)}, f32[4,128,128]{2,1,0:T(8,128)S(1)}, u32[]{:S(2)}, u32[]{:S(2)}) collective-permute-start(f32[4,128,128]{2,1,0:T(8,128)S(1)} %get-tuple-element.21), channel_id=1, source_target_pairs={{3,1},{4,2},{5,3},{6,4},{7,5},{11,9},{12,10},{13,11},{14,12},{15,1... | collective-permute-start | bytes 786440 | tf_op jit(solution)/shard_map/ppermute | solution.py:273
  43.1 4.6 %collective-permute-start.7 = (f32[4,128,128]{2,1,0:T(8,128)S(1)}, f32[4,128,128]{2,1,0:T(8,128)S(1)}, u32[]{:S(2)}, u32[]{:S(2)}) collective-permute-start(f32[4,128,128]{2,1,0:T(8,128)S(1)} %get-tuple-element.22), channel_id=1, source_target_pairs={{0,2},{1,3},{2,4},{3,5},{4,6},{8,10},{9,11},{10,12},{11,13},{12,14... | collective-permute-start | bytes 786440 | tf_op jit(solution)/shard_map/ppermute | solution.py:274
  47.7 0.7 collective-permute-start.8
  48.4 7.8 %all-to-all-done = f32[128,16,128]{2,1,0:T(8,128)S(1)} async-done(((f32[128,16,128]{2,1,0:T(8,128)}), f32[128,16,128]{2,1,0:T(8,128)S(1)}, u32[]{:S(2)}, u32[]{:S(2)}) %all-to-all-start) | async-done | bytes 1048608 | tf_op jit(solution)/shard_map/all_to_all | solution.py:241
  56.2 3.6 %alpha_kernel.1 = (f32[20,16,128]{2,1,0:T(8,128)S(1)}, f32[20,16,128]{2,1,0:T(8,128)S(1)}, f32[20,16,128]{2,1,0:T(8,128)S(1)}, f32[20,16,128]{2,1,0:T(8,128)S(1)}) custom-call(s32[4]{0:T(128)S(1)} %pad_add_fusion.where, s32[64]{0:T(128)S(1)} %get-tuple-element.32.cols, s32[64]{0:T(128)S(1)} %convert_reduce_fusion.owners, f32[32,64,128]{2,1,0:T(8,128)S(1)} %bitcast.6, ...), custom_call_target="tpu_custom_call" | custom-call | flops 40000000000 | bytes 7340032 | tf_op jit(solution)/shard_map/alpha_kernel/pallas_call | solution.py:211
  59.8 3.6 %collective-permute-start.9 = (f32[20,16,128]{2,1,0:T(8,128)S(1)}, f32[20,16,128]{2,1,0:T(8,128)S(1)}, u32[]{:S(2)}, u32[]{:S(2)}) collective-permute-start(f32[20,16,128]{2,1,0:T(8,128)S(1)} %get-tuple-element.27), channel_id=1, source_target_pairs={{0,2},{2,4},{4,6},{6,0},{1,3},{3,5},{5,7},{7,1},{8,10},{10,12},{12... | collective-permute-start | bytes 491528 | tf_op jit(solution)/shard_map/ppermute | solution.py:193
  63.4 0.9 collective-permute-start.10
  64.3 1.8 %collective-permute-start.11 = (f32[20,16,128]{2,1,0:T(8,128)S(1)}, f32[20,16,128]{2,1,0:T(8,128)S(1)}, u32[]{:S(2)}, u32[]{:S(2)}) collective-permute-start(f32[20,16,128]{2,1,0:T(8,128)S(1)} %get-tuple-element.29), channel_id=1, source_target_pairs={{0,6},{2,0},{4,2},{6,4},{1,7},{3,1},{5,3},{7,5},{8,14},{10,8},{12,... | collective-permute-start | bytes 491528 | tf_op jit(solution)/shard_map/ppermute | solution.py:193
  66.2 8.9 %collective-permute-done.9.p1 = f32[20,16,128]{2,1,0:T(8,128)S(1)} collective-permute-done((f32[20,16,128]{2,1,0:T(8,128)S(1)}, f32[20,16,128]{2,1,0:T(8,128)S(1)}, u32[]{:S(2)}, u32[]{:S(2)}) %collective-permute-start.9) | collective-permute-done | bytes 163872 | tf_op jit(solution)/shard_map/ppermute | solution.py:193
  75.0 2.5 %collective-permute-done.10.p2 = f32[20,16,128]{2,1,0:T(8,128)S(1)} collective-permute-done((f32[20,16,128]{2,1,0:T(8,128)S(1)}, f32[20,16,128]{2,1,0:T(8,128)S(1)}, u32[]{:S(2)}, u32[]{:S(2)}) %collective-permute-start.10) | collective-permute-done | bytes 163872 | tf_op jit(solution)/shard_map/ppermute | solution.py:193
  77.5 0.8 collective-permute-done.11.p3
  78.4 0.6 strings_kernel.1
  79.0 22.4 %all_to_all.14.back_ref = f32[32,16,128]{2,1,0:T(8,128)S(1)} all-to-all(f32[32,16,128]{2,1,0:T(8,128)S(1)} %strings_kernel.1), channel_id=1, replica_groups=mesh['y'=4,'h'=2,'x'=4,'z'=4,'c'=2] {'y','h','x'}, dimensions={0} | all-to-all | bytes 524288 | tf_op jit(solution)/shard_map/all_to_all | solution.py:301
  101.5 0.8 final_kernel.1
  (20 shorter events, 0.2 us)
Async XLA Ops:
  0.0 22.4 %copy-start.1 = (f32[32,128,128]{2,1,0:T(8,128)S(1)}, f32[32,128,128]{2,1,0:T(8,128)}, u32[]{:S(2)}) copy-start(f32[32,128,128]{2,1,0:T(8,128)} %h0.1) | copy-start | bytes 6291460
  0.0 22.3 %copy-start.3 = (s32[32]{0:T(128)S(1)}, s32[32]{0:T(128)}, u32[]{:S(2)}) copy-start(s32[32]{0:T(128)} %param.7) | copy-start | bytes 388
  0.0 22.0 %copy-start.4 = (s32[32]{0:T(128)S(1)}, s32[32]{0:T(128)}, u32[]{:S(2)}) copy-start(s32[32]{0:T(128)} %param.6) | copy-start | bytes 388
  0.0 22.4 %collective-permute-start.4 = (f32[32,128,128]{2,1,0:T(8,128)}, f32[32,128,128]{2,1,0:T(8,128)}, u32[]{:S(2)}, u32[]{:S(2)}) collective-permute-start(f32[32,128,128]{2,1,0:T(8,128)} %h0.1), channel_id=1, source_target_pairs={{0,1},{1,0},{2,3},{3,2},{4,5},{5,4},{6,7},{7,6},{8,9},{9,8},{10,11... | collective-permute-start | bytes 6291464 | tf_op jit(solution)/shard_map/ppermute | solution.py:189
  0.1 25.9 %collective-permute-start.1 = (f32[128,512]{1,0:T(8,128)}, f32[128,512]{1,0:T(8,128)S(1)}, u32[]{:S(2)}, u32[]{:S(2)}) collective-permute-start(f32[128,512]{1,0:T(8,128)} %c_ref.1), channel_id=1, source_target_pairs={{0,2},{2,4},{4,6},{6,0},{1,3},{3,5},{5,7},{7,1},{8,10},{10,12},{12... | collective-permute-start | bytes 786440 | tf_op jit(solution)/shard_map/ppermute | solution.py:193
  2.1 28.7 %collective-permute-start.2 = (f32[128,512]{1,0:T(8,128)}, f32[128,512]{1,0:T(8,128)}, u32[]{:S(2)}, u32[]{:S(2)}) collective-permute-start(f32[128,512]{1,0:T(8,128)} %c_ref.1), channel_id=1, source_target_pairs={{0,4},{2,6},{4,0},{6,2},{1,5},{3,7},{5,1},{7,3},{8,12},{10,14},{12... | collective-permute-start | bytes 786440 | tf_op jit(solution)/shard_map/ppermute | solution.py:193
  4.3 30.1 %collective-permute-start.3 = (f32[128,512]{1,0:T(8,128)}, f32[128,512]{1,0:T(8,128)}, u32[]{:S(2)}, u32[]{:S(2)}) collective-permute-start(f32[128,512]{1,0:T(8,128)} %c_ref.1), channel_id=1, source_target_pairs={{0,6},{2,0},{4,2},{6,4},{1,7},{3,1},{5,3},{7,5},{8,14},{10,8},{12,... | collective-permute-start | bytes 786440 | tf_op jit(solution)/shard_map/ppermute | solution.py:193
  5.5 16.8 %collective-permute-start = (s32[32]{0:T(128)}, s32[32]{0:T(128)S(1)}, u32[]{:S(2)}, u32[]{:S(2)}) collective-permute-start(s32[32]{0:T(128)} %param.7), channel_id=1, source_target_pairs={{0,1},{1,0},{2,3},{3,2},{4,5},{5,4},{6,7},{7,6},{8,9},{9,8},{10,11... | collective-permute-start | bytes 392 | tf_op jit(solution)/shard_map/ppermute | solution.py:189
  7.7 48.5 %all-to-all-start = ((f32[128,16,128]{2,1,0:T(8,128)}), f32[128,16,128]{2,1,0:T(8,128)S(1)}, u32[]{:S(2)}, u32[]{:S(2)}) async-start(f32[128,16,128]{2,1,0:T(8,128)} %bitcast.4), calls=%async_computation | async-start | bytes 2097152 | tf_op jit(solution)/shard_map/all_to_all | solution.py:241
  22.4 12.1 %copy-start.2 = (f32[128,512]{1,0:T(8,128)S(1)}, f32[128,512]{1,0:T(8,128)}, u32[]{:S(2)}) copy-start(f32[128,512]{1,0:T(8,128)} %c_ref.1) | copy-start | bytes 786436
  26.0 12.9 %copy-start = (bf16[64,128,256]{2,1,0:T(8,128)(2,1)}, bf16[64,128,256]{2,1,0:T(8,128)(2,1)S(1)}, u32[]{:S(2)}) copy-start(bf16[64,128,256]{2,1,0:T(8,128)(2,1)S(1)} %blocks_kernel.1.blocks.source) | copy-start | bytes 12582916
  38.9 2.7 %collective-permute-start.5 = (f32[16,128,128]{2,1,0:T(8,128)S(1)}, f32[16,128,128]{2,1,0:T(8,128)S(1)}, u32[]{:S(2)}, u32[]{:S(2)}) collective-permute-start(f32[16,128,128]{2,1,0:T(8,128)S(1)} %get-tuple-element.19), channel_id=1, source_target_pairs={{0,1},{1,0},{2,3},{3,2},{4,5},{5,4},{6,7},{7,6},{8,9},{9,8},{10,11... | collective-permute-start | bytes 3145736 | tf_op jit(solution)/shard_map/ppermute | solution.py:189
  41.9 22.5 %collective-permute-start.6 = (f32[4,128,128]{2,1,0:T(8,128)S(1)}, f32[4,128,128]{2,1,0:T(8,128)S(1)}, u32[]{:S(2)}, u32[]{:S(2)}) collective-permute-start(f32[4,128,128]{2,1,0:T(8,128)S(1)} %get-tuple-element.21), channel_id=1, source_target_pairs={{3,1},{4,2},{5,3},{6,4},{7,5},{11,9},{12,10},{13,11},{14,12},{15,1... | collective-permute-start | bytes 786440 | tf_op jit(solution)/shard_map/ppermute | solution.py:273
  43.1 22.9 %collective-permute-start.7 = (f32[4,128,128]{2,1,0:T(8,128)S(1)}, f32[4,128,128]{2,1,0:T(8,128)S(1)}, u32[]{:S(2)}, u32[]{:S(2)}) collective-permute-start(f32[4,128,128]{2,1,0:T(8,128)S(1)} %get-tuple-element.22), channel_id=1, source_target_pairs={{0,2},{1,3},{2,4},{3,5},{4,6},{8,10},{9,11},{10,12},{11,13},{12,14... | collective-permute-start | bytes 786440 | tf_op jit(solution)/shard_map/ppermute | solution.py:274
  47.7 18.4 %collective-permute-start.8 = (f32[4,128,128]{2,1,0:T(8,128)S(1)}, f32[4,128,128]{2,1,0:T(8,128)S(1)}, u32[]{:S(2)}, u32[]{:S(2)}) collective-permute-start(f32[4,128,128]{2,1,0:T(8,128)S(1)} %get-tuple-element.23), channel_id=1, source_target_pairs={{0,4},{7,3},{8,12},{15,11},{16,20},{23,19},{24,28},{31,27},{32,36}... | collective-permute-start | bytes 786440 | tf_op jit(solution)/shard_map/ppermute | solution.py:275
  59.8 15.3 %collective-permute-start.9 = (f32[20,16,128]{2,1,0:T(8,128)S(1)}, f32[20,16,128]{2,1,0:T(8,128)S(1)}, u32[]{:S(2)}, u32[]{:S(2)}) collective-permute-start(f32[20,16,128]{2,1,0:T(8,128)S(1)} %get-tuple-element.27), channel_id=1, source_target_pairs={{0,2},{2,4},{4,6},{6,0},{1,3},{3,5},{5,7},{7,1},{8,10},{10,12},{12... | collective-permute-start | bytes 491528 | tf_op jit(solution)/shard_map/ppermute | solution.py:193
  63.4 14.1 %collective-permute-start.10 = (f32[20,16,128]{2,1,0:T(8,128)S(1)}, f32[20,16,128]{2,1,0:T(8,128)S(1)}, u32[]{:S(2)}, u32[]{:S(2)}) collective-permute-start(f32[20,16,128]{2,1,0:T(8,128)S(1)} %get-tuple-element.28), channel_id=1, source_target_pairs={{0,4},{2,6},{4,0},{6,2},{1,5},{3,7},{5,1},{7,3},{8,12},{10,14},{12... | collective-permute-start | bytes 491528 | tf_op jit(solution)/shard_map/ppermute | solution.py:193
  64.3 14.0 %collective-permute-start.11 = (f32[20,16,128]{2,1,0:T(8,128)S(1)}, f32[20,16,128]{2,1,0:T(8,128)S(1)}, u32[]{:S(2)}, u32[]{:S(2)}) collective-permute-start(f32[20,16,128]{2,1,0:T(8,128)S(1)} %get-tuple-element.29), channel_id=1, source_target_pairs={{0,6},{2,0},{4,2},{6,4},{1,7},{3,1},{5,3},{7,5},{8,14},{10,8},{12,... | collective-permute-start | bytes 491528 | tf_op jit(solution)/shard_map/ppermute | solution.py:193

commit v13 on v11

--- a/solution.py
+++ b/solution.py
@@ -32,16 +32,17 @@
 def turn_kernel(c_ref, at_ref, buf, turned, sem, out_sem):
     loads, stores = [], []
     for t in range(4):
-        span = pl.ds(128 * t, 128)
-        loads.append(pltpu.make_async_copy(c_ref.at[:, span], buf.at[t], sem.at[t]))
+        span = pl.ds(32 * t, 32)
+        loads.append(pltpu.make_async_copy(c_ref.at[span], buf.at[span], sem.at[t]))
         for plane in range(4):
             home = at_ref.at[pl.ds(8 * t, 8), plane]
             stores.append(pltpu.make_async_copy(turned.at[t], home, out_sem.at[t, plane]))
     for load in loads:
         load.start()
-    for t, load in enumerate(loads):
+    for load in loads:
         load.wait()
-        turned[t] = jnp.transpose(buf[t]).reshape(8, 16, 128)
+    for t in range(4):
+        turned[t] = jnp.transpose(buf[:, 128 * t : 128 * (t + 1)]).reshape(8, 16, 128)
         for store in stores[4 * t : 4 * t + 4]:
             store.start()
     for store in stores:
@@ -229,7 +230,7 @@
         [HBM],
         pltpu.with_memory_space_constraint(coeffs, pltpu.HBM),
         scratch=[
-            pltpu.VMEM((4, 128, 128), F32),
+            pltpu.VMEM((128, 512), F32),
             pltpu.VMEM((4, 8, 16, 128), F32),
             pltpu.SemaphoreType.DMA((4,)),
             pltpu.SemaphoreType.DMA((4, 4)),

time: 103 us -> 103 us (level)
  no operation moved by 1% of the time
where the time goes in v13:
time: 103 us; the launch traced here: 102 us
  starting transfers between devices  32.5 us (32%)
  waiting for transfers between devices  29.9 us (29%)
  blocking collectives  22 us (21%)
  Pallas kernels  16.7 us (16%)
    all_to_all x1, blocking collectives, local(): back = lax.all_to_all(total, ROWS, 0, 0, tiled=True)  22 us
    ppermute x6, waiting for transfers between devices, shift(): return lax.ppermute(value, 'z', [(i, (i + by) % 4) for i in range(4)])  20.4 us
    pallas_call x8, Pallas kernels, call(): pl.pallas_call(kernel, out_shape=outs, in_specs=in_specs, out_specs=space...  16.7 us
    all_to_all x1, starting transfers between devices, local(): lax.all_to_all(at.reshape(2048, 128), ROWS + ('z',), 0, 0, tiled=True)  14.1 us
    ppermute x6, starting transfers between devices, shift(): return lax.ppermute(value, 'z', [(i, (i + by) % 4) for i in range(4)])  11.7 us
    all_to_all x1, waiting for transfers between devices, local(): lax.all_to_all(at.reshape(2048, 128), ROWS + ('z',), 0, 0, tiled=True)  6.83 us
    ppermute x1, starting transfers between devices, local(): up = lax.ppermute(up, ('z', 'c'), [(0, 2), (1, 3), (2, 4), (3, 5), (4, 6)])  4.55 us
    ppermute x3, waiting for transfers between devices, swap(): return lax.ppermute(value, 'c', [(0, 1), (1, 0)])  2.65 us
  transfers between devices with their start and end apart: 13, of which 7 were waited for; matrix products, arithmetic and copies ran while one was open for 1% of the time, Pallas kernels for 15%

profile of v13, /device:TPU:32, one launch (start us, length us, event | category | flops | bytes accessed | tf_op | source)
XLA Modules:
  0.0 101.8 jit_solution(8531604722284654516)
XLA Ops:
  0.0 0.1 collective-permute-start.4
  0.1 2.0 %collective-permute-start.1 = (f32[128,512]{1,0:T(8,128)}, f32[128,512]{1,0:T(8,128)S(1)}, u32[]{:S(2)}, u32[]{:S(2)}) collective-permute-start(f32[128,512]{1,0:T(8,128)} %c_ref.1), channel_id=1, source_target_pairs={{0,2},{2,4},{4,6},{6,0},{1,3},{3,5},{5,7},{7,1},{8,10},{10,12},{12... | collective-permute-start | bytes 786440 | tf_op jit(solution)/shard_map/ppermute | solution.py:192
  2.1 2.2 %collective-permute-start.2 = (f32[128,512]{1,0:T(8,128)}, f32[128,512]{1,0:T(8,128)}, u32[]{:S(2)}, u32[]{:S(2)}) collective-permute-start(f32[128,512]{1,0:T(8,128)} %c_ref.1), channel_id=1, source_target_pairs={{0,4},{2,6},{4,0},{6,2},{1,5},{3,7},{5,1},{7,3},{8,12},{10,14},{12... | collective-permute-start | bytes 786440 | tf_op jit(solution)/shard_map/ppermute | solution.py:192
  4.3 1.2 %collective-permute-start.3 = (f32[128,512]{1,0:T(8,128)}, f32[128,512]{1,0:T(8,128)}, u32[]{:S(2)}, u32[]{:S(2)}) collective-permute-start(f32[128,512]{1,0:T(8,128)} %c_ref.1), channel_id=1, source_target_pairs={{0,6},{2,0},{4,2},{6,4},{1,7},{3,1},{5,3},{7,5},{8,14},{10,8},{12,... | collective-permute-start | bytes 786440 | tf_op jit(solution)/shard_map/ppermute | solution.py:192
  5.5 2.2 %turn_kernel.1 = f32[32,4,16,128]{3,2,1,0:T(8,128)} custom-call(f32[128,512]{1,0:T(8,128)} %c_ref.1), custom_call_target="tpu_custom_call" | custom-call | bytes 1048576 | tf_op jit(solution)/shard_map/turn_kernel/pallas_call | solution.py:210
  7.7 14.1 %all-to-all-start = ((f32[128,16,128]{2,1,0:T(8,128)}), f32[128,16,128]{2,1,0:T(8,128)S(1)}, u32[]{:S(2)}, u32[]{:S(2)}) async-start(f32[128,16,128]{2,1,0:T(8,128)} %bitcast.4), calls=%async_computation | async-start | bytes 2097152 | tf_op jit(solution)/shard_map/all_to_all | solution.py:240
  22.0 0.1 add.55
  22.1 0.1 select_reduce_fusion
  22.2 0.1 convert_reduce_fusion.owners
  22.2 0.1 pad_add_fusion.where
  22.3 0.1 compare_select_fusion.6
  22.5 3.6 %blocks_kernel.1.blocks.source = bf16[64,128,256]{2,1,0:T(8,128)(2,1)S(1)} custom-call(f32[32,128,128]{2,1,0:T(8,128)S(1)} %copy-done.1, f32[32,128,128]{2,1,0:T(8,128)} %collective-permute-done.4.h1), custom_call_target="tpu_custom_call" | custom-call | bytes 8388608 | tf_op jit(solution)/shard_map/blocks_kernel/pallas_call | solution.py:210
  26.1 4.6 %collective-permute-done.2.w2 = f32[128,512]{1,0:T(8,128)} collective-permute-done((f32[128,512]{1,0:T(8,128)}, f32[128,512]{1,0:T(8,128)}, u32[]{:S(2)}, u32[]{:S(2)}) %collective-permute-start.2) | collective-permute-done | bytes 262176 | tf_op jit(solution)/shard_map/ppermute | solution.py:192
  30.7 3.5 %collective-permute-done.3.w3 = f32[128,512]{1,0:T(8,128)} collective-permute-done((f32[128,512]{1,0:T(8,128)}, f32[128,512]{1,0:T(8,128)}, u32[]{:S(2)}, u32[]{:S(2)}) %collective-permute-start.3) | collective-permute-done | bytes 262176 | tf_op jit(solution)/shard_map/ppermute | solution.py:192
  34.2 5.6 %beta_kernel.1 = (f32[16,128,128]{2,1,0:T(8,128)S(1)}, f32[16,128,128]{2,1,0:T(8,128)S(1)}) custom-call(s32[4]{0:T(128)S(1)} %pad_add_fusion.where, s32[64]{0:T(128)S(1)} %get-tuple-element.32.cols, s32[64]{0:T(128)S(1)} %get-tuple-element.31.slots, f32[128,512]{1,0:T(8,128)S(1)} %copy-done.2, f32[128,512]{1,0:T(8,128)S(1)} %collective-permute-done.1.w1, ...), custom_call_target="tpu_custom_call" | custom-call | flops 40000000000 | bytes 7340032 | tf_op jit(solution)/shard_map/beta_kernel/pallas_call | solution.py:210
  39.9 0.1 collective-permute-start.5
  40.0 2.6 %collective-permute-done.5.got_ref = f32[16,128,128]{2,1,0:T(8,128)S(1)} collective-permute-done((f32[16,128,128]{2,1,0:T(8,128)S(1)}, f32[16,128,128]{2,1,0:T(8,128)S(1)}, u32[]{:S(2)}, u32[]{:S(2)}) %collective-permute-start.5) | collective-permute-done | bytes 1048608 | tf_op jit(solution)/shard_map/ppermute | solution.py:188
  42.6 0.2 cores_kernel.1
  42.8 1.3 %collective-permute-start.6 = (f32[4,128,128]{2,1,0:T(8,128)S(1)}, f32[4,128,128]{2,1,0:T(8,128)S(1)}, u32[]{:S(2)}, u32[]{:S(2)}) collective-permute-start(f32[4,128,128]{2,1,0:T(8,128)S(1)} %get-tuple-element.21), channel_id=1, source_target_pairs={{3,1},{4,2},{5,3},{6,4},{7,5},{11,9},{12,10},{13,11},{14,12},{15,1... | collective-permute-start | bytes 786440 | tf_op jit(solution)/shard_map/ppermute | solution.py:272
  44.1 4.6 %collective-permute-start.7 = (f32[4,128,128]{2,1,0:T(8,128)S(1)}, f32[4,128,128]{2,1,0:T(8,128)S(1)}, u32[]{:S(2)}, u32[]{:S(2)}) collective-permute-start(f32[4,128,128]{2,1,0:T(8,128)S(1)} %get-tuple-element.22), channel_id=1, source_target_pairs={{0,2},{1,3},{2,4},{3,5},{4,6},{8,10},{9,11},{10,12},{11,13},{12,14... | collective-permute-start | bytes 786440 | tf_op jit(solution)/shard_map/ppermute | solution.py:273
  48.6 0.7 collective-permute-start.8
  49.3 6.8 %all-to-all-done = f32[128,16,128]{2,1,0:T(8,128)S(1)} async-done(((f32[128,16,128]{2,1,0:T(8,128)}), f32[128,16,128]{2,1,0:T(8,128)S(1)}, u32[]{:S(2)}, u32[]{:S(2)}) %all-to-all-start) | async-done | bytes 1048608 | tf_op jit(solution)/shard_map/all_to_all | solution.py:240
  56.2 3.6 %alpha_kernel.1 = (f32[20,16,128]{2,1,0:T(8,128)S(1)}, f32[20,16,128]{2,1,0:T(8,128)S(1)}, f32[20,16,128]{2,1,0:T(8,128)S(1)}, f32[20,16,128]{2,1,0:T(8,128)S(1)}) custom-call(s32[4]{0:T(128)S(1)} %pad_add_fusion.where, s32[64]{0:T(128)S(1)} %get-tuple-element.32.cols, s32[64]{0:T(128)S(1)} %convert_reduce_fusion.owners, f32[32,64,128]{2,1,0:T(8,128)S(1)} %bitcast.6, ...), custom_call_target="tpu_custom_call" | custom-call | flops 40000000000 | bytes 7340032 | tf_op jit(solution)/shard_map/alpha_kernel/pallas_call | solution.py:210
  59.8 3.7 %collective-permute-start.9 = (f32[20,16,128]{2,1,0:T(8,128)S(1)}, f32[20,16,128]{2,1,0:T(8,128)S(1)}, u32[]{:S(2)}, u32[]{:S(2)}) collective-permute-start(f32[20,16,128]{2,1,0:T(8,128)S(1)} %get-tuple-element.27), channel_id=1, source_target_pairs={{0,2},{2,4},{4,6},{6,0},{1,3},{3,5},{5,7},{7,1},{8,10},{10,12},{12... | collective-permute-start | bytes 491528 | tf_op jit(solution)/shard_map/ppermute | solution.py:192
  63.4 0.9 collective-permute-start.10
  64.3 1.8 %collective-permute-start.11 = (f32[20,16,128]{2,1,0:T(8,128)S(1)}, f32[20,16,128]{2,1,0:T(8,128)S(1)}, u32[]{:S(2)}, u32[]{:S(2)}) collective-permute-start(f32[20,16,128]{2,1,0:T(8,128)S(1)} %get-tuple-element.29), channel_id=1, source_target_pairs={{0,6},{2,0},{4,2},{6,4},{1,7},{3,1},{5,3},{7,5},{8,14},{10,8},{12,... | collective-permute-start | bytes 491528 | tf_op jit(solution)/shard_map/ppermute | solution.py:192
  66.2 8.9 %collective-permute-done.9.p1 = f32[20,16,128]{2,1,0:T(8,128)S(1)} collective-permute-done((f32[20,16,128]{2,1,0:T(8,128)S(1)}, f32[20,16,128]{2,1,0:T(8,128)S(1)}, u32[]{:S(2)}, u32[]{:S(2)}) %collective-permute-start.9) | collective-permute-done | bytes 163872 | tf_op jit(solution)/shard_map/ppermute | solution.py:192
  75.0 2.6 %collective-permute-done.10.p2 = f32[20,16,128]{2,1,0:T(8,128)S(1)} collective-permute-done((f32[20,16,128]{2,1,0:T(8,128)S(1)}, f32[20,16,128]{2,1,0:T(8,128)S(1)}, u32[]{:S(2)}, u32[]{:S(2)}) %collective-permute-start.10) | collective-permute-done | bytes 163872 | tf_op jit(solution)/shard_map/ppermute | solution.py:192
  77.6 0.8 collective-permute-done.11.p3
  78.4 0.6 strings_kernel.1
  79.0 22.0 %all_to_all.14.back_ref = f32[32,16,128]{2,1,0:T(8,128)S(1)} all-to-all(f32[32,16,128]{2,1,0:T(8,128)S(1)} %strings_kernel.1), channel_id=1, replica_groups=mesh['y'=4,'h'=2,'x'=4,'z'=4,'c'=2] {'y','h','x'}, dimensions={0} | all-to-all | bytes 524288 | tf_op jit(solution)/shard_map/all_to_all | solution.py:300
  101.0 0.8 final_kernel.1
  (20 shorter events, 0.2 us)
Async XLA Ops:
  0.0 22.4 %copy-start.1 = (f32[32,128,128]{2,1,0:T(8,128)S(1)}, f32[32,128,128]{2,1,0:T(8,128)}, u32[]{:S(2)}) copy-start(f32[32,128,128]{2,1,0:T(8,128)} %h0.1) | copy-start | bytes 6291460
  0.0 22.3 %copy-start.3 = (s32[32]{0:T(128)S(1)}, s32[32]{0:T(128)}, u32[]{:S(2)}) copy-start(s32[32]{0:T(128)} %param.7) | copy-start | bytes 388
  0.0 22.1 %copy-start.4 = (s32[32]{0:T(128)S(1)}, s32[32]{0:T(128)}, u32[]{:S(2)}) copy-start(s32[32]{0:T(128)} %param.6) | copy-start | bytes 388
  0.0 22.4 %collective-permute-start.4 = (f32[32,128,128]{2,1,0:T(8,128)}, f32[32,128,128]{2,1,0:T(8,128)}, u32[]{:S(2)}, u32[]{:S(2)}) collective-permute-start(f32[32,128,128]{2,1,0:T(8,128)} %h0.1), channel_id=1, source_target_pairs={{0,1},{1,0},{2,3},{3,2},{4,5},{5,4},{6,7},{7,6},{8,9},{9,8},{10,11... | collective-permute-start | bytes 6291464 | tf_op jit(solution)/shard_map/ppermute | solution.py:188
  0.1 26.0 %collective-permute-start.1 = (f32[128,512]{1,0:T(8,128)}, f32[128,512]{1,0:T(8,128)S(1)}, u32[]{:S(2)}, u32[]{:S(2)}) collective-permute-start(f32[128,512]{1,0:T(8,128)} %c_ref.1), channel_id=1, source_target_pairs={{0,2},{2,4},{4,6},{6,0},{1,3},{3,5},{5,7},{7,1},{8,10},{10,12},{12... | collective-permute-start | bytes 786440 | tf_op jit(solution)/shard_map/ppermute | solution.py:192
  2.1 28.6 %collective-permute-start.2 = (f32[128,512]{1,0:T(8,128)}, f32[128,512]{1,0:T(8,128)}, u32[]{:S(2)}, u32[]{:S(2)}) collective-permute-start(f32[128,512]{1,0:T(8,128)} %c_ref.1), channel_id=1, source_target_pairs={{0,4},{2,6},{4,0},{6,2},{1,5},{3,7},{5,1},{7,3},{8,12},{10,14},{12... | collective-permute-start | bytes 786440 | tf_op jit(solution)/shard_map/ppermute | solution.py:192
  4.3 29.9 %collective-permute-start.3 = (f32[128,512]{1,0:T(8,128)}, f32[128,512]{1,0:T(8,128)}, u32[]{:S(2)}, u32[]{:S(2)}) collective-permute-start(f32[128,512]{1,0:T(8,128)} %c_ref.1), channel_id=1, source_target_pairs={{0,6},{2,0},{4,2},{6,4},{1,7},{3,1},{5,3},{7,5},{8,14},{10,8},{12,... | collective-permute-start | bytes 786440 | tf_op jit(solution)/shard_map/ppermute | solution.py:192
  5.5 16.8 %collective-permute-start = (s32[32]{0:T(128)}, s32[32]{0:T(128)S(1)}, u32[]{:S(2)}, u32[]{:S(2)}) collective-permute-start(s32[32]{0:T(128)} %param.7), channel_id=1, source_target_pairs={{0,1},{1,0},{2,3},{3,2},{4,5},{5,4},{6,7},{7,6},{8,9},{9,8},{10,11... | collective-permute-start | bytes 392 | tf_op jit(solution)/shard_map/ppermute | solution.py:188
  7.7 48.5 %all-to-all-start = ((f32[128,16,128]{2,1,0:T(8,128)}), f32[128,16,128]{2,1,0:T(8,128)S(1)}, u32[]{:S(2)}, u32[]{:S(2)}) async-start(f32[128,16,128]{2,1,0:T(8,128)} %bitcast.4), calls=%async_computation | async-start | bytes 2097152 | tf_op jit(solution)/shard_map/all_to_all | solution.py:240
  22.4 11.8 %copy-start.2 = (f32[128,512]{1,0:T(8,128)S(1)}, f32[128,512]{1,0:T(8,128)}, u32[]{:S(2)}) copy-start(f32[128,512]{1,0:T(8,128)} %c_ref.1) | copy-start | bytes 786436
  26.1 13.8 %copy-start = (bf16[64,128,256]{2,1,0:T(8,128)(2,1)}, bf16[64,128,256]{2,1,0:T(8,128)(2,1)S(1)}, u32[]{:S(2)}) copy-start(bf16[64,128,256]{2,1,0:T(8,128)(2,1)S(1)} %blocks_kernel.1.blocks.source) | copy-start | bytes 12582916
  39.9 2.7 %collective-permute-start.5 = (f32[16,128,128]{2,1,0:T(8,128)S(1)}, f32[16,128,128]{2,1,0:T(8,128)S(1)}, u32[]{:S(2)}, u32[]{:S(2)}) collective-permute-start(f32[16,128,128]{2,1,0:T(8,128)S(1)} %get-tuple-element.19), channel_id=1, source_target_pairs={{0,1},{1,0},{2,3},{3,2},{4,5},{5,4},{6,7},{7,6},{8,9},{9,8},{10,11... | collective-permute-start | bytes 3145736 | tf_op jit(solution)/shard_map/ppermute | solution.py:188
  42.8 21.5 %collective-permute-start.6 = (f32[4,128,128]{2,1,0:T(8,128)S(1)}, f32[4,128,128]{2,1,0:T(8,128)S(1)}, u32[]{:S(2)}, u32[]{:S(2)}) collective-permute-start(f32[4,128,128]{2,1,0:T(8,128)S(1)} %get-tuple-element.21), channel_id=1, source_target_pairs={{3,1},{4,2},{5,3},{6,4},{7,5},{11,9},{12,10},{13,11},{14,12},{15,1... | collective-permute-start | bytes 786440 | tf_op jit(solution)/shard_map/ppermute | solution.py:272
  44.1 22.0 %collective-permute-start.7 = (f32[4,128,128]{2,1,0:T(8,128)S(1)}, f32[4,128,128]{2,1,0:T(8,128)S(1)}, u32[]{:S(2)}, u32[]{:S(2)}) collective-permute-start(f32[4,128,128]{2,1,0:T(8,128)S(1)} %get-tuple-element.22), channel_id=1, source_target_pairs={{0,2},{1,3},{2,4},{3,5},{4,6},{8,10},{9,11},{10,12},{11,13},{12,14... | collective-permute-start | bytes 786440 | tf_op jit(solution)/shard_map/ppermute | solution.py:273
  48.6 17.5 %collective-permute-start.8 = (f32[4,128,128]{2,1,0:T(8,128)S(1)}, f32[4,128,128]{2,1,0:T(8,128)S(1)}, u32[]{:S(2)}, u32[]{:S(2)}) collective-permute-start(f32[4,128,128]{2,1,0:T(8,128)S(1)} %get-tuple-element.23), channel_id=1, source_target_pairs={{0,4},{7,3},{8,12},{15,11},{16,20},{23,19},{24,28},{31,27},{32,36}... | collective-permute-start | bytes 786440 | tf_op jit(solution)/shard_map/ppermute | solution.py:274
  59.8 15.3 %collective-permute-start.9 = (f32[20,16,128]{2,1,0:T(8,128)S(1)}, f32[20,16,128]{2,1,0:T(8,128)S(1)}, u32[]{:S(2)}, u32[]{:S(2)}) collective-permute-start(f32[20,16,128]{2,1,0:T(8,128)S(1)} %get-tuple-element.27), channel_id=1, source_target_pairs={{0,2},{2,4},{4,6},{6,0},{1,3},{3,5},{5,7},{7,1},{8,10},{10,12},{12... | collective-permute-start | bytes 491528 | tf_op jit(solution)/shard_map/ppermute | solution.py:192
  63.4 14.2 %collective-permute-start.10 = (f32[20,16,128]{2,1,0:T(8,128)S(1)}, f32[20,16,128]{2,1,0:T(8,128)S(1)}, u32[]{:S(2)}, u32[]{:S(2)}) collective-permute-start(f32[20,16,128]{2,1,0:T(8,128)S(1)} %get-tuple-element.28), channel_id=1, source_target_pairs={{0,4},{2,6},{4,0},{6,2},{1,5},{3,7},{5,1},{7,3},{8,12},{10,14},{12... | collective-permute-start | bytes 491528 | tf_op jit(solution)/shard_map/ppermute | solution.py:192
  64.3 14.1 %collective-permute-start.11 = (f32[20,16,128]{2,1,0:T(8,128)S(1)}, f32[20,16,128]{2,1,0:T(8,128)S(1)}, u32[]{:S(2)}, u32[]{:S(2)}) collective-permute-start(f32[20,16,128]{2,1,0:T(8,128)S(1)} %get-tuple-element.29), channel_id=1, source_target_pairs={{0,6},{2,0},{4,2},{6,4},{1,7},{3,1},{5,3},{7,5},{8,14},{10,8},{12,... | collective-permute-start | bytes 491528 | tf_op jit(solution)/shard_map/ppermute | solution.py:192

commit v14 on v13

--- a/solution.py
+++ b/solution.py
@@ -96,7 +96,8 @@
         return count + jnp.where(slots[n] < TRASH, 1, 0)
 
     count = lax.fori_loop(0, 64, note, 0)
-    list_ref[count] = 0
+    for u in range(3):
+        list_ref[count + u] = 0
     for k, load in enumerate(loads):
         home = 4 * jnp.bitwise_and(z - k + 4, 3)
         load.wait()
@@ -105,14 +106,14 @@
             stack[home + t, :128] = high
             stack[home + t, 128:] = low
 
-    @pl.loop(0, lax.shift_right_logical(count + 1, 1))
+    @pl.loop(0, lax.shift_right_logical(count + 3, 2))
     def _(step):
         terms = []
-        for u in range(2):
-            n = list_ref[2 * step + u]
+        for u in range(4):
+            n = list_ref[4 * step + u]
             column = cols[n]
             left = stack[4 * lax.shift_right_logical(column, 3) + jnp.bitwise_and(column, 3)]
-            slot = jnp.where(2 * step + u < count, slots[n], TRASH)
+            slot = jnp.where(4 * step + u < count, slots[n], TRASH)
             terms.append((slot, product(left, blocks[n])))
         for slot, term in terms:
             acc[slot] += term
@@ -222,7 +223,8 @@
 def local(coeffs, hblocks, hcount, hcols):
     z, c = lax.axis_index("z"), lax.axis_index("c")
     where = jnp.stack([z, z, z, c]).astype(jnp.int32)
-    rows = [coeffs] + [shift(coeffs, k) for k in (1, 2, 3)]
+    across = shift(coeffs, 2)
+    rows = [coeffs, shift(coeffs, 1), across, shift(coeffs, 3)]
     cols, owners, slots = tables(hcount, hcols, z, c)
     at = call(
         turn_kernel,

time: 103 us -> 103 us (level)
  Pallas kernels: 16.7 us -> 15.2 us
  waiting for transfers between devices: 29.9 us -> 31.3 us
    pallas_call x8, Pallas kernels: 16.7 us -> 15.2 us  [call(): pl.pallas_call(kernel, out_shape=outs, in_specs=in_specs, out_specs=space...]
    all_to_all x1, waiting for transfers between devices: 6.83 us -> 8.27 us  [local(): lax.all_to_all(at.reshape(2048, 128), ROWS + ('z',), 0, 0, tiled=True)]
  transfers between devices with their start and end apart: 13 -> 13, of which waited for: 7 -> 7; matrix products, arithmetic and copies ran while one was open for 1% -> 1% of each run, Pallas kernels for 15% -> 13%
where the time goes in v14:
time: 103 us; the launch traced here: 102 us
  starting transfers between devices  32.5 us (32%)
  waiting for transfers between devices  31.3 us (30%)
  blocking collectives  22.5 us (22%)
  Pallas kernels  15.2 us (15%)
    all_to_all x1, blocking collectives, local(): back = lax.all_to_all(total, ROWS, 0, 0, tiled=True)  22.5 us
    ppermute x6, waiting for transfers between devices, shift(): return lax.ppermute(value, 'z', [(i, (i + by) % 4) for i in range(4)])  20.4 us
    pallas_call x8, Pallas kernels, call(): pl.pallas_call(kernel, out_shape=outs, in_specs=in_specs, out_specs=space...  15.2 us
    all_to_all x1, starting transfers between devices, local(): lax.all_to_all(at.reshape(2048, 128), ROWS + ('z',), 0, 0, tiled=True)  14.1 us
    ppermute x6, starting transfers between devices, shift(): return lax.ppermute(value, 'z', [(i, (i + by) % 4) for i in range(4)])  11.7 us
    all_to_all x1, waiting for transfers between devices, local(): lax.all_to_all(at.reshape(2048, 128), ROWS + ('z',), 0, 0, tiled=True)  8.27 us
    ppermute x1, starting transfers between devices, local(): up = lax.ppermute(up, ('z', 'c'), [(0, 2), (1, 3), (2, 4), (3, 5), (4, 6)])  4.55 us
    ppermute x3, waiting for transfers between devices, swap(): return lax.ppermute(value, 'c', [(0, 1), (1, 0)])  2.65 us
  transfers between devices with their start and end apart: 13, of which 7 were waited for; matrix products, arithmetic and copies ran while one was open for 1% of the time, Pallas kernels for 13%

profile of v14, /device:TPU:32, one launch (start us, length us, event | category | flops | bytes accessed | tf_op | source)
XLA Modules:
  0.0 102.3 jit_solution(16733672419886541768)
XLA Ops:
  0.0 0.1 collective-permute-start.4
  0.1 2.0 %collective-permute-start.1 = (f32[128,512]{1,0:T(8,128)}, f32[128,512]{1,0:T(8,128)S(1)}, u32[]{:S(2)}, u32[]{:S(2)}) collective-permute-start(f32[128,512]{1,0:T(8,128)} %c_ref.1), channel_id=1, source_target_pairs={{0,2},{2,4},{4,6},{6,0},{1,3},{3,5},{5,7},{7,1},{8,10},{10,12},{12... | collective-permute-start | bytes 786440 | tf_op jit(solution)/shard_map/ppermute | solution.py:193
  2.1 2.2 %collective-permute-start.2 = (f32[128,512]{1,0:T(8,128)}, f32[128,512]{1,0:T(8,128)}, u32[]{:S(2)}, u32[]{:S(2)}) collective-permute-start(f32[128,512]{1,0:T(8,128)} %c_ref.1), channel_id=1, source_target_pairs={{0,4},{2,6},{4,0},{6,2},{1,5},{3,7},{5,1},{7,3},{8,12},{10,14},{12... | collective-permute-start | bytes 786440 | tf_op jit(solution)/shard_map/ppermute | solution.py:193
  4.3 1.2 %collective-permute-start.3 = (f32[128,512]{1,0:T(8,128)}, f32[128,512]{1,0:T(8,128)}, u32[]{:S(2)}, u32[]{:S(2)}) collective-permute-start(f32[128,512]{1,0:T(8,128)} %c_ref.1), channel_id=1, source_target_pairs={{0,6},{2,0},{4,2},{6,4},{1,7},{3,1},{5,3},{7,5},{8,14},{10,8},{12,... | collective-permute-start | bytes 786440 | tf_op jit(solution)/shard_map/ppermute | solution.py:193
  5.5 2.2 %turn_kernel.1 = f32[32,4,16,128]{3,2,1,0:T(8,128)} custom-call(f32[128,512]{1,0:T(8,128)} %c_ref.1), custom_call_target="tpu_custom_call" | custom-call | bytes 1048576 | tf_op jit(solution)/shard_map/turn_kernel/pallas_call | solution.py:211
  7.7 14.1 %all-to-all-start = ((f32[128,16,128]{2,1,0:T(8,128)}), f32[128,16,128]{2,1,0:T(8,128)S(1)}, u32[]{:S(2)}, u32[]{:S(2)}) async-start(f32[128,16,128]{2,1,0:T(8,128)} %bitcast.4), calls=%async_computation | async-start | bytes 2097152 | tf_op jit(solution)/shard_map/all_to_all | solution.py:242
  21.8 0.1 add_multiply_fusion
  22.0 0.1 add.55
  22.1 0.1 select_reduce_fusion
  22.2 0.1 convert_reduce_fusion.owners
  22.3 0.1 compare_select_fusion.6
  22.5 3.6 %blocks_kernel.1.blocks.source = bf16[64,128,256]{2,1,0:T(8,128)(2,1)S(1)} custom-call(f32[32,128,128]{2,1,0:T(8,128)S(1)} %copy-done.1, f32[32,128,128]{2,1,0:T(8,128)} %collective-permute-done.4.h1), custom_call_target="tpu_custom_call" | custom-call | bytes 8388608 | tf_op jit(solution)/shard_map/blocks_kernel/pallas_call | solution.py:211
  26.1 4.6 %collective-permute-done.2.w2 = f32[128,512]{1,0:T(8,128)} collective-permute-done((f32[128,512]{1,0:T(8,128)}, f32[128,512]{1,0:T(8,128)}, u32[]{:S(2)}, u32[]{:S(2)}) %collective-permute-start.2) | collective-permute-done | bytes 262176 | tf_op jit(solution)/shard_map/ppermute | solution.py:193
  30.7 3.5 %collective-permute-done.3.w3 = f32[128,512]{1,0:T(8,128)} collective-permute-done((f32[128,512]{1,0:T(8,128)}, f32[128,512]{1,0:T(8,128)}, u32[]{:S(2)}, u32[]{:S(2)}) %collective-permute-start.3) | collective-permute-done | bytes 262176 | tf_op jit(solution)/shard_map/ppermute | solution.py:193
  34.2 4.2 %beta_kernel.1 = (f32[16,128,128]{2,1,0:T(8,128)S(1)}, f32[16,128,128]{2,1,0:T(8,128)S(1)}) custom-call(s32[4]{0:T(128)S(1)} %pad_add_fusion.where, s32[64]{0:T(128)S(1)} %get-tuple-element.32.cols, s32[64]{0:T(128)S(1)} %get-tuple-element.31.slots, f32[128,512]{1,0:T(8,128)S(1)} %copy-done.2, f32[128,512]{1,0:T(8,128)S(1)} %collective-permute-done.1.w1, ...), custom_call_target="tpu_custom_call" | custom-call | flops 40000000000 | bytes 7340032 | tf_op jit(solution)/shard_map/beta_kernel/pallas_call | solution.py:211
  38.4 0.1 collective-permute-start.5
  38.5 2.6 %collective-permute-done.5.got_ref = f32[16,128,128]{2,1,0:T(8,128)S(1)} collective-permute-done((f32[16,128,128]{2,1,0:T(8,128)S(1)}, f32[16,128,128]{2,1,0:T(8,128)S(1)}, u32[]{:S(2)}, u32[]{:S(2)}) %collective-permute-start.5) | collective-permute-done | bytes 1048608 | tf_op jit(solution)/shard_map/ppermute | solution.py:189
  41.2 0.2 cores_kernel.1
  41.3 1.3 %collective-permute-start.6 = (f32[4,128,128]{2,1,0:T(8,128)S(1)}, f32[4,128,128]{2,1,0:T(8,128)S(1)}, u32[]{:S(2)}, u32[]{:S(2)}) collective-permute-start(f32[4,128,128]{2,1,0:T(8,128)S(1)} %get-tuple-element.21), channel_id=1, source_target_pairs={{3,1},{4,2},{5,3},{6,4},{7,5},{11,9},{12,10},{13,11},{14,12},{15,1... | collective-permute-start | bytes 786440 | tf_op jit(solution)/shard_map/ppermute | solution.py:274
  42.6 4.6 %collective-permute-start.7 = (f32[4,128,128]{2,1,0:T(8,128)S(1)}, f32[4,128,128]{2,1,0:T(8,128)S(1)}, u32[]{:S(2)}, u32[]{:S(2)}) collective-permute-start(f32[4,128,128]{2,1,0:T(8,128)S(1)} %get-tuple-element.22), channel_id=1, source_target_pairs={{0,2},{1,3},{2,4},{3,5},{4,6},{8,10},{9,11},{10,12},{11,13},{12,14... | collective-permute-start | bytes 786440 | tf_op jit(solution)/shard_map/ppermute | solution.py:275
  47.2 0.7 collective-permute-start.8
  47.9 8.3 %all-to-all-done = f32[128,16,128]{2,1,0:T(8,128)S(1)} async-done(((f32[128,16,128]{2,1,0:T(8,128)}), f32[128,16,128]{2,1,0:T(8,128)S(1)}, u32[]{:S(2)}, u32[]{:S(2)}) %all-to-all-start) | async-done | bytes 1048608 | tf_op jit(solution)/shard_map/all_to_all | solution.py:242
  56.2 3.6 %alpha_kernel.1 = (f32[20,16,128]{2,1,0:T(8,128)S(1)}, f32[20,16,128]{2,1,0:T(8,128)S(1)}, f32[20,16,128]{2,1,0:T(8,128)S(1)}, f32[20,16,128]{2,1,0:T(8,128)S(1)}) custom-call(s32[4]{0:T(128)S(1)} %pad_add_fusion.where, s32[64]{0:T(128)S(1)} %get-tuple-element.32.cols, s32[64]{0:T(128)S(1)} %convert_reduce_fusion.owners, f32[32,64,128]{2,1,0:T(8,128)S(1)} %bitcast.6, ...), custom_call_target="tpu_custom_call" | custom-call | flops 40000000000 | bytes 7340032 | tf_op jit(solution)/shard_map/alpha_kernel/pallas_call | solution.py:211
  59.8 3.7 %collective-permute-start.9 = (f32[20,16,128]{2,1,0:T(8,128)S(1)}, f32[20,16,128]{2,1,0:T(8,128)S(1)}, u32[]{:S(2)}, u32[]{:S(2)}) collective-permute-start(f32[20,16,128]{2,1,0:T(8,128)S(1)} %get-tuple-element.27), channel_id=1, source_target_pairs={{0,2},{2,4},{4,6},{6,0},{1,3},{3,5},{5,7},{7,1},{8,10},{10,12},{12... | collective-permute-start | bytes 491528 | tf_op jit(solution)/shard_map/ppermute | solution.py:193
  63.4 0.9 collective-permute-start.10
  64.3 1.8 %collective-permute-start.11 = (f32[20,16,128]{2,1,0:T(8,128)S(1)}, f32[20,16,128]{2,1,0:T(8,128)S(1)}, u32[]{:S(2)}, u32[]{:S(2)}) collective-permute-start(f32[20,16,128]{2,1,0:T(8,128)S(1)} %get-tuple-element.29), channel_id=1, source_target_pairs={{0,6},{2,0},{4,2},{6,4},{1,7},{3,1},{5,3},{7,5},{8,14},{10,8},{12,... | collective-permute-start | bytes 491528 | tf_op jit(solution)/shard_map/ppermute | solution.py:193
  66.2 8.9 %collective-permute-done.9.p1 = f32[20,16,128]{2,1,0:T(8,128)S(1)} collective-permute-done((f32[20,16,128]{2,1,0:T(8,128)S(1)}, f32[20,16,128]{2,1,0:T(8,128)S(1)}, u32[]{:S(2)}, u32[]{:S(2)}) %collective-permute-start.9) | collective-permute-done | bytes 163872 | tf_op jit(solution)/shard_map/ppermute | solution.py:193
  75.1 2.5 %collective-permute-done.10.p2 = f32[20,16,128]{2,1,0:T(8,128)S(1)} collective-permute-done((f32[20,16,128]{2,1,0:T(8,128)S(1)}, f32[20,16,128]{2,1,0:T(8,128)S(1)}, u32[]{:S(2)}, u32[]{:S(2)}) %collective-permute-start.10) | collective-permute-done | bytes 163872 | tf_op jit(solution)/shard_map/ppermute | solution.py:193
  77.5 0.8 collective-permute-done.11.p3
  78.4 0.6 strings_kernel.1
  79.0 22.5 %all_to_all.14.back_ref = f32[32,16,128]{2,1,0:T(8,128)S(1)} all-to-all(f32[32,16,128]{2,1,0:T(8,128)S(1)} %strings_kernel.1), channel_id=1, replica_groups=mesh['y'=4,'h'=2,'x'=4,'z'=4,'c'=2] {'y','h','x'}, dimensions={0} | all-to-all | bytes 524288 | tf_op jit(solution)/shard_map/all_to_all | solution.py:302
  101.5 0.8 final_kernel.1
  (20 shorter events, 0.2 us)
Async XLA Ops:
  0.0 22.4 %copy-start.1 = (f32[32,128,128]{2,1,0:T(8,128)S(1)}, f32[32,128,128]{2,1,0:T(8,128)}, u32[]{:S(2)}) copy-start(f32[32,128,128]{2,1,0:T(8,128)} %h0.1) | copy-start | bytes 6291460
  0.0 22.3 %copy-start.3 = (s32[32]{0:T(128)S(1)}, s32[32]{0:T(128)}, u32[]{:S(2)}) copy-start(s32[32]{0:T(128)} %param.7) | copy-start | bytes 388
  0.0 22.1 %copy-start.4 = (s32[32]{0:T(128)S(1)}, s32[32]{0:T(128)}, u32[]{:S(2)}) copy-start(s32[32]{0:T(128)} %param.6) | copy-start | bytes 388
  0.0 22.4 %collective-permute-start.4 = (f32[32,128,128]{2,1,0:T(8,128)}, f32[32,128,128]{2,1,0:T(8,128)}, u32[]{:S(2)}, u32[]{:S(2)}) collective-permute-start(f32[32,128,128]{2,1,0:T(8,128)} %h0.1), channel_id=1, source_target_pairs={{0,1},{1,0},{2,3},{3,2},{4,5},{5,4},{6,7},{7,6},{8,9},{9,8},{10,11... | collective-permute-start | bytes 6291464 | tf_op jit(solution)/shard_map/ppermute | solution.py:189
  0.1 26.0 %collective-permute-start.1 = (f32[128,512]{1,0:T(8,128)}, f32[128,512]{1,0:T(8,128)S(1)}, u32[]{:S(2)}, u32[]{:S(2)}) collective-permute-start(f32[128,512]{1,0:T(8,128)} %c_ref.1), channel_id=1, source_target_pairs={{0,2},{2,4},{4,6},{6,0},{1,3},{3,5},{5,7},{7,1},{8,10},{10,12},{12... | collective-permute-start | bytes 786440 | tf_op jit(solution)/shard_map/ppermute | solution.py:193
  2.1 28.6 %collective-permute-start.2 = (f32[128,512]{1,0:T(8,128)}, f32[128,512]{1,0:T(8,128)}, u32[]{:S(2)}, u32[]{:S(2)}) collective-permute-start(f32[128,512]{1,0:T(8,128)} %c_ref.1), channel_id=1, source_target_pairs={{0,4},{2,6},{4,0},{6,2},{1,5},{3,7},{5,1},{7,3},{8,12},{10,14},{12... | collective-permute-start | bytes 786440 | tf_op jit(solution)/shard_map/ppermute | solution.py:193
  4.3 29.9 %collective-permute-start.3 = (f32[128,512]{1,0:T(8,128)}, f32[128,512]{1,0:T(8,128)}, u32[]{:S(2)}, u32[]{:S(2)}) collective-permute-start(f32[128,512]{1,0:T(8,128)} %c_ref.1), channel_id=1, source_target_pairs={{0,6},{2,0},{4,2},{6,4},{1,7},{3,1},{5,3},{7,5},{8,14},{10,8},{12,... | collective-permute-start | bytes 786440 | tf_op jit(solution)/shard_map/ppermute | solution.py:193
  5.5 16.8 %collective-permute-start = (s32[32]{0:T(128)}, s32[32]{0:T(128)S(1)}, u32[]{:S(2)}, u32[]{:S(2)}) collective-permute-start(s32[32]{0:T(128)} %param.7), channel_id=1, source_target_pairs={{0,1},{1,0},{2,3},{3,2},{4,5},{5,4},{6,7},{7,6},{8,9},{9,8},{10,11... | collective-permute-start | bytes 392 | tf_op jit(solution)/shard_map/ppermute | solution.py:189
  7.7 48.5 %all-to-all-start = ((f32[128,16,128]{2,1,0:T(8,128)}), f32[128,16,128]{2,1,0:T(8,128)S(1)}, u32[]{:S(2)}, u32[]{:S(2)}) async-start(f32[128,16,128]{2,1,0:T(8,128)} %bitcast.4), calls=%async_computation | async-start | bytes 2097152 | tf_op jit(solution)/shard_map/all_to_all | solution.py:242
  22.4 11.8 %copy-start.2 = (f32[128,512]{1,0:T(8,128)S(1)}, f32[128,512]{1,0:T(8,128)}, u32[]{:S(2)}) copy-start(f32[128,512]{1,0:T(8,128)} %c_ref.1) | copy-start | bytes 786436
  26.1 12.4 %copy-start = (bf16[64,128,256]{2,1,0:T(8,128)(2,1)}, bf16[64,128,256]{2,1,0:T(8,128)(2,1)S(1)}, u32[]{:S(2)}) copy-start(bf16[64,128,256]{2,1,0:T(8,128)(2,1)S(1)} %blocks_kernel.1.blocks.source) | copy-start | bytes 12582916
  38.4 2.7 %collective-permute-start.5 = (f32[16,128,128]{2,1,0:T(8,128)S(1)}, f32[16,128,128]{2,1,0:T(8,128)S(1)}, u32[]{:S(2)}, u32[]{:S(2)}) collective-permute-start(f32[16,128,128]{2,1,0:T(8,128)S(1)} %get-tuple-element.19), channel_id=1, source_target_pairs={{0,1},{1,0},{2,3},{3,2},{4,5},{5,4},{6,7},{7,6},{8,9},{9,8},{10,11... | collective-permute-start | bytes 3145736 | tf_op jit(solution)/shard_map/ppermute | solution.py:189
  41.3 23.0 %collective-permute-start.6 = (f32[4,128,128]{2,1,0:T(8,128)S(1)}, f32[4,128,128]{2,1,0:T(8,128)S(1)}, u32[]{:S(2)}, u32[]{:S(2)}) collective-permute-start(f32[4,128,128]{2,1,0:T(8,128)S(1)} %get-tuple-element.21), channel_id=1, source_target_pairs={{3,1},{4,2},{5,3},{6,4},{7,5},{11,9},{12,10},{13,11},{14,12},{15,1... | collective-permute-start | bytes 786440 | tf_op jit(solution)/shard_map/ppermute | solution.py:274
  42.6 23.5 %collective-permute-start.7 = (f32[4,128,128]{2,1,0:T(8,128)S(1)}, f32[4,128,128]{2,1,0:T(8,128)S(1)}, u32[]{:S(2)}, u32[]{:S(2)}) collective-permute-start(f32[4,128,128]{2,1,0:T(8,128)S(1)} %get-tuple-element.22), channel_id=1, source_target_pairs={{0,2},{1,3},{2,4},{3,5},{4,6},{8,10},{9,11},{10,12},{11,13},{12,14... | collective-permute-start | bytes 786440 | tf_op jit(solution)/shard_map/ppermute | solution.py:275
  47.2 18.9 %collective-permute-start.8 = (f32[4,128,128]{2,1,0:T(8,128)S(1)}, f32[4,128,128]{2,1,0:T(8,128)S(1)}, u32[]{:S(2)}, u32[]{:S(2)}) collective-permute-start(f32[4,128,128]{2,1,0:T(8,128)S(1)} %get-tuple-element.23), channel_id=1, source_target_pairs={{0,4},{7,3},{8,12},{15,11},{16,20},{23,19},{24,28},{31,27},{32,36}... | collective-permute-start | bytes 786440 | tf_op jit(solution)/shard_map/ppermute | solution.py:276
  59.8 15.3 %collective-permute-start.9 = (f32[20,16,128]{2,1,0:T(8,128)S(1)}, f32[20,16,128]{2,1,0:T(8,128)S(1)}, u32[]{:S(2)}, u32[]{:S(2)}) collective-permute-start(f32[20,16,128]{2,1,0:T(8,128)S(1)} %get-tuple-element.27), channel_id=1, source_target_pairs={{0,2},{2,4},{4,6},{6,0},{1,3},{3,5},{5,7},{7,1},{8,10},{10,12},{12... | collective-permute-start | bytes 491528 | tf_op jit(solution)/shard_map/ppermute | solution.py:193
  63.4 14.1 %collective-permute-start.10 = (f32[20,16,128]{2,1,0:T(8,128)S(1)}, f32[20,16,128]{2,1,0:T(8,128)S(1)}, u32[]{:S(2)}, u32[]{:S(2)}) collective-permute-start(f32[20,16,128]{2,1,0:T(8,128)S(1)} %get-tuple-element.28), channel_id=1, source_target_pairs={{0,4},{2,6},{4,0},{6,2},{1,5},{3,7},{5,1},{7,3},{8,12},{10,14},{12... | collective-permute-start | bytes 491528 | tf_op jit(solution)/shard_map/ppermute | solution.py:193
  64.3 14.0 %collective-permute-start.11 = (f32[20,16,128]{2,1,0:T(8,128)S(1)}, f32[20,16,128]{2,1,0:T(8,128)S(1)}, u32[]{:S(2)}, u32[]{:S(2)}) collective-permute-start(f32[20,16,128]{2,1,0:T(8,128)S(1)} %get-tuple-element.29), channel_id=1, source_target_pairs={{0,6},{2,0},{4,2},{6,4},{1,7},{3,1},{5,3},{7,5},{8,14},{10,8},{12,... | collective-permute-start | bytes 491528 | tf_op jit(solution)/shard_map/ppermute | solution.py:193

commit v15 on v11

--- a/solution.py
+++ b/solution.py
@@ -268,9 +268,9 @@
         [VMEM] * 2,
         keep, swap(send),
     )
+    edge = lax.ppermute(edge, ("z", "c"), [(0, 4), (7, 3)])
     down = lax.ppermute(down, ("z", "c"), [(3, 1), (4, 2), (5, 3), (6, 4), (7, 5)])
     up = lax.ppermute(up, ("z", "c"), [(0, 2), (1, 3), (2, 4), (3, 5), (4, 6)])
-    edge = lax.ppermute(edge, ("z", "c"), [(0, 4), (7, 3)])
     beta, done = call(
         planes_kernel,
         (shape(4, 128, 128), shape(8, 128)),

time: 103 us -> 103 us (level)
  no operation moved by 1% of the time
where the time goes in v15:
time: 103 us; the launch traced here: 102 us
  starting transfers between devices  32.5 us (32%)
  waiting for transfers between devices  30.1 us (29%)
  blocking collectives  21.7 us (21%)
  Pallas kernels  16.4 us (16%)
    all_to_all x1, blocking collectives, local(): back = lax.all_to_all(total, ROWS, 0, 0, tiled=True)  21.7 us
    ppermute x6, waiting for transfers between devices, shift(): return lax.ppermute(value, 'z', [(i, (i + by) % 4) for i in range(4)])  20.6 us
    pallas_call x8, Pallas kernels, call(): pl.pallas_call(kernel, out_shape=outs, in_specs=in_specs, out_specs=space...  16.4 us
    all_to_all x1, starting transfers between devices, local(): lax.all_to_all(at.reshape(2048, 128), ROWS + ('z',), 0, 0, tiled=True)  14.1 us
    ppermute x6, starting transfers between devices, shift(): return lax.ppermute(value, 'z', [(i, (i + by) % 4) for i in range(4)])  11.7 us
    all_to_all x1, waiting for transfers between devices, local(): lax.all_to_all(at.reshape(2048, 128), ROWS + ('z',), 0, 0, tiled=True)  6.85 us
    ppermute x1, starting transfers between devices, local(): up = lax.ppermute(up, ('z', 'c'), [(0, 2), (1, 3), (2, 4), (3, 5), (4, 6)])  4.55 us
    ppermute x3, waiting for transfers between devices, swap(): return lax.ppermute(value, 'c', [(0, 1), (1, 0)])  2.65 us
  transfers between devices with their start and end apart: 13, of which 7 were waited for; matrix products, arithmetic and copies ran while one was open for 1% of the time, Pallas kernels for 15%

profile of v15, /device:TPU:32, one launch (start us, length us, event | category | flops | bytes accessed | tf_op | source)
XLA Modules:
  0.0 101.5 jit_solution(9464079005896875084)
XLA Ops:
  0.0 0.1 collective-permute-start.4
  0.1 2.0 %collective-permute-start.1 = (f32[128,512]{1,0:T(8,128)}, f32[128,512]{1,0:T(8,128)S(1)}, u32[]{:S(2)}, u32[]{:S(2)}) collective-permute-start(f32[128,512]{1,0:T(8,128)} %c_ref.1), channel_id=1, source_target_pairs={{0,2},{2,4},{4,6},{6,0},{1,3},{3,5},{5,7},{7,1},{8,10},{10,12},{12... | collective-permute-start | bytes 786440 | tf_op jit(solution)/shard_map/ppermute | solution.py:191
  2.1 2.2 %collective-permute-start.2 = (f32[128,512]{1,0:T(8,128)}, f32[128,512]{1,0:T(8,128)}, u32[]{:S(2)}, u32[]{:S(2)}) collective-permute-start(f32[128,512]{1,0:T(8,128)} %c_ref.1), channel_id=1, source_target_pairs={{0,4},{2,6},{4,0},{6,2},{1,5},{3,7},{5,1},{7,3},{8,12},{10,14},{12... | collective-permute-start | bytes 786440 | tf_op jit(solution)/shard_map/ppermute | solution.py:191
  4.3 1.2 %collective-permute-start.3 = (f32[128,512]{1,0:T(8,128)}, f32[128,512]{1,0:T(8,128)}, u32[]{:S(2)}, u32[]{:S(2)}) collective-permute-start(f32[128,512]{1,0:T(8,128)} %c_ref.1), channel_id=1, source_target_pairs={{0,6},{2,0},{4,2},{6,4},{1,7},{3,1},{5,3},{7,5},{8,14},{10,8},{12,... | collective-permute-start | bytes 786440 | tf_op jit(solution)/shard_map/ppermute | solution.py:191
  5.5 2.2 %turn_kernel.1 = f32[32,4,16,128]{3,2,1,0:T(8,128)} custom-call(f32[128,512]{1,0:T(8,128)} %c_ref.1), custom_call_target="tpu_custom_call" | custom-call | bytes 1048576 | tf_op jit(solution)/shard_map/turn_kernel/pallas_call | solution.py:209
  7.7 14.1 %all-to-all-start = ((f32[128,16,128]{2,1,0:T(8,128)}), f32[128,16,128]{2,1,0:T(8,128)S(1)}, u32[]{:S(2)}, u32[]{:S(2)}) async-start(f32[128,16,128]{2,1,0:T(8,128)} %bitcast.4), calls=%async_computation | async-start | bytes 2097152 | tf_op jit(solution)/shard_map/all_to_all | solution.py:239
  21.8 0.1 add_multiply_fusion
  21.9 0.1 add.55
  22.0 0.1 select_reduce_fusion
  22.1 0.1 convert_reduce_fusion.owners
  22.3 0.1 compare_select_fusion.6
  22.4 3.6 %blocks_kernel.1.blocks.source = bf16[64,128,256]{2,1,0:T(8,128)(2,1)S(1)} custom-call(f32[32,128,128]{2,1,0:T(8,128)S(1)} %copy-done.1, f32[32,128,128]{2,1,0:T(8,128)} %collective-permute-done.4.h1), custom_call_target="tpu_custom_call" | custom-call | bytes 8388608 | tf_op jit(solution)/shard_map/blocks_kernel/pallas_call | solution.py:209
  26.0 4.8 %collective-permute-done.2.w2 = f32[128,512]{1,0:T(8,128)} collective-permute-done((f32[128,512]{1,0:T(8,128)}, f32[128,512]{1,0:T(8,128)}, u32[]{:S(2)}, u32[]{:S(2)}) %collective-permute-start.2) | collective-permute-done | bytes 262176 | tf_op jit(solution)/shard_map/ppermute | solution.py:191
  30.8 3.6 %collective-permute-done.3.w3 = f32[128,512]{1,0:T(8,128)} collective-permute-done((f32[128,512]{1,0:T(8,128)}, f32[128,512]{1,0:T(8,128)}, u32[]{:S(2)}, u32[]{:S(2)}) %collective-permute-start.3) | collective-permute-done | bytes 262176 | tf_op jit(solution)/shard_map/ppermute | solution.py:191
  34.4 5.4 %beta_kernel.1 = (f32[16,128,128]{2,1,0:T(8,128)S(1)}, f32[16,128,128]{2,1,0:T(8,128)S(1)}) custom-call(s32[4]{0:T(128)S(1)} %pad_add_fusion.where, s32[64]{0:T(128)S(1)} %get-tuple-element.32.cols, s32[64]{0:T(128)S(1)} %get-tuple-element.31.slots, f32[128,512]{1,0:T(8,128)S(1)} %copy-done.2, f32[128,512]{1,0:T(8,128)S(1)} %collective-permute-done.1.w1, ...), custom_call_target="tpu_custom_call" | custom-call | flops 40000000000 | bytes 7340032 | tf_op jit(solution)/shard_map/beta_kernel/pallas_call | solution.py:209
  39.9 0.1 collective-permute-start.5
  40.0 2.6 %collective-permute-done.5.got_ref = f32[16,128,128]{2,1,0:T(8,128)S(1)} collective-permute-done((f32[16,128,128]{2,1,0:T(8,128)S(1)}, f32[16,128,128]{2,1,0:T(8,128)S(1)}, u32[]{:S(2)}, u32[]{:S(2)}) %collective-permute-start.5) | collective-permute-done | bytes 1048608 | tf_op jit(solution)/shard_map/ppermute | solution.py:187
  42.6 0.2 cores_kernel.1
  42.8 1.3 %collective-permute-start.6 = (f32[4,128,128]{2,1,0:T(8,128)S(1)}, f32[4,128,128]{2,1,0:T(8,128)S(1)}, u32[]{:S(2)}, u32[]{:S(2)}) collective-permute-start(f32[4,128,128]{2,1,0:T(8,128)S(1)} %get-tuple-element.21), channel_id=1, source_target_pairs={{3,1},{4,2},{5,3},{6,4},{7,5},{11,9},{12,10},{13,11},{14,12},{15,1... | collective-permute-start | bytes 786440 | tf_op jit(solution)/shard_map/ppermute | solution.py:272
  44.1 4.6 %collective-permute-start.7 = (f32[4,128,128]{2,1,0:T(8,128)S(1)}, f32[4,128,128]{2,1,0:T(8,128)S(1)}, u32[]{:S(2)}, u32[]{:S(2)}) collective-permute-start(f32[4,128,128]{2,1,0:T(8,128)S(1)} %get-tuple-element.22), channel_id=1, source_target_pairs={{0,2},{1,3},{2,4},{3,5},{4,6},{8,10},{9,11},{10,12},{11,13},{12,14... | collective-permute-start | bytes 786440 | tf_op jit(solution)/shard_map/ppermute | solution.py:273
  48.6 0.7 collective-permute-start.8
  49.3 6.9 %all-to-all-done = f32[128,16,128]{2,1,0:T(8,128)S(1)} async-done(((f32[128,16,128]{2,1,0:T(8,128)}), f32[128,16,128]{2,1,0:T(8,128)S(1)}, u32[]{:S(2)}, u32[]{:S(2)}) %all-to-all-start) | async-done | bytes 1048608 | tf_op jit(solution)/shard_map/all_to_all | solution.py:239
  56.2 3.6 %alpha_kernel.1 = (f32[20,16,128]{2,1,0:T(8,128)S(1)}, f32[20,16,128]{2,1,0:T(8,128)S(1)}, f32[20,16,128]{2,1,0:T(8,128)S(1)}, f32[20,16,128]{2,1,0:T(8,128)S(1)}) custom-call(s32[4]{0:T(128)S(1)} %pad_add_fusion.where, s32[64]{0:T(128)S(1)} %get-tuple-element.32.cols, s32[64]{0:T(128)S(1)} %convert_reduce_fusion.owners, f32[32,64,128]{2,1,0:T(8,128)S(1)} %bitcast.6, ...), custom_call_target="tpu_custom_call" | custom-call | flops 40000000000 | bytes 7340032 | tf_op jit(solution)/shard_map/alpha_kernel/pallas_call | solution.py:209
  59.8 3.6 %collective-permute-start.9 = (f32[20,16,128]{2,1,0:T(8,128)S(1)}, f32[20,16,128]{2,1,0:T(8,128)S(1)}, u32[]{:S(2)}, u32[]{:S(2)}) collective-permute-start(f32[20,16,128]{2,1,0:T(8,128)S(1)} %get-tuple-element.27), channel_id=1, source_target_pairs={{0,2},{2,4},{4,6},{6,0},{1,3},{3,5},{5,7},{7,1},{8,10},{10,12},{12... | collective-permute-start | bytes 491528 | tf_op jit(solution)/shard_map/ppermute | solution.py:191
  63.4 0.9 collective-permute-start.10
  64.3 1.8 %collective-permute-start.11 = (f32[20,16,128]{2,1,0:T(8,128)S(1)}, f32[20,16,128]{2,1,0:T(8,128)S(1)}, u32[]{:S(2)}, u32[]{:S(2)}) collective-permute-start(f32[20,16,128]{2,1,0:T(8,128)S(1)} %get-tuple-element.29), channel_id=1, source_target_pairs={{0,6},{2,0},{4,2},{6,4},{1,7},{3,1},{5,3},{7,5},{8,14},{10,8},{12,... | collective-permute-start | bytes 491528 | tf_op jit(solution)/shard_map/ppermute | solution.py:191
  66.2 8.8 %collective-permute-done.9.p1 = f32[20,16,128]{2,1,0:T(8,128)S(1)} collective-permute-done((f32[20,16,128]{2,1,0:T(8,128)S(1)}, f32[20,16,128]{2,1,0:T(8,128)S(1)}, u32[]{:S(2)}, u32[]{:S(2)}) %collective-permute-start.9) | collective-permute-done | bytes 163872 | tf_op jit(solution)/shard_map/ppermute | solution.py:191
  75.0 2.5 %collective-permute-done.10.p2 = f32[20,16,128]{2,1,0:T(8,128)S(1)} collective-permute-done((f32[20,16,128]{2,1,0:T(8,128)S(1)}, f32[20,16,128]{2,1,0:T(8,128)S(1)}, u32[]{:S(2)}, u32[]{:S(2)}) %collective-permute-start.10) | collective-permute-done | bytes 163872 | tf_op jit(solution)/shard_map/ppermute | solution.py:191
  77.5 0.8 collective-permute-done.11.p3
  78.4 0.6 strings_kernel.1
  79.0 21.7 %all_to_all.14.back_ref = f32[32,16,128]{2,1,0:T(8,128)S(1)} all-to-all(f32[32,16,128]{2,1,0:T(8,128)S(1)} %strings_kernel.1), channel_id=1, replica_groups=mesh['y'=4,'h'=2,'x'=4,'z'=4,'c'=2] {'y','h','x'}, dimensions={0} | all-to-all | bytes 524288 | tf_op jit(solution)/shard_map/all_to_all | solution.py:299
  100.7 0.8 final_kernel.1
  (20 shorter events, 0.2 us)
Async XLA Ops:
  0.0 22.4 %copy-start.1 = (f32[32,128,128]{2,1,0:T(8,128)S(1)}, f32[32,128,128]{2,1,0:T(8,128)}, u32[]{:S(2)}) copy-start(f32[32,128,128]{2,1,0:T(8,128)} %h0.1) | copy-start | bytes 6291460
  0.0 22.3 %copy-start.3 = (s32[32]{0:T(128)S(1)}, s32[32]{0:T(128)}, u32[]{:S(2)}) copy-start(s32[32]{0:T(128)} %param.7) | copy-start | bytes 388
  0.0 22.0 %copy-start.4 = (s32[32]{0:T(128)S(1)}, s32[32]{0:T(128)}, u32[]{:S(2)}) copy-start(s32[32]{0:T(128)} %param.6) | copy-start | bytes 388
  0.0 22.4 %collective-permute-start.4 = (f32[32,128,128]{2,1,0:T(8,128)}, f32[32,128,128]{2,1,0:T(8,128)}, u32[]{:S(2)}, u32[]{:S(2)}) collective-permute-start(f32[32,128,128]{2,1,0:T(8,128)} %h0.1), channel_id=1, source_target_pairs={{0,1},{1,0},{2,3},{3,2},{4,5},{5,4},{6,7},{7,6},{8,9},{9,8},{10,11... | collective-permute-start | bytes 6291464 | tf_op jit(solution)/shard_map/ppermute | solution.py:187
  0.1 25.9 %collective-permute-start.1 = (f32[128,512]{1,0:T(8,128)}, f32[128,512]{1,0:T(8,128)S(1)}, u32[]{:S(2)}, u32[]{:S(2)}) collective-permute-start(f32[128,512]{1,0:T(8,128)} %c_ref.1), channel_id=1, source_target_pairs={{0,2},{2,4},{4,6},{6,0},{1,3},{3,5},{5,7},{7,1},{8,10},{10,12},{12... | collective-permute-start | bytes 786440 | tf_op jit(solution)/shard_map/ppermute | solution.py:191
  2.1 28.7 %collective-permute-start.2 = (f32[128,512]{1,0:T(8,128)}, f32[128,512]{1,0:T(8,128)}, u32[]{:S(2)}, u32[]{:S(2)}) collective-permute-start(f32[128,512]{1,0:T(8,128)} %c_ref.1), channel_id=1, source_target_pairs={{0,4},{2,6},{4,0},{6,2},{1,5},{3,7},{5,1},{7,3},{8,12},{10,14},{12... | collective-permute-start | bytes 786440 | tf_op jit(solution)/shard_map/ppermute | solution.py:191
  4.3 30.1 %collective-permute-start.3 = (f32[128,512]{1,0:T(8,128)}, f32[128,512]{1,0:T(8,128)}, u32[]{:S(2)}, u32[]{:S(2)}) collective-permute-start(f32[128,512]{1,0:T(8,128)} %c_ref.1), channel_id=1, source_target_pairs={{0,6},{2,0},{4,2},{6,4},{1,7},{3,1},{5,3},{7,5},{8,14},{10,8},{12,... | collective-permute-start | bytes 786440 | tf_op jit(solution)/shard_map/ppermute | solution.py:191
  5.5 16.8 %collective-permute-start = (s32[32]{0:T(128)}, s32[32]{0:T(128)S(1)}, u32[]{:S(2)}, u32[]{:S(2)}) collective-permute-start(s32[32]{0:T(128)} %param.7), channel_id=1, source_target_pairs={{0,1},{1,0},{2,3},{3,2},{4,5},{5,4},{6,7},{7,6},{8,9},{9,8},{10,11... | collective-permute-start | bytes 392 | tf_op jit(solution)/shard_map/ppermute | solution.py:187
  7.7 48.5 %all-to-all-start = ((f32[128,16,128]{2,1,0:T(8,128)}), f32[128,16,128]{2,1,0:T(8,128)S(1)}, u32[]{:S(2)}, u32[]{:S(2)}) async-start(f32[128,16,128]{2,1,0:T(8,128)} %bitcast.4), calls=%async_computation | async-start | bytes 2097152 | tf_op jit(solution)/shard_map/all_to_all | solution.py:239
  22.4 12.1 %copy-start.2 = (f32[128,512]{1,0:T(8,128)S(1)}, f32[128,512]{1,0:T(8,128)}, u32[]{:S(2)}) copy-start(f32[128,512]{1,0:T(8,128)} %c_ref.1) | copy-start | bytes 786436
  26.0 13.8 %copy-start = (bf16[64,128,256]{2,1,0:T(8,128)(2,1)}, bf16[64,128,256]{2,1,0:T(8,128)(2,1)S(1)}, u32[]{:S(2)}) copy-start(bf16[64,128,256]{2,1,0:T(8,128)(2,1)S(1)} %blocks_kernel.1.blocks.source) | copy-start | bytes 12582916
  39.9 2.7 %collective-permute-start.5 = (f32[16,128,128]{2,1,0:T(8,128)S(1)}, f32[16,128,128]{2,1,0:T(8,128)S(1)}, u32[]{:S(2)}, u32[]{:S(2)}) collective-permute-start(f32[16,128,128]{2,1,0:T(8,128)S(1)} %get-tuple-element.19), channel_id=1, source_target_pairs={{0,1},{1,0},{2,3},{3,2},{4,5},{5,4},{6,7},{7,6},{8,9},{9,8},{10,11... | collective-permute-start | bytes 3145736 | tf_op jit(solution)/shard_map/ppermute | solution.py:187
  42.8 21.5 %collective-permute-start.6 = (f32[4,128,128]{2,1,0:T(8,128)S(1)}, f32[4,128,128]{2,1,0:T(8,128)S(1)}, u32[]{:S(2)}, u32[]{:S(2)}) collective-permute-start(f32[4,128,128]{2,1,0:T(8,128)S(1)} %get-tuple-element.21), channel_id=1, source_target_pairs={{3,1},{4,2},{5,3},{6,4},{7,5},{11,9},{12,10},{13,11},{14,12},{15,1... | collective-permute-start | bytes 786440 | tf_op jit(solution)/shard_map/ppermute | solution.py:272
  44.1 22.0 %collective-permute-start.7 = (f32[4,128,128]{2,1,0:T(8,128)S(1)}, f32[4,128,128]{2,1,0:T(8,128)S(1)}, u32[]{:S(2)}, u32[]{:S(2)}) collective-permute-start(f32[4,128,128]{2,1,0:T(8,128)S(1)} %get-tuple-element.22), channel_id=1, source_target_pairs={{0,2},{1,3},{2,4},{3,5},{4,6},{8,10},{9,11},{10,12},{11,13},{12,14... | collective-permute-start | bytes 786440 | tf_op jit(solution)/shard_map/ppermute | solution.py:273
  48.6 17.5 %collective-permute-start.8 = (f32[4,128,128]{2,1,0:T(8,128)S(1)}, f32[4,128,128]{2,1,0:T(8,128)S(1)}, u32[]{:S(2)}, u32[]{:S(2)}) collective-permute-start(f32[4,128,128]{2,1,0:T(8,128)S(1)} %get-tuple-element.23), channel_id=1, source_target_pairs={{0,4},{7,3},{8,12},{15,11},{16,20},{23,19},{24,28},{31,27},{32,36}... | collective-permute-start | bytes 786440 | tf_op jit(solution)/shard_map/ppermute | solution.py:271
  59.8 15.2 %collective-permute-start.9 = (f32[20,16,128]{2,1,0:T(8,128)S(1)}, f32[20,16,128]{2,1,0:T(8,128)S(1)}, u32[]{:S(2)}, u32[]{:S(2)}) collective-permute-start(f32[20,16,128]{2,1,0:T(8,128)S(1)} %get-tuple-element.27), channel_id=1, source_target_pairs={{0,2},{2,4},{4,6},{6,0},{1,3},{3,5},{5,7},{7,1},{8,10},{10,12},{12... | collective-permute-start | bytes 491528 | tf_op jit(solution)/shard_map/ppermute | solution.py:191
  63.4 14.1 %collective-permute-start.10 = (f32[20,16,128]{2,1,0:T(8,128)S(1)}, f32[20,16,128]{2,1,0:T(8,128)S(1)}, u32[]{:S(2)}, u32[]{:S(2)}) collective-permute-start(f32[20,16,128]{2,1,0:T(8,128)S(1)} %get-tuple-element.28), channel_id=1, source_target_pairs={{0,4},{2,6},{4,0},{6,2},{1,5},{3,7},{5,1},{7,3},{8,12},{10,14},{12... | collective-permute-start | bytes 491528 | tf_op jit(solution)/shard_map/ppermute | solution.py:191
  64.3 14.1 %collective-permute-start.11 = (f32[20,16,128]{2,1,0:T(8,128)S(1)}, f32[20,16,128]{2,1,0:T(8,128)S(1)}, u32[]{:S(2)}, u32[]{:S(2)}) collective-permute-start(f32[20,16,128]{2,1,0:T(8,128)S(1)} %get-tuple-element.29), channel_id=1, source_target_pairs={{0,6},{2,0},{4,2},{6,4},{1,7},{3,1},{5,3},{7,5},{8,14},{10,8},{12,... | collective-permute-start | bytes 491528 | tf_op jit(solution)/shard_map/ppermute | solution.py:191
